TPU v7x, 256 devices: a whole 4x4x8 slice. The times are simulated.
256 devices in a mesh: dp: 16 (over z_lo, x, core), frame: 16 (over y, z_hi).
Axes of the slice: x: 4, y: 4, z: 8 (z_hi: 4, z_lo: 2; z = z_hi * 2 + z_lo), core: 2. Of those that a mesh axis runs over, the one named last changes fastest.
Arguments:
- clips: bfloat16 [16, 32, 16, 32, 320], P('dp', 'frame'), may hold values from -15 to 15
- cotangent: bfloat16 [16, 32, 16, 32, 320], P('dp', 'frame'), may hold values from -6 to 6
- spatial_weight: bfloat16 [3, 3, 320, 320], replicated, may hold values from -0.109375 to 0.109375
- temporal_weight: bfloat16 [3, 320, 320], replicated, may hold values from -0.1875 to 0.1875
- gain_one: float32 [320], replicated, may hold values from 0.1 to 1.9
- gain_two: float32 [320], replicated, may hold values from 0.1 to 1.9
Outputs:
- output: bfloat16 [16, 32, 16, 32, 320], P('dp', 'frame')
- input_grad: bfloat16 [16, 32, 16, 32, 320], P('dp', 'frame')
- spatial_grad: bfloat16 [3, 3, 320, 320], replicated
- temporal_grad: bfloat16 [3, 320, 320], replicated
All inputs are finite; a program needn't handle non-finite values.
Results may differ from a plain program's by a relative error of at most 0.0035.
The roundings to bfloat16 on the way count: a program that leaves them out, or rounds other values in their place, can miss the bound.
Values may be sent and summed in bfloat16 or wider, within the bound.
No kernel may reach another device: no remote copies, remote signals or barrier semaphores. Data moves between devices by JAX's collectives and lax.ppermute only.
A program may use at most 64 MiB of HBM per device.

v0:
```python
import jax
import jax.numpy as jnp
from jax import lax
from jax.sharding import PartitionSpec as P

GROUPS = 32


epsilon = 1e-05


def silu_slope(value):
    sigma = jax.nn.sigmoid(value)
    return sigma * (1.0 + value * (1.0 - sigma))


def group_view(value, groups):
    return value.reshape(value.shape[:-1] + (groups, value.shape[-1] // groups))


def spatial_conv(acts, weight):
    height, width = (acts.shape[1], acts.shape[2])
    padded = jnp.pad(acts, ((0, 0), (1, 1), (1, 1), (0, 0)))
    total = jnp.zeros(acts.shape[:-1] + (weight.shape[-1],), jnp.float32)
    for row_tap in range(3):
        for col_tap in range(3):
            window = padded[:, row_tap : row_tap + height, col_tap : col_tap + width, :]
            total = total + jnp.dot(
                window, weight[row_tap, col_tap], preferred_element_type=jnp.float32
            )
    return total


def spatial_back(grads, acts, weight):
    height, width, chans = (acts.shape[1], acts.shape[2], acts.shape[3])
    padded = jnp.pad(acts, ((0, 0), (1, 1), (1, 1), (0, 0)))
    grad_pad = jnp.pad(grads, ((0, 0), (1, 1), (1, 1), (0, 0)))
    flat_grads = grads.reshape(-1, grads.shape[-1])
    acts_grad = jnp.zeros(acts.shape, jnp.float32)
    pieces = []
    for row_tap in range(3):
        for col_tap in range(3):
            moved = grad_pad[
                :, 2 - row_tap : 2 - row_tap + height, 2 - col_tap : 2 - col_tap + width, :
            ]
            acts_grad = acts_grad + jnp.dot(
                moved, weight[row_tap, col_tap].T, preferred_element_type=jnp.float32
            )
            window = padded[:, row_tap : row_tap + height, col_tap : col_tap + width, :].reshape(
                -1, chans
            )
            pieces.append(jnp.dot(window.T, flat_grads, preferred_element_type=jnp.float32))
    return (acts_grad, jnp.stack(pieces).reshape(3, 3, chans, -1))


def temporal_conv(padded, weight):
    length = padded.shape[0] - 2
    total = jnp.zeros((length,) + padded.shape[1:-1] + (weight.shape[-1],), jnp.float32)
    for frame_tap in range(3):
        total = total + jnp.dot(
            padded[frame_tap : frame_tap + length],
            weight[frame_tap],
            preferred_element_type=jnp.float32,
        )
    return total


def temporal_back(grad_pad, padded, weight):
    length = padded.shape[0] - 2
    chans = padded.shape[-1]
    grads = grad_pad[1 : 1 + length].reshape(-1, grad_pad.shape[-1])
    mixed_grad = jnp.zeros((length,) + padded.shape[1:], jnp.float32)
    pieces = []
    for frame_tap in range(3):
        moved = grad_pad[2 - frame_tap : 2 - frame_tap + length]
        mixed_grad = mixed_grad + jnp.dot(
            moved, weight[frame_tap].T, preferred_element_type=jnp.float32
        )
        window = padded[frame_tap : frame_tap + length].reshape(-1, chans)
        pieces.append(jnp.dot(window.T, grads, preferred_element_type=jnp.float32))
    return (mixed_grad, jnp.stack(pieces))


def frame_pad(value):
    return jnp.pad(value, ((1, 1), (0, 0), (0, 0), (0, 0)))


def on_device(clips, cotangent, spatial_weight, temporal_weight, gain_one, gain_two):
    groups = GROUPS
    single = clips[0]
    single_grad = cotangent[0]
    inputs = single.astype(jnp.float32)
    view_one = group_view(inputs, groups)
    mean_one = jnp.mean(view_one, axis=(1, 2, 4), keepdims=True)
    var_one = jnp.mean(view_one * view_one, axis=(1, 2, 4), keepdims=True) - mean_one * mean_one
    inv_one = lax.rsqrt(var_one + epsilon)
    hat_one = ((view_one - mean_one) * inv_one).reshape(inputs.shape)
    pre_one = hat_one * gain_one
    acts = jax.nn.silu(pre_one).astype(jnp.bfloat16)
    hidden = (inputs + spatial_conv(acts, spatial_weight)).astype(jnp.bfloat16)
    hidden_full = hidden.astype(jnp.float32)
    view_two = group_view(hidden_full, groups)
    count = (
        view_two.shape[0]
        * lax.axis_size("frame")
        * view_two.shape[1]
        * view_two.shape[2]
        * view_two.shape[4]
    )
    local_sums = jnp.sum(view_two, axis=(0, 1, 2, 4))
    local_squares = jnp.sum(view_two * view_two, axis=(0, 1, 2, 4))
    total_sums, total_squares = lax.psum((local_sums, local_squares), "frame")
    mean_two = (total_sums / count)[:, None]
    var_two = (total_squares / count)[:, None] - mean_two * mean_two
    inv_two = lax.rsqrt(var_two + epsilon)
    hat_two = ((view_two - mean_two) * inv_two).reshape(inputs.shape)
    pre_two = hat_two * gain_two
    mixed = jax.nn.silu(pre_two).astype(jnp.bfloat16)
    rows_mixed, rows_grad = (
        lax.all_to_all(mixed[None], "frame", split_axis=2, concat_axis=1, tiled=True),
        lax.all_to_all(cotangent, "frame", split_axis=2, concat_axis=1, tiled=True),
    )
    mixed_pad = frame_pad(rows_mixed[0])
    temporal_rows = temporal_conv(mixed_pad, temporal_weight).astype(jnp.bfloat16)
    grad_rows, temporal_sum = temporal_back(frame_pad(rows_grad[0]), mixed_pad, temporal_weight)
    grad_rows = grad_rows.astype(jnp.bfloat16)
    back_temporal, back_grad = (
        lax.all_to_all(temporal_rows[None], "frame", split_axis=1, concat_axis=2, tiled=True),
        lax.all_to_all(grad_rows[None], "frame", split_axis=1, concat_axis=2, tiled=True),
    )
    temporal = back_temporal[0]
    mixed_grad = back_grad[0]
    output = (hidden_full + temporal.astype(jnp.float32)).astype(jnp.bfloat16)
    dhat_two = mixed_grad.astype(jnp.float32) * silu_slope(pre_two) * gain_two
    grad_view = group_view(dhat_two, groups)
    hat_view = group_view(hat_two, groups)
    local_first = jnp.sum(grad_view, axis=(0, 1, 2, 4))
    local_second = jnp.sum(grad_view * hat_view, axis=(0, 1, 2, 4))
    total_first, total_second = lax.psum((local_first, local_second), "frame")
    first = (total_first / count)[:, None]
    second = (total_second / count)[:, None]
    hidden_grad = single_grad.astype(jnp.float32) + (
        inv_two * (grad_view - first - hat_view * second)
    ).reshape(inputs.shape)
    hidden_low = hidden_grad.astype(jnp.bfloat16)
    acts_grad, spatial_sum = spatial_back(hidden_low, acts, spatial_weight)
    dhat_one = acts_grad * silu_slope(pre_one) * gain_one
    grad_one = group_view(dhat_one, groups)
    hat_onev = group_view(hat_one, groups)
    first_one = jnp.mean(grad_one, axis=(1, 2, 4), keepdims=True)
    second_one = jnp.mean(grad_one * hat_onev, axis=(1, 2, 4), keepdims=True)
    input_grad = (
        hidden_grad
        + (inv_one * (grad_one - first_one - hat_onev * second_one)).reshape(inputs.shape)
    ).astype(jnp.bfloat16)
    spatial_total, temporal_total = lax.psum((spatial_sum, temporal_sum), ("dp", "frame"))
    return (
        output[None],
        input_grad[None],
        spatial_total.astype(jnp.bfloat16),
        temporal_total.astype(jnp.bfloat16),
    )


def solution(mesh):
    return jax.shard_map(
        on_device,
        mesh=mesh,
        in_specs=(
            P("dp", "frame", None, None, None),
            P("dp", "frame", None, None, None),
            P(),
            P(),
            P(),
            P(),
        ),
        out_specs=(
            P("dp", "frame", None, None, None),
            P("dp", "frame", None, None, None),
            P(),
            P(),
        ),
        check_vma=False,
    )
```

profile of v0, /device:TPU:1, one launch (start us, length us, event | category | flops | bytes accessed | tf_op | source)
XLA Modules:
  0.0 335.1 jit_solution(10906879949854221706)
XLA Ops:
  0.6 2.2 copy.22
  2.9 11.9 %all-to-all-start.2 = ((bf16[1,2,16,32,320]{4,3,1,0,2:T(8,128)(2,1)}), bf16[1,2,16,32,320]{4,3,1,0,2:T(8,128)(2,1)S(1)}, u32[]{:S(2)}, u32[]{:S(2)}) async-start(bf16[1,2,16,32,320]{4,3,1,0,2:T(8,128)(2,1)} %copy.22), calls=%async_computation.2 | async-start | bytes 1572864 | tf_op jit(solution)/shard_map/all_to_all | solution.py:121
  16.4 2.9 fusion.99
  19.2 1.8 fusion.98
  21.0 1.8 fusion.97
  22.8 1.8 fusion.96
  24.6 1.8 fusion.95
  26.4 1.8 fusion.93
  28.2 1.8 fusion.94
  30.0 5.7 %all-to-all-done.2 = bf16[1,2,16,32,320]{4,3,1,0,2:T(8,128)(2,1)S(1)} async-done(((bf16[1,2,16,32,320]{4,3,1,0,2:T(8,128)(2,1)}), bf16[1,2,16,32,320]{4,3,1,0,2:T(8,128)(2,1)S(1)}, u32[]{:S(2)}, u32[]{:S(2)}) %all-to-all-start.2) | async-done | bytes 655392 | tf_op jit(solution)/shard_map/all_to_all | solution.py:121
  35.8 0.6 fusion.80
  36.4 0.6 fusion.121
  37.1 1.6 fusion.54
  38.7 6.1 %all-to-all-start.3 = ((bf16[1,32,1,32,320]{4,3,2,0,1:T(8,128)(2,1)}), bf16[1,32,1,32,320]{4,3,2,0,1:T(8,128)(2,1)S(1)}, u32[]{:S(2)}, u32[]{:S(2)}) async-start(bf16[1,32,1,32,320]{4,3,2,0,1:T(8,128)(2,1)} %fusion.54), calls=%async_computation.3 | async-start | bytes 1572864 | tf_op jit(solution)/shard_map/all_to_all | solution.py:129
  44.8 1.8 fusion.72
  48.2 3.1 convert_reduce_fusion.1
  51.8 40.1 %all-reduce.6 = (f32[32]{0:T(128)S(1)}, f32[32]{0:T(128)S(1)}) all-reduce(f32[32]{0:T(128)S(1)} %reduce_sum.112, f32[32]{0:T(128)S(1)} %reduce_sum.106), channel_id=1, replica_groups=mesh['dp'=16,'frame'=16] {'frame'}, use_global_device_ids=true, to_apply=%region_9.10 | all-reduce | flops 64 | bytes 512 | tf_op jit(solution)/shard_map/psum | solution.py:112
  92.2 2.5 fusion.180
  95.2 32.3 %all-reduce.5 = (f32[32]{0:T(128)S(1)}, f32[32]{0:T(128)S(1)}) all-reduce(f32[32]{0:T(128)S(1)} %reduce_sum.145, f32[32]{0:T(128)S(1)} %reduce_sum.115), channel_id=1, replica_groups=mesh['dp'=16,'frame'=16] {'frame'}, use_global_device_ids=true, to_apply=%region_15.16 | all-reduce | flops 64 | bytes 512 | tf_op jit(solution)/shard_map/psum | solution.py:139
  127.9 2.3 fusion.151
  130.9 0.6 fusion.69
  131.5 0.6 fusion.68
  132.2 0.6 fusion.108
  132.8 0.6 fusion.67
  133.5 0.6 fusion.66
  134.2 0.6 fusion.64
  134.8 0.6 fusion.65
  135.5 1.3 fusion.63
  136.8 2.8 fusion.179
  140.4 1.0 copy.18
  141.4 4.0 %all-to-all-start = ((bf16[1,2,16,32,320]{4,3,1,0,2:T(8,128)(2,1)}), bf16[1,2,16,32,320]{4,3,1,0,2:T(8,128)(2,1)S(1)}, u32[]{:S(2)}, u32[]{:S(2)}) async-start(bf16[1,2,16,32,320]{4,3,1,0,2:T(8,128)(2,1)} %copy.18), calls=%async_computation | async-start | bytes 1572864 | tf_op jit(solution)/shard_map/all_to_all | solution.py:120
  145.4 1.3 fusion.62
  146.8 1.3 fusion.61
  148.1 1.4 fusion.60
  149.4 1.3 fusion.59
  150.7 1.3 fusion.58
  152.1 1.3 fusion.57
  153.4 1.3 fusion.56
  154.7 1.3 fusion.55
  156.0 3.9 %all-to-all-done = bf16[1,2,16,32,320]{4,3,1,0,2:T(8,128)(2,1)S(1)} async-done(((bf16[1,2,16,32,320]{4,3,1,0,2:T(8,128)(2,1)}), bf16[1,2,16,32,320]{4,3,1,0,2:T(8,128)(2,1)S(1)}, u32[]{:S(2)}, u32[]{:S(2)}) %all-to-all-start) | async-done | bytes 655392 | tf_op jit(solution)/shard_map/all_to_all | solution.py:120
  160.0 1.6 fusion.83
  161.6 1.0 pad_slice_fusion.25
  163.4 1.5 fusion.53
  165.0 5.3 %all-to-all-start.1 = ((bf16[1,32,1,32,320]{4,3,2,0,1:T(8,128)(2,1)}), bf16[1,32,1,32,320]{4,3,2,0,1:T(8,128)(2,1)}, u32[]{:S(2)}, u32[]{:S(2)}) async-start(bf16[1,32,1,32,320]{4,3,2,0,1:T(8,128)(2,1)} %fusion.53), calls=%async_computation.1 | async-start | bytes 1572864 | tf_op jit(solution)/shard_map/all_to_all | solution.py:128
  170.3 1.7 convolution_bitcast_fusion
  173.0 1.2 pad_maximum_fusion
  174.2 156.8 %all-reduce.8 = (bf16[3,3,320,320]{3,2,1,0:T(8,128)(2,1)}, bf16[3,320,320]{2,1,0:T(8,128)(2,1)}) all-reduce(f32[3,3,320,320]{3,2,1,0:T(8,128)} %bitcast.347, f32[3,320,320]{2,1,0:T(8,128)} %pad_maximum_fusion), channel_id=1, replica_groups=mesh['dp'=16,'frame'=16] {'dp','frame'}, use_global_device_ids=true, to_apply=%region_20.21 | all-reduce | flops 1228800 | bytes 7372800 | tf_op jit(solution)/shard_map/psum | solution.py:156
  331.1 4.0 %fusion.76 = (bf16[1,2,16,32,320]{4,3,2,1,0:T(8,128)(2,1)}, bf16[1,2,16,32,320]{4,3,2,1,0:T(8,128)(2,1)}) fusion(bf16[1,2,16,32,320]{4,3,2,1,0:T(8,128)(2,1)S(1)} %copy-done, f32[2,16,32,320]{3,2,1,0:T(8,128)} %get-tuple-element.29, f32[2,320]{1,0:T(2,128)S(1)} %mul.203, f32[2,320]{1,0:T(2,128)S(1)} %sub.107, f32[2,320]{1,0:T(2,128)S(1)} %mul.167, ...), kind=kLoop, calls=%fused_computation.114 | loop fusion | flops 6881280 | bytes 6568960 | tf_op jit(solution)/shard_map/broadcast_in_dim | solution.py:159
  (81 shorter events, 8.1 us)
Async XLA Ops:
  0.6 14.1 %copy-start = (bf16[1,2,16,32,320]{4,3,2,1,0:T(8,128)(2,1)S(1)}, bf16[1,2,16,32,320]{4,3,2,1,0:T(8,128)(2,1)}, u32[]{:S(2)}) copy-start(bf16[1,2,16,32,320]{4,3,2,1,0:T(8,128)(2,1)} %param.6) | copy-start | bytes 1966084
  2.9 13.0 %copy-start.16 = (f32[320]{0:T(512)S(1)}, f32[320]{0:T(512)}, u32[]{:S(2)}) copy-start(f32[320]{0:T(512)} %param.10) | copy-start | bytes 3844
  2.9 32.9 %all-to-all-start.2 = ((bf16[1,2,16,32,320]{4,3,1,0,2:T(8,128)(2,1)}), bf16[1,2,16,32,320]{4,3,1,0,2:T(8,128)(2,1)S(1)}, u32[]{:S(2)}, u32[]{:S(2)}) async-start(bf16[1,2,16,32,320]{4,3,1,0,2:T(8,128)(2,1)} %copy.22), calls=%async_computation.2 | async-start | bytes 1572864 | tf_op jit(solution)/shard_map/all_to_all | solution.py:121
  16.4 2.9 copy-start.6
  28.2 7.6 %copy-start.14 = (bf16[3,320,320]{2,1,0:T(8,128)(2,1)S(1)}, bf16[3,320,320]{2,1,0:T(8,128)(2,1)}, u32[]{:S(2)}) copy-start(bf16[3,320,320]{2,1,0:T(8,128)(2,1)} %param.9) | copy-start | bytes 1843204
  35.8 1.3 copy-start.4
  38.7 53.5 %all-to-all-start.3 = ((bf16[1,32,1,32,320]{4,3,2,0,1:T(8,128)(2,1)}), bf16[1,32,1,32,320]{4,3,2,0,1:T(8,128)(2,1)S(1)}, u32[]{:S(2)}, u32[]{:S(2)}) async-start(bf16[1,32,1,32,320]{4,3,2,0,1:T(8,128)(2,1)} %fusion.54), calls=%async_computation.3 | async-start | bytes 1572864 | tf_op jit(solution)/shard_map/all_to_all | solution.py:129
  44.8 1.9 copy-start.8
  44.8 2.0 copy-start.9
  44.8 2.5 copy-start.10
  44.8 2.9 copy-start.11
  44.8 3.4 %copy-start.12 = (f32[2,16,32,320]{3,2,1,0:T(8,128)S(1)}, f32[2,16,32,320]{3,2,1,0:T(8,128)}, u32[]{:S(2)}) copy-start(f32[2,16,32,320]{3,2,1,0:T(8,128)} %fusion.95) | copy-start | bytes 3932164
  48.2 44.1 %copy-start.17 = (f32[320]{0:T(512)S(1)}, f32[320]{0:T(512)}, u32[]{:S(2)}) copy-start(f32[320]{0:T(512)} %param.11) | copy-start | bytes 3844
  51.3 76.6 %copy-start.2 = (bf16[2,16,32,320]{3,2,1,0:T(8,128)(2,1)}, bf16[2,16,32,320]{3,2,1,0:T(8,128)(2,1)S(1)}, u32[]{:S(2)}) copy-start(bf16[2,16,32,320]{3,2,1,0:T(8,128)(2,1)S(1)} %get-tuple-element.28) | copy-start | bytes 1966084
  127.9 2.3 copy-start.7
  136.8 3.7 %copy-start.13 = (bf16[1,2,16,32,320]{4,3,2,1,0:T(8,128)(2,1)S(1)}, bf16[1,2,16,32,320]{4,3,2,1,0:T(8,128)(2,1)}, u32[]{:S(2)}) copy-start(bf16[1,2,16,32,320]{4,3,2,1,0:T(8,128)(2,1)} %get-tuple-element.19) | copy-start | bytes 1966084
  141.4 18.5 %all-to-all-start = ((bf16[1,2,16,32,320]{4,3,1,0,2:T(8,128)(2,1)}), bf16[1,2,16,32,320]{4,3,1,0,2:T(8,128)(2,1)S(1)}, u32[]{:S(2)}, u32[]{:S(2)}) async-start(bf16[1,2,16,32,320]{4,3,1,0,2:T(8,128)(2,1)} %copy.18), calls=%async_computation | async-start | bytes 1572864 | tf_op jit(solution)/shard_map/all_to_all | solution.py:120
  161.5 1.3 copy-start.15
  165.0 5.3 %copy-start.5 = (bf16[1,2,16,32,320]{4,3,1,0,2:T(8,128)(2,1)S(1)}, bf16[1,2,16,32,320]{4,3,1,0,2:T(8,128)(2,1)}, u32[]{:S(2)}) copy-start(bf16[1,2,16,32,320]{4,3,1,0,2:T(8,128)(2,1)} %copy-done.4) | copy-start | bytes 1966084
  165.0 166.1 %all-to-all-start.1 = ((bf16[1,32,1,32,320]{4,3,2,0,1:T(8,128)(2,1)}), bf16[1,32,1,32,320]{4,3,2,0,1:T(8,128)(2,1)}, u32[]{:S(2)}, u32[]{:S(2)}) async-start(bf16[1,32,1,32,320]{4,3,2,0,1:T(8,128)(2,1)} %fusion.53), calls=%async_computation.1 | async-start | bytes 1572864 | tf_op jit(solution)/shard_map/all_to_all | solution.py:128
  174.2 156.8 %copy-start.1 = (f32[2,16,32,320]{3,2,1,0:T(8,128)S(1)}, f32[2,16,32,320]{3,2,1,0:T(8,128)}, u32[]{:S(2)}) copy-start(f32[2,16,32,320]{3,2,1,0:T(8,128)} %get-tuple-element.18) | copy-start | bytes 3932164
  174.2 156.8 %copy-start.3 = (bf16[2,16,32,320]{3,2,1,0:T(8,128)(2,1)S(1)}, bf16[2,16,32,320]{3,2,1,0:T(8,128)(2,1)}, u32[]{:S(2)}) copy-start(bf16[2,16,32,320]{3,2,1,0:T(8,128)(2,1)} %copy-done.2) | copy-start | bytes 1966084
where the time goes:
time: 337 us; the launch traced here: 335 us
  blocking collectives  229 us (68%)
  matrix products  47.8 us (14%)
  starting transfers between devices  27.2 us (8%)
  other arithmetic  11.6 us (3%)
  waiting for transfers between devices  9.68 us (3%)
  local copies, waits for them, and re-layouts  8.45 us (3%)
    psum x1, blocking collectives, on_device(): lax.psum((spatial_sum, temporal_sum), ('dp', 'frame'))  157 us
    psum x1, blocking collectives, on_device(): total_sums, total_squares = lax.psum((local_sums, local_squares), 'frame')  40.1 us
    psum x1, blocking collectives, on_device(): total_first, total_second = lax.psum((local_first, local_second), 'frame')  32.3 us
    dot_general x9, matrix products, spatial_conv(): jnp.dot(window, weight[row_tap, col_tap], preferred_element_type=jnp.floa...  18.6 us
    dot_general x9, matrix products, spatial_back(): jnp.dot(window.T, flat_grads, preferred_element_type=jnp.float32)  11.9 us
    all_to_all x1, starting transfers between devices, on_device(): lax.all_to_all(cotangent, 'frame', split_axis=2, concat_axis=1, tiled=True)  11.9 us
    dot_general x9, matrix products, spatial_back(): jnp.dot(moved, weight[row_tap, col_tap].T, preferred_element_type=jnp.flo...  7.98 us
  transfers between devices with their start and end apart: 4, of which 2 were waited for; matrix products, arithmetic and copies ran while one was open for 11% of the time, Pallas kernels for 0%

commit v1 on v0

v1 whole, which is shorter than its diff:
```python
import functools

import jax
import jax.numpy as jnp
from jax import lax
from jax.experimental import pallas as pl
from jax.experimental.pallas import tpu as pltpu
from jax.sharding import Mesh, PartitionSpec as P

epsilon = 1e-05

GROUPS = 32
DP = ("zl", "x", "c")
FRAME = ("y", "zh")
PLANE = ("x", "y")
LINE = ("zl", "zh")

C = 320
W = 32
PAD = 384
HALF = C // 2
PIX = 512
ROWS = 2 * PIX
STEP = 128
F32 = jnp.float32
BF16 = jnp.bfloat16

PARAMS = pltpu.CompilerParams(vmem_limit_bytes=56 * 1024 * 1024)


def call(body, out, scratch=(), flops=0):
    return pl.pallas_call(
        body,
        out_shape=out,
        scratch_shapes=list(scratch),
        compiler_params=PARAMS,
        cost_estimate=pl.CostEstimate(flops=flops, transcendentals=0, bytes_accessed=8_000_000),
    )


def shape(dims, kind):
    return jax.ShapeDtypeStruct(dims, kind)


def at(step, size=STEP):
    return pl.ds(pl.multiple_of(step * size, size), size)


def group_sum(rows):
    per = C // GROUPS
    one = lax.broadcasted_iota(jnp.int32, (C, C), 0) * 6554 >> 16
    two = lax.broadcasted_iota(jnp.int32, (C, C), 1) * 6554 >> 16
    assert per == 10
    same = jnp.where(one == two, 1.0, 0.0).astype(F32)
    return jnp.dot(rows, same, precision=lax.Precision.HIGHEST, preferred_element_type=F32)


def fold(value):
    return jnp.sum(value.reshape(value.shape[0] // 8, 8, value.shape[1]), axis=0)


def column(width):
    return lax.broadcasted_iota(jnp.int32, (STEP, width), 0) & (W - 1)


def four(*sums):
    return jnp.concatenate([jnp.sum(s, axis=0, keepdims=True) for s in sums] + [jnp.zeros((8 - len(sums), C), F32)])


def sigmoid(value):
    return 1.0 / (1.0 + jnp.exp(-value))


def forward_body(x_ref, w_ref, gain_ref, h0_ref, h1_ref, acts_ref, stat_ref, sums_ref, wf, x3, y):
    for i in range(3):
        for j in range(3):
            wf[C * j : C * (j + 1), PAD * i : PAD * i + C] = w_ref[3 * i + j]
    zero = jnp.zeros((8, C), F32)

    def moments(step, carry):
        value = x_ref[at(step), :].astype(F32)
        return carry[0] + fold(value), carry[1] + fold(value * value)

    half = PIX // STEP
    s0, q0 = lax.fori_loop(0, half, moments, (zero, zero))
    s1, q1 = lax.fori_loop(half, 2 * half, moments, (zero, zero))
    grouped = group_sum(four(s0, q0, s1, q1)) * (1.0 / (PIX * C // GROUPS))
    stats = []
    for f in range(2):
        mean = grouped[2 * f : 2 * f + 1]
        var = grouped[2 * f + 1 : 2 * f + 2] - mean * mean
        stats += [mean, lax.rsqrt(var + epsilon)]
    stat_ref[...] = jnp.concatenate(stats + [jnp.zeros((4, C), F32)])
    gain = gain_ref[...]
    edge = column(C)

    def activate(step, mean, scale):
        value = x_ref[at(step), :].astype(F32)
        pre = (value - mean) * scale * gain
        act = pre / (1.0 + jnp.exp(-pre))
        low = act.astype(BF16)
        acts_ref[at(step), :] = low
        act = low.astype(F32)
        x3[at(step), 0:C] = jnp.where(edge == 0, 0.0, pltpu.roll(act, 1, 0)).astype(BF16)
        x3[at(step), C : 2 * C] = low
        x3[at(step), 2 * C : 3 * C] = jnp.where(
            edge == W - 1, 0.0, pltpu.roll(act, STEP - 1, 0)
        ).astype(BF16)

    total = (zero, zero)
    for f in range(2):
        mean, scale = stats[2 * f], stats[2 * f + 1]

        def act_step(step, carry, mean=mean, scale=scale):
            activate(step, mean, scale)
            return carry

        lax.fori_loop(f * half, (f + 1) * half, act_step, 0)
        y[f, 0:W, :] = jnp.zeros((W, 3 * PAD), F32)
        y[f, W + PIX : 2 * W + PIX, :] = jnp.zeros((W, 3 * PAD), F32)
        y[f, W : W + PIX, :] = jnp.dot(
            x3[f * PIX : (f + 1) * PIX, :], wf[...], preferred_element_type=F32
        )

        h_ref = (h0_ref, h1_ref)[f]

        def finish(step, carry, f=f, h_ref=h_ref):
            base = pl.multiple_of(step * STEP, STEP)
            conv = (
                y[f, pl.ds(base, STEP), 0:C]
                + y[f, pl.ds(base + W, STEP), PAD : PAD + C]
                + y[f, pl.ds(base + 2 * W, STEP), 2 * PAD : 2 * PAD + C]
            )
            value = x_ref[pl.ds(base + f * PIX, STEP), :].astype(F32)
            low = (value + conv).astype(BF16)
            h_ref[pl.ds(base, STEP), :] = low
            value = low.astype(F32)
            return carry[0] + fold(value), carry[1] + fold(value * value)

        total = lax.fori_loop(0, half, finish, total)
    spread(total, sums_ref)


def spread(total, sums_ref):
    first = jnp.sum(total[0], axis=0, keepdims=True)
    second = jnp.sum(total[1], axis=0, keepdims=True)
    both = jnp.concatenate([first, second])
    for k in range(sums_ref.shape[0]):
        sums_ref[k] = both


def forward(x, weight, gain, peers):
    return call(
        forward_body,
        (
            shape((PIX, C), BF16),
            shape((PIX, C), BF16),
            shape((ROWS, C), BF16),
            shape((8, C), F32),
            shape((peers, 2, C), F32),
        ),
        (
            pltpu.VMEM((3 * C, 3 * PAD), BF16),
            pltpu.VMEM((ROWS, 3 * C), BF16),
            pltpu.VMEM((2, PIX + 2 * W, 3 * PAD), F32),
        ),
        flops=2_500_000_000,
    )(x, weight, gain)


def times_transposed(a, b):
    return lax.dot_general(a, b, (((1,), (1,)), ((), ())), preferred_element_type=F32)


def mixed_grad_body(before_ref, cot_ref, after_ref, w_ref, out_ref):
    for f in range(2):
        last = cot_ref[0:PIX, :] if f else before_ref[...]
        here = cot_ref[f * PIX : (f + 1) * PIX, :]
        later = after_ref[...] if f else cot_ref[PIX:ROWS, :]
        total = times_transposed(later, w_ref[0])
        total = total + times_transposed(here, w_ref[1])
        total = total + times_transposed(last, w_ref[2])
        out_ref[f * PIX : (f + 1) * PIX, :] = total.astype(BF16)


def mixed_gradient(before, cot, after, weight):
    return call(mixed_grad_body, shape((ROWS, C), BF16), flops=1_500_000_000)(
        before, cot, after, weight
    )


def clip_stats(sums_ref, count):
    total = jnp.sum(sums_ref[...], axis=0)
    grouped = group_sum(jnp.concatenate([total, jnp.zeros((6, C), F32)])) * (1.0 / count)
    return grouped[0:1], grouped[1:2]


def slope_body(count, sums_ref, h0_ref, h1_ref, grad_ref, gain_ref, dhat_ref, stat_ref, out_ref):
    mean, square = clip_stats(sums_ref, count)
    scale = lax.rsqrt(square - mean * mean + epsilon)
    stat_ref[...] = jnp.concatenate([mean, scale, jnp.zeros((6, C), F32)])
    gain = gain_ref[...]
    zero = jnp.zeros((8, C), F32)
    total = (zero, zero)
    for f, h_ref in enumerate((h0_ref, h1_ref)):

        def step_body(step, carry, f=f, h_ref=h_ref):
            base = pl.multiple_of(step * STEP, STEP)
            hat = (h_ref[pl.ds(base, STEP), :].astype(F32) - mean) * scale
            pre = hat * gain
            s = sigmoid(pre)
            slope = s * (1.0 + pre * (1.0 - s))
            dhat = grad_ref[pl.ds(base + f * PIX, STEP), :].astype(F32) * slope * gain
            dhat_ref[pl.ds(base + f * PIX, STEP), :] = dhat
            return carry[0] + fold(dhat), carry[1] + fold(dhat * hat)

        total = lax.fori_loop(0, PIX // STEP, step_body, total)
    spread(total, out_ref)


def slopes(sums, h0, h1, grad, gain, count):
    return call(
        functools.partial(slope_body, count),
        (shape((ROWS, C), F32), shape((8, C), F32), shape(sums.shape, F32)),
    )(sums, h0, h1, grad, gain)


def temporal_body(
    place_ref, hb_ref, h0_ref, h1_ref, ha_ref, cot_ref, w_ref, stat_ref, gain_ref,
    out_ref, keep_ref, give_ref, mx, mxt,
):
    mean, scale = stat_ref[0:1, :], stat_ref[1:2, :]
    gain = gain_ref[...]
    live = (place_ref[1], None, None, place_ref[2])
    for n, h_ref in enumerate((hb_ref, h0_ref, h1_ref, ha_ref)):

        def step_body(step, carry, n=n, h_ref=h_ref):
            base = pl.multiple_of(step * STEP, STEP)
            pre = (h_ref[pl.ds(base, STEP), :].astype(F32) - mean) * scale * gain
            act = pre / (1.0 + jnp.exp(-pre))
            if live[n] is not None:
                act = jnp.where(live[n] != 0, act, 0.0)
            act = act.astype(BF16)
            mx[pl.ds(base + n * PIX, STEP), :] = act
            return carry

        lax.fori_loop(0, PIX // STEP, step_body, 0)
    for n in range(4 * PIX // STEP):
        mxt[:, n * STEP : (n + 1) * STEP] = mx[n * STEP : (n + 1) * STEP, :].T
    for f, h_ref in enumerate((h0_ref, h1_ref)):
        total = None
        for k in range(3):
            part = jnp.dot(
                mx[(f + k) * PIX : (f + k + 1) * PIX, :], w_ref[k], preferred_element_type=F32
            )
            total = part if total is None else total + part
        low = total.astype(BF16).astype(F32)
        out_ref[f * PIX : (f + 1) * PIX, :] = (h_ref[...].astype(F32) + low).astype(BF16)
    core = place_ref[0]
    for k in range(3):
        part = jnp.dot(
            mxt[:, k * PIX : k * PIX + ROWS], cot_ref[...], preferred_element_type=F32
        )
        left, right = part[:, 0:HALF], part[:, HALF:C]
        keep_ref[k * C : (k + 1) * C, 0:HALF] = jnp.where(core == 0, left, right)
        give_ref[k * C : (k + 1) * C, 0:HALF] = jnp.where(core == 0, right, left)


SMEM = pl.BlockSpec(memory_space=pltpu.SMEM)
VMEM = pl.BlockSpec(memory_space=pltpu.VMEM)


def call_with_place(body, operands, out, scratch=(), flops=0):
    return pl.pallas_call(
        body,
        out_shape=out,
        in_specs=[SMEM] + [VMEM] * operands,
        scratch_shapes=list(scratch),
        compiler_params=PARAMS,
        cost_estimate=pl.CostEstimate(flops=flops, transcendentals=0, bytes_accessed=8_000_000),
    )


def temporal(place, before, h0, h1, after, cot, weight, stat, gain):
    return call_with_place(
        temporal_body,
        8,
        (shape((ROWS, C), BF16), shape((3 * C, 256), F32), shape((3 * C, 256), F32)),
        (pltpu.VMEM((4 * PIX, C), BF16), pltpu.VMEM((C, 4 * PIX), BF16)),
        flops=3_000_000_000,
    )(place, before, h0, h1, after, cot, weight, stat, gain)


def turned_body(acts_ref, out_ref):
    lane = lax.broadcasted_iota(jnp.int32, (C, STEP), 1) & (W - 1)
    for step in range(ROWS // STEP):
        turned = acts_ref[step * STEP : (step + 1) * STEP, :].astype(F32).T
        where = slice(step * STEP, (step + 1) * STEP)
        out_ref[0:C, where] = jnp.where(lane == 0, 0.0, pltpu.roll(turned, 1, 1)).astype(BF16)
        out_ref[C : 2 * C, where] = turned.astype(BF16)
        out_ref[2 * C : 3 * C, where] = jnp.where(
            lane == W - 1, 0.0, pltpu.roll(turned, STEP - 1, 1)
        ).astype(BF16)


def turned(acts):
    return call(turned_body, shape((3 * C, ROWS), BF16), flops=500_000_000)(acts)


def hidden_grad_body(
    count, place_ref, sums_ref, stat_ref, dhat_ref, h0_ref, h1_ref, cot_ref,
    grad_ref, low_ref, keep_ref, give_ref,
):
    first, second = clip_stats(sums_ref, count)
    mean, scale = stat_ref[0:1, :], stat_ref[1:2, :]
    core = place_ref[0]
    for f, h_ref in enumerate((h0_ref, h1_ref)):

        def step_body(step, carry, f=f, h_ref=h_ref):
            base = pl.multiple_of(step * STEP, STEP)
            here = pl.ds(base + f * PIX, STEP)
            hat = (h_ref[pl.ds(base, STEP), :].astype(F32) - mean) * scale
            grad = cot_ref[here, :].astype(F32) + scale * (dhat_ref[here, :] - first - hat * second)
            grad_ref[here, :] = grad
            low = grad.astype(BF16)
            low_ref[here, :] = low
            left, right = grad[:, 0:HALF], grad[:, HALF:C]
            keep_ref[here, :] = jnp.where(core == 0, left, right).astype(BF16)
            give_ref[here, :] = jnp.where(core == 0, right, left).astype(BF16)
            return carry

        lax.fori_loop(0, PIX // STEP, step_body, 0)


def hidden_gradient(place, sums, stat, dhat, h0, h1, cot, count):
    return call_with_place(
        functools.partial(hidden_grad_body, count),
        7 - 1,
        (
            shape((ROWS, C), F32),
            shape((ROWS, C), BF16),
            shape((ROWS, HALF), BF16),
            shape((ROWS, HALF), BF16),
        ),
    )(place, sums, stat, dhat, h0, h1, cot)


def row_taps(value):
    none = jnp.zeros((W, value.shape[1]), value.dtype)
    return (
        jnp.concatenate([value[W:], none]),
        value,
        jnp.concatenate([none, value[: PIX - W]]),
    )


def weight_grad_body(
    mine_turned_ref, other_turned_ref, mine_ref, other_ref, keep_ref, got_ref, out_ref, rhs
):
    total = None
    for n, (ref, turned_ref) in enumerate(
        ((mine_ref, mine_turned_ref), (other_ref, other_turned_ref))
    ):
        for f in range(2):
            where = slice(f * PIX, (f + 1) * PIX)
            for i, tap in enumerate(row_taps(ref[where, :])):
                rhs[n, where, i * HALF : (i + 1) * HALF] = tap
        part = jnp.dot(turned_ref[...], rhs[n], preferred_element_type=F32)
        total = part if total is None else total + part
    out_ref[0 : 3 * C, 0 : 3 * HALF] = total
    out_ref[0 : 3 * C, 3 * HALF : 4 * HALF] = keep_ref[:, 0:HALF] + got_ref[:, 0:HALF]
    out_ref[3 * C :, :] = jnp.zeros((1024 - 3 * C, 4 * HALF), F32)


def weight_gradients(mine_turned, other_turned, mine, other, keep, got):
    return call(
        weight_grad_body,
        shape((1024, 4 * HALF), F32),
        (pltpu.VMEM((2, ROWS, 3 * HALF), BF16),),
        flops=2_500_000_000,
    )(mine_turned, other_turned, mine, other, keep, got)


def input_grad_body(low_ref, grad_ref, x_ref, stat_ref, gain_ref, w_ref, out_ref, wb, rows, z, dh):
    for j in range(3):
        for i in range(3):
            wb[PAD * j : PAD * j + C, C * i : C * (i + 1)] = w_ref[3 * i + j]
        wb[PAD * j + C : PAD * (j + 1), :] = jnp.zeros((PAD - C, 3 * C), BF16)
    gain = gain_ref[...]
    edge = column(C)
    half = PIX // STEP
    for f in range(2):
        mean, scale = stat_ref[2 * f : 2 * f + 1, :], stat_ref[2 * f + 1 : 2 * f + 2, :]
        for i, tap in enumerate(row_taps(low_ref[f * PIX : (f + 1) * PIX, :])):
            rows[:, i * C : (i + 1) * C] = tap
        z[...] = times_transposed(rows[...], wb[...])

        def step_body(step, carry, f=f, mean=mean, scale=scale):
            base = pl.multiple_of(step * STEP, STEP)
            here = pl.ds(base, STEP)
            right = jnp.where(edge == W - 1, 0.0, pltpu.roll(z[here, 0:C], STEP - 1, 0))
            left = jnp.where(edge == 0, 0.0, pltpu.roll(z[here, 2 * PAD : 2 * PAD + C], 1, 0))
            acts_grad = right + z[here, PAD : PAD + C] + left
            hat = (x_ref[pl.ds(base + f * PIX, STEP), :].astype(F32) - mean) * scale
            pre = hat * gain
            s = sigmoid(pre)
            dhat = acts_grad * (s * (1.0 + pre * (1.0 - s))) * gain
            dh[here, :] = dhat
            return carry[0] + fold(dhat), carry[1] + fold(dhat * hat)

        zero = jnp.zeros((8, C), F32)
        sums = lax.fori_loop(0, half, step_body, (zero, zero))
        grouped = group_sum(four(*sums)) * (1.0 / (PIX * C // GROUPS))
        first, second = grouped[0:1], grouped[1:2]

        def last_body(step, carry, f=f, mean=mean, scale=scale, first=first, second=second):
            base = pl.multiple_of(step * STEP, STEP)
            there = pl.ds(base + f * PIX, STEP)
            hat = (x_ref[there, :].astype(F32) - mean) * scale
            value = grad_ref[there, :] + scale * (dh[pl.ds(base, STEP), :] - first - hat * second)
            out_ref[there, :] = value.astype(BF16)
            return carry

        lax.fori_loop(0, half, last_body, 0)


def input_gradient(low, grad, x, stat, gain, weight):
    return call(
        input_grad_body,
        shape((ROWS, C), BF16),
        (
            pltpu.VMEM((3 * PAD, 3 * C), BF16),
            pltpu.VMEM((PIX, 3 * C), BF16),
            pltpu.VMEM((PIX, 3 * PAD), F32),
            pltpu.VMEM((PIX, C), F32),
        ),
        flops=2_500_000_000,
    )(low, grad, x, stat, gain, weight)


def unpack_body(place_ref, mine_ref, other_ref, spatial_ref, temporal_ref):
    core = place_ref[0]
    for j in range(3):
        here = slice(j * C, (j + 1) * C)
        mine, other = mine_ref[here, :], other_ref[here, :]
        left = jnp.where(core == 0, mine, other)
        right = jnp.where(core == 0, other, mine)
        for i in range(4):
            lanes = slice(i * HALF, (i + 1) * HALF)
            if i < 3:
                spatial_ref[3 * i + j, :, 0:HALF] = left[:, lanes]
                spatial_ref[3 * i + j, :, HALF:C] = right[:, lanes]
            else:
                temporal_ref[j, :, 0:HALF] = left[:, lanes]
                temporal_ref[j, :, HALF:C] = right[:, lanes]


def unpack(place, mine, other):
    return call_with_place(
        unpack_body, 2, (shape((9, C, C), BF16), shape((3, C, C), BF16))
    )(place, mine, other)


def neighbours(first, second):
    size = lax.axis_size(FRAME)
    before = lax.ppermute(second, FRAME, [(i, i + 1) for i in range(size - 1)])
    after = lax.ppermute(first, FRAME, [(i + 1, i) for i in range(size - 1)])
    return before, after


def swap_cores(value):
    return lax.ppermute(value, "c", [(0, 1), (1, 0)])


def everyone_total(value, beside):
    plane, line = lax.axis_size(PLANE), lax.axis_size(LINE)
    width = value.shape[1]
    value = value.reshape(plane, 1024 // plane, width)
    value = lax.all_to_all(value, PLANE, 0, 0)
    value, beside = lax.optimization_barrier((value, beside))
    value = jnp.sum(value, axis=0)
    value = value.reshape(line, 1024 // plane // line, width)
    value = jnp.sum(lax.all_to_all(value, LINE, 0, 0), axis=0).astype(BF16)
    value = jnp.broadcast_to(value[None], (line,) + value.shape)
    value = lax.all_to_all(value, LINE, 0, 0).reshape(1024 // plane, width)
    value = jnp.broadcast_to(value[None], (plane,) + value.shape)
    return lax.all_to_all(value, PLANE, 0, 0).reshape(1024, width), beside


def on_device(clips, cotangent, spatial_weight, temporal_weight, gain_one, gain_two):
    size = lax.axis_size(FRAME)
    place = lax.axis_index(FRAME)
    place = jnp.stack(
        [lax.axis_index("c"), (place > 0).astype(jnp.int32), (place < size - 1).astype(jnp.int32)]
    )
    count = float(size * ROWS * C // GROUPS)
    x = clips.reshape(ROWS, C)
    cot = cotangent.reshape(ROWS, C)
    spatial_weight = spatial_weight.reshape(9, C, C)
    gain_one = gain_one.reshape(1, C)
    gain_two = gain_two.reshape(1, C)
    cot_before, cot_after = neighbours(cot[:PIX], cot[PIX:])
    h0, h1, acts, stat_one, sums = forward(x, spatial_weight, gain_one, size)
    sums = lax.all_to_all(sums, FRAME, 0, 0)
    before, after = neighbours(h0, h1)
    mine_turned = turned(acts)
    mixed_grad = mixed_gradient(cot_before, cot, cot_after, temporal_weight)
    sums, mine_turned, mixed_grad = lax.optimization_barrier((sums, mine_turned, mixed_grad))
    other_turned = swap_cores(mine_turned)
    dhat, stat_two, sums = slopes(sums, h0, h1, mixed_grad, gain_two, count)
    sums = lax.all_to_all(sums, FRAME, 0, 0)
    output, temporal_keep, temporal_give = temporal(
        place, before, h0, h1, after, cot, temporal_weight, stat_two, gain_two
    )
    sums, temporal_give, other_turned = lax.optimization_barrier(
        (sums, temporal_give, other_turned)
    )
    temporal_got = swap_cores(temporal_give)
    grad, low, low_keep, low_give = hidden_gradient(
        place, sums, stat_two, dhat, h0, h1, cot, count
    )
    low_got = swap_cores(low_give)
    packed = weight_gradients(
        mine_turned, other_turned, low_keep, low_got, temporal_keep, temporal_got
    )
    packed, low = lax.optimization_barrier((packed, low))
    input_grad = input_gradient(low, grad, x, stat_one, gain_one, spatial_weight)
    mine, input_grad = everyone_total(packed, input_grad)
    other = swap_cores(mine)
    spatial_grad, temporal_grad = unpack(place, mine, other)
    return (
        output.reshape(clips.shape),
        input_grad.reshape(clips.shape),
        spatial_grad.reshape(3, 3, C, C),
        temporal_grad,
    )


def solution(mesh):
    fine = Mesh(mesh.devices.reshape(2, 4, 2, 4, 4), ("zl", "x", "c", "y", "zh"))
    return jax.shard_map(
        on_device,
        mesh=fine,
        in_specs=(P(DP, FRAME), P(DP, FRAME), P(), P(), P(), P()),
        out_specs=(P(DP, FRAME), P(DP, FRAME), P(), P()),
        check_vma=False,
    )
```

time: 337 us -> 193 us (0.57)
  blocking collectives: 229 us -> 43.6 us
  Pallas kernels: 0 us -> 55.8 us
  matrix products: 47.8 us -> 0 us
  waiting for transfers between devices: 9.68 us -> 35 us
  starting transfers between devices: 27.2 us -> 50.4 us
  other arithmetic: 11.6 us -> 0.8 us
    psum x3 -> x0, blocking collectives: 229 us -> none  [the longest x1 157 us: on_device(): lax.psum((spatial_sum, temporal_sum), ('dp', 'frame'))]
    pallas_call x0 -> x9, Pallas kernels: none -> 55.8 us  [the longest x1 10.4 us: input_gradient(): call(input_grad_body, shape((ROWS, C), BF16), (pltpu.VMEM((3 * PAD, 3 * C...]
    dot_general x36 -> x0, matrix products: 47.8 us -> none  [the longest x9 18.6 us: spatial_conv(): jnp.dot(window, weight[row_tap, col_tap], preferred_element_type=jnp.floa...]
    all_to_all x0 -> x3, blocking collectives: none -> 43.6 us  [the longest x1 22 us: everyone_total(): return (lax.all_to_all(value, PLANE, 0, 0).reshape(1024, width), beside)]
    ppermute x0 -> x8, starting transfers between devices: none -> 20.8 us  [the longest x4 9.76 us: swap_cores(): return lax.ppermute(value, 'c', [(0, 1), (1, 0)])]
    all_to_all x4 -> x3, waiting for transfers between devices: 9.68 us -> 25.2 us  [the longest x1 24.3 us: everyone_total(): value = lax.all_to_all(value, PLANE, 0, 0)]
    ppermute x0 -> x8, waiting for transfers between devices: none -> 9.86 us  [the longest x2 5.39 us: neighbours(): after = lax.ppermute(first, FRAME, [(i + 1, i) for i in range(size - 1)])]
    broadcast_in_dim x1 -> x0, other arithmetic: 4.04 us -> none  [on_device(): input_grad[None]]
  transfers between devices with their start and end apart: 4 -> 11, of which waited for: 2 -> 5; matrix products, arithmetic and copies ran while one was open for 11% -> 1% of each run, Pallas kernels for 0% -> 23%
where the time goes in v1:
time: 193 us
  Pallas kernels  55.8 us (29%)
  starting transfers between devices  50.4 us (26%)
  blocking collectives  43.6 us (23%)
  waiting for transfers between devices  35 us (18%)
  local copies, waits for them, and re-layouts  6.31 us (3%)
    all_to_all x1, waiting for transfers between devices, everyone_total(): value = lax.all_to_all(value, PLANE, 0, 0)  24.3 us
    all_to_all x2, starting transfers between devices, on_device(): sums = lax.all_to_all(sums, FRAME, 0, 0)  23.1 us
    all_to_all x1, blocking collectives, everyone_total(): return (lax.all_to_all(value, PLANE, 0, 0).reshape(1024, width), beside)  22 us
    all_to_all x1, blocking collectives, everyone_total(): value = jnp.sum(lax.all_to_all(value, LINE, 0, 0), axis=0).astype(BF16)  12.1 us
    pallas_call x1, Pallas kernels, input_gradient(): call(input_grad_body, shape((ROWS, C), BF16), (pltpu.VMEM((3 * PAD, 3 * C...  10.4 us
    ppermute x4, starting transfers between devices, swap_cores(): return lax.ppermute(value, 'c', [(0, 1), (1, 0)])  9.76 us
    all_to_all x1, blocking collectives, everyone_total(): value = lax.all_to_all(value, LINE, 0, 0).reshape(1024 // plane, width)  9.52 us
    pallas_call x1, Pallas kernels, forward(): call(forward_body, (shape((PIX, C), BF16), shape((PIX, C), BF16), shape((...  9.38 us
  transfers between devices with their start and end apart: 11, of which 5 were waited for; matrix products, arithmetic and copies ran while one was open for 1% of the time, Pallas kernels for 23%

profile of v1, /device:TPU:1, one launch (start us, length us, event | category | flops | bytes accessed | tf_op | source)
XLA Modules:
  0.0 192.7 jit_solution(15593719096792071544)
XLA Ops:
  0.6 1.2 fusion
  1.8 5.7 %collective-permute-start.2 = (bf16[512,320]{1,0:T(8,128)(2,1)S(1)}, bf16[512,320]{1,0:T(8,128)(2,1)S(1)}, u32[]{:S(2)}, u32[]{:S(2)}) collective-permute-start(bf16[512,320]{1,0:T(8,128)(2,1)S(1)} %bitcast.23), channel_id=1, source_target_pairs={{0,1},{1,2},{2,3},{3,4},{4,5},{5,6},{6,7},{7,8},{8,9},{9,10},{10,1... | collective-permute-start | bytes 983048 | tf_op jit(solution)/shard_map/ppermute | solution.py:466
  7.6 1.3 collective-permute-start.3
  8.9 1.3 reshape.49.gain_ref
  10.2 9.4 %shard_map.93 = (bf16[512,320]{1,0:T(8,128)(2,1)}, bf16[512,320]{1,0:T(8,128)(2,1)}, bf16[1024,320]{1,0:T(8,128)(2,1)}, f32[8,320]{1,0:T(8,128)}, f32[16,2,320]{2,1,0:T(2,128)}) custom-call(bf16[1024,320]{1,0:T(8,128)(2,1)} %bitcast.28, bf16[9,320,320]{2,1,0:T(8,128)(2,1)} %bitcast.25, f32[1,320]{1,0:T(1,128)} %reshape.49.gain_ref), custom_call_target="tpu_custom_call" | custom-call | flops 2500000000 | bytes 8000000 | tf_op jit(solution)/shard_map/pallas_call | solution.py:153
  19.5 12.1 %all-to-all-start = ((f32[16,2,320]{2,1,0:T(2,128)}), f32[16,2,320]{2,1,0:T(2,128)S(1)}, u32[]{:S(2)}, u32[]{:S(2)}) async-start(f32[16,2,320]{2,1,0:T(2,128)} %get-tuple-element.33), calls=%async_computation | async-start | bytes 98304 | tf_op jit(solution)/shard_map/all_to_all | solution.py:504
  31.6 3.1 %shard_map.94.mine_turned_ref = bf16[960,1024]{1,0:T(8,128)(2,1)} custom-call(bf16[1024,320]{1,0:T(8,128)(2,1)} %get-tuple-element.34.acts_ref), custom_call_target="tpu_custom_call" | custom-call | flops 500000000 | bytes 8000000 | tf_op jit(solution)/shard_map/pallas_call | solution.py:307
  34.7 0.0 collective-permute-done.2.before_ref
  34.7 0.0 collective-permute-done.3.after_ref
  34.7 0.0 copy-start.12
  34.7 0.8 copy-done.12
  35.5 0.1 copy-done.11
  35.6 4.2 %shard_map.95.grad_ref = bf16[1024,320]{1,0:T(8,128)(2,1)} custom-call(bf16[512,320]{1,0:T(8,128)(2,1)} %copy-done.11, bf16[1024,320]{1,0:T(8,128)(2,1)} %bitcast.18, bf16[512,320]{1,0:T(8,128)(2,1)} %copy-done.12, bf16[3,320,320]{2,1,0:T(8,128)(2,1)} %w_ref.3), custom_call_target="tpu_custom_call" | custom-call | flops 1500000000 | bytes 8000000 | tf_op jit(solution)/shard_map/pallas_call | solution.py:187
  39.8 0.8 all-to-all-done.sums_ref
  40.7 2.6 %collective-permute-start.4 = (bf16[960,1024]{1,0:T(8,128)(2,1)S(1)}, bf16[960,1024]{1,0:T(8,128)(2,1)}, u32[]{:S(2)}, u32[]{:S(2)}) collective-permute-start(bf16[960,1024]{1,0:T(8,128)(2,1)S(1)} %copy-done), channel_id=1, source_target_pairs={{0,16},{16,0},{1,17},{17,1},{2,18},{18,2},{3,19},{19,3},{4,20},{20... | collective-permute-start | bytes 5898248 | tf_op jit(solution)/shard_map/ppermute | solution.py:472
  43.2 2.7 %collective-permute-start = (bf16[512,320]{1,0:T(8,128)(2,1)S(1)}, bf16[512,320]{1,0:T(8,128)(2,1)S(1)}, u32[]{:S(2)}, u32[]{:S(2)}) collective-permute-start(bf16[512,320]{1,0:T(8,128)(2,1)S(1)} %copy-done.3), channel_id=1, source_target_pairs={{0,1},{1,2},{2,3},{3,4},{4,5},{5,6},{6,7},{7,8},{8,9},{9,10},{10,1... | collective-permute-start | bytes 983048 | tf_op jit(solution)/shard_map/ppermute | solution.py:466
  45.9 1.3 collective-permute-start.1
  47.2 0.6 reshape.51.gain_ref
  47.8 0.7 pad_add_fusion.place_ref
  48.5 0.0 copy-done.7
  48.5 4.2 %shard_map.96 = (f32[1024,320]{1,0:T(8,128)}, f32[8,320]{1,0:T(8,128)}, f32[16,2,320]{2,1,0:T(2,128)}) custom-call(f32[16,2,320]{2,1,0:T(2,128)} %copy-done.7, bf16[512,320]{1,0:T(8,128)(2,1)} %get-tuple-element.32.h0_ref, bf16[512,320]{1,0:T(8,128)(2,1)} %get-tuple-element.31.h1_ref, bf16[1024,320]{1,0:T(8,128)(2,1)} %shard_map.95.grad_ref, ...), custom_call_target="tpu_custom_call" | custom-call | bytes 8000000 | tf_op jit(solution)/shard_map/pallas_call | solution.py:222
  52.6 11.0 %all-to-all-start.1 = ((f32[16,2,320]{2,1,0:T(2,128)}), f32[16,2,320]{2,1,0:T(2,128)S(1)}, u32[]{:S(2)}, u32[]{:S(2)}) async-start(f32[16,2,320]{2,1,0:T(2,128)} %get-tuple-element.40), calls=%async_computation.1 | async-start | bytes 98304 | tf_op jit(solution)/shard_map/all_to_all | solution.py:511
  63.6 0.0 collective-permute-done.hb_ref
  63.6 0.0 copy-start.10
  63.6 5.4 %collective-permute-done.1.ha_ref = bf16[512,320]{1,0:T(8,128)(2,1)} collective-permute-done((bf16[512,320]{1,0:T(8,128)(2,1)S(1)}, bf16[512,320]{1,0:T(8,128)(2,1)}, u32[]{:S(2)}, u32[]{:S(2)}) %collective-permute-start.1) | collective-permute-done | bytes 327712 | tf_op jit(solution)/shard_map/ppermute | solution.py:467
  69.0 7.3 %shard_map.97 = (bf16[1024,320]{1,0:T(8,128)(2,1)}, f32[960,256]{1,0:T(8,128)}, f32[960,256]{1,0:T(8,128)}) custom-call(s32[3]{0:T(128)} %pad_add_fusion.place_ref, bf16[512,320]{1,0:T(8,128)(2,1)} %copy-done.10, bf16[512,320]{1,0:T(8,128)(2,1)} %get-tuple-element.32.h0_ref, bf16[512,320]{1,0:T(8,128)(2,1)} %get-tuple-element.31.h1_ref, ...), custom_call_target="tpu_custom_call" | custom-call | flops 3000000000 | bytes 8000000 | tf_op jit(solution)/shard_map/pallas_call | solution.py:285
  76.4 0.0 all-to-all-done.1.sums_ref
  76.4 0.0 collective-permute-done.4.other_turned_ref
  76.4 1.3 collective-permute-start.6
  77.7 5.5 %shard_map.98 = (f32[1024,320]{1,0:T(8,128)}, bf16[1024,320]{1,0:T(8,128)(2,1)}, bf16[1024,160]{1,0:T(8,128)(2,1)}, bf16[1024,160]{1,0:T(8,128)(2,1)}) custom-call(s32[3]{0:T(128)} %pad_add_fusion.place_ref, f32[16,2,320]{2,1,0:T(2,128)} %copy-done.8, f32[8,320]{1,0:T(8,128)} %get-tuple-element.37.stat_ref, f32[1024,320]{1,0:T(8,128)} %get-tuple-element.44.dhat_ref, ...), custom_call_target="tpu_custom_call" | custom-call | bytes 8000000 | tf_op jit(solution)/shard_map/pallas_call | solution.py:336
  83.2 0.3 collective-permute-start.5
  83.5 1.8 collective-permute-done.5.other_ref
  85.3 0.0 collective-permute-done.6.got_ref
  85.3 0.8 copy-done.6
  86.1 0.4 copy-done.5
  86.5 6.9 %shard_map.99 = f32[1024,640]{1,0:T(8,128)} custom-call(bf16[960,1024]{1,0:T(8,128)(2,1)} %shard_map.94.mine_turned_ref, bf16[960,1024]{1,0:T(8,128)(2,1)} %collective-permute-done.4.other_turned_ref, bf16[1024,160]{1,0:T(8,128)(2,1)} %get-tuple-element.45.mine_ref, bf16[1024,160]{1,0:T(8,128)(2,1)} %copy-done.6, f32[960,256]{1,0:T(8,128)} %get-tuple-element.47.keep_ref, ...), custom_call_target="tpu_custom_call" | custom-call | flops 2500000000 | bytes 8000000 | tf_op jit(solution)/shard_map/pallas_call | solution.py:376
  93.3 6.5 %all-to-all-start.2 = ((f32[16,64,640]{2,1,0:T(8,128)}), f32[16,64,640]{2,1,0:T(8,128)S(1)}, u32[]{:S(2)}, u32[]{:S(2)}) async-start(f32[16,64,640]{2,1,0:T(8,128)} %bitcast.15), calls=%async_computation.2 | async-start | bytes 5242880 | tf_op jit(solution)/shard_map/all_to_all | solution.py:479
  99.9 10.4 %shard_map.100 = bf16[1024,320]{1,0:T(8,128)(2,1)} custom-call(bf16[1024,320]{1,0:T(8,128)(2,1)} %get-tuple-element.51.low_ref, f32[1024,320]{1,0:T(8,128)} %get-tuple-element.52.grad_ref, bf16[1024,320]{1,0:T(8,128)(2,1)} %bitcast.29, f32[8,320]{1,0:T(8,128)} %get-tuple-element.53.stat_ref, f32[1,320]{1,0:T(1,128)} %reshape.49.gain_ref, ...), custom_call_target="tpu_custom_call" | custom-call | flops 2500000000 | bytes 8000000 | tf_op jit(solution)/shard_map/pallas_call | solution.py:428
  110.3 24.3 %all-to-all-done.2 = f32[16,64,640]{2,1,0:T(8,128)S(1)} async-done(((f32[16,64,640]{2,1,0:T(8,128)}), f32[16,64,640]{2,1,0:T(8,128)S(1)}, u32[]{:S(2)}, u32[]{:S(2)}) %all-to-all-start.2) | async-done | bytes 2621472 | tf_op jit(solution)/shard_map/all_to_all | solution.py:479
  134.6 0.1 reduce_sum.18
  134.7 12.1 %all_to_all.30 = f32[8,8,640]{2,1,0:T(8,128)S(1)} all-to-all(f32[8,8,640]{2,1,0:T(8,128)S(1)} %bitcast.21), channel_id=1, replica_groups=mesh['zl'=2,'x'=4,'c'=2,'y'=4,'zh'=4] {'zl','zh'}, dimensions={0} | all-to-all | bytes 327680 | tf_op jit(solution)/shard_map/all_to_all | solution.py:483
  146.8 9.5 %all_to_all.31 = bf16[8,8,640]{2,1,0:T(8,128)(2,1)S(1)} all-to-all(bf16[8,8,640]{2,1,0:T(8,128)(2,1)S(1)} %broadcast_in_dim.6), channel_id=1, replica_groups=mesh['zl'=2,'x'=4,'c'=2,'y'=4,'zh'=4] {'zl','zh'}, dimensions={0} | all-to-all | bytes 163840 | tf_op jit(solution)/shard_map/all_to_all | solution.py:485
  156.3 0.1 broadcast_in_dim.15
  156.5 22.0 %all_to_all.32 = bf16[16,64,640]{2,1,0:T(8,128)(2,1)S(1)} all-to-all(bf16[16,64,640]{2,1,0:T(8,128)(2,1)S(1)} %broadcast_in_dim.15), channel_id=1, replica_groups=mesh['zl'=2,'x'=4,'c'=2,'y'=4,'zh'=4] {'x','y'}, dimensions={0} | all-to-all | bytes 2621440 | tf_op jit(solution)/shard_map/all_to_all | solution.py:487
  178.5 5.6 %collective-permute-start.7 = (bf16[1024,640]{1,0:T(8,128)(2,1)S(1)}, bf16[1024,640]{1,0:T(8,128)(2,1)S(1)}, u32[]{:S(2)}, u32[]{:S(2)}) collective-permute-start(bf16[1024,640]{1,0:T(8,128)(2,1)S(1)} %bitcast.16), channel_id=1, source_target_pairs={{0,16},{16,0},{1,17},{17,1},{2,18},{18,2},{3,19},{19,3},{4,20},{20... | collective-permute-start | bytes 3932168 | tf_op jit(solution)/shard_map/ppermute | solution.py:472
  184.1 2.7 %collective-permute-done.7.other_ref = bf16[1024,640]{1,0:T(8,128)(2,1)S(1)} collective-permute-done((bf16[1024,640]{1,0:T(8,128)(2,1)S(1)}, bf16[1024,640]{1,0:T(8,128)(2,1)S(1)}, u32[]{:S(2)}, u32[]{:S(2)}) %collective-permute-start.7) | collective-permute-done | bytes 1310752 | tf_op jit(solution)/shard_map/ppermute | solution.py:472
  186.8 1.1 copy-done.4
  187.8 4.8 %shard_map.101 = (bf16[9,320,320]{2,1,0:T(8,128)(2,1)}, bf16[3,320,320]{2,1,0:T(8,128)(2,1)}) custom-call(s32[3]{0:T(128)} %pad_add_fusion.place_ref, bf16[1024,640]{1,0:T(8,128)(2,1)} %bitcast.17, bf16[1024,640]{1,0:T(8,128)(2,1)} %copy-done.4), custom_call_target="tpu_custom_call" | custom-call | bytes 8000000 | tf_op jit(solution)/shard_map/pallas_call | solution.py:459
  (20 shorter events, 0.1 us)
Async XLA Ops:
  1.8 32.9 %collective-permute-start.2 = (bf16[512,320]{1,0:T(8,128)(2,1)S(1)}, bf16[512,320]{1,0:T(8,128)(2,1)S(1)}, u32[]{:S(2)}, u32[]{:S(2)}) collective-permute-start(bf16[512,320]{1,0:T(8,128)(2,1)S(1)} %bitcast.23), channel_id=1, source_target_pairs={{0,1},{1,2},{2,3},{3,4},{4,5},{5,6},{6,7},{7,8},{8,9},{9,10},{10,1... | collective-permute-start | bytes 983048 | tf_op jit(solution)/shard_map/ppermute | solution.py:466
  7.6 27.1 %collective-permute-start.3 = (bf16[512,320]{1,0:T(8,128)(2,1)S(1)}, bf16[512,320]{1,0:T(8,128)(2,1)S(1)}, u32[]{:S(2)}, u32[]{:S(2)}) collective-permute-start(bf16[512,320]{1,0:T(8,128)(2,1)S(1)} %bitcast.22), channel_id=1, source_target_pairs={{1,0},{2,1},{3,2},{4,3},{5,4},{6,5},{7,6},{8,7},{9,8},{10,9},{11,1... | collective-permute-start | bytes 983048 | tf_op jit(solution)/shard_map/ppermute | solution.py:467
  19.5 21.1 %all-to-all-start = ((f32[16,2,320]{2,1,0:T(2,128)}), f32[16,2,320]{2,1,0:T(2,128)S(1)}, u32[]{:S(2)}, u32[]{:S(2)}) async-start(f32[16,2,320]{2,1,0:T(2,128)} %get-tuple-element.33), calls=%async_computation | async-start | bytes 98304 | tf_op jit(solution)/shard_map/all_to_all | solution.py:504
  34.7 0.9 copy-start.11
  34.7 0.8 copy-start.12
  35.6 5.1 %copy-start = (bf16[960,1024]{1,0:T(8,128)(2,1)S(1)}, bf16[960,1024]{1,0:T(8,128)(2,1)}, u32[]{:S(2)}) copy-start(bf16[960,1024]{1,0:T(8,128)(2,1)} %shard_map.94.mine_turned_ref) | copy-start | bytes 5898244
  35.6 7.6 %copy-start.3 = (bf16[512,320]{1,0:T(8,128)(2,1)S(1)}, bf16[512,320]{1,0:T(8,128)(2,1)}, u32[]{:S(2)}) copy-start(bf16[512,320]{1,0:T(8,128)(2,1)} %get-tuple-element.31.h1_ref) | copy-start | bytes 983044
  35.6 10.3 %copy-start.2 = (bf16[512,320]{1,0:T(8,128)(2,1)S(1)}, bf16[512,320]{1,0:T(8,128)(2,1)}, u32[]{:S(2)}) copy-start(bf16[512,320]{1,0:T(8,128)(2,1)} %get-tuple-element.32.h0_ref) | copy-start | bytes 983044
  35.6 11.6 %copy-start.9 = (f32[320]{0:T(512)S(1)}, f32[320]{0:T(512)}, u32[]{:S(2)}) copy-start(f32[320]{0:T(512)} %param.11) | copy-start | bytes 3844
  40.7 7.8 %copy-start.7 = (f32[16,2,320]{2,1,0:T(2,128)}, f32[16,2,320]{2,1,0:T(2,128)S(1)}, u32[]{:S(2)}) copy-start(f32[16,2,320]{2,1,0:T(2,128)S(1)} %all-to-all-done.sums_ref) | copy-start | bytes 122884
  40.7 35.7 %collective-permute-start.4 = (bf16[960,1024]{1,0:T(8,128)(2,1)S(1)}, bf16[960,1024]{1,0:T(8,128)(2,1)}, u32[]{:S(2)}, u32[]{:S(2)}) collective-permute-start(bf16[960,1024]{1,0:T(8,128)(2,1)S(1)} %copy-done), channel_id=1, source_target_pairs={{0,16},{16,0},{1,17},{17,1},{2,18},{18,2},{3,19},{19,3},{4,20},{20... | collective-permute-start | bytes 5898248 | tf_op jit(solution)/shard_map/ppermute | solution.py:472
  43.2 20.4 %collective-permute-start = (bf16[512,320]{1,0:T(8,128)(2,1)S(1)}, bf16[512,320]{1,0:T(8,128)(2,1)S(1)}, u32[]{:S(2)}, u32[]{:S(2)}) collective-permute-start(bf16[512,320]{1,0:T(8,128)(2,1)S(1)} %copy-done.3), channel_id=1, source_target_pairs={{0,1},{1,2},{2,3},{3,4},{4,5},{5,6},{6,7},{7,8},{8,9},{9,10},{10,1... | collective-permute-start | bytes 983048 | tf_op jit(solution)/shard_map/ppermute | solution.py:466
  45.9 23.1 %collective-permute-start.1 = (bf16[512,320]{1,0:T(8,128)(2,1)S(1)}, bf16[512,320]{1,0:T(8,128)(2,1)}, u32[]{:S(2)}, u32[]{:S(2)}) collective-permute-start(bf16[512,320]{1,0:T(8,128)(2,1)S(1)} %copy-done.2), channel_id=1, source_target_pairs={{1,0},{2,1},{3,2},{4,3},{5,4},{6,5},{7,6},{8,7},{9,8},{10,9},{11,1... | collective-permute-start | bytes 983048 | tf_op jit(solution)/shard_map/ppermute | solution.py:467
  52.6 23.7 %all-to-all-start.1 = ((f32[16,2,320]{2,1,0:T(2,128)}), f32[16,2,320]{2,1,0:T(2,128)S(1)}, u32[]{:S(2)}, u32[]{:S(2)}) async-start(f32[16,2,320]{2,1,0:T(2,128)} %get-tuple-element.40), calls=%async_computation.1 | async-start | bytes 98304 | tf_op jit(solution)/shard_map/all_to_all | solution.py:511
  63.6 5.4 %copy-start.10 = (bf16[512,320]{1,0:T(8,128)(2,1)}, bf16[512,320]{1,0:T(8,128)(2,1)S(1)}, u32[]{:S(2)}) copy-start(bf16[512,320]{1,0:T(8,128)(2,1)S(1)} %collective-permute-done.hb_ref) | copy-start | bytes 983044
  76.4 1.3 copy-start.8
  76.4 8.9 %collective-permute-start.6 = (f32[960,256]{1,0:T(8,128)}, f32[960,256]{1,0:T(8,128)S(1)}, u32[]{:S(2)}, u32[]{:S(2)}) collective-permute-start(f32[960,256]{1,0:T(8,128)} %get-tuple-element.48), channel_id=1, source_target_pairs={{0,16},{16,0},{1,17},{17,1},{2,18},{18,2},{3,19},{19,3},{4,20},{20... | collective-permute-start | bytes 2949128 | tf_op jit(solution)/shard_map/ppermute | solution.py:472
  83.2 2.1 %collective-permute-start.5 = (bf16[1024,160]{1,0:T(8,128)(2,1)}, bf16[1024,160]{1,0:T(8,128)(2,1)S(1)}, u32[]{:S(2)}, u32[]{:S(2)}) collective-permute-start(bf16[1024,160]{1,0:T(8,128)(2,1)} %get-tuple-element.46), channel_id=1, source_target_pairs={{0,16},{16,0},{1,17},{17,1},{2,18},{18,2},{3,19},{19,3},{4,20},{20... | collective-permute-start | bytes 983048 | tf_op jit(solution)/shard_map/ppermute | solution.py:472
  85.3 0.8 copy-start.6
  85.3 1.2 copy-start.5
  93.3 41.3 %all-to-all-start.2 = ((f32[16,64,640]{2,1,0:T(8,128)}), f32[16,64,640]{2,1,0:T(8,128)S(1)}, u32[]{:S(2)}, u32[]{:S(2)}) async-start(f32[16,64,640]{2,1,0:T(8,128)} %bitcast.15), calls=%async_computation.2 | async-start | bytes 5242880 | tf_op jit(solution)/shard_map/all_to_all | solution.py:479
  178.5 8.3 %copy-start.1 = (bf16[16,64,640]{2,1,0:T(8,128)(2,1)}, bf16[16,64,640]{2,1,0:T(8,128)(2,1)S(1)}, u32[]{:S(2)}) copy-start(bf16[16,64,640]{2,1,0:T(8,128)(2,1)S(1)} %all_to_all.32) | copy-start | bytes 3932164
  178.5 8.3 %collective-permute-start.7 = (bf16[1024,640]{1,0:T(8,128)(2,1)S(1)}, bf16[1024,640]{1,0:T(8,128)(2,1)S(1)}, u32[]{:S(2)}, u32[]{:S(2)}) collective-permute-start(bf16[1024,640]{1,0:T(8,128)(2,1)S(1)} %bitcast.16), channel_id=1, source_target_pairs={{0,16},{16,0},{1,17},{17,1},{2,18},{18,2},{3,19},{19,3},{4,20},{20... | collective-permute-start | bytes 3932168 | tf_op jit(solution)/shard_map/ppermute | solution.py:472
  186.8 1.1 copy-start.4

commit v2 on v1

--- a/solution.py
+++ b/solution.py
@@ -25,15 +25,15 @@
 F32 = jnp.float32
 BF16 = jnp.bfloat16
 
-PARAMS = pltpu.CompilerParams(vmem_limit_bytes=56 * 1024 * 1024)
-
-
-def call(body, out, scratch=(), flops=0):
+MIB = 1024 * 1024
+
+
+def call(body, out, scratch=(), flops=0, limit=12):
     return pl.pallas_call(
         body,
         out_shape=out,
         scratch_shapes=list(scratch),
-        compiler_params=PARAMS,
+        compiler_params=pltpu.CompilerParams(vmem_limit_bytes=limit * MIB),
         cost_estimate=pl.CostEstimate(flops=flops, transcendentals=0, bytes_accessed=8_000_000),
     )
 
@@ -71,7 +71,7 @@
     return 1.0 / (1.0 + jnp.exp(-value))
 
 
-def forward_body(x_ref, w_ref, gain_ref, h0_ref, h1_ref, acts_ref, stat_ref, sums_ref, wf, x3, y):
+def forward_body(x_ref, w_ref, gain_ref, h0_ref, h1_ref, turned_ref, stat_ref, sums_ref, wf, x3, y):
     for i in range(3):
         for j in range(3):
             wf[C * j : C * (j + 1), PAD * i : PAD * i + C] = w_ref[3 * i + j]
@@ -91,7 +91,7 @@
         var = grouped[2 * f + 1 : 2 * f + 2] - mean * mean
         stats += [mean, lax.rsqrt(var + epsilon)]
     stat_ref[...] = jnp.concatenate(stats + [jnp.zeros((4, C), F32)])
-    gain = gain_ref[...]
+    gain = gain_ref[...].reshape(1, C)
     edge = column(C)
 
     def activate(step, mean, scale):
@@ -99,7 +99,6 @@
         pre = (value - mean) * scale * gain
         act = pre / (1.0 + jnp.exp(-pre))
         low = act.astype(BF16)
-        acts_ref[at(step), :] = low
         act = low.astype(F32)
         x3[at(step), 0:C] = jnp.where(edge == 0, 0.0, pltpu.roll(act, 1, 0)).astype(BF16)
         x3[at(step), C : 2 * C] = low
@@ -122,6 +121,7 @@
             x3[f * PIX : (f + 1) * PIX, :], wf[...], preferred_element_type=F32
         )
 
+        turn(x3[f * PIX : (f + 1) * PIX, C : 2 * C], turned_ref, f * PIX)
         h_ref = (h0_ref, h1_ref)[f]
 
         def finish(step, carry, f=f, h_ref=h_ref):
@@ -149,13 +149,28 @@
         sums_ref[k] = both
 
 
+def turn(acts, out_ref, base):
+    rows = lax.broadcasted_iota(jnp.int32, (C, C), 0)
+    same = jnp.where(rows == lax.broadcasted_iota(jnp.int32, (C, C), 1), 1.0, 0.0).astype(BF16)
+    lane = lax.broadcasted_iota(jnp.int32, (C, STEP), 1) & (W - 1)
+    moved = times_transposed(same, acts)
+    for step in range(PIX // STEP):
+        part = moved[:, step * STEP : (step + 1) * STEP]
+        where = slice(base + step * STEP, base + (step + 1) * STEP)
+        out_ref[0:C, where] = jnp.where(lane == 0, 0.0, pltpu.roll(part, 1, 1)).astype(BF16)
+        out_ref[C : 2 * C, where] = part.astype(BF16)
+        out_ref[2 * C : 3 * C, where] = jnp.where(
+            lane == W - 1, 0.0, pltpu.roll(part, STEP - 1, 1)
+        ).astype(BF16)
+
+
 def forward(x, weight, gain, peers):
     return call(
         forward_body,
         (
             shape((PIX, C), BF16),
             shape((PIX, C), BF16),
-            shape((ROWS, C), BF16),
+            shape((3 * C, ROWS), BF16),
             shape((8, C), F32),
             shape((peers, 2, C), F32),
         ),
@@ -165,6 +180,7 @@
             pltpu.VMEM((2, PIX + 2 * W, 3 * PAD), F32),
         ),
         flops=2_500_000_000,
+        limit=20,
     )(x, weight, gain)
 
 
@@ -195,11 +211,13 @@
     return grouped[0:1], grouped[1:2]
 
 
-def slope_body(count, sums_ref, h0_ref, h1_ref, grad_ref, gain_ref, dhat_ref, stat_ref, out_ref):
+def slope_body(
+    count, sums_ref, h0_ref, h1_ref, grad_ref, cot_ref, gain_ref, part_ref, stat_ref, out_ref
+):
     mean, square = clip_stats(sums_ref, count)
     scale = lax.rsqrt(square - mean * mean + epsilon)
     stat_ref[...] = jnp.concatenate([mean, scale, jnp.zeros((6, C), F32)])
-    gain = gain_ref[...]
+    gain = gain_ref[...].reshape(1, C)
     zero = jnp.zeros((8, C), F32)
     total = (zero, zero)
     for f, h_ref in enumerate((h0_ref, h1_ref)):
@@ -211,27 +229,28 @@
             s = sigmoid(pre)
             slope = s * (1.0 + pre * (1.0 - s))
             dhat = grad_ref[pl.ds(base + f * PIX, STEP), :].astype(F32) * slope * gain
-            dhat_ref[pl.ds(base + f * PIX, STEP), :] = dhat
+            there = pl.ds(base + f * PIX, STEP)
+            part_ref[there, :] = cot_ref[there, :].astype(F32) + scale * dhat
             return carry[0] + fold(dhat), carry[1] + fold(dhat * hat)
 
         total = lax.fori_loop(0, PIX // STEP, step_body, total)
     spread(total, out_ref)
 
 
-def slopes(sums, h0, h1, grad, gain, count):
+def slopes(sums, h0, h1, grad, cot, gain, count):
     return call(
         functools.partial(slope_body, count),
         (shape((ROWS, C), F32), shape((8, C), F32), shape(sums.shape, F32)),
-    )(sums, h0, h1, grad, gain)
-
-
-def temporal_body(
-    place_ref, hb_ref, h0_ref, h1_ref, ha_ref, cot_ref, w_ref, stat_ref, gain_ref,
-    out_ref, keep_ref, give_ref, mx, mxt,
+    )(sums, h0, h1, grad, cot, gain)
+
+
+def mixed_body(
+    hb_ref, h0_ref, h1_ref, ha_ref, cot_ref, stat_ref, gain_ref, mx_ref, keep_ref, give_ref, turned
 ):
     mean, scale = stat_ref[0:1, :], stat_ref[1:2, :]
-    gain = gain_ref[...]
-    live = (place_ref[1], None, None, place_ref[2])
+    gain = gain_ref[...].reshape(1, C)
+    place = lax.axis_index(FRAME)
+    live = (place > 0, None, None, place < lax.axis_size(FRAME) - 1)
     for n, h_ref in enumerate((hb_ref, h0_ref, h1_ref, ha_ref)):
 
         def step_body(step, carry, n=n, h_ref=h_ref):
@@ -239,91 +258,69 @@
             pre = (h_ref[pl.ds(base, STEP), :].astype(F32) - mean) * scale * gain
             act = pre / (1.0 + jnp.exp(-pre))
             if live[n] is not None:
-                act = jnp.where(live[n] != 0, act, 0.0)
-            act = act.astype(BF16)
-            mx[pl.ds(base + n * PIX, STEP), :] = act
+                act = jnp.where(live[n], act, 0.0)
+            mx_ref[pl.ds(base + n * PIX, STEP), :] = act.astype(BF16)
             return carry
 
         lax.fori_loop(0, PIX // STEP, step_body, 0)
     for n in range(4 * PIX // STEP):
-        mxt[:, n * STEP : (n + 1) * STEP] = mx[n * STEP : (n + 1) * STEP, :].T
+        where = slice(n * STEP, (n + 1) * STEP)
+        turned[:, where] = mx_ref[where, :].T
+    core = lax.axis_index("c")
+    for k in range(3):
+        part = jnp.dot(
+            turned[:, k * PIX : k * PIX + ROWS], cot_ref[...], preferred_element_type=F32
+        )
+        left, right = part[:, 0:HALF], part[:, HALF:C]
+        keep_ref[k * C : (k + 1) * C, 0:HALF] = jnp.where(core == 0, left, right)
+        give_ref[k * C : (k + 1) * C, 0:HALF] = jnp.where(core == 0, right, left)
+
+
+def mixed_frames(before, h0, h1, after, cot, stat, gain):
+    return call(
+        mixed_body,
+        (shape((4 * PIX, C), BF16), shape((3 * C, 256), F32), shape((3 * C, 256), F32)),
+        (pltpu.VMEM((C, 4 * PIX), BF16),),
+        flops=1_500_000_000,
+    )(before, h0, h1, after, cot, stat, gain)
+
+
+def temporal_body(mx_ref, h0_ref, h1_ref, w_ref, out_ref):
     for f, h_ref in enumerate((h0_ref, h1_ref)):
         total = None
         for k in range(3):
             part = jnp.dot(
-                mx[(f + k) * PIX : (f + k + 1) * PIX, :], w_ref[k], preferred_element_type=F32
+                mx_ref[(f + k) * PIX : (f + k + 1) * PIX, :],
+                w_ref[k],
+                preferred_element_type=F32,
             )
             total = part if total is None else total + part
         low = total.astype(BF16).astype(F32)
         out_ref[f * PIX : (f + 1) * PIX, :] = (h_ref[...].astype(F32) + low).astype(BF16)
-    core = place_ref[0]
-    for k in range(3):
-        part = jnp.dot(
-            mxt[:, k * PIX : k * PIX + ROWS], cot_ref[...], preferred_element_type=F32
-        )
-        left, right = part[:, 0:HALF], part[:, HALF:C]
-        keep_ref[k * C : (k + 1) * C, 0:HALF] = jnp.where(core == 0, left, right)
-        give_ref[k * C : (k + 1) * C, 0:HALF] = jnp.where(core == 0, right, left)
-
-
-SMEM = pl.BlockSpec(memory_space=pltpu.SMEM)
-VMEM = pl.BlockSpec(memory_space=pltpu.VMEM)
-
-
-def call_with_place(body, operands, out, scratch=(), flops=0):
-    return pl.pallas_call(
-        body,
-        out_shape=out,
-        in_specs=[SMEM] + [VMEM] * operands,
-        scratch_shapes=list(scratch),
-        compiler_params=PARAMS,
-        cost_estimate=pl.CostEstimate(flops=flops, transcendentals=0, bytes_accessed=8_000_000),
-    )
-
-
-def temporal(place, before, h0, h1, after, cot, weight, stat, gain):
-    return call_with_place(
-        temporal_body,
-        8,
-        (shape((ROWS, C), BF16), shape((3 * C, 256), F32), shape((3 * C, 256), F32)),
-        (pltpu.VMEM((4 * PIX, C), BF16), pltpu.VMEM((C, 4 * PIX), BF16)),
-        flops=3_000_000_000,
-    )(place, before, h0, h1, after, cot, weight, stat, gain)
-
-
-def turned_body(acts_ref, out_ref):
-    lane = lax.broadcasted_iota(jnp.int32, (C, STEP), 1) & (W - 1)
-    for step in range(ROWS // STEP):
-        turned = acts_ref[step * STEP : (step + 1) * STEP, :].astype(F32).T
-        where = slice(step * STEP, (step + 1) * STEP)
-        out_ref[0:C, where] = jnp.where(lane == 0, 0.0, pltpu.roll(turned, 1, 1)).astype(BF16)
-        out_ref[C : 2 * C, where] = turned.astype(BF16)
-        out_ref[2 * C : 3 * C, where] = jnp.where(
-            lane == W - 1, 0.0, pltpu.roll(turned, STEP - 1, 1)
-        ).astype(BF16)
-
-
-def turned(acts):
-    return call(turned_body, shape((3 * C, ROWS), BF16), flops=500_000_000)(acts)
+
+
+def temporal(mixed, h0, h1, weight):
+    return call(temporal_body, shape((ROWS, C), BF16), flops=1_500_000_000)(mixed, h0, h1, weight)
+
+
+def whole_grad(part_ref, h_ref, stat_ref, sums, base, f):
+    mean, scale = stat_ref[0:1, :], stat_ref[1:2, :]
+    hat = (h_ref[pl.ds(base, STEP), :].astype(F32) - mean) * scale
+    return part_ref[pl.ds(base + f * PIX, STEP), :] - scale * (sums[0] + hat * sums[1])
 
 
 def hidden_grad_body(
-    count, place_ref, sums_ref, stat_ref, dhat_ref, h0_ref, h1_ref, cot_ref,
-    grad_ref, low_ref, keep_ref, give_ref,
+    count, sums_ref, stat_ref, part_ref, h0_ref, h1_ref, keep_ref, give_ref, total_ref
 ):
-    first, second = clip_stats(sums_ref, count)
-    mean, scale = stat_ref[0:1, :], stat_ref[1:2, :]
-    core = place_ref[0]
+    sums = clip_stats(sums_ref, count)
+    total_ref[...] = jnp.concatenate([*sums, jnp.zeros((6, C), F32)])
+    core = lax.axis_index("c")
     for f, h_ref in enumerate((h0_ref, h1_ref)):
 
         def step_body(step, carry, f=f, h_ref=h_ref):
             base = pl.multiple_of(step * STEP, STEP)
             here = pl.ds(base + f * PIX, STEP)
-            hat = (h_ref[pl.ds(base, STEP), :].astype(F32) - mean) * scale
-            grad = cot_ref[here, :].astype(F32) + scale * (dhat_ref[here, :] - first - hat * second)
-            grad_ref[here, :] = grad
-            low = grad.astype(BF16)
-            low_ref[here, :] = low
+            grad = whole_grad(part_ref, h_ref, stat_ref, sums, base, f)
             left, right = grad[:, 0:HALF], grad[:, HALF:C]
             keep_ref[here, :] = jnp.where(core == 0, left, right).astype(BF16)
             give_ref[here, :] = jnp.where(core == 0, right, left).astype(BF16)
@@ -332,17 +329,11 @@
         lax.fori_loop(0, PIX // STEP, step_body, 0)
 
 
-def hidden_gradient(place, sums, stat, dhat, h0, h1, cot, count):
-    return call_with_place(
+def hidden_gradient(sums, stat, part, h0, h1, count):
+    return call(
         functools.partial(hidden_grad_body, count),
-        7 - 1,
-        (
-            shape((ROWS, C), F32),
-            shape((ROWS, C), BF16),
-            shape((ROWS, HALF), BF16),
-            shape((ROWS, HALF), BF16),
-        ),
-    )(place, sums, stat, dhat, h0, h1, cot)
+        (shape((ROWS, HALF), BF16), shape((ROWS, HALF), BF16), shape((8, C), F32)),
+    )(sums, stat, part, h0, h1)
 
 
 def row_taps(value):
@@ -367,31 +358,46 @@
                 rhs[n, where, i * HALF : (i + 1) * HALF] = tap
         part = jnp.dot(turned_ref[...], rhs[n], preferred_element_type=F32)
         total = part if total is None else total + part
-    out_ref[0 : 3 * C, 0 : 3 * HALF] = total
-    out_ref[0 : 3 * C, 3 * HALF : 4 * HALF] = keep_ref[:, 0:HALF] + got_ref[:, 0:HALF]
-    out_ref[3 * C :, :] = jnp.zeros((1024 - 3 * C, 4 * HALF), F32)
+    out_ref[0 : 3 * C, 0 : 3 * HALF] = total.astype(BF16)
+    kept = keep_ref[:, 0:HALF] + got_ref[:, 0:HALF]
+    out_ref[0 : 3 * C, 3 * HALF : 4 * HALF] = kept.astype(BF16)
+    out_ref[3 * C :, :] = jnp.zeros((1024 - 3 * C, 4 * HALF), BF16)
 
 
 def weight_gradients(mine_turned, other_turned, mine, other, keep, got):
     return call(
         weight_grad_body,
-        shape((1024, 4 * HALF), F32),
+        shape((1024, 4 * HALF), BF16),
         (pltpu.VMEM((2, ROWS, 3 * HALF), BF16),),
         flops=2_500_000_000,
     )(mine_turned, other_turned, mine, other, keep, got)
 
 
-def input_grad_body(low_ref, grad_ref, x_ref, stat_ref, gain_ref, w_ref, out_ref, wb, rows, z, dh):
+def input_grad_body(
+    part_ref, h0_ref, h1_ref, clip_ref, total_ref, x_ref, stat_ref, gain_ref, w_ref,
+    out_ref, wb, rows, z, dh, grads, lows,
+):
+    clip_sums = total_ref[0:1, :], total_ref[1:2, :]
     for j in range(3):
         for i in range(3):
             wb[PAD * j : PAD * j + C, C * i : C * (i + 1)] = w_ref[3 * i + j]
         wb[PAD * j + C : PAD * (j + 1), :] = jnp.zeros((PAD - C, 3 * C), BF16)
-    gain = gain_ref[...]
+    gain = gain_ref[...].reshape(1, C)
     edge = column(C)
     half = PIX // STEP
     for f in range(2):
         mean, scale = stat_ref[2 * f : 2 * f + 1, :], stat_ref[2 * f + 1 : 2 * f + 2, :]
-        for i, tap in enumerate(row_taps(low_ref[f * PIX : (f + 1) * PIX, :])):
+        h_ref = (h0_ref, h1_ref)[f]
+
+        def grad_body(step, carry, f=f, h_ref=h_ref):
+            base = pl.multiple_of(step * STEP, STEP)
+            grad = whole_grad(part_ref, h_ref, clip_ref, clip_sums, base, f)
+            grads[pl.ds(base, STEP), :] = grad
+            lows[pl.ds(base, STEP), :] = grad.astype(BF16)
+            return carry
+
+        lax.fori_loop(0, half, grad_body, 0)
+        for i, tap in enumerate(row_taps(lows[...])):
             rows[:, i * C : (i + 1) * C] = tap
         z[...] = times_transposed(rows[...], wb[...])
 
@@ -417,14 +423,15 @@
             base = pl.multiple_of(step * STEP, STEP)
             there = pl.ds(base + f * PIX, STEP)
             hat = (x_ref[there, :].astype(F32) - mean) * scale
-            value = grad_ref[there, :] + scale * (dh[pl.ds(base, STEP), :] - first - hat * second)
+            here = pl.ds(base, STEP)
+            value = grads[here, :] + scale * (dh[here, :] - first - hat * second)
             out_ref[there, :] = value.astype(BF16)
             return carry
 
         lax.fori_loop(0, half, last_body, 0)
 
 
-def input_gradient(low, grad, x, stat, gain, weight):
+def input_gradient(part, h0, h1, clip_stat, total, x, stat, gain, weight):
     return call(
         input_grad_body,
         shape((ROWS, C), BF16),
@@ -433,13 +440,16 @@
             pltpu.VMEM((PIX, 3 * C), BF16),
             pltpu.VMEM((PIX, 3 * PAD), F32),
             pltpu.VMEM((PIX, C), F32),
+            pltpu.VMEM((PIX, C), F32),
+            pltpu.VMEM((PIX, C), BF16),
         ),
         flops=2_500_000_000,
-    )(low, grad, x, stat, gain, weight)
-
-
-def unpack_body(place_ref, mine_ref, other_ref, spatial_ref, temporal_ref):
-    core = place_ref[0]
+        limit=16,
+    )(part, h0, h1, clip_stat, total, x, stat, gain, weight)
+
+
+def unpack_body(mine_ref, other_ref, spatial_ref, temporal_ref):
+    core = lax.axis_index("c")
     for j in range(3):
         here = slice(j * C, (j + 1) * C)
         mine, other = mine_ref[here, :], other_ref[here, :]
@@ -455,10 +465,8 @@
                 temporal_ref[j, :, HALF:C] = right[:, lanes]
 
 
-def unpack(place, mine, other):
-    return call_with_place(
-        unpack_body, 2, (shape((9, C, C), BF16), shape((3, C, C), BF16))
-    )(place, mine, other)
+def unpack(mine, other):
+    return call(unpack_body, (shape((9, C, C), BF16), shape((3, C, C), BF16)))(mine, other)
 
 
 def neighbours(first, second):
@@ -472,62 +480,61 @@
     return lax.ppermute(value, "c", [(0, 1), (1, 0)])
 
 
-def everyone_total(value, beside):
+def everyone_total(value):
+    plane = lax.axis_size(PLANE)
+    value = value.reshape(plane, 1024 // plane, value.shape[1])
+    return lax.all_to_all(value, PLANE, 0, 0)
+
+
+def everyone_share(value):
     plane, line = lax.axis_size(PLANE), lax.axis_size(LINE)
-    width = value.shape[1]
-    value = value.reshape(plane, 1024 // plane, width)
-    value = lax.all_to_all(value, PLANE, 0, 0)
-    value, beside = lax.optimization_barrier((value, beside))
-    value = jnp.sum(value, axis=0)
+    width = value.shape[2]
+    value = jnp.sum(value.astype(F32), axis=0)
     value = value.reshape(line, 1024 // plane // line, width)
     value = jnp.sum(lax.all_to_all(value, LINE, 0, 0), axis=0).astype(BF16)
     value = jnp.broadcast_to(value[None], (line,) + value.shape)
     value = lax.all_to_all(value, LINE, 0, 0).reshape(1024 // plane, width)
     value = jnp.broadcast_to(value[None], (plane,) + value.shape)
-    return lax.all_to_all(value, PLANE, 0, 0).reshape(1024, width), beside
+    return lax.all_to_all(value, PLANE, 0, 0).reshape(1024, width)
 
 
 def on_device(clips, cotangent, spatial_weight, temporal_weight, gain_one, gain_two):
     size = lax.axis_size(FRAME)
-    place = lax.axis_index(FRAME)
-    place = jnp.stack(
-        [lax.axis_index("c"), (place > 0).astype(jnp.int32), (place < size - 1).astype(jnp.int32)]
-    )
     count = float(size * ROWS * C // GROUPS)
     x = clips.reshape(ROWS, C)
     cot = cotangent.reshape(ROWS, C)
     spatial_weight = spatial_weight.reshape(9, C, C)
-    gain_one = gain_one.reshape(1, C)
-    gain_two = gain_two.reshape(1, C)
+    barrier = lax.optimization_barrier
     cot_before, cot_after = neighbours(cot[:PIX], cot[PIX:])
-    h0, h1, acts, stat_one, sums = forward(x, spatial_weight, gain_one, size)
+    h0, h1, mine_turned, stat_one, sums = forward(x, spatial_weight, gain_one, size)
+    before, after = neighbours(h0, h1)
     sums = lax.all_to_all(sums, FRAME, 0, 0)
-    before, after = neighbours(h0, h1)
-    mine_turned = turned(acts)
     mixed_grad = mixed_gradient(cot_before, cot, cot_after, temporal_weight)
-    sums, mine_turned, mixed_grad = lax.optimization_barrier((sums, mine_turned, mixed_grad))
+    sums, mixed_grad = barrier((sums, mixed_grad))
+    part, clip_stat, sums = slopes(sums, h0, h1, mixed_grad, cot, gain_two, count)
+    sums, before, after = barrier((sums, before, after))
+    sums = lax.all_to_all(sums, FRAME, 0, 0)
     other_turned = swap_cores(mine_turned)
-    dhat, stat_two, sums = slopes(sums, h0, h1, mixed_grad, gain_two, count)
-    sums = lax.all_to_all(sums, FRAME, 0, 0)
-    output, temporal_keep, temporal_give = temporal(
-        place, before, h0, h1, after, cot, temporal_weight, stat_two, gain_two
-    )
-    sums, temporal_give, other_turned = lax.optimization_barrier(
-        (sums, temporal_give, other_turned)
-    )
+    mixed, temporal_keep, temporal_give = mixed_frames(
+        before, h0, h1, after, cot, clip_stat, gain_two
+    )
+    sums, temporal_give, other_turned = barrier((sums, temporal_give, other_turned))
     temporal_got = swap_cores(temporal_give)
-    grad, low, low_keep, low_give = hidden_gradient(
-        place, sums, stat_two, dhat, h0, h1, cot, count
-    )
+    low_keep, low_give, total = hidden_gradient(sums, clip_stat, part, h0, h1, count)
     low_got = swap_cores(low_give)
     packed = weight_gradients(
         mine_turned, other_turned, low_keep, low_got, temporal_keep, temporal_got
     )
-    packed, low = lax.optimization_barrier((packed, low))
-    input_grad = input_gradient(low, grad, x, stat_one, gain_one, spatial_weight)
-    mine, input_grad = everyone_total(packed, input_grad)
+    packed, mixed, part = barrier((packed, mixed, part))
+    output = temporal(mixed, h0, h1, temporal_weight)
+    input_grad = input_gradient(
+        part, h0, h1, clip_stat, total, x, stat_one, gain_one, spatial_weight
+    )
+    shares = everyone_total(packed)
+    shares, output, input_grad = barrier((shares, output, input_grad))
+    mine = everyone_share(shares)
     other = swap_cores(mine)
-    spatial_grad, temporal_grad = unpack(place, mine, other)
+    spatial_grad, temporal_grad = unpack(mine, other)
     return (
         output.reshape(clips.shape),
         input_grad.reshape(clips.shape),

time: 193 us -> 173 us (0.90)
  Pallas kernels: 55.8 us -> 36.3 us
  local copies, waits for them, and re-layouts: 6.31 us -> 15.6 us
  starting transfers between devices: 50.4 us -> 45.9 us
  blocking collectives: 43.6 us -> 40.2 us
  waiting for transfers between devices: 35 us -> 32 us
    all_to_all x1, waiting for transfers between devices: 24.3 us -> 7.53 us  [everyone_total(): return lax.all_to_all(value, PLANE, 0, 0)]
    pallas_call x5, Pallas kernels: 27.6 us -> 16.1 us  [the longest x1 4.53 us: weight_gradients(): call(weight_grad_body, shape((1024, 4 * HALF), BF16), (pltpu.VMEM((2, ROW...]
    unnamed x26 -> x44, local copies, waits for them, and re-layouts: 3.12 us -> 14.5 us
    all_to_all x2, starting transfers between devices: 23.1 us -> 15 us  [on_device(): sums = lax.all_to_all(sums, FRAME, 0, 0)]
    all_to_all x2, waiting for transfers between devices: 0.83 us -> 7.74 us  [on_device(): sums = lax.all_to_all(sums, FRAME, 0, 0)]
    ppermute x2, waiting for transfers between devices: 5.39 us -> 12.2 us  [neighbours(): after = lax.ppermute(first, FRAME, [(i + 1, i) for i in range(size - 1)])]
    all_to_all x3, blocking collectives: 43.6 us -> 40.2 us  [the longest x1 18 us: everyone_share(): return lax.all_to_all(value, PLANE, 0, 0).reshape(1024, width)]
    ppermute x2, starting transfers between devices: 8.43 us -> 11.3 us  [neighbours(): before = lax.ppermute(second, FRAME, [(i, i + 1) for i in range(size - 1)])]
  transfers between devices with their start and end apart: 11 -> 11, of which waited for: 5 -> 6; matrix products, arithmetic and copies ran while one was open for 1% -> 1% of each run, Pallas kernels for 23% -> 12%
where the time goes in v2:
time: 173 us; the launch traced here: 172 us
  starting transfers between devices  45.9 us (27%)
  blocking collectives  40.2 us (23%)
  Pallas kernels  36.3 us (21%)
  waiting for transfers between devices  32 us (18%)
  local copies, waits for them, and re-layouts  15.6 us (9%)
    all_to_all x1, blocking collectives, everyone_share(): return lax.all_to_all(value, PLANE, 0, 0).reshape(1024, width)  18 us
    all_to_all x2, starting transfers between devices, on_device(): sums = lax.all_to_all(sums, FRAME, 0, 0)  15 us
    unnamed x44, local copies, waits for them, and re-layouts  14.5 us
    all_to_all x1, blocking collectives, everyone_share(): value = jnp.sum(lax.all_to_all(value, LINE, 0, 0), axis=0).astype(BF16)  12.6 us
    ppermute x4, starting transfers between devices, swap_cores(): return lax.ppermute(value, 'c', [(0, 1), (1, 0)])  12.2 us
    ppermute x2, waiting for transfers between devices, neighbours(): after = lax.ppermute(first, FRAME, [(i + 1, i) for i in range(size - 1)])  12.2 us
    ppermute x2, starting transfers between devices, neighbours(): before = lax.ppermute(second, FRAME, [(i, i + 1) for i in range(size - 1)])  11.3 us
    all_to_all x1, blocking collectives, everyone_share(): value = lax.all_to_all(value, LINE, 0, 0).reshape(1024 // plane, width)  9.62 us
  transfers between devices with their start and end apart: 11, of which 6 were waited for; matrix products, arithmetic and copies ran while one was open for 1% of the time, Pallas kernels for 12%

profile of v2, /device:TPU:1, one launch (start us, length us, event | category | flops | bytes accessed | tf_op | source)
XLA Modules:
  0.0 172.3 jit_solution(17874071098779205546)
XLA Ops:
  0.6 0.0 copy-start.5
  0.6 1.6 copy-done.5
  2.3 1.1 copy-done.8
  3.4 0.7 copy-done.16
  4.1 7.8 %shard_map.93 = (bf16[512,320]{1,0:T(8,128)(2,1)S(1)}, bf16[512,320]{1,0:T(8,128)(2,1)S(1)}, bf16[960,1024]{1,0:T(8,128)(2,1)}, f32[8,320]{1,0:T(8,128)S(1)}, f32[16,2,320]{2,1,0:T(2,128)}) custom-call(bf16[1024,320]{1,0:T(8,128)(2,1)S(1)} %bitcast.20, bf16[9,320,320]{2,1,0:T(8,128)(2,1)S(1)} %bitcast.18, f32[320]{0:T(512)S(1)} %copy-done.16), custom_call_target="tpu_custom_call" | custom-call | flops 2500000000 | bytes 8000000 | tf_op jit(solution)/shard_map/pallas_call | solution.py:168
  11.9 3.2 %collective-permute-start.4 = (bf16[960,1024]{1,0:T(8,128)(2,1)}, bf16[960,1024]{1,0:T(8,128)(2,1)}, u32[]{:S(2)}, u32[]{:S(2)}) collective-permute-start(bf16[960,1024]{1,0:T(8,128)(2,1)} %get-tuple-element.34.mine_turned_ref), channel_id=1, source_target_pairs={{0,16},{16,0},{1,17},{17,1},{2,18},{18,2},{3,19},{19,3},{4,20},{20... | collective-permute-start | bytes 5898248 | tf_op jit(solution)/shard_map/ppermute | solution.py:480
  15.1 1.0 fusion
  16.1 3.2 %collective-permute-start = (bf16[512,320]{1,0:T(8,128)(2,1)}, bf16[512,320]{1,0:T(8,128)(2,1)S(1)}, u32[]{:S(2)}, u32[]{:S(2)}) collective-permute-start(bf16[512,320]{1,0:T(8,128)(2,1)} %bitcast.2), channel_id=1, source_target_pairs={{0,1},{1,2},{2,3},{3,4},{4,5},{5,6},{6,7},{7,8},{8,9},{9,10},{10,1... | collective-permute-start | bytes 983048 | tf_op jit(solution)/shard_map/ppermute | solution.py:474
  19.2 1.3 collective-permute-start.1
  20.5 1.3 collective-permute-start.3
  21.8 8.1 %collective-permute-start.2 = (bf16[512,320]{1,0:T(8,128)(2,1)S(1)}, bf16[512,320]{1,0:T(8,128)(2,1)}, u32[]{:S(2)}, u32[]{:S(2)}) collective-permute-start(bf16[512,320]{1,0:T(8,128)(2,1)S(1)} %get-tuple-element.38.h1_ref), channel_id=1, source_target_pairs={{0,1},{1,2},{2,3},{3,4},{4,5},{5,6},{6,7},{7,8},{8,9},{9,10},{10,1... | collective-permute-start | bytes 983048 | tf_op jit(solution)/shard_map/ppermute | solution.py:474
  29.9 9.5 %all-to-all-start = ((f32[16,2,320]{2,1,0:T(2,128)}), f32[16,2,320]{2,1,0:T(2,128)S(1)}, u32[]{:S(2)}, u32[]{:S(2)}) async-start(f32[16,2,320]{2,1,0:T(2,128)} %get-tuple-element.35), calls=%async_computation | async-start | bytes 98304 | tf_op jit(solution)/shard_map/all_to_all | solution.py:511
  39.4 0.0 copy-start.12
  39.5 0.7 copy-done.12
  40.2 12.2 %collective-permute-done.1.after_ref = bf16[512,320]{1,0:T(8,128)(2,1)S(1)} collective-permute-done((bf16[512,320]{1,0:T(8,128)(2,1)}, bf16[512,320]{1,0:T(8,128)(2,1)S(1)}, u32[]{:S(2)}, u32[]{:S(2)}) %collective-permute-start.1) | collective-permute-done | bytes 327712 | tf_op jit(solution)/shard_map/ppermute | solution.py:475
  52.4 0.7 copy-done.14
  53.1 1.0 copy-done.13
  54.1 1.0 copy-done.15
  55.1 1.6 shard_map.94.grad_ref
  56.7 0.9 copy-done.2
  57.6 5.7 %all-to-all-done.sums_ref = f32[16,2,320]{2,1,0:T(2,128)S(1)} async-done(((f32[16,2,320]{2,1,0:T(2,128)}), f32[16,2,320]{2,1,0:T(2,128)S(1)}, u32[]{:S(2)}, u32[]{:S(2)}) %all-to-all-start) | async-done | bytes 40992 | tf_op jit(solution)/shard_map/all_to_all | solution.py:511
  63.3 1.1 copy-done.3
  64.4 2.4 %shard_map.95 = (f32[1024,320]{1,0:T(8,128)S(1)}, f32[8,320]{1,0:T(8,128)S(1)}, f32[16,2,320]{2,1,0:T(2,128)}) custom-call(f32[16,2,320]{2,1,0:T(2,128)S(1)} %all-to-all-done.sums_ref, bf16[512,320]{1,0:T(8,128)(2,1)S(1)} %get-tuple-element.37.h0_ref, bf16[512,320]{1,0:T(8,128)(2,1)S(1)} %get-tuple-element.38.h1_ref, bf16[1024,320]{1,0:T(8,128)(2,1)S(1)} %copy-done.3, ...), custom_call_target="tpu_custom_call" | custom-call | bytes 8000000 | tf_op jit(solution)/shard_map/pallas_call | solution.py:241
  66.8 5.5 %all-to-all-start.1 = ((f32[16,2,320]{2,1,0:T(2,128)}), f32[16,2,320]{2,1,0:T(2,128)S(1)}, u32[]{:S(2)}, u32[]{:S(2)}) async-start(f32[16,2,320]{2,1,0:T(2,128)} %get-tuple-element.41), calls=%async_computation.1 | async-start | bytes 98304 | tf_op jit(solution)/shard_map/all_to_all | solution.py:516
  72.3 4.0 %shard_map.96 = (bf16[2048,320]{1,0:T(8,128)(2,1)S(1)}, f32[960,256]{1,0:T(8,128)S(1)}, f32[960,256]{1,0:T(8,128)S(1)}) custom-call(bf16[512,320]{1,0:T(8,128)(2,1)} %collective-permute-done.2.hb_ref, bf16[512,320]{1,0:T(8,128)(2,1)S(1)} %get-tuple-element.37.h0_ref, bf16[512,320]{1,0:T(8,128)(2,1)S(1)} %get-tuple-element.38.h1_ref, ...), custom_call_target="tpu_custom_call" | custom-call | flops 1500000000 | bytes 8000000 | tf_op jit(solution)/shard_map/pallas_call | solution.py:280
  76.3 1.0 copy-done.7
  77.3 0.9 copy-done.18
  78.2 1.1 copy-done.20
  79.4 2.0 %all-to-all-done.1.sums_ref = f32[16,2,320]{2,1,0:T(2,128)S(1)} async-done(((f32[16,2,320]{2,1,0:T(2,128)}), f32[16,2,320]{2,1,0:T(2,128)S(1)}, u32[]{:S(2)}, u32[]{:S(2)}) %all-to-all-start.1) | async-done | bytes 40992 | tf_op jit(solution)/shard_map/all_to_all | solution.py:516
  81.4 2.6 %collective-permute-start.6 = (f32[960,256]{1,0:T(8,128)}, f32[960,256]{1,0:T(8,128)S(1)}, u32[]{:S(2)}, u32[]{:S(2)}) collective-permute-start(f32[960,256]{1,0:T(8,128)} %copy-done.7), channel_id=1, source_target_pairs={{0,16},{16,0},{1,17},{17,1},{2,18},{18,2},{3,19},{19,3},{4,20},{20... | collective-permute-start | bytes 2949128 | tf_op jit(solution)/shard_map/ppermute | solution.py:480
  84.0 1.9 %shard_map.97 = (bf16[1024,160]{1,0:T(8,128)(2,1)S(1)}, bf16[1024,160]{1,0:T(8,128)(2,1)S(1)}, f32[8,320]{1,0:T(8,128)S(1)}) custom-call(f32[16,2,320]{2,1,0:T(2,128)S(1)} %all-to-all-done.1.sums_ref, f32[8,320]{1,0:T(8,128)S(1)} %get-tuple-element.44.stat_ref.clip_ref, f32[1024,320]{1,0:T(8,128)S(1)} %get-tuple-element.56.part_ref, ...), custom_call_target="tpu_custom_call" | custom-call | bytes 8000000 | tf_op jit(solution)/shard_map/pallas_call | solution.py:333
  85.9 0.3 collective-permute-start.5
  86.1 1.9 %collective-permute-done.5.other_ref = bf16[1024,160]{1,0:T(8,128)(2,1)S(1)} collective-permute-done((bf16[1024,160]{1,0:T(8,128)(2,1)S(1)}, bf16[1024,160]{1,0:T(8,128)(2,1)S(1)}, u32[]{:S(2)}, u32[]{:S(2)}) %collective-permute-start.5) | collective-permute-done | bytes 327712 | tf_op jit(solution)/shard_map/ppermute | solution.py:480
  88.0 4.5 %shard_map.98 = bf16[1024,640]{1,0:T(8,128)(2,1)S(1)} custom-call(bf16[960,1024]{1,0:T(8,128)(2,1)} %get-tuple-element.34.mine_turned_ref, bf16[960,1024]{1,0:T(8,128)(2,1)} %collective-permute-done.4.other_turned_ref, bf16[1024,160]{1,0:T(8,128)(2,1)S(1)} %get-tuple-element.49.mine_ref, bf16[1024,160]{1,0:T(8,128)(2,1)S(1)} %collective-permute-done.5.other_ref, ...), custom_call_target="tpu_custom_call" | custom-call | flops 2500000000 | bytes 8000000 | tf_op jit(solution)/shard_map/pallas_call | solution.py:368
  92.6 1.0 copy-done.1
  93.6 4.9 %all-to-all-start.2 = ((bf16[16,64,640]{2,1,0:T(8,128)(2,1)}), bf16[16,64,640]{2,1,0:T(8,128)(2,1)}, u32[]{:S(2)}, u32[]{:S(2)}) async-start(bf16[16,64,640]{2,1,0:T(8,128)(2,1)} %bitcast.17), calls=%async_computation.2 | async-start | bytes 2621440 | tf_op jit(solution)/shard_map/all_to_all | solution.py:486
  98.6 1.4 copy-done.21
  100.0 2.5 %shard_map.99 = bf16[1024,320]{1,0:T(8,128)(2,1)} custom-call(bf16[2048,320]{1,0:T(8,128)(2,1)S(1)} %copy-done.21, bf16[512,320]{1,0:T(8,128)(2,1)S(1)} %get-tuple-element.37.h0_ref, bf16[512,320]{1,0:T(8,128)(2,1)S(1)} %get-tuple-element.38.h1_ref, bf16[3,320,320]{2,1,0:T(8,128)(2,1)S(1)} %copy-done.11), custom_call_target="tpu_custom_call" | custom-call | flops 1500000000 | bytes 8000000 | tf_op jit(solution)/shard_map/pallas_call | solution.py:303
  102.5 8.5 %shard_map.100 = bf16[1024,320]{1,0:T(8,128)(2,1)} custom-call(f32[1024,320]{1,0:T(8,128)S(1)} %get-tuple-element.56.part_ref, bf16[512,320]{1,0:T(8,128)(2,1)S(1)} %get-tuple-element.37.h0_ref, bf16[512,320]{1,0:T(8,128)(2,1)S(1)} %get-tuple-element.38.h1_ref, f32[8,320]{1,0:T(8,128)S(1)} %get-tuple-element.44.stat_ref.clip_ref, ...), custom_call_target="tpu_custom_call" | custom-call | flops 2500000000 | bytes 8000000 | tf_op jit(solution)/shard_map/pallas_call | solution.py:435
  111.0 7.5 %all-to-all-done.2 = bf16[16,64,640]{2,1,0:T(8,128)(2,1)} async-done(((bf16[16,64,640]{2,1,0:T(8,128)(2,1)}), bf16[16,64,640]{2,1,0:T(8,128)(2,1)}, u32[]{:S(2)}, u32[]{:S(2)}) %all-to-all-start.2) | async-done | bytes 1310752 | tf_op jit(solution)/shard_map/all_to_all | solution.py:486
  118.5 1.5 convert_reduce_fusion
  120.0 12.6 %all_to_all.30 = f32[8,8,640]{2,1,0:T(8,128)S(1)} all-to-all(f32[8,8,640]{2,1,0:T(8,128)S(1)} %bitcast.22), channel_id=1, replica_groups=mesh['zl'=2,'x'=4,'c'=2,'y'=4,'zh'=4] {'zl','zh'}, dimensions={0} | all-to-all | bytes 327680 | tf_op jit(solution)/shard_map/all_to_all | solution.py:494
  132.6 9.6 %all_to_all.31 = bf16[8,8,640]{2,1,0:T(8,128)(2,1)S(1)} all-to-all(bf16[8,8,640]{2,1,0:T(8,128)(2,1)S(1)} %broadcast_in_dim.6), channel_id=1, replica_groups=mesh['zl'=2,'x'=4,'c'=2,'y'=4,'zh'=4] {'zl','zh'}, dimensions={0} | all-to-all | bytes 163840 | tf_op jit(solution)/shard_map/all_to_all | solution.py:496
  142.3 0.1 broadcast_in_dim.15
  142.4 18.0 %all_to_all.32 = bf16[16,64,640]{2,1,0:T(8,128)(2,1)S(1)} all-to-all(bf16[16,64,640]{2,1,0:T(8,128)(2,1)S(1)} %broadcast_in_dim.15), channel_id=1, replica_groups=mesh['zl'=2,'x'=4,'c'=2,'y'=4,'zh'=4] {'x','y'}, dimensions={0} | all-to-all | bytes 2621440 | tf_op jit(solution)/shard_map/all_to_all | solution.py:498
  160.4 6.1 %collective-permute-start.7 = (bf16[1024,640]{1,0:T(8,128)(2,1)S(1)}, bf16[1024,640]{1,0:T(8,128)(2,1)S(1)}, u32[]{:S(2)}, u32[]{:S(2)}) collective-permute-start(bf16[1024,640]{1,0:T(8,128)(2,1)S(1)} %bitcast.12), channel_id=1, source_target_pairs={{0,16},{16,0},{1,17},{17,1},{2,18},{18,2},{3,19},{19,3},{4,20},{20... | collective-permute-start | bytes 3932168 | tf_op jit(solution)/shard_map/ppermute | solution.py:480
  166.4 2.7 %collective-permute-done.7.other_ref = bf16[1024,640]{1,0:T(8,128)(2,1)S(1)} collective-permute-done((bf16[1024,640]{1,0:T(8,128)(2,1)S(1)}, bf16[1024,640]{1,0:T(8,128)(2,1)S(1)}, u32[]{:S(2)}, u32[]{:S(2)}) %collective-permute-start.7) | collective-permute-done | bytes 1310752 | tf_op jit(solution)/shard_map/ppermute | solution.py:480
  169.1 3.2 %shard_map.101 = (bf16[9,320,320]{2,1,0:T(8,128)(2,1)}, bf16[3,320,320]{2,1,0:T(8,128)(2,1)}) custom-call(bf16[1024,640]{1,0:T(8,128)(2,1)S(1)} %bitcast.13, bf16[1024,640]{1,0:T(8,128)(2,1)S(1)} %collective-permute-done.7.other_ref), custom_call_target="tpu_custom_call" | custom-call | bytes 8000000 | tf_op jit(solution)/shard_map/pallas_call | solution.py:469
  (35 shorter events, 0.1 us)
Async XLA Ops:
  0.6 1.6 copy-start.5
  2.3 1.1 copy-start.8
  3.4 0.7 copy-start.16
  4.1 11.0 %copy-start = (bf16[1,2,16,32,320]{4,3,2,1,0:T(8,128)(2,1)S(1)}, bf16[1,2,16,32,320]{4,3,2,1,0:T(8,128)(2,1)}, u32[]{:S(2)}) copy-start(bf16[1,2,16,32,320]{4,3,2,1,0:T(8,128)(2,1)} %param.7) | copy-start | bytes 1966084
  11.9 41.2 %copy-start.10 = (bf16[3,320,320]{2,1,0:T(8,128)(2,1)S(1)}, bf16[3,320,320]{2,1,0:T(8,128)(2,1)}, u32[]{:S(2)}) copy-start(bf16[3,320,320]{2,1,0:T(8,128)(2,1)} %w_ref.3) | copy-start | bytes 1843204
  11.9 69.5 %collective-permute-start.4 = (bf16[960,1024]{1,0:T(8,128)(2,1)}, bf16[960,1024]{1,0:T(8,128)(2,1)}, u32[]{:S(2)}, u32[]{:S(2)}) collective-permute-start(bf16[960,1024]{1,0:T(8,128)(2,1)} %get-tuple-element.34.mine_turned_ref), channel_id=1, source_target_pairs={{0,16},{16,0},{1,17},{17,1},{2,18},{18,2},{3,19},{19,3},{4,20},{20... | collective-permute-start | bytes 5898248 | tf_op jit(solution)/shard_map/ppermute | solution.py:480
  16.1 23.4 %collective-permute-start = (bf16[512,320]{1,0:T(8,128)(2,1)}, bf16[512,320]{1,0:T(8,128)(2,1)S(1)}, u32[]{:S(2)}, u32[]{:S(2)}) collective-permute-start(bf16[512,320]{1,0:T(8,128)(2,1)} %bitcast.2), channel_id=1, source_target_pairs={{0,1},{1,2},{2,3},{3,4},{4,5},{5,6},{6,7},{7,8},{8,9},{9,10},{10,1... | collective-permute-start | bytes 983048 | tf_op jit(solution)/shard_map/ppermute | solution.py:474
  19.2 33.1 %collective-permute-start.1 = (bf16[512,320]{1,0:T(8,128)(2,1)}, bf16[512,320]{1,0:T(8,128)(2,1)S(1)}, u32[]{:S(2)}, u32[]{:S(2)}) collective-permute-start(bf16[512,320]{1,0:T(8,128)(2,1)} %bitcast.4), channel_id=1, source_target_pairs={{1,0},{2,1},{3,2},{4,3},{5,4},{6,5},{7,6},{8,7},{9,8},{10,9},{11,1... | collective-permute-start | bytes 983048 | tf_op jit(solution)/shard_map/ppermute | solution.py:475
  20.5 46.3 %collective-permute-start.3 = (bf16[512,320]{1,0:T(8,128)(2,1)S(1)}, bf16[512,320]{1,0:T(8,128)(2,1)}, u32[]{:S(2)}, u32[]{:S(2)}) collective-permute-start(bf16[512,320]{1,0:T(8,128)(2,1)S(1)} %get-tuple-element.37.h0_ref), channel_id=1, source_target_pairs={{1,0},{2,1},{3,2},{4,3},{5,4},{6,5},{7,6},{8,7},{9,8},{10,9},{11,1... | collective-permute-start | bytes 983048 | tf_op jit(solution)/shard_map/ppermute | solution.py:475
  21.8 45.0 %collective-permute-start.2 = (bf16[512,320]{1,0:T(8,128)(2,1)S(1)}, bf16[512,320]{1,0:T(8,128)(2,1)}, u32[]{:S(2)}, u32[]{:S(2)}) collective-permute-start(bf16[512,320]{1,0:T(8,128)(2,1)S(1)} %get-tuple-element.38.h1_ref), channel_id=1, source_target_pairs={{0,1},{1,2},{2,3},{3,4},{4,5},{5,6},{6,7},{7,8},{8,9},{9,10},{10,1... | collective-permute-start | bytes 983048 | tf_op jit(solution)/shard_map/ppermute | solution.py:474
  29.9 33.4 %all-to-all-start = ((f32[16,2,320]{2,1,0:T(2,128)}), f32[16,2,320]{2,1,0:T(2,128)S(1)}, u32[]{:S(2)}, u32[]{:S(2)}) async-start(f32[16,2,320]{2,1,0:T(2,128)} %get-tuple-element.35), calls=%async_computation | async-start | bytes 98304 | tf_op jit(solution)/shard_map/all_to_all | solution.py:511
  39.4 0.7 copy-start.12
  52.3 0.7 copy-start.14
  53.1 1.0 copy-start.13
  54.1 1.0 copy-start.15
  55.1 8.2 %copy-start.4 = (f32[320]{0:T(512)S(1)}, f32[320]{0:T(512)}, u32[]{:S(2)}) copy-start(f32[320]{0:T(512)} %gain_ref.6) | copy-start | bytes 3844
  56.7 0.9 copy-start.2
  63.3 1.1 copy-start.3
  66.8 14.6 %all-to-all-start.1 = ((f32[16,2,320]{2,1,0:T(2,128)}), f32[16,2,320]{2,1,0:T(2,128)S(1)}, u32[]{:S(2)}, u32[]{:S(2)}) async-start(f32[16,2,320]{2,1,0:T(2,128)} %get-tuple-element.41), calls=%async_computation.1 | async-start | bytes 98304 | tf_op jit(solution)/shard_map/all_to_all | solution.py:516
  76.3 1.0 copy-start.7
  77.3 0.9 copy-start.18
  78.2 1.1 copy-start.20
  81.4 6.7 %copy-start.19 = (f32[960,256]{1,0:T(8,128)S(1)}, f32[960,256]{1,0:T(8,128)}, u32[]{:S(2)}) copy-start(f32[960,256]{1,0:T(8,128)} %copy-done.18) | copy-start | bytes 2949124
  81.4 6.6 %collective-permute-start.6 = (f32[960,256]{1,0:T(8,128)}, f32[960,256]{1,0:T(8,128)S(1)}, u32[]{:S(2)}, u32[]{:S(2)}) collective-permute-start(f32[960,256]{1,0:T(8,128)} %copy-done.7), channel_id=1, source_target_pairs={{0,16},{16,0},{1,17},{17,1},{2,18},{18,2},{3,19},{19,3},{4,20},{20... | collective-permute-start | bytes 2949128 | tf_op jit(solution)/shard_map/ppermute | solution.py:480
  85.9 2.2 %collective-permute-start.5 = (bf16[1024,160]{1,0:T(8,128)(2,1)S(1)}, bf16[1024,160]{1,0:T(8,128)(2,1)S(1)}, u32[]{:S(2)}, u32[]{:S(2)}) collective-permute-start(bf16[1024,160]{1,0:T(8,128)(2,1)S(1)} %get-tuple-element.50), channel_id=1, source_target_pairs={{0,16},{16,0},{1,17},{17,1},{2,18},{18,2},{3,19},{19,3},{4,20},{20... | collective-permute-start | bytes 983048 | tf_op jit(solution)/shard_map/ppermute | solution.py:480
  92.6 1.1 copy-start.1
  93.6 4.9 %copy-start.11 = (bf16[3,320,320]{2,1,0:T(8,128)(2,1)S(1)}, bf16[3,320,320]{2,1,0:T(8,128)(2,1)}, u32[]{:S(2)}) copy-start(bf16[3,320,320]{2,1,0:T(8,128)(2,1)} %w_ref.3) | copy-start | bytes 1843204
  93.6 24.8 %all-to-all-start.2 = ((bf16[16,64,640]{2,1,0:T(8,128)(2,1)}), bf16[16,64,640]{2,1,0:T(8,128)(2,1)}, u32[]{:S(2)}, u32[]{:S(2)}) async-start(bf16[16,64,640]{2,1,0:T(8,128)(2,1)} %bitcast.17), calls=%async_computation.2 | async-start | bytes 2621440 | tf_op jit(solution)/shard_map/all_to_all | solution.py:486
  98.6 1.4 copy-start.21
  100.0 2.5 %copy-start.6 = (bf16[3,3,320,320]{3,2,1,0:T(8,128)(2,1)S(1)}, bf16[3,3,320,320]{3,2,1,0:T(8,128)(2,1)}, u32[]{:S(2)}) copy-start(bf16[3,3,320,320]{3,2,1,0:T(8,128)(2,1)} %param.8) | copy-start | bytes 5529604
  100.0 2.5 %copy-start.9 = (bf16[1,2,16,32,320]{4,3,2,1,0:T(8,128)(2,1)S(1)}, bf16[1,2,16,32,320]{4,3,2,1,0:T(8,128)(2,1)}, u32[]{:S(2)}) copy-start(bf16[1,2,16,32,320]{4,3,2,1,0:T(8,128)(2,1)} %param.6) | copy-start | bytes 1966084
  100.0 2.5 %copy-start.17 = (f32[320]{0:T(512)S(1)}, f32[320]{0:T(512)}, u32[]{:S(2)}) copy-start(f32[320]{0:T(512)} %gain_ref.7) | copy-start | bytes 3844
  160.4 8.7 %collective-permute-start.7 = (bf16[1024,640]{1,0:T(8,128)(2,1)S(1)}, bf16[1024,640]{1,0:T(8,128)(2,1)S(1)}, u32[]{:S(2)}, u32[]{:S(2)}) collective-permute-start(bf16[1024,640]{1,0:T(8,128)(2,1)S(1)} %bitcast.12), channel_id=1, source_target_pairs={{0,16},{16,0},{1,17},{17,1},{2,18},{18,2},{3,19},{19,3},{4,20},{20... | collective-permute-start | bytes 3932168 | tf_op jit(solution)/shard_map/ppermute | solution.py:480

commit v3 on v2

--- a/solution.py
+++ b/solution.py
@@ -40,6 +40,10 @@
 
 def shape(dims, kind):
     return jax.ShapeDtypeStruct(dims, kind)
+
+
+def inner(dims, kind):
+    return pltpu.VMEM(dims, kind)
 
 
 def at(step, size=STEP):
@@ -507,12 +511,12 @@
     barrier = lax.optimization_barrier
     cot_before, cot_after = neighbours(cot[:PIX], cot[PIX:])
     h0, h1, mine_turned, stat_one, sums = forward(x, spatial_weight, gain_one, size)
-    before, after = neighbours(h0, h1)
     sums = lax.all_to_all(sums, FRAME, 0, 0)
+    edge0, edge1, cot_before, cot_after = barrier((h0, h1, cot_before, cot_after))
+    before, after = neighbours(edge0, edge1)
     mixed_grad = mixed_gradient(cot_before, cot, cot_after, temporal_weight)
-    sums, mixed_grad = barrier((sums, mixed_grad))
+    sums, mixed_grad, mine_turned = barrier((sums, mixed_grad, mine_turned))
     part, clip_stat, sums = slopes(sums, h0, h1, mixed_grad, cot, gain_two, count)
-    sums, before, after = barrier((sums, before, after))
     sums = lax.all_to_all(sums, FRAME, 0, 0)
     other_turned = swap_cores(mine_turned)
     mixed, temporal_keep, temporal_give = mixed_frames(

time: 173 us -> 168 us (0.971)
  waiting for transfers between devices: 32 us -> 29.9 us
    all_to_all x2, starting transfers between devices: 15 us -> 18.4 us  [on_device(): sums = lax.all_to_all(sums, FRAME, 0, 0)]
    unnamed x44 -> x38, local copies, waits for them, and re-layouts: 14.5 us -> 11.6 us
    ppermute x2, starting transfers between devices: 11.3 us -> 8.7 us  [neighbours(): before = lax.ppermute(second, FRAME, [(i, i + 1) for i in range(size - 1)])]
    ppermute x4, starting transfers between devices: 12.2 us -> 10.2 us  [swap_cores(): return lax.ppermute(value, 'c', [(0, 1), (1, 0)])]
  transfers between devices with their start and end apart: 11 -> 11, of which waited for: 6 -> 6; matrix products, arithmetic and copies ran while one was open for 1% -> 0% of each run, Pallas kernels for 12% -> 17%
where the time goes in v3:
time: 168 us
  starting transfers between devices  45.1 us (27%)
  blocking collectives  41.1 us (24%)
  Pallas kernels  35.2 us (21%)
  waiting for transfers between devices  29.9 us (18%)
  local copies, waits for them, and re-layouts  13.9 us (8%)
    all_to_all x2, starting transfers between devices, on_device(): sums = lax.all_to_all(sums, FRAME, 0, 0)  18.4 us
    all_to_all x1, blocking collectives, everyone_share(): return lax.all_to_all(value, PLANE, 0, 0).reshape(1024, width)  18 us
    all_to_all x1, blocking collectives, everyone_share(): value = jnp.sum(lax.all_to_all(value, LINE, 0, 0), axis=0).astype(BF16)  13.5 us
    ppermute x2, waiting for transfers between devices, neighbours(): after = lax.ppermute(first, FRAME, [(i + 1, i) for i in range(size - 1)])  11.7 us
    unnamed x38, local copies, waits for them, and re-layouts  11.6 us
    ppermute x4, starting transfers between devices, swap_cores(): return lax.ppermute(value, 'c', [(0, 1), (1, 0)])  10.2 us
    all_to_all x1, blocking collectives, everyone_share(): value = lax.all_to_all(value, LINE, 0, 0).reshape(1024 // plane, width)  9.62 us
    ppermute x2, starting transfers between devices, neighbours(): before = lax.ppermute(second, FRAME, [(i, i + 1) for i in range(size - 1)])  8.7 us
  transfers between devices with their start and end apart: 11, of which 6 were waited for; matrix products, arithmetic and copies ran while one was open for 0% of the time, Pallas kernels for 17%

profile of v3, /device:TPU:1, one launch (start us, length us, event | category | flops | bytes accessed | tf_op | source)
XLA Modules:
  0.0 167.6 jit_solution(14831319859158672121)
XLA Ops:
  0.6 0.0 copy-start.10
  0.7 2.1 %fusion = (bf16[1,1,16,32,320]{4,3,2,1,0:T(8,128)(2,1)}, bf16[1,1,16,32,320]{4,3,2,1,0:T(8,128)(2,1)}) fusion(bf16[1,2,16,32,320]{4,3,2,1,0:T(8,128)(2,1)} %param.7), kind=kLoop, calls=%fused_computation.1 | loop fusion | bytes 1310720 | tf_op jit(solution)/shard_map/slice | solution.py:512
  2.8 5.7 %collective-permute-start = (bf16[512,320]{1,0:T(8,128)(2,1)}, bf16[512,320]{1,0:T(8,128)(2,1)S(1)}, u32[]{:S(2)}, u32[]{:S(2)}) collective-permute-start(bf16[512,320]{1,0:T(8,128)(2,1)} %bitcast.2), channel_id=1, source_target_pairs={{0,1},{1,2},{2,3},{3,4},{4,5},{5,6},{6,7},{7,8},{8,9},{9,10},{10,1... | collective-permute-start | bytes 983048 | tf_op jit(solution)/shard_map/ppermute | solution.py:478
  8.5 1.3 collective-permute-start.1
  9.9 0.0 copy-start.5
  9.9 1.6 copy-done.5
  11.5 7.2 %shard_map.93 = (bf16[512,320]{1,0:T(8,128)(2,1)S(1)}, bf16[512,320]{1,0:T(8,128)(2,1)S(1)}, bf16[960,1024]{1,0:T(8,128)(2,1)S(1)}, f32[8,320]{1,0:T(8,128)S(1)}, f32[16,2,320]{2,1,0:T(2,128)}) custom-call(bf16[1024,320]{1,0:T(8,128)(2,1)S(1)} %bitcast.20, bf16[9,320,320]{2,1,0:T(8,128)(2,1)S(1)} %bitcast.18, f32[320]{0:T(512)S(1)} %copy-done.14), custom_call_target="tpu_custom_call" | custom-call | flops 2500000000 | bytes 8000000 | tf_op jit(solution)/shard_map/pallas_call | solution.py:172
  18.7 1.3 copy-done.7
  20.0 12.1 %all-to-all-start = ((f32[16,2,320]{2,1,0:T(2,128)}), f32[16,2,320]{2,1,0:T(2,128)S(1)}, u32[]{:S(2)}, u32[]{:S(2)}) async-start(f32[16,2,320]{2,1,0:T(2,128)} %get-tuple-element.36), calls=%async_computation | async-start | bytes 98304 | tf_op jit(solution)/shard_map/all_to_all | solution.py:514
  32.1 0.3 collective-permute-done.1.after_ref
  32.4 1.6 shard_map.94.grad_ref
  34.0 0.0 copy-start.2
  34.0 0.9 copy-done.2
  34.9 6.2 %all-to-all-done.sums_ref = f32[16,2,320]{2,1,0:T(2,128)S(1)} async-done(((f32[16,2,320]{2,1,0:T(2,128)}), f32[16,2,320]{2,1,0:T(2,128)S(1)}, u32[]{:S(2)}, u32[]{:S(2)}) %all-to-all-start) | async-done | bytes 40992 | tf_op jit(solution)/shard_map/all_to_all | solution.py:514
  41.1 2.6 %collective-permute-start.4 = (bf16[960,1024]{1,0:T(8,128)(2,1)}, bf16[960,1024]{1,0:T(8,128)(2,1)}, u32[]{:S(2)}, u32[]{:S(2)}) collective-permute-start(bf16[960,1024]{1,0:T(8,128)(2,1)} %copy-done.7), channel_id=1, source_target_pairs={{0,16},{16,0},{1,17},{17,1},{2,18},{18,2},{3,19},{19,3},{4,20},{20... | collective-permute-start | bytes 5898248 | tf_op jit(solution)/shard_map/ppermute | solution.py:484
  43.6 3.0 %collective-permute-start.2 = (bf16[512,320]{1,0:T(8,128)(2,1)S(1)}, bf16[512,320]{1,0:T(8,128)(2,1)}, u32[]{:S(2)}, u32[]{:S(2)}) collective-permute-start(bf16[512,320]{1,0:T(8,128)(2,1)S(1)} %get-tuple-element.46.h1_ref), channel_id=1, source_target_pairs={{0,1},{1,2},{2,3},{3,4},{4,5},{5,6},{6,7},{7,8},{8,9},{9,10},{10,1... | collective-permute-start | bytes 983048 | tf_op jit(solution)/shard_map/ppermute | solution.py:478
  46.6 1.3 collective-permute-start.3
  47.9 0.0 copy-start.3
  47.9 1.1 copy-done.3
  49.0 2.4 %shard_map.95 = (f32[1024,320]{1,0:T(8,128)S(1)}, f32[8,320]{1,0:T(8,128)S(1)}, f32[16,2,320]{2,1,0:T(2,128)}) custom-call(f32[16,2,320]{2,1,0:T(2,128)S(1)} %all-to-all-done.sums_ref, bf16[512,320]{1,0:T(8,128)(2,1)S(1)} %get-tuple-element.47.h0_ref, bf16[512,320]{1,0:T(8,128)(2,1)S(1)} %get-tuple-element.46.h1_ref, bf16[1024,320]{1,0:T(8,128)(2,1)S(1)} %copy-done.3, ...), custom_call_target="tpu_custom_call" | custom-call | bytes 8000000 | tf_op jit(solution)/shard_map/pallas_call | solution.py:245
  51.4 6.3 %all-to-all-start.1 = ((f32[16,2,320]{2,1,0:T(2,128)}), f32[16,2,320]{2,1,0:T(2,128)S(1)}, u32[]{:S(2)}, u32[]{:S(2)}) async-start(f32[16,2,320]{2,1,0:T(2,128)} %get-tuple-element.45), calls=%async_computation.1 | async-start | bytes 98304 | tf_op jit(solution)/shard_map/all_to_all | solution.py:520
  57.8 0.0 collective-permute-done.2.hb_ref
  57.8 11.4 %collective-permute-done.3.ha_ref = bf16[512,320]{1,0:T(8,128)(2,1)} collective-permute-done((bf16[512,320]{1,0:T(8,128)(2,1)S(1)}, bf16[512,320]{1,0:T(8,128)(2,1)}, u32[]{:S(2)}, u32[]{:S(2)}) %collective-permute-start.3) | collective-permute-done | bytes 327712 | tf_op jit(solution)/shard_map/ppermute | solution.py:479
  69.2 4.0 %shard_map.96 = (bf16[2048,320]{1,0:T(8,128)(2,1)S(1)}, f32[960,256]{1,0:T(8,128)S(1)}, f32[960,256]{1,0:T(8,128)S(1)}) custom-call(bf16[512,320]{1,0:T(8,128)(2,1)} %collective-permute-done.2.hb_ref, bf16[512,320]{1,0:T(8,128)(2,1)S(1)} %get-tuple-element.47.h0_ref, bf16[512,320]{1,0:T(8,128)(2,1)S(1)} %get-tuple-element.46.h1_ref, ...), custom_call_target="tpu_custom_call" | custom-call | flops 1500000000 | bytes 8000000 | tf_op jit(solution)/shard_map/pallas_call | solution.py:284
  73.2 1.0 copy-done.9
  74.2 0.9 copy-done.15
  75.1 1.1 copy-done.17
  76.3 1.3 collective-permute-start.6
  77.5 1.9 %shard_map.97 = (bf16[1024,160]{1,0:T(8,128)(2,1)S(1)}, bf16[1024,160]{1,0:T(8,128)(2,1)S(1)}, f32[8,320]{1,0:T(8,128)S(1)}) custom-call(f32[16,2,320]{2,1,0:T(2,128)S(1)} %all-to-all-done.1.sums_ref, f32[8,320]{1,0:T(8,128)S(1)} %get-tuple-element.48.stat_ref.clip_ref, f32[1024,320]{1,0:T(8,128)S(1)} %get-tuple-element.60.part_ref, ...), custom_call_target="tpu_custom_call" | custom-call | bytes 8000000 | tf_op jit(solution)/shard_map/pallas_call | solution.py:337
  79.4 0.3 collective-permute-start.5
  79.7 1.9 %collective-permute-done.5.other_ref = bf16[1024,160]{1,0:T(8,128)(2,1)S(1)} collective-permute-done((bf16[1024,160]{1,0:T(8,128)(2,1)S(1)}, bf16[1024,160]{1,0:T(8,128)(2,1)S(1)}, u32[]{:S(2)}, u32[]{:S(2)}) %collective-permute-start.5) | collective-permute-done | bytes 327712 | tf_op jit(solution)/shard_map/ppermute | solution.py:484
  81.6 1.2 copy-done.16
  82.8 3.9 %shard_map.98 = bf16[1024,640]{1,0:T(8,128)(2,1)S(1)} custom-call(bf16[960,1024]{1,0:T(8,128)(2,1)S(1)} %copy-done.8, bf16[960,1024]{1,0:T(8,128)(2,1)} %collective-permute-done.4.other_turned_ref, bf16[1024,160]{1,0:T(8,128)(2,1)S(1)} %get-tuple-element.53.mine_ref, bf16[1024,160]{1,0:T(8,128)(2,1)S(1)} %collective-permute-done.5.other_ref, ...), custom_call_target="tpu_custom_call" | custom-call | flops 2500000000 | bytes 8000000 | tf_op jit(solution)/shard_map/pallas_call | solution.py:372
  86.8 0.0 copy-start.1
  86.8 1.0 copy-done.1
  87.8 5.2 %all-to-all-start.2 = ((bf16[16,64,640]{2,1,0:T(8,128)(2,1)}), bf16[16,64,640]{2,1,0:T(8,128)(2,1)}, u32[]{:S(2)}, u32[]{:S(2)}) async-start(bf16[16,64,640]{2,1,0:T(8,128)(2,1)} %bitcast.17), calls=%async_computation.2 | async-start | bytes 2621440 | tf_op jit(solution)/shard_map/all_to_all | solution.py:490
  93.0 1.4 copy-done.18
  94.5 2.5 %shard_map.99 = bf16[1024,320]{1,0:T(8,128)(2,1)} custom-call(bf16[2048,320]{1,0:T(8,128)(2,1)S(1)} %copy-done.18, bf16[512,320]{1,0:T(8,128)(2,1)S(1)} %get-tuple-element.47.h0_ref, bf16[512,320]{1,0:T(8,128)(2,1)S(1)} %get-tuple-element.46.h1_ref, bf16[3,320,320]{2,1,0:T(8,128)(2,1)S(1)} %copy-done.13), custom_call_target="tpu_custom_call" | custom-call | flops 1500000000 | bytes 8000000 | tf_op jit(solution)/shard_map/pallas_call | solution.py:307
  97.0 8.5 %shard_map.100 = bf16[1024,320]{1,0:T(8,128)(2,1)} custom-call(f32[1024,320]{1,0:T(8,128)S(1)} %get-tuple-element.60.part_ref, bf16[512,320]{1,0:T(8,128)(2,1)S(1)} %get-tuple-element.47.h0_ref, bf16[512,320]{1,0:T(8,128)(2,1)S(1)} %get-tuple-element.46.h1_ref, f32[8,320]{1,0:T(8,128)S(1)} %get-tuple-element.48.stat_ref.clip_ref, ...), custom_call_target="tpu_custom_call" | custom-call | flops 2500000000 | bytes 8000000 | tf_op jit(solution)/shard_map/pallas_call | solution.py:439
  105.4 7.5 %all-to-all-done.2 = bf16[16,64,640]{2,1,0:T(8,128)(2,1)} async-done(((bf16[16,64,640]{2,1,0:T(8,128)(2,1)}), bf16[16,64,640]{2,1,0:T(8,128)(2,1)}, u32[]{:S(2)}, u32[]{:S(2)}) %all-to-all-start.2) | async-done | bytes 1310752 | tf_op jit(solution)/shard_map/all_to_all | solution.py:490
  112.9 1.5 convert_reduce_fusion
  114.4 13.5 %all_to_all.30 = f32[8,8,640]{2,1,0:T(8,128)S(1)} all-to-all(f32[8,8,640]{2,1,0:T(8,128)S(1)} %bitcast.22), channel_id=1, replica_groups=mesh['zl'=2,'x'=4,'c'=2,'y'=4,'zh'=4] {'zl','zh'}, dimensions={0} | all-to-all | bytes 327680 | tf_op jit(solution)/shard_map/all_to_all | solution.py:498
  127.9 9.6 %all_to_all.31 = bf16[8,8,640]{2,1,0:T(8,128)(2,1)S(1)} all-to-all(bf16[8,8,640]{2,1,0:T(8,128)(2,1)S(1)} %broadcast_in_dim.6), channel_id=1, replica_groups=mesh['zl'=2,'x'=4,'c'=2,'y'=4,'zh'=4] {'zl','zh'}, dimensions={0} | all-to-all | bytes 163840 | tf_op jit(solution)/shard_map/all_to_all | solution.py:500
  137.5 0.1 broadcast_in_dim.15
  137.7 18.0 %all_to_all.32 = bf16[16,64,640]{2,1,0:T(8,128)(2,1)S(1)} all-to-all(bf16[16,64,640]{2,1,0:T(8,128)(2,1)S(1)} %broadcast_in_dim.15), channel_id=1, replica_groups=mesh['zl'=2,'x'=4,'c'=2,'y'=4,'zh'=4] {'x','y'}, dimensions={0} | all-to-all | bytes 2621440 | tf_op jit(solution)/shard_map/all_to_all | solution.py:502
  155.7 6.1 %collective-permute-start.7 = (bf16[1024,640]{1,0:T(8,128)(2,1)S(1)}, bf16[1024,640]{1,0:T(8,128)(2,1)S(1)}, u32[]{:S(2)}, u32[]{:S(2)}) collective-permute-start(bf16[1024,640]{1,0:T(8,128)(2,1)S(1)} %bitcast.12), channel_id=1, source_target_pairs={{0,16},{16,0},{1,17},{17,1},{2,18},{18,2},{3,19},{19,3},{4,20},{20... | collective-permute-start | bytes 3932168 | tf_op jit(solution)/shard_map/ppermute | solution.py:484
  161.8 2.7 %collective-permute-done.7.other_ref = bf16[1024,640]{1,0:T(8,128)(2,1)S(1)} collective-permute-done((bf16[1024,640]{1,0:T(8,128)(2,1)S(1)}, bf16[1024,640]{1,0:T(8,128)(2,1)S(1)}, u32[]{:S(2)}, u32[]{:S(2)}) %collective-permute-start.7) | collective-permute-done | bytes 1310752 | tf_op jit(solution)/shard_map/ppermute | solution.py:484
  164.4 3.2 %shard_map.101 = (bf16[9,320,320]{2,1,0:T(8,128)(2,1)}, bf16[3,320,320]{2,1,0:T(8,128)(2,1)}) custom-call(bf16[1024,640]{1,0:T(8,128)(2,1)S(1)} %bitcast.13, bf16[1024,640]{1,0:T(8,128)(2,1)S(1)} %collective-permute-done.7.other_ref), custom_call_target="tpu_custom_call" | custom-call | bytes 8000000 | tf_op jit(solution)/shard_map/pallas_call | solution.py:473
  (29 shorter events, 0.1 us)
Async XLA Ops:
  0.6 9.2 %copy-start.14 = (f32[320]{0:T(512)S(1)}, f32[320]{0:T(512)}, u32[]{:S(2)}) copy-start(f32[320]{0:T(512)} %gain_ref.7) | copy-start | bytes 3844
  0.6 9.2 %copy-start.10 = (bf16[1,2,16,32,320]{4,3,2,1,0:T(8,128)(2,1)S(1)}, bf16[1,2,16,32,320]{4,3,2,1,0:T(8,128)(2,1)}, u32[]{:S(2)}) copy-start(bf16[1,2,16,32,320]{4,3,2,1,0:T(8,128)(2,1)} %param.6) | copy-start | bytes 1966084
  2.8 29.3 %collective-permute-start = (bf16[512,320]{1,0:T(8,128)(2,1)}, bf16[512,320]{1,0:T(8,128)(2,1)S(1)}, u32[]{:S(2)}, u32[]{:S(2)}) collective-permute-start(bf16[512,320]{1,0:T(8,128)(2,1)} %bitcast.2), channel_id=1, source_target_pairs={{0,1},{1,2},{2,3},{3,4},{4,5},{5,6},{6,7},{7,8},{8,9},{9,10},{10,1... | collective-permute-start | bytes 983048 | tf_op jit(solution)/shard_map/ppermute | solution.py:478
  8.5 23.8 %collective-permute-start.1 = (bf16[512,320]{1,0:T(8,128)(2,1)}, bf16[512,320]{1,0:T(8,128)(2,1)S(1)}, u32[]{:S(2)}, u32[]{:S(2)}) collective-permute-start(bf16[512,320]{1,0:T(8,128)(2,1)} %bitcast.3), channel_id=1, source_target_pairs={{1,0},{2,1},{3,2},{4,3},{5,4},{6,5},{7,6},{8,7},{9,8},{10,9},{11,1... | collective-permute-start | bytes 983048 | tf_op jit(solution)/shard_map/ppermute | solution.py:479
  9.9 1.6 copy-start.5
  11.5 20.9 %copy-start = (bf16[1,2,16,32,320]{4,3,2,1,0:T(8,128)(2,1)S(1)}, bf16[1,2,16,32,320]{4,3,2,1,0:T(8,128)(2,1)}, u32[]{:S(2)}) copy-start(bf16[1,2,16,32,320]{4,3,2,1,0:T(8,128)(2,1)} %param.7) | copy-start | bytes 1966084
  11.5 20.9 %copy-start.12 = (bf16[3,320,320]{2,1,0:T(8,128)(2,1)S(1)}, bf16[3,320,320]{2,1,0:T(8,128)(2,1)}, u32[]{:S(2)}) copy-start(bf16[3,320,320]{2,1,0:T(8,128)(2,1)} %w_ref.3) | copy-start | bytes 1843204
  18.7 1.3 copy-start.7
  20.0 21.1 %all-to-all-start = ((f32[16,2,320]{2,1,0:T(2,128)}), f32[16,2,320]{2,1,0:T(2,128)S(1)}, u32[]{:S(2)}, u32[]{:S(2)}) async-start(f32[16,2,320]{2,1,0:T(2,128)} %get-tuple-element.36), calls=%async_computation | async-start | bytes 98304 | tf_op jit(solution)/shard_map/all_to_all | solution.py:514
  32.4 15.5 %copy-start.4 = (f32[320]{0:T(512)S(1)}, f32[320]{0:T(512)}, u32[]{:S(2)}) copy-start(f32[320]{0:T(512)} %gain_ref.6) | copy-start | bytes 3844
  34.0 0.9 copy-start.2
  41.1 35.2 %collective-permute-start.4 = (bf16[960,1024]{1,0:T(8,128)(2,1)}, bf16[960,1024]{1,0:T(8,128)(2,1)}, u32[]{:S(2)}, u32[]{:S(2)}) collective-permute-start(bf16[960,1024]{1,0:T(8,128)(2,1)} %copy-done.7), channel_id=1, source_target_pairs={{0,16},{16,0},{1,17},{17,1},{2,18},{18,2},{3,19},{19,3},{4,20},{20... | collective-permute-start | bytes 5898248 | tf_op jit(solution)/shard_map/ppermute | solution.py:484
  43.6 14.1 %collective-permute-start.2 = (bf16[512,320]{1,0:T(8,128)(2,1)S(1)}, bf16[512,320]{1,0:T(8,128)(2,1)}, u32[]{:S(2)}, u32[]{:S(2)}) collective-permute-start(bf16[512,320]{1,0:T(8,128)(2,1)S(1)} %get-tuple-element.46.h1_ref), channel_id=1, source_target_pairs={{0,1},{1,2},{2,3},{3,4},{4,5},{5,6},{6,7},{7,8},{8,9},{9,10},{10,1... | collective-permute-start | bytes 983048 | tf_op jit(solution)/shard_map/ppermute | solution.py:478
  46.6 22.6 %collective-permute-start.3 = (bf16[512,320]{1,0:T(8,128)(2,1)S(1)}, bf16[512,320]{1,0:T(8,128)(2,1)}, u32[]{:S(2)}, u32[]{:S(2)}) collective-permute-start(bf16[512,320]{1,0:T(8,128)(2,1)S(1)} %get-tuple-element.47.h0_ref), channel_id=1, source_target_pairs={{1,0},{2,1},{3,2},{4,3},{5,4},{6,5},{7,6},{8,7},{9,8},{10,9},{11,1... | collective-permute-start | bytes 983048 | tf_op jit(solution)/shard_map/ppermute | solution.py:479
  47.9 1.1 copy-start.3
  51.4 24.8 %all-to-all-start.1 = ((f32[16,2,320]{2,1,0:T(2,128)}), f32[16,2,320]{2,1,0:T(2,128)S(1)}, u32[]{:S(2)}, u32[]{:S(2)}) async-start(f32[16,2,320]{2,1,0:T(2,128)} %get-tuple-element.45), calls=%async_computation.1 | async-start | bytes 98304 | tf_op jit(solution)/shard_map/all_to_all | solution.py:520
  73.2 1.0 copy-start.9
  74.2 0.9 copy-start.15
  75.1 1.1 copy-start.17
  76.3 5.3 %copy-start.8 = (bf16[960,1024]{1,0:T(8,128)(2,1)S(1)}, bf16[960,1024]{1,0:T(8,128)(2,1)}, u32[]{:S(2)}) copy-start(bf16[960,1024]{1,0:T(8,128)(2,1)} %copy-done.7) | copy-start | bytes 5898244
  76.3 5.3 %collective-permute-start.6 = (f32[960,256]{1,0:T(8,128)}, f32[960,256]{1,0:T(8,128)S(1)}, u32[]{:S(2)}, u32[]{:S(2)}) collective-permute-start(f32[960,256]{1,0:T(8,128)} %copy-done.9), channel_id=1, source_target_pairs={{0,16},{16,0},{1,17},{17,1},{2,18},{18,2},{3,19},{19,3},{4,20},{20... | collective-permute-start | bytes 2949128 | tf_op jit(solution)/shard_map/ppermute | solution.py:484
  79.4 2.2 %collective-permute-start.5 = (bf16[1024,160]{1,0:T(8,128)(2,1)S(1)}, bf16[1024,160]{1,0:T(8,128)(2,1)S(1)}, u32[]{:S(2)}, u32[]{:S(2)}) collective-permute-start(bf16[1024,160]{1,0:T(8,128)(2,1)S(1)} %get-tuple-element.54), channel_id=1, source_target_pairs={{0,16},{16,0},{1,17},{17,1},{2,18},{18,2},{3,19},{19,3},{4,20},{20... | collective-permute-start | bytes 983048 | tf_op jit(solution)/shard_map/ppermute | solution.py:484
  81.6 1.2 copy-start.16
  86.8 1.1 copy-start.1
  87.8 5.2 %copy-start.13 = (bf16[3,320,320]{2,1,0:T(8,128)(2,1)S(1)}, bf16[3,320,320]{2,1,0:T(8,128)(2,1)}, u32[]{:S(2)}) copy-start(bf16[3,320,320]{2,1,0:T(8,128)(2,1)} %w_ref.3) | copy-start | bytes 1843204
  87.8 25.1 %all-to-all-start.2 = ((bf16[16,64,640]{2,1,0:T(8,128)(2,1)}), bf16[16,64,640]{2,1,0:T(8,128)(2,1)}, u32[]{:S(2)}, u32[]{:S(2)}) async-start(bf16[16,64,640]{2,1,0:T(8,128)(2,1)} %bitcast.17), calls=%async_computation.2 | async-start | bytes 2621440 | tf_op jit(solution)/shard_map/all_to_all | solution.py:490
  93.0 1.4 copy-start.18
  94.4 2.5 %copy-start.6 = (bf16[3,3,320,320]{3,2,1,0:T(8,128)(2,1)S(1)}, bf16[3,3,320,320]{3,2,1,0:T(8,128)(2,1)}, u32[]{:S(2)}) copy-start(bf16[3,3,320,320]{3,2,1,0:T(8,128)(2,1)} %param.8) | copy-start | bytes 5529604
  94.4 2.5 %copy-start.11 = (bf16[1,2,16,32,320]{4,3,2,1,0:T(8,128)(2,1)S(1)}, bf16[1,2,16,32,320]{4,3,2,1,0:T(8,128)(2,1)}, u32[]{:S(2)}) copy-start(bf16[1,2,16,32,320]{4,3,2,1,0:T(8,128)(2,1)} %param.6) | copy-start | bytes 1966084
  155.7 8.7 %collective-permute-start.7 = (bf16[1024,640]{1,0:T(8,128)(2,1)S(1)}, bf16[1024,640]{1,0:T(8,128)(2,1)S(1)}, u32[]{:S(2)}, u32[]{:S(2)}) collective-permute-start(bf16[1024,640]{1,0:T(8,128)(2,1)S(1)} %bitcast.12), channel_id=1, source_target_pairs={{0,16},{16,0},{1,17},{17,1},{2,18},{18,2},{3,19},{19,3},{4,20},{20... | collective-permute-start | bytes 3932168 | tf_op jit(solution)/shard_map/ppermute | solution.py:484

commit v4 on v3

--- a/solution.py
+++ b/solution.py
@@ -28,13 +28,21 @@
 MIB = 1024 * 1024
 
 
-def call(body, out, scratch=(), flops=0, limit=12):
+VMEM = pl.BlockSpec(memory_space=pltpu.VMEM)
+FAR = pl.BlockSpec(memory_space=pltpu.HBM)
+
+
+def call(body, out, scratch=(), flops=0, limit=12, ins=None, outs=None):
+    specs = {}
+    if ins is not None:
+        specs = {"in_specs": ins, "out_specs": outs}
     return pl.pallas_call(
         body,
         out_shape=out,
         scratch_shapes=list(scratch),
         compiler_params=pltpu.CompilerParams(vmem_limit_bytes=limit * MIB),
         cost_estimate=pl.CostEstimate(flops=flops, transcendentals=0, bytes_accessed=8_000_000),
+        **specs,
     )
 
 
@@ -42,8 +50,8 @@
     return jax.ShapeDtypeStruct(dims, kind)
 
 
-def inner(dims, kind):
-    return pltpu.VMEM(dims, kind)
+def far(dims, kind):
+    return pltpu.HBM(dims, kind)
 
 
 def at(step, size=STEP):
@@ -75,10 +83,12 @@
     return 1.0 / (1.0 + jnp.exp(-value))
 
 
-def forward_body(x_ref, w_ref, gain_ref, h0_ref, h1_ref, turned_ref, stat_ref, sums_ref, wf, x3, y):
-    for i in range(3):
-        for j in range(3):
-            wf[C * j : C * (j + 1), PAD * i : PAD * i + C] = w_ref[3 * i + j]
+def forward_body(
+    x_ref, far_w_ref, gain_ref, h0_ref, h1_ref, far_turned_ref, stat_ref, sums_ref,
+    w_ref, wf, x3, y, turned, w_sem, turned_sem,
+):
+    fetch = pltpu.make_async_copy(far_w_ref, w_ref, w_sem)
+    fetch.start()
     zero = jnp.zeros((8, C), F32)
 
     def moments(step, carry):
@@ -111,6 +121,7 @@
         ).astype(BF16)
 
     total = (zero, zero)
+    sends = []
     for f in range(2):
         mean, scale = stats[2 * f], stats[2 * f + 1]
 
@@ -119,13 +130,23 @@
             return carry
 
         lax.fori_loop(f * half, (f + 1) * half, act_step, 0)
+        if f == 0:
+            fetch.wait()
+            for i in range(3):
+                for j in range(3):
+                    wf[C * j : C * (j + 1), PAD * i : PAD * i + C] = w_ref[3 * i + j]
         y[f, 0:W, :] = jnp.zeros((W, 3 * PAD), F32)
         y[f, W + PIX : 2 * W + PIX, :] = jnp.zeros((W, 3 * PAD), F32)
         y[f, W : W + PIX, :] = jnp.dot(
             x3[f * PIX : (f + 1) * PIX, :], wf[...], preferred_element_type=F32
         )
 
-        turn(x3[f * PIX : (f + 1) * PIX, C : 2 * C], turned_ref, f * PIX)
+        turn(x3[f * PIX : (f + 1) * PIX, C : 2 * C], turned.at[f])
+        send = pltpu.make_async_copy(
+            turned.at[f], far_turned_ref.at[:, f * PIX : (f + 1) * PIX], turned_sem.at[f]
+        )
+        send.start()
+        sends.append(send)
         h_ref = (h0_ref, h1_ref)[f]
 
         def finish(step, carry, f=f, h_ref=h_ref):
@@ -143,6 +164,8 @@
 
         total = lax.fori_loop(0, half, finish, total)
     spread(total, sums_ref)
+    for send in sends:
+        send.wait()
 
 
 def spread(total, sums_ref):
@@ -153,14 +176,14 @@
         sums_ref[k] = both
 
 
-def turn(acts, out_ref, base):
+def turn(acts, out_ref):
     rows = lax.broadcasted_iota(jnp.int32, (C, C), 0)
     same = jnp.where(rows == lax.broadcasted_iota(jnp.int32, (C, C), 1), 1.0, 0.0).astype(BF16)
     lane = lax.broadcasted_iota(jnp.int32, (C, STEP), 1) & (W - 1)
     moved = times_transposed(same, acts)
     for step in range(PIX // STEP):
         part = moved[:, step * STEP : (step + 1) * STEP]
-        where = slice(base + step * STEP, base + (step + 1) * STEP)
+        where = slice(step * STEP, (step + 1) * STEP)
         out_ref[0:C, where] = jnp.where(lane == 0, 0.0, pltpu.roll(part, 1, 1)).astype(BF16)
         out_ref[C : 2 * C, where] = part.astype(BF16)
         out_ref[2 * C : 3 * C, where] = jnp.where(
@@ -174,45 +197,50 @@
         (
             shape((PIX, C), BF16),
             shape((PIX, C), BF16),
-            shape((3 * C, ROWS), BF16),
+            far((3 * C, ROWS), BF16),
             shape((8, C), F32),
             shape((peers, 2, C), F32),
         ),
         (
+            pltpu.VMEM((9, C, C), BF16),
             pltpu.VMEM((3 * C, 3 * PAD), BF16),
             pltpu.VMEM((ROWS, 3 * C), BF16),
             pltpu.VMEM((2, PIX + 2 * W, 3 * PAD), F32),
+            pltpu.VMEM((2, 3 * C, PIX), BF16),
+            pltpu.SemaphoreType.DMA,
+            pltpu.SemaphoreType.DMA((2,)),
         ),
         flops=2_500_000_000,
-        limit=20,
-    )(x, weight, gain)
+        limit=24,
+        ins=[VMEM, FAR, VMEM],
+        outs=(VMEM, VMEM, FAR, VMEM, VMEM),
+    )(x, pltpu.with_memory_space_constraint(weight, pltpu.HBM), gain)
 
 
 def times_transposed(a, b):
     return lax.dot_general(a, b, (((1,), (1,)), ((), ())), preferred_element_type=F32)
-
-
-def mixed_grad_body(before_ref, cot_ref, after_ref, w_ref, out_ref):
-    for f in range(2):
-        last = cot_ref[0:PIX, :] if f else before_ref[...]
-        here = cot_ref[f * PIX : (f + 1) * PIX, :]
-        later = after_ref[...] if f else cot_ref[PIX:ROWS, :]
-        total = times_transposed(later, w_ref[0])
-        total = total + times_transposed(here, w_ref[1])
-        total = total + times_transposed(last, w_ref[2])
-        out_ref[f * PIX : (f + 1) * PIX, :] = total.astype(BF16)
-
-
-def mixed_gradient(before, cot, after, weight):
-    return call(mixed_grad_body, shape((ROWS, C), BF16), flops=1_500_000_000)(
-        before, cot, after, weight
-    )
 
 
 def clip_stats(sums_ref, count):
     total = jnp.sum(sums_ref[...], axis=0)
     grouped = group_sum(jnp.concatenate([total, jnp.zeros((6, C), F32)])) * (1.0 / count)
     return grouped[0:1], grouped[1:2]
+
+
+def mixed_grad_body(before_ref, cot_ref, after_ref, w_ref, out_ref):
+    for f in range(2):
+        last = cot_ref[0:PIX, :] if f else before_ref[...]
+        later = after_ref[...] if f else cot_ref[PIX:ROWS, :]
+        total = times_transposed(later, w_ref[0])
+        total = total + times_transposed(cot_ref[f * PIX : (f + 1) * PIX, :], w_ref[1])
+        total = total + times_transposed(last, w_ref[2])
+        out_ref[f * PIX : (f + 1) * PIX, :] = total.astype(BF16)
+
+
+def mixed_gradient(before, cot, after, weight):
+    return call(mixed_grad_body, far((ROWS, C), BF16), flops=1_500_000_000)(
+        before, cot, after, weight
+    )
 
 
 def slope_body(
@@ -228,12 +256,12 @@
 
         def step_body(step, carry, f=f, h_ref=h_ref):
             base = pl.multiple_of(step * STEP, STEP)
+            there = pl.ds(base + f * PIX, STEP)
             hat = (h_ref[pl.ds(base, STEP), :].astype(F32) - mean) * scale
             pre = hat * gain
             s = sigmoid(pre)
             slope = s * (1.0 + pre * (1.0 - s))
-            dhat = grad_ref[pl.ds(base + f * PIX, STEP), :].astype(F32) * slope * gain
-            there = pl.ds(base + f * PIX, STEP)
+            dhat = grad_ref[there, :].astype(F32) * slope * gain
             part_ref[there, :] = cot_ref[there, :].astype(F32) + scale * dhat
             return carry[0] + fold(dhat), carry[1] + fold(dhat * hat)
 
@@ -249,7 +277,8 @@
 
 
 def mixed_body(
-    hb_ref, h0_ref, h1_ref, ha_ref, cot_ref, stat_ref, gain_ref, mx_ref, keep_ref, give_ref, turned
+    hb_ref, h0_ref, h1_ref, ha_ref, cot_ref, stat_ref, gain_ref, sums_ref,
+    far_mx_ref, keep_ref, give_ref, mx_ref, turned, sem,
 ):
     mean, scale = stat_ref[0:1, :], stat_ref[1:2, :]
     gain = gain_ref[...].reshape(1, C)
@@ -267,6 +296,8 @@
             return carry
 
         lax.fori_loop(0, PIX // STEP, step_body, 0)
+    send = pltpu.make_async_copy(mx_ref, far_mx_ref, sem)
+    send.start()
     for n in range(4 * PIX // STEP):
         where = slice(n * STEP, (n + 1) * STEP)
         turned[:, where] = mx_ref[where, :].T
@@ -278,15 +309,23 @@
         left, right = part[:, 0:HALF], part[:, HALF:C]
         keep_ref[k * C : (k + 1) * C, 0:HALF] = jnp.where(core == 0, left, right)
         give_ref[k * C : (k + 1) * C, 0:HALF] = jnp.where(core == 0, right, left)
-
-
-def mixed_frames(before, h0, h1, after, cot, stat, gain):
+    send.wait()
+
+
+def mixed_frames(before, h0, h1, after, cot, stat, gain, sums):
     return call(
         mixed_body,
-        (shape((4 * PIX, C), BF16), shape((3 * C, 256), F32), shape((3 * C, 256), F32)),
-        (pltpu.VMEM((C, 4 * PIX), BF16),),
+        (far((4 * PIX, C), BF16), shape((3 * C, 256), F32), shape((3 * C, 256), F32)),
+        (
+            pltpu.VMEM((4 * PIX, C), BF16),
+            pltpu.VMEM((C, 4 * PIX), BF16),
+            pltpu.SemaphoreType.DMA,
+        ),
         flops=1_500_000_000,
-    )(before, h0, h1, after, cot, stat, gain)
+        limit=12,
+        ins=[VMEM] * 8,
+        outs=(FAR, VMEM, VMEM),
+    )(before, h0, h1, after, cot, stat, gain, sums)
 
 
 def temporal_body(mx_ref, h0_ref, h1_ref, w_ref, out_ref):
@@ -511,25 +550,26 @@
     barrier = lax.optimization_barrier
     cot_before, cot_after = neighbours(cot[:PIX], cot[PIX:])
     h0, h1, mine_turned, stat_one, sums = forward(x, spatial_weight, gain_one, size)
-    sums = lax.all_to_all(sums, FRAME, 0, 0)
     edge0, edge1, cot_before, cot_after = barrier((h0, h1, cot_before, cot_after))
     before, after = neighbours(edge0, edge1)
+    sums = lax.all_to_all(sums, FRAME, 0, 0)
     mixed_grad = mixed_gradient(cot_before, cot, cot_after, temporal_weight)
-    sums, mixed_grad, mine_turned = barrier((sums, mixed_grad, mine_turned))
-    part, clip_stat, sums = slopes(sums, h0, h1, mixed_grad, cot, gain_two, count)
+    sums, mine_turned, mixed_grad = barrier((sums, mine_turned, mixed_grad))
+    other_turned = swap_cores(mine_turned)
+    part, clip_stat, sums = slopes(
+        sums, h0, h1, mixed_grad, cot, gain_two, count
+    )
     sums = lax.all_to_all(sums, FRAME, 0, 0)
-    other_turned = swap_cores(mine_turned)
     mixed, temporal_keep, temporal_give = mixed_frames(
-        before, h0, h1, after, cot, clip_stat, gain_two
-    )
-    sums, temporal_give, other_turned = barrier((sums, temporal_give, other_turned))
+        before, h0, h1, after, cot, clip_stat, gain_two, sums
+    )
     temporal_got = swap_cores(temporal_give)
     low_keep, low_give, total = hidden_gradient(sums, clip_stat, part, h0, h1, count)
     low_got = swap_cores(low_give)
     packed = weight_gradients(
         mine_turned, other_turned, low_keep, low_got, temporal_keep, temporal_got
     )
-    packed, mixed, part = barrier((packed, mixed, part))
+    packed, mixed, total = barrier((packed, mixed, total))
     output = temporal(mixed, h0, h1, temporal_weight)
     input_grad = input_gradient(
         part, h0, h1, clip_stat, total, x, stat_one, gain_one, spatial_weight

time: 168 us -> 161 us (0.958)
  blocking collectives: 41.1 us -> 59.8 us
  waiting for transfers between devices: 29.9 us -> 18.6 us
  local copies, waits for them, and re-layouts: 13.9 us -> 5.93 us
  starting transfers between devices: 45.1 us -> 39.2 us
    all_to_all x0 -> x1, blocking collectives: none -> 18.7 us  [on_device(): sums = lax.all_to_all(sums, FRAME, 0, 0)]
    ppermute x2, waiting for transfers between devices: 11.7 us -> 2.4 us  [neighbours(): after = lax.ppermute(first, FRAME, [(i + 1, i) for i in range(size - 1)])]
    unnamed x38 -> x24, local copies, waits for them, and re-layouts: 11.6 us -> 3.62 us
    all_to_all x2 -> x1, starting transfers between devices: 18.4 us -> 12.1 us  [on_device(): sums = lax.all_to_all(sums, FRAME, 0, 0)]
    all_to_all x2 -> x1, waiting for transfers between devices: 6.21 us -> 4.1 us  [on_device(): sums = lax.all_to_all(sums, FRAME, 0, 0)]
  transfers between devices with their start and end apart: 11 -> 10, of which waited for: 6 -> 5; matrix products, arithmetic and copies ran while one was open for 0% -> 0% of each run, Pallas kernels for 17% -> 18%
where the time goes in v4:
time: 161 us; the launch traced here: 160 us
  blocking collectives  59.8 us (37%)
  starting transfers between devices  39.2 us (24%)
  Pallas kernels  34.7 us (22%)
  waiting for transfers between devices  18.6 us (12%)
  local copies, waits for them, and re-layouts  5.93 us (4%)
    all_to_all x1, blocking collectives, on_device(): sums = lax.all_to_all(sums, FRAME, 0, 0)  18.7 us
    all_to_all x1, blocking collectives, everyone_share(): return lax.all_to_all(value, PLANE, 0, 0).reshape(1024, width)  18 us
    all_to_all x1, blocking collectives, everyone_share(): value = jnp.sum(lax.all_to_all(value, LINE, 0, 0), axis=0).astype(BF16)  13.5 us
    all_to_all x1, starting transfers between devices, on_device(): sums = lax.all_to_all(sums, FRAME, 0, 0)  12.1 us
    ppermute x4, starting transfers between devices, swap_cores(): return lax.ppermute(value, 'c', [(0, 1), (1, 0)])  10.4 us
    all_to_all x1, blocking collectives, everyone_share(): value = lax.all_to_all(value, LINE, 0, 0).reshape(1024 // plane, width)  9.62 us
    pallas_call x1, Pallas kernels, input_gradient(): call(input_grad_body, shape((ROWS, C), BF16), (pltpu.VMEM((3 * PAD, 3 * C...  8.47 us
    ppermute x2, starting transfers between devices, neighbours(): before = lax.ppermute(second, FRAME, [(i, i + 1) for i in range(size - 1)])  7.97 us
  transfers between devices with their start and end apart: 10, of which 5 were waited for; matrix products, arithmetic and copies ran while one was open for 0% of the time, Pallas kernels for 18%

profile of v4, /device:TPU:1, one launch (start us, length us, event | category | flops | bytes accessed | tf_op | source)
XLA Modules:
  0.0 160.5 jit_solution(14004388716734842048)
XLA Ops:
  0.6 0.0 copy-start.6
  0.7 2.1 %fusion = (bf16[1,1,16,32,320]{4,3,2,1,0:T(8,128)(2,1)}, bf16[1,1,16,32,320]{4,3,2,1,0:T(8,128)(2,1)}) fusion(bf16[1,2,16,32,320]{4,3,2,1,0:T(8,128)(2,1)} %param.7), kind=kLoop, calls=%fused_computation.1 | loop fusion | bytes 1310720 | tf_op jit(solution)/shard_map/slice | solution.py:551
  2.8 5.7 %collective-permute-start = (bf16[512,320]{1,0:T(8,128)(2,1)}, bf16[512,320]{1,0:T(8,128)(2,1)S(1)}, u32[]{:S(2)}, u32[]{:S(2)}) collective-permute-start(bf16[512,320]{1,0:T(8,128)(2,1)} %bitcast.2), channel_id=1, source_target_pairs={{0,1},{1,2},{2,3},{3,4},{4,5},{5,6},{6,7},{7,8},{8,9},{9,10},{10,1... | collective-permute-start | bytes 983048 | tf_op jit(solution)/shard_map/ppermute | solution.py:517
  8.5 1.3 collective-permute-start.1
  9.8 0.0 copy-done.10
  9.9 0.0 copy-done.6
  9.9 0.0 copy-start
  9.9 0.0 copy-start.8
  9.9 7.9 %shard_map.93 = (bf16[512,320]{1,0:T(8,128)(2,1)S(1)}, bf16[512,320]{1,0:T(8,128)(2,1)S(1)}, bf16[960,1024]{1,0:T(8,128)(2,1)}, f32[8,320]{1,0:T(8,128)S(1)}, f32[16,2,320]{2,1,0:T(2,128)}) custom-call(bf16[1024,320]{1,0:T(8,128)(2,1)S(1)} %bitcast.20, bf16[9,320,320]{2,1,0:T(8,128)(2,1)} %bitcast.18, f32[320]{0:T(512)S(1)} %copy-done.10), custom_call_target="tpu_custom_call" | custom-call | flops 2500000000 | bytes 8000000 | tf_op jit(solution)/shard_map/pallas_call | solution.py:195
  17.8 12.1 %all-to-all-start = ((f32[16,2,320]{2,1,0:T(2,128)}), f32[16,2,320]{2,1,0:T(2,128)S(1)}, u32[]{:S(2)}, u32[]{:S(2)}) async-start(f32[16,2,320]{2,1,0:T(2,128)} %get-tuple-element.33), calls=%async_computation | async-start | bytes 98304 | tf_op jit(solution)/shard_map/all_to_all | solution.py:555
  30.0 0.0 collective-permute-done.before_ref
  30.0 2.4 %collective-permute-done.1.after_ref = bf16[512,320]{1,0:T(8,128)(2,1)S(1)} collective-permute-done((bf16[512,320]{1,0:T(8,128)(2,1)}, bf16[512,320]{1,0:T(8,128)(2,1)S(1)}, u32[]{:S(2)}, u32[]{:S(2)}) %collective-permute-start.1) | collective-permute-done | bytes 327712 | tf_op jit(solution)/shard_map/ppermute | solution.py:518
  32.4 0.0 copy-done
  32.4 2.5 %shard_map.94.grad_ref = bf16[1024,320]{1,0:T(8,128)(2,1)} custom-call(bf16[512,320]{1,0:T(8,128)(2,1)S(1)} %collective-permute-done.before_ref, bf16[1024,320]{1,0:T(8,128)(2,1)S(1)} %bitcast.14, bf16[512,320]{1,0:T(8,128)(2,1)S(1)} %collective-permute-done.1.after_ref, bf16[3,320,320]{2,1,0:T(8,128)(2,1)S(1)} %copy-done.8), custom_call_target="tpu_custom_call" | custom-call | flops 1500000000 | bytes 8000000 | tf_op jit(solution)/shard_map/pallas_call | solution.py:241
  34.9 4.1 %all-to-all-done.sums_ref = f32[16,2,320]{2,1,0:T(2,128)S(1)} async-done(((f32[16,2,320]{2,1,0:T(2,128)}), f32[16,2,320]{2,1,0:T(2,128)S(1)}, u32[]{:S(2)}, u32[]{:S(2)}) %all-to-all-start) | async-done | bytes 40992 | tf_op jit(solution)/shard_map/all_to_all | solution.py:555
  39.0 2.6 %collective-permute-start.2 = (bf16[960,1024]{1,0:T(8,128)(2,1)}, bf16[960,1024]{1,0:T(8,128)(2,1)S(1)}, u32[]{:S(2)}, u32[]{:S(2)}) collective-permute-start(bf16[960,1024]{1,0:T(8,128)(2,1)} %get-tuple-element.39.mine_turned_ref), channel_id=1, source_target_pairs={{0,16},{16,0},{1,17},{17,1},{2,18},{18,2},{3,19},{19,3},{4,20},{20... | collective-permute-start | bytes 5898248 | tf_op jit(solution)/shard_map/ppermute | solution.py:523
  41.5 2.2 %collective-permute-start.4 = (bf16[512,320]{1,0:T(8,128)(2,1)S(1)}, bf16[512,320]{1,0:T(8,128)(2,1)S(1)}, u32[]{:S(2)}, u32[]{:S(2)}) collective-permute-start(bf16[512,320]{1,0:T(8,128)(2,1)S(1)} %get-tuple-element.47.h1_ref), channel_id=1, source_target_pairs={{0,1},{1,2},{2,3},{3,4},{4,5},{5,6},{6,7},{7,8},{8,9},{9,10},{10,1... | collective-permute-start | bytes 983048 | tf_op jit(solution)/shard_map/ppermute | solution.py:517
  43.8 1.3 collective-permute-start.5
  45.1 0.0 copy-start.2
  45.1 1.1 copy-done.2
  46.2 1.8 %shard_map.95 = (f32[1024,320]{1,0:T(8,128)S(1)}, f32[8,320]{1,0:T(8,128)S(1)}, f32[16,2,320]{2,1,0:T(2,128)S(1)}) custom-call(f32[16,2,320]{2,1,0:T(2,128)S(1)} %all-to-all-done.sums_ref, bf16[512,320]{1,0:T(8,128)(2,1)S(1)} %get-tuple-element.48.h0_ref, bf16[512,320]{1,0:T(8,128)(2,1)S(1)} %get-tuple-element.47.h1_ref, bf16[1024,320]{1,0:T(8,128)(2,1)S(1)} %copy-done.2, ...), custom_call_target="tpu_custom_call" | custom-call | bytes 8000000 | tf_op jit(solution)/shard_map/pallas_call | solution.py:273
  48.0 18.7 %all_to_all.30.sums_ref = f32[16,2,320]{2,1,0:T(2,128)S(1)} all-to-all(f32[16,2,320]{2,1,0:T(2,128)S(1)} %get-tuple-element.42), channel_id=1, replica_groups=mesh['zl'=2,'x'=4,'c'=2,'y'=4,'zh'=4] {'y','zh'}, dimensions={0} | all-to-all | bytes 81920 | tf_op jit(solution)/shard_map/all_to_all | solution.py:562
  66.7 0.0 collective-permute-done.4.hb_ref
  66.7 0.0 collective-permute-done.5.ha_ref
  66.7 4.0 %shard_map.97 = (bf16[2048,320]{1,0:T(8,128)(2,1)}, f32[960,256]{1,0:T(8,128)S(1)}, f32[960,256]{1,0:T(8,128)S(1)}) custom-call(bf16[512,320]{1,0:T(8,128)(2,1)S(1)} %collective-permute-done.4.hb_ref, bf16[512,320]{1,0:T(8,128)(2,1)S(1)} %get-tuple-element.48.h0_ref, bf16[512,320]{1,0:T(8,128)(2,1)S(1)} %get-tuple-element.47.h1_ref, ...), custom_call_target="tpu_custom_call" | custom-call | flops 1500000000 | bytes 8000000 | tf_op jit(solution)/shard_map/pallas_call | solution.py:316
  70.7 0.0 copy-start.5
  70.7 1.5 collective-permute-start.6
  72.2 1.9 %shard_map.96 = (bf16[1024,160]{1,0:T(8,128)(2,1)S(1)}, bf16[1024,160]{1,0:T(8,128)(2,1)S(1)}, f32[8,320]{1,0:T(8,128)S(1)}) custom-call(f32[16,2,320]{2,1,0:T(2,128)S(1)} %all_to_all.30.sums_ref, f32[8,320]{1,0:T(8,128)S(1)} %get-tuple-element.43.stat_ref.clip_ref, f32[1024,320]{1,0:T(8,128)S(1)} %get-tuple-element.44.part_ref, ...), custom_call_target="tpu_custom_call" | custom-call | bytes 8000000 | tf_op jit(solution)/shard_map/pallas_call | solution.py:376
  74.1 0.3 collective-permute-start.3
  74.4 1.9 %collective-permute-done.3.other_ref = bf16[1024,160]{1,0:T(8,128)(2,1)S(1)} collective-permute-done((bf16[1024,160]{1,0:T(8,128)(2,1)S(1)}, bf16[1024,160]{1,0:T(8,128)(2,1)S(1)}, u32[]{:S(2)}, u32[]{:S(2)}) %collective-permute-start.3) | collective-permute-done | bytes 327712 | tf_op jit(solution)/shard_map/ppermute | solution.py:523
  76.3 0.0 collective-permute-done.6.got_ref
  76.3 0.0 collective-permute-done.2.other_turned_ref
  76.3 2.4 %shard_map.98 = bf16[1024,640]{1,0:T(8,128)(2,1)S(1)} custom-call(bf16[960,1024]{1,0:T(8,128)(2,1)S(1)} %copy-done.5, bf16[960,1024]{1,0:T(8,128)(2,1)S(1)} %collective-permute-done.2.other_turned_ref, bf16[1024,160]{1,0:T(8,128)(2,1)S(1)} %get-tuple-element.45.mine_ref, bf16[1024,160]{1,0:T(8,128)(2,1)S(1)} %collective-permute-done.3.other_ref, ...), custom_call_target="tpu_custom_call" | custom-call | flops 2500000000 | bytes 8000000 | tf_op jit(solution)/shard_map/pallas_call | solution.py:411
  78.7 0.0 copy-start.1
  78.7 1.0 copy-done.1
  79.8 6.1 %all-to-all-start.2 = ((bf16[16,64,640]{2,1,0:T(8,128)(2,1)}), bf16[16,64,640]{2,1,0:T(8,128)(2,1)}, u32[]{:S(2)}, u32[]{:S(2)}) async-start(bf16[16,64,640]{2,1,0:T(8,128)(2,1)} %bitcast.17), calls=%async_computation.2 | async-start | bytes 2621440 | tf_op jit(solution)/shard_map/all_to_all | solution.py:529
  85.9 1.4 copy-done.11
  87.3 2.5 %shard_map.99 = bf16[1024,320]{1,0:T(8,128)(2,1)} custom-call(bf16[2048,320]{1,0:T(8,128)(2,1)S(1)} %copy-done.11, bf16[512,320]{1,0:T(8,128)(2,1)S(1)} %get-tuple-element.48.h0_ref, bf16[512,320]{1,0:T(8,128)(2,1)S(1)} %get-tuple-element.47.h1_ref, bf16[3,320,320]{2,1,0:T(8,128)(2,1)S(1)} %copy-done.9), custom_call_target="tpu_custom_call" | custom-call | flops 1500000000 | bytes 8000000 | tf_op jit(solution)/shard_map/pallas_call | solution.py:346
  89.8 8.5 %shard_map.100 = bf16[1024,320]{1,0:T(8,128)(2,1)} custom-call(f32[1024,320]{1,0:T(8,128)S(1)} %get-tuple-element.44.part_ref, bf16[512,320]{1,0:T(8,128)(2,1)S(1)} %get-tuple-element.48.h0_ref, bf16[512,320]{1,0:T(8,128)(2,1)S(1)} %get-tuple-element.47.h1_ref, f32[8,320]{1,0:T(8,128)S(1)} %get-tuple-element.43.stat_ref.clip_ref, ...), custom_call_target="tpu_custom_call" | custom-call | flops 2500000000 | bytes 8000000 | tf_op jit(solution)/shard_map/pallas_call | solution.py:478
  98.3 7.5 %all-to-all-done.2 = bf16[16,64,640]{2,1,0:T(8,128)(2,1)} async-done(((bf16[16,64,640]{2,1,0:T(8,128)(2,1)}), bf16[16,64,640]{2,1,0:T(8,128)(2,1)}, u32[]{:S(2)}, u32[]{:S(2)}) %all-to-all-start.2) | async-done | bytes 1310752 | tf_op jit(solution)/shard_map/all_to_all | solution.py:529
  105.8 1.5 convert_reduce_fusion
  107.3 13.5 %all_to_all.31 = f32[8,8,640]{2,1,0:T(8,128)S(1)} all-to-all(f32[8,8,640]{2,1,0:T(8,128)S(1)} %bitcast.22), channel_id=1, replica_groups=mesh['zl'=2,'x'=4,'c'=2,'y'=4,'zh'=4] {'zl','zh'}, dimensions={0} | all-to-all | bytes 327680 | tf_op jit(solution)/shard_map/all_to_all | solution.py:537
  120.8 9.6 %all_to_all.32 = bf16[8,8,640]{2,1,0:T(8,128)(2,1)S(1)} all-to-all(bf16[8,8,640]{2,1,0:T(8,128)(2,1)S(1)} %broadcast_in_dim.6), channel_id=1, replica_groups=mesh['zl'=2,'x'=4,'c'=2,'y'=4,'zh'=4] {'zl','zh'}, dimensions={0} | all-to-all | bytes 163840 | tf_op jit(solution)/shard_map/all_to_all | solution.py:539
  130.4 0.1 broadcast_in_dim.15
  130.6 18.0 %all_to_all.33 = bf16[16,64,640]{2,1,0:T(8,128)(2,1)S(1)} all-to-all(bf16[16,64,640]{2,1,0:T(8,128)(2,1)S(1)} %broadcast_in_dim.15), channel_id=1, replica_groups=mesh['zl'=2,'x'=4,'c'=2,'y'=4,'zh'=4] {'x','y'}, dimensions={0} | all-to-all | bytes 2621440 | tf_op jit(solution)/shard_map/all_to_all | solution.py:541
  148.6 6.1 %collective-permute-start.7 = (bf16[1024,640]{1,0:T(8,128)(2,1)S(1)}, bf16[1024,640]{1,0:T(8,128)(2,1)S(1)}, u32[]{:S(2)}, u32[]{:S(2)}) collective-permute-start(bf16[1024,640]{1,0:T(8,128)(2,1)S(1)} %bitcast.12), channel_id=1, source_target_pairs={{0,16},{16,0},{1,17},{17,1},{2,18},{18,2},{3,19},{19,3},{4,20},{20... | collective-permute-start | bytes 3932168 | tf_op jit(solution)/shard_map/ppermute | solution.py:523
  154.6 2.7 %collective-permute-done.7.other_ref = bf16[1024,640]{1,0:T(8,128)(2,1)S(1)} collective-permute-done((bf16[1024,640]{1,0:T(8,128)(2,1)S(1)}, bf16[1024,640]{1,0:T(8,128)(2,1)S(1)}, u32[]{:S(2)}, u32[]{:S(2)}) %collective-permute-start.7) | collective-permute-done | bytes 1310752 | tf_op jit(solution)/shard_map/ppermute | solution.py:523
  157.3 3.2 %shard_map.101 = (bf16[9,320,320]{2,1,0:T(8,128)(2,1)}, bf16[3,320,320]{2,1,0:T(8,128)(2,1)}) custom-call(bf16[1024,640]{1,0:T(8,128)(2,1)S(1)} %bitcast.13, bf16[1024,640]{1,0:T(8,128)(2,1)S(1)} %collective-permute-done.7.other_ref), custom_call_target="tpu_custom_call" | custom-call | bytes 8000000 | tf_op jit(solution)/shard_map/pallas_call | solution.py:512
  (14 shorter events, 0.0 us)
Async XLA Ops:
  0.6 9.2 %copy-start.10 = (f32[320]{0:T(512)S(1)}, f32[320]{0:T(512)}, u32[]{:S(2)}) copy-start(f32[320]{0:T(512)} %gain_ref.7) | copy-start | bytes 3844
  0.6 9.2 %copy-start.6 = (bf16[1,2,16,32,320]{4,3,2,1,0:T(8,128)(2,1)S(1)}, bf16[1,2,16,32,320]{4,3,2,1,0:T(8,128)(2,1)}, u32[]{:S(2)}) copy-start(bf16[1,2,16,32,320]{4,3,2,1,0:T(8,128)(2,1)} %param.6) | copy-start | bytes 1966084
  2.8 27.2 %collective-permute-start = (bf16[512,320]{1,0:T(8,128)(2,1)}, bf16[512,320]{1,0:T(8,128)(2,1)S(1)}, u32[]{:S(2)}, u32[]{:S(2)}) collective-permute-start(bf16[512,320]{1,0:T(8,128)(2,1)} %bitcast.2), channel_id=1, source_target_pairs={{0,1},{1,2},{2,3},{3,4},{4,5},{5,6},{6,7},{7,8},{8,9},{9,10},{10,1... | collective-permute-start | bytes 983048 | tf_op jit(solution)/shard_map/ppermute | solution.py:517
  8.5 23.8 %collective-permute-start.1 = (bf16[512,320]{1,0:T(8,128)(2,1)}, bf16[512,320]{1,0:T(8,128)(2,1)S(1)}, u32[]{:S(2)}, u32[]{:S(2)}) collective-permute-start(bf16[512,320]{1,0:T(8,128)(2,1)} %bitcast.3), channel_id=1, source_target_pairs={{1,0},{2,1},{3,2},{4,3},{5,4},{6,5},{7,6},{8,7},{9,8},{10,9},{11,1... | collective-permute-start | bytes 983048 | tf_op jit(solution)/shard_map/ppermute | solution.py:518
  9.9 22.5 %copy-start = (bf16[1,2,16,32,320]{4,3,2,1,0:T(8,128)(2,1)S(1)}, bf16[1,2,16,32,320]{4,3,2,1,0:T(8,128)(2,1)}, u32[]{:S(2)}) copy-start(bf16[1,2,16,32,320]{4,3,2,1,0:T(8,128)(2,1)} %param.7) | copy-start | bytes 1966084
  9.9 22.5 %copy-start.8 = (bf16[3,320,320]{2,1,0:T(8,128)(2,1)S(1)}, bf16[3,320,320]{2,1,0:T(8,128)(2,1)}, u32[]{:S(2)}) copy-start(bf16[3,320,320]{2,1,0:T(8,128)(2,1)} %w_ref.3) | copy-start | bytes 1843204
  17.8 21.1 %all-to-all-start = ((f32[16,2,320]{2,1,0:T(2,128)}), f32[16,2,320]{2,1,0:T(2,128)S(1)}, u32[]{:S(2)}, u32[]{:S(2)}) async-start(f32[16,2,320]{2,1,0:T(2,128)} %get-tuple-element.33), calls=%async_computation | async-start | bytes 98304 | tf_op jit(solution)/shard_map/all_to_all | solution.py:555
  32.4 12.7 %copy-start.3 = (f32[320]{0:T(512)S(1)}, f32[320]{0:T(512)}, u32[]{:S(2)}) copy-start(f32[320]{0:T(512)} %gain_ref.6) | copy-start | bytes 3844
  39.0 37.3 %collective-permute-start.2 = (bf16[960,1024]{1,0:T(8,128)(2,1)}, bf16[960,1024]{1,0:T(8,128)(2,1)S(1)}, u32[]{:S(2)}, u32[]{:S(2)}) collective-permute-start(bf16[960,1024]{1,0:T(8,128)(2,1)} %get-tuple-element.39.mine_turned_ref), channel_id=1, source_target_pairs={{0,16},{16,0},{1,17},{17,1},{2,18},{18,2},{3,19},{19,3},{4,20},{20... | collective-permute-start | bytes 5898248 | tf_op jit(solution)/shard_map/ppermute | solution.py:523
  41.5 25.2 %collective-permute-start.4 = (bf16[512,320]{1,0:T(8,128)(2,1)S(1)}, bf16[512,320]{1,0:T(8,128)(2,1)S(1)}, u32[]{:S(2)}, u32[]{:S(2)}) collective-permute-start(bf16[512,320]{1,0:T(8,128)(2,1)S(1)} %get-tuple-element.47.h1_ref), channel_id=1, source_target_pairs={{0,1},{1,2},{2,3},{3,4},{4,5},{5,6},{6,7},{7,8},{8,9},{9,10},{10,1... | collective-permute-start | bytes 983048 | tf_op jit(solution)/shard_map/ppermute | solution.py:517
  43.8 22.9 %collective-permute-start.5 = (bf16[512,320]{1,0:T(8,128)(2,1)S(1)}, bf16[512,320]{1,0:T(8,128)(2,1)S(1)}, u32[]{:S(2)}, u32[]{:S(2)}) collective-permute-start(bf16[512,320]{1,0:T(8,128)(2,1)S(1)} %get-tuple-element.48.h0_ref), channel_id=1, source_target_pairs={{1,0},{2,1},{3,2},{4,3},{5,4},{6,5},{7,6},{8,7},{9,8},{10,9},{11,1... | collective-permute-start | bytes 983048 | tf_op jit(solution)/shard_map/ppermute | solution.py:518
  45.1 1.1 copy-start.2
  70.7 5.6 %copy-start.5 = (bf16[960,1024]{1,0:T(8,128)(2,1)S(1)}, bf16[960,1024]{1,0:T(8,128)(2,1)}, u32[]{:S(2)}) copy-start(bf16[960,1024]{1,0:T(8,128)(2,1)} %get-tuple-element.39.mine_turned_ref) | copy-start | bytes 5898244
  70.7 5.6 %collective-permute-start.6 = (f32[960,256]{1,0:T(8,128)S(1)}, f32[960,256]{1,0:T(8,128)S(1)}, u32[]{:S(2)}, u32[]{:S(2)}) collective-permute-start(f32[960,256]{1,0:T(8,128)S(1)} %get-tuple-element.50), channel_id=1, source_target_pairs={{0,16},{16,0},{1,17},{17,1},{2,18},{18,2},{3,19},{19,3},{4,20},{20... | collective-permute-start | bytes 2949128 | tf_op jit(solution)/shard_map/ppermute | solution.py:523
  74.1 2.2 %collective-permute-start.3 = (bf16[1024,160]{1,0:T(8,128)(2,1)S(1)}, bf16[1024,160]{1,0:T(8,128)(2,1)S(1)}, u32[]{:S(2)}, u32[]{:S(2)}) collective-permute-start(bf16[1024,160]{1,0:T(8,128)(2,1)S(1)} %get-tuple-element.46), channel_id=1, source_target_pairs={{0,16},{16,0},{1,17},{17,1},{2,18},{18,2},{3,19},{19,3},{4,20},{20... | collective-permute-start | bytes 983048 | tf_op jit(solution)/shard_map/ppermute | solution.py:523
  78.7 1.1 copy-start.1
  79.8 6.1 %copy-start.9 = (bf16[3,320,320]{2,1,0:T(8,128)(2,1)S(1)}, bf16[3,320,320]{2,1,0:T(8,128)(2,1)}, u32[]{:S(2)}) copy-start(bf16[3,320,320]{2,1,0:T(8,128)(2,1)} %w_ref.3) | copy-start | bytes 1843204
  79.8 26.0 %all-to-all-start.2 = ((bf16[16,64,640]{2,1,0:T(8,128)(2,1)}), bf16[16,64,640]{2,1,0:T(8,128)(2,1)}, u32[]{:S(2)}, u32[]{:S(2)}) async-start(bf16[16,64,640]{2,1,0:T(8,128)(2,1)} %bitcast.17), calls=%async_computation.2 | async-start | bytes 2621440 | tf_op jit(solution)/shard_map/all_to_all | solution.py:529
  85.9 1.4 copy-start.11
  87.3 2.5 %copy-start.4 = (bf16[3,3,320,320]{3,2,1,0:T(8,128)(2,1)S(1)}, bf16[3,3,320,320]{3,2,1,0:T(8,128)(2,1)}, u32[]{:S(2)}) copy-start(bf16[3,3,320,320]{3,2,1,0:T(8,128)(2,1)} %param.8) | copy-start | bytes 5529604
  87.3 2.5 %copy-start.7 = (bf16[1,2,16,32,320]{4,3,2,1,0:T(8,128)(2,1)S(1)}, bf16[1,2,16,32,320]{4,3,2,1,0:T(8,128)(2,1)}, u32[]{:S(2)}) copy-start(bf16[1,2,16,32,320]{4,3,2,1,0:T(8,128)(2,1)} %param.6) | copy-start | bytes 1966084
  148.6 8.7 %collective-permute-start.7 = (bf16[1024,640]{1,0:T(8,128)(2,1)S(1)}, bf16[1024,640]{1,0:T(8,128)(2,1)S(1)}, u32[]{:S(2)}, u32[]{:S(2)}) collective-permute-start(bf16[1024,640]{1,0:T(8,128)(2,1)S(1)} %bitcast.12), channel_id=1, source_target_pairs={{0,16},{16,0},{1,17},{17,1},{2,18},{18,2},{3,19},{19,3},{4,20},{20... | collective-permute-start | bytes 3932168 | tf_op jit(solution)/shard_map/ppermute | solution.py:523

commit v5 on v4

--- a/solution.py
+++ b/solution.py
@@ -276,10 +276,46 @@
     )(sums, h0, h1, grad, cot, gain)
 
 
+def mix(h_ref, base, mean, scale, gain):
+    pre = (h_ref[pl.ds(base, STEP), :].astype(F32) - mean) * scale * gain
+    return pre / (1.0 + jnp.exp(-pre))
+
+
 def mixed_body(
-    hb_ref, h0_ref, h1_ref, ha_ref, cot_ref, stat_ref, gain_ref, sums_ref,
-    far_mx_ref, keep_ref, give_ref, mx_ref, turned, sem,
+    h0_ref, h1_ref, before_ref, cot_ref, after_ref, stat_ref, gain_ref, sums_ref,
+    keep_ref, give_ref, turned,
 ):
+    mean, scale = stat_ref[0:1, :], stat_ref[1:2, :]
+    gain = gain_ref[...].reshape(1, C)
+    for f, h_ref in enumerate((h0_ref, h1_ref)):
+        for step in range(PIX // STEP):
+            act = mix(h_ref, step * STEP, mean, scale, gain).astype(BF16)
+            turned[:, f * PIX + step * STEP : f * PIX + (step + 1) * STEP] = act.T
+    core = lax.axis_index("c")
+    first, second = turned[:, 0:PIX], turned[:, PIX:ROWS]
+    for k in range(3):
+        if k == 1:
+            part = jnp.dot(turned[...], cot_ref[...], preferred_element_type=F32)
+        else:
+            one = cot_ref[PIX:ROWS, :] if k == 0 else before_ref[...]
+            two = after_ref[...] if k == 0 else cot_ref[0:PIX, :]
+            part = jnp.dot(first, one, preferred_element_type=F32)
+            part = part + jnp.dot(second, two, preferred_element_type=F32)
+        left, right = part[:, 0:HALF], part[:, HALF:C]
+        keep_ref[k * C : (k + 1) * C, 0:HALF] = jnp.where(core == 0, left, right)
+        give_ref[k * C : (k + 1) * C, 0:HALF] = jnp.where(core == 0, right, left)
+
+
+def temporal_gradient(h0, h1, before, cot, after, stat, gain, sums):
+    return call(
+        mixed_body,
+        (shape((3 * C, 256), F32), shape((3 * C, 256), F32)),
+        (pltpu.VMEM((C, ROWS), BF16),),
+        flops=1_500_000_000,
+    )(h0, h1, before, cot, after, stat, gain, sums)
+
+
+def temporal_body(hb_ref, h0_ref, h1_ref, ha_ref, stat_ref, gain_ref, w_ref, out_ref, mx_ref):
     mean, scale = stat_ref[0:1, :], stat_ref[1:2, :]
     gain = gain_ref[...].reshape(1, C)
     place = lax.axis_index(FRAME)
@@ -288,47 +324,13 @@
 
         def step_body(step, carry, n=n, h_ref=h_ref):
             base = pl.multiple_of(step * STEP, STEP)
-            pre = (h_ref[pl.ds(base, STEP), :].astype(F32) - mean) * scale * gain
-            act = pre / (1.0 + jnp.exp(-pre))
+            act = mix(h_ref, base, mean, scale, gain)
             if live[n] is not None:
                 act = jnp.where(live[n], act, 0.0)
             mx_ref[pl.ds(base + n * PIX, STEP), :] = act.astype(BF16)
             return carry
 
         lax.fori_loop(0, PIX // STEP, step_body, 0)
-    send = pltpu.make_async_copy(mx_ref, far_mx_ref, sem)
-    send.start()
-    for n in range(4 * PIX // STEP):
-        where = slice(n * STEP, (n + 1) * STEP)
-        turned[:, where] = mx_ref[where, :].T
-    core = lax.axis_index("c")
-    for k in range(3):
-        part = jnp.dot(
-            turned[:, k * PIX : k * PIX + ROWS], cot_ref[...], preferred_element_type=F32
-        )
-        left, right = part[:, 0:HALF], part[:, HALF:C]
-        keep_ref[k * C : (k + 1) * C, 0:HALF] = jnp.where(core == 0, left, right)
-        give_ref[k * C : (k + 1) * C, 0:HALF] = jnp.where(core == 0, right, left)
-    send.wait()
-
-
-def mixed_frames(before, h0, h1, after, cot, stat, gain, sums):
-    return call(
-        mixed_body,
-        (far((4 * PIX, C), BF16), shape((3 * C, 256), F32), shape((3 * C, 256), F32)),
-        (
-            pltpu.VMEM((4 * PIX, C), BF16),
-            pltpu.VMEM((C, 4 * PIX), BF16),
-            pltpu.SemaphoreType.DMA,
-        ),
-        flops=1_500_000_000,
-        limit=12,
-        ins=[VMEM] * 8,
-        outs=(FAR, VMEM, VMEM),
-    )(before, h0, h1, after, cot, stat, gain, sums)
-
-
-def temporal_body(mx_ref, h0_ref, h1_ref, w_ref, out_ref):
     for f, h_ref in enumerate((h0_ref, h1_ref)):
         total = None
         for k in range(3):
@@ -342,8 +344,13 @@
         out_ref[f * PIX : (f + 1) * PIX, :] = (h_ref[...].astype(F32) + low).astype(BF16)
 
 
-def temporal(mixed, h0, h1, weight):
-    return call(temporal_body, shape((ROWS, C), BF16), flops=1_500_000_000)(mixed, h0, h1, weight)
+def temporal(before, h0, h1, after, stat, gain, weight):
+    return call(
+        temporal_body,
+        shape((ROWS, C), BF16),
+        (pltpu.VMEM((4 * PIX, C), BF16),),
+        flops=1_500_000_000,
+    )(before, h0, h1, after, stat, gain, weight)
 
 
 def whole_grad(part_ref, h_ref, stat_ref, sums, base, f):
@@ -389,30 +396,43 @@
 
 
 def weight_grad_body(
-    mine_turned_ref, other_turned_ref, mine_ref, other_ref, keep_ref, got_ref, out_ref, rhs
+    mine_turned_ref, other_turned_ref, mine_ref, other_ref, keep_ref, got_ref, far_ref, rhs, out, sem
 ):
-    total = None
-    for n, (ref, turned_ref) in enumerate(
-        ((mine_ref, mine_turned_ref), (other_ref, other_turned_ref))
-    ):
+    for n, ref in enumerate((mine_ref, other_ref)):
         for f in range(2):
             where = slice(f * PIX, (f + 1) * PIX)
             for i, tap in enumerate(row_taps(ref[where, :])):
                 rhs[n, where, i * HALF : (i + 1) * HALF] = tap
-        part = jnp.dot(turned_ref[...], rhs[n], preferred_element_type=F32)
-        total = part if total is None else total + part
-    out_ref[0 : 3 * C, 0 : 3 * HALF] = total.astype(BF16)
-    kept = keep_ref[:, 0:HALF] + got_ref[:, 0:HALF]
-    out_ref[0 : 3 * C, 3 * HALF : 4 * HALF] = kept.astype(BF16)
-    out_ref[3 * C :, :] = jnp.zeros((1024 - 3 * C, 4 * HALF), BF16)
+    sends = []
+    for j in range(3):
+        here = slice(j * C, (j + 1) * C)
+        total = jnp.dot(mine_turned_ref[here, :], rhs[0], preferred_element_type=F32)
+        total = total + jnp.dot(other_turned_ref[here, :], rhs[1], preferred_element_type=F32)
+        out[here, 0 : 3 * HALF] = total.astype(BF16)
+        kept = keep_ref[here, 0:HALF] + got_ref[here, 0:HALF]
+        out[here, 3 * HALF : 4 * HALF] = kept.astype(BF16)
+        if j == 2:
+            out[3 * C :, :] = jnp.zeros((1024 - 3 * C, 4 * HALF), BF16)
+            here = slice(j * C, 1024)
+        send = pltpu.make_async_copy(out.at[here, :], far_ref.at[here, :], sem.at[j])
+        send.start()
+        sends.append(send)
+    for send in sends:
+        send.wait()
 
 
 def weight_gradients(mine_turned, other_turned, mine, other, keep, got):
     return call(
         weight_grad_body,
-        shape((1024, 4 * HALF), BF16),
-        (pltpu.VMEM((2, ROWS, 3 * HALF), BF16),),
+        far((1024, 4 * HALF), BF16),
+        (
+            pltpu.VMEM((2, ROWS, 3 * HALF), BF16),
+            pltpu.VMEM((1024, 4 * HALF), BF16),
+            pltpu.SemaphoreType.DMA((3,)),
+        ),
         flops=2_500_000_000,
+        ins=[VMEM] * 6,
+        outs=FAR,
     )(mine_turned, other_turned, mine, other, keep, got)
 
 
@@ -536,9 +556,13 @@
     value = value.reshape(line, 1024 // plane // line, width)
     value = jnp.sum(lax.all_to_all(value, LINE, 0, 0), axis=0).astype(BF16)
     value = jnp.broadcast_to(value[None], (line,) + value.shape)
-    value = lax.all_to_all(value, LINE, 0, 0).reshape(1024 // plane, width)
+    return lax.all_to_all(value, LINE, 0, 0).reshape(1024 // plane, width)
+
+
+def everyone_gets(value):
+    plane = lax.axis_size(PLANE)
     value = jnp.broadcast_to(value[None], (plane,) + value.shape)
-    return lax.all_to_all(value, PLANE, 0, 0).reshape(1024, width)
+    return lax.all_to_all(value, PLANE, 0, 0).reshape(1024, value.shape[2])
 
 
 def on_device(clips, cotangent, spatial_weight, temporal_weight, gain_one, gain_two):
@@ -550,18 +574,14 @@
     barrier = lax.optimization_barrier
     cot_before, cot_after = neighbours(cot[:PIX], cot[PIX:])
     h0, h1, mine_turned, stat_one, sums = forward(x, spatial_weight, gain_one, size)
-    edge0, edge1, cot_before, cot_after = barrier((h0, h1, cot_before, cot_after))
-    before, after = neighbours(edge0, edge1)
     sums = lax.all_to_all(sums, FRAME, 0, 0)
     mixed_grad = mixed_gradient(cot_before, cot, cot_after, temporal_weight)
     sums, mine_turned, mixed_grad = barrier((sums, mine_turned, mixed_grad))
     other_turned = swap_cores(mine_turned)
-    part, clip_stat, sums = slopes(
-        sums, h0, h1, mixed_grad, cot, gain_two, count
-    )
+    part, clip_stat, sums = slopes(sums, h0, h1, mixed_grad, cot, gain_two, count)
     sums = lax.all_to_all(sums, FRAME, 0, 0)
-    mixed, temporal_keep, temporal_give = mixed_frames(
-        before, h0, h1, after, cot, clip_stat, gain_two, sums
+    temporal_keep, temporal_give = temporal_gradient(
+        h0, h1, cot_before, cot, cot_after, clip_stat, gain_two, sums
     )
     temporal_got = swap_cores(temporal_give)
     low_keep, low_give, total = hidden_gradient(sums, clip_stat, part, h0, h1, count)
@@ -569,14 +589,17 @@
     packed = weight_gradients(
         mine_turned, other_turned, low_keep, low_got, temporal_keep, temporal_got
     )
-    packed, mixed, total = barrier((packed, mixed, total))
-    output = temporal(mixed, h0, h1, temporal_weight)
+    packed, total, edge0, edge1 = barrier((packed, total, h0, h1))
+    shares = everyone_total(packed)
+    before, after = neighbours(edge0, edge1)
     input_grad = input_gradient(
         part, h0, h1, clip_stat, total, x, stat_one, gain_one, spatial_weight
     )
-    shares = everyone_total(packed)
-    shares, output, input_grad = barrier((shares, output, input_grad))
+    shares, input_grad, before, after = barrier((shares, input_grad, before, after))
     mine = everyone_share(shares)
+    mine, before, after = barrier((mine, before, after))
+    output = temporal(before, h0, h1, after, clip_stat, gain_two, temporal_weight)
+    mine, output = barrier((everyone_gets(mine), output))
     other = swap_cores(mine)
     spatial_grad, temporal_grad = unpack(mine, other)
     return (

time: 161 us -> 157 us (0.975)
  blocking collectives: 59.8 us -> 34.4 us
  waiting for transfers between devices: 18.6 us -> 29.4 us
  starting transfers between devices: 39.2 us -> 45 us
  local copies, waits for them, and re-layouts: 5.93 us -> 10 us
    all_to_all x2 -> x1, blocking collectives: 27.6 us -> 9.61 us  [everyone_share(): return lax.all_to_all(value, LINE, 0, 0).reshape(1024 // plane, width)]
    all_to_all x0 -> x1, waiting for transfers between devices: none -> 10.2 us  [everyone_gets(): return lax.all_to_all(value, PLANE, 0, 0).reshape(1024, value.shape[2])]
    ppermute x2, waiting for transfers between devices: 2.4 us -> 10.5 us  [neighbours(): after = lax.ppermute(first, FRAME, [(i + 1, i) for i in range(size - 1)])]
    all_to_all x1, waiting for transfers between devices: 7.52 us -> 0.01 us  [everyone_total(): return lax.all_to_all(value, PLANE, 0, 0)]
    all_to_all x0 -> x1, starting transfers between devices: none -> 6.89 us  [everyone_gets(): return lax.all_to_all(value, PLANE, 0, 0).reshape(1024, value.shape[2])]
    all_to_all x1, blocking collectives: 18.7 us -> 11.9 us  [on_device(): sums = lax.all_to_all(sums, FRAME, 0, 0)]
    unnamed x24 -> x42, local copies, waits for them, and re-layouts: 3.62 us -> 6.66 us
  transfers between devices with their start and end apart: 10 -> 11, of which waited for: 5 -> 6; matrix products, arithmetic and copies ran while one was open for 0% -> 0% of each run, Pallas kernels for 18% -> 18%
where the time goes in v5:
time: 157 us; the launch traced here: 156 us
  starting transfers between devices  45 us (29%)
  Pallas kernels  34.6 us (22%)
  blocking collectives  34.4 us (22%)
  waiting for transfers between devices  29.4 us (19%)
  local copies, waits for them, and re-layouts  10 us (6%)
    all_to_all x1, blocking collectives, everyone_share(): value = jnp.sum(lax.all_to_all(value, LINE, 0, 0), axis=0).astype(BF16)  12.9 us
    all_to_all x1, starting transfers between devices, on_device(): sums = lax.all_to_all(sums, FRAME, 0, 0)  12.1 us
    all_to_all x1, blocking collectives, on_device(): sums = lax.all_to_all(sums, FRAME, 0, 0)  11.9 us
    ppermute x2, waiting for transfers between devices, neighbours(): after = lax.ppermute(first, FRAME, [(i + 1, i) for i in range(size - 1)])  10.5 us
    ppermute x4, starting transfers between devices, swap_cores(): return lax.ppermute(value, 'c', [(0, 1), (1, 0)])  10.4 us
    all_to_all x1, waiting for transfers between devices, everyone_gets(): return lax.all_to_all(value, PLANE, 0, 0).reshape(1024, value.shape[2])  10.2 us
    all_to_all x1, blocking collectives, everyone_share(): return lax.all_to_all(value, LINE, 0, 0).reshape(1024 // plane, width)  9.61 us
    pallas_call x1, Pallas kernels, input_gradient(): call(input_grad_body, shape((ROWS, C), BF16), (pltpu.VMEM((3 * PAD, 3 * C...  8.47 us
  transfers between devices with their start and end apart: 11, of which 6 were waited for; matrix products, arithmetic and copies ran while one was open for 0% of the time, Pallas kernels for 18%

profile of v5, /device:TPU:1, one launch (start us, length us, event | category | flops | bytes accessed | tf_op | source)
XLA Modules:
  0.0 155.9 jit_solution(9824175716231167473)
XLA Ops:
  0.6 0.0 copy-start.17
  0.6 0.0 copy-start.5
  0.7 2.1 %fusion = (bf16[1,1,16,32,320]{4,3,2,1,0:T(8,128)(2,1)}, bf16[1,1,16,32,320]{4,3,2,1,0:T(8,128)(2,1)}) fusion(bf16[1,2,16,32,320]{4,3,2,1,0:T(8,128)(2,1)} %param.7), kind=kLoop, calls=%fused_computation.1 | loop fusion | bytes 1310720 | tf_op jit(solution)/shard_map/slice | solution.py:575
  2.8 5.7 %collective-permute-start = (bf16[512,320]{1,0:T(8,128)(2,1)}, bf16[512,320]{1,0:T(8,128)(2,1)S(1)}, u32[]{:S(2)}, u32[]{:S(2)}) collective-permute-start(bf16[512,320]{1,0:T(8,128)(2,1)} %bitcast.2), channel_id=1, source_target_pairs={{0,1},{1,2},{2,3},{3,4},{4,5},{5,6},{6,7},{7,8},{8,9},{9,10},{10,1... | collective-permute-start | bytes 983048 | tf_op jit(solution)/shard_map/ppermute | solution.py:537
  8.5 1.3 collective-permute-start.1
  9.9 0.0 copy-start
  9.9 0.0 copy-start.7
  9.9 7.9 %shard_map.93 = (bf16[512,320]{1,0:T(8,128)(2,1)S(1)}, bf16[512,320]{1,0:T(8,128)(2,1)S(1)}, bf16[960,1024]{1,0:T(8,128)(2,1)}, f32[8,320]{1,0:T(8,128)S(1)}, f32[16,2,320]{2,1,0:T(2,128)}) custom-call(bf16[1024,320]{1,0:T(8,128)(2,1)S(1)} %bitcast.19, bf16[9,320,320]{2,1,0:T(8,128)(2,1)} %bitcast.17, f32[320]{0:T(512)S(1)} %copy-done.17), custom_call_target="tpu_custom_call" | custom-call | flops 2500000000 | bytes 8000000 | tf_op jit(solution)/shard_map/pallas_call | solution.py:195
  17.9 12.1 %all-to-all-start = ((f32[16,2,320]{2,1,0:T(2,128)}), f32[16,2,320]{2,1,0:T(2,128)S(1)}, u32[]{:S(2)}, u32[]{:S(2)}) async-start(f32[16,2,320]{2,1,0:T(2,128)} %get-tuple-element.35), calls=%async_computation | async-start | bytes 98304 | tf_op jit(solution)/shard_map/all_to_all | solution.py:577
  30.0 0.0 copy-start.9
  30.0 2.4 %collective-permute-done.1.after_ref = bf16[512,320]{1,0:T(8,128)(2,1)S(1)} collective-permute-done((bf16[512,320]{1,0:T(8,128)(2,1)}, bf16[512,320]{1,0:T(8,128)(2,1)S(1)}, u32[]{:S(2)}, u32[]{:S(2)}) %collective-permute-start.1) | collective-permute-done | bytes 327712 | tf_op jit(solution)/shard_map/ppermute | solution.py:538
  32.4 0.0 copy-start.2
  32.4 2.5 %shard_map.94.grad_ref = bf16[1024,320]{1,0:T(8,128)(2,1)} custom-call(bf16[512,320]{1,0:T(8,128)(2,1)S(1)} %collective-permute-done.before_ref, bf16[1024,320]{1,0:T(8,128)(2,1)S(1)} %bitcast.14, bf16[512,320]{1,0:T(8,128)(2,1)S(1)} %collective-permute-done.1.after_ref, bf16[3,320,320]{2,1,0:T(8,128)(2,1)S(1)} %copy-done.7), custom_call_target="tpu_custom_call" | custom-call | flops 1500000000 | bytes 8000000 | tf_op jit(solution)/shard_map/pallas_call | solution.py:241
  34.9 4.1 %all-to-all-done.sums_ref = f32[16,2,320]{2,1,0:T(2,128)S(1)} async-done(((f32[16,2,320]{2,1,0:T(2,128)}), f32[16,2,320]{2,1,0:T(2,128)S(1)}, u32[]{:S(2)}, u32[]{:S(2)}) %all-to-all-start) | async-done | bytes 40992 | tf_op jit(solution)/shard_map/all_to_all | solution.py:577
  39.0 2.6 %collective-permute-start.2 = (bf16[960,1024]{1,0:T(8,128)(2,1)}, bf16[960,1024]{1,0:T(8,128)(2,1)S(1)}, u32[]{:S(2)}, u32[]{:S(2)}) collective-permute-start(bf16[960,1024]{1,0:T(8,128)(2,1)} %get-tuple-element.37.mine_turned_ref), channel_id=1, source_target_pairs={{0,16},{16,0},{1,17},{17,1},{2,18},{18,2},{3,19},{19,3},{4,20},{20... | collective-permute-start | bytes 5898248 | tf_op jit(solution)/shard_map/ppermute | solution.py:543
  41.5 1.1 copy-done.1
  42.7 1.8 %shard_map.95 = (f32[1024,320]{1,0:T(8,128)S(1)}, f32[8,320]{1,0:T(8,128)S(1)}, f32[16,2,320]{2,1,0:T(2,128)S(1)}) custom-call(f32[16,2,320]{2,1,0:T(2,128)S(1)} %all-to-all-done.sums_ref, bf16[512,320]{1,0:T(8,128)(2,1)S(1)} %get-tuple-element.54.h0_ref, bf16[512,320]{1,0:T(8,128)(2,1)S(1)} %get-tuple-element.53.h1_ref, bf16[1024,320]{1,0:T(8,128)(2,1)S(1)} %copy-done.1, ...), custom_call_target="tpu_custom_call" | custom-call | bytes 8000000 | tf_op jit(solution)/shard_map/pallas_call | solution.py:273
  44.5 11.9 %all_to_all.30.sums_ref = f32[16,2,320]{2,1,0:T(2,128)S(1)} all-to-all(f32[16,2,320]{2,1,0:T(2,128)S(1)} %get-tuple-element.42), channel_id=1, replica_groups=mesh['zl'=2,'x'=4,'c'=2,'y'=4,'zh'=4] {'y','zh'}, dimensions={0} | all-to-all | bytes 81920 | tf_op jit(solution)/shard_map/all_to_all | solution.py:582
  56.4 1.8 %shard_map.97 = (f32[960,256]{1,0:T(8,128)S(1)}, f32[960,256]{1,0:T(8,128)S(1)}) custom-call(bf16[512,320]{1,0:T(8,128)(2,1)S(1)} %get-tuple-element.54.h0_ref, bf16[512,320]{1,0:T(8,128)(2,1)S(1)} %get-tuple-element.53.h1_ref, bf16[512,320]{1,0:T(8,128)(2,1)S(1)} %copy-done.10, bf16[1024,320]{1,0:T(8,128)(2,1)S(1)} %bitcast.16, ...), custom_call_target="tpu_custom_call" | custom-call | flops 1500000000 | bytes 8000000 | tf_op jit(solution)/shard_map/pallas_call | solution.py:310
  58.2 0.0 copy-start.4
  58.2 0.9 collective-permute-start.4
  59.1 1.9 %shard_map.96 = (bf16[1024,160]{1,0:T(8,128)(2,1)S(1)}, bf16[1024,160]{1,0:T(8,128)(2,1)S(1)}, f32[8,320]{1,0:T(8,128)S(1)}) custom-call(f32[16,2,320]{2,1,0:T(2,128)S(1)} %all_to_all.30.sums_ref, f32[8,320]{1,0:T(8,128)S(1)} %get-tuple-element.43.stat_ref.clip_ref, f32[1024,320]{1,0:T(8,128)S(1)} %get-tuple-element.44.part_ref, ...), custom_call_target="tpu_custom_call" | custom-call | bytes 8000000 | tf_op jit(solution)/shard_map/pallas_call | solution.py:383
  61.0 0.3 collective-permute-start.3
  61.3 1.9 %collective-permute-done.3.other_ref = bf16[1024,160]{1,0:T(8,128)(2,1)S(1)} collective-permute-done((bf16[1024,160]{1,0:T(8,128)(2,1)S(1)}, bf16[1024,160]{1,0:T(8,128)(2,1)S(1)}, u32[]{:S(2)}, u32[]{:S(2)}) %collective-permute-start.3) | collective-permute-done | bytes 327712 | tf_op jit(solution)/shard_map/ppermute | solution.py:543
  63.2 3.2 %shard_map.98 = bf16[1024,640]{1,0:T(8,128)(2,1)} custom-call(bf16[960,1024]{1,0:T(8,128)(2,1)S(1)} %copy-done.4, bf16[960,1024]{1,0:T(8,128)(2,1)S(1)} %collective-permute-done.2.other_turned_ref, bf16[1024,160]{1,0:T(8,128)(2,1)S(1)} %get-tuple-element.45.mine_ref, bf16[1024,160]{1,0:T(8,128)(2,1)S(1)} %collective-permute-done.3.other_ref, ...), custom_call_target="tpu_custom_call" | custom-call | flops 2500000000 | bytes 8000000 | tf_op jit(solution)/shard_map/pallas_call | solution.py:425
  66.4 0.0 copy-start.6
  66.4 4.9 %all-to-all-start.2 = ((bf16[16,64,640]{2,1,0:T(8,128)(2,1)}), bf16[16,64,640]{2,1,0:T(8,128)(2,1)}, u32[]{:S(2)}, u32[]{:S(2)}) async-start(bf16[16,64,640]{2,1,0:T(8,128)(2,1)} %bitcast.21), calls=%async_computation.2 | async-start | bytes 2621440 | tf_op jit(solution)/shard_map/all_to_all | solution.py:549
  71.3 2.5 %collective-permute-start.5 = (bf16[512,320]{1,0:T(8,128)(2,1)S(1)}, bf16[512,320]{1,0:T(8,128)(2,1)S(1)}, u32[]{:S(2)}, u32[]{:S(2)}) collective-permute-start(bf16[512,320]{1,0:T(8,128)(2,1)S(1)} %get-tuple-element.53.h1_ref), channel_id=1, source_target_pairs={{0,1},{1,2},{2,3},{3,4},{4,5},{5,6},{6,7},{7,8},{8,9},{9,10},{10,1... | collective-permute-start | bytes 983048 | tf_op jit(solution)/shard_map/ppermute | solution.py:537
  73.8 1.3 collective-permute-start.6
  75.1 0.0 copy-start.3
  75.1 1.6 %copy-done.3 = bf16[3,3,320,320]{3,2,1,0:T(8,128)(2,1)S(1)} copy-done((bf16[3,3,320,320]{3,2,1,0:T(8,128)(2,1)S(1)}, bf16[3,3,320,320]{3,2,1,0:T(8,128)(2,1)}, u32[]{:S(2)}) %copy-start.3) | copy-done | bytes 1843224
  76.7 0.7 copy-done.16
  77.4 0.7 copy-done.18
  78.1 0.7 copy-done.20
  78.8 8.5 %shard_map.99 = bf16[1024,320]{1,0:T(8,128)(2,1)} custom-call(f32[1024,320]{1,0:T(8,128)S(1)} %get-tuple-element.44.part_ref, bf16[512,320]{1,0:T(8,128)(2,1)S(1)} %get-tuple-element.54.h0_ref, bf16[512,320]{1,0:T(8,128)(2,1)S(1)} %get-tuple-element.53.h1_ref, f32[8,320]{1,0:T(8,128)S(1)} %get-tuple-element.43.stat_ref.clip_ref, f32[8,320]{1,0:T(8,128)S(1)} %copy-done.16, ...), custom_call_target="tpu_custom_call" | custom-call | flops 2500000000 | bytes 8000000 | tf_op jit(solution)/shard_map/pallas_call | solution.py:498
  87.3 8.1 %collective-permute-done.6.ha_ref = bf16[512,320]{1,0:T(8,128)(2,1)S(1)} collective-permute-done((bf16[512,320]{1,0:T(8,128)(2,1)S(1)}, bf16[512,320]{1,0:T(8,128)(2,1)S(1)}, u32[]{:S(2)}, u32[]{:S(2)}) %collective-permute-start.6) | collective-permute-done | bytes 327712 | tf_op jit(solution)/shard_map/ppermute | solution.py:538
  95.4 0.7 copy-done.13
  96.2 1.5 convert_reduce_fusion
  97.7 12.9 %all_to_all.31 = f32[8,8,640]{2,1,0:T(8,128)S(1)} all-to-all(f32[8,8,640]{2,1,0:T(8,128)S(1)} %bitcast.22), channel_id=1, replica_groups=mesh['zl'=2,'x'=4,'c'=2,'y'=4,'zh'=4] {'zl','zh'}, dimensions={0} | all-to-all | bytes 327680 | tf_op jit(solution)/shard_map/all_to_all | solution.py:557
  110.6 9.6 %all_to_all.32 = bf16[8,8,640]{2,1,0:T(8,128)(2,1)S(1)} all-to-all(bf16[8,8,640]{2,1,0:T(8,128)(2,1)S(1)} %broadcast_in_dim.4), channel_id=1, replica_groups=mesh['zl'=2,'x'=4,'c'=2,'y'=4,'zh'=4] {'zl','zh'}, dimensions={0} | all-to-all | bytes 163840 | tf_op jit(solution)/shard_map/all_to_all | solution.py:559
  120.2 1.2 broadcast_in_dim.5
  121.4 6.9 %all-to-all-start.5 = ((bf16[16,64,640]{2,1,0:T(8,128)(2,1)}), bf16[16,64,640]{2,1,0:T(8,128)(2,1)S(1)}, u32[]{:S(2)}, u32[]{:S(2)}) async-start(bf16[16,64,640]{2,1,0:T(8,128)(2,1)} %broadcast_in_dim.5), calls=%async_computation.5 | async-start | bytes 2621440 | tf_op jit(solution)/shard_map/all_to_all | solution.py:565
  128.3 1.0 copy-done.14
  129.3 3.9 %shard_map.100 = bf16[1024,320]{1,0:T(8,128)(2,1)} custom-call(bf16[512,320]{1,0:T(8,128)(2,1)S(1)} %collective-permute-done.5.hb_ref, bf16[512,320]{1,0:T(8,128)(2,1)S(1)} %get-tuple-element.54.h0_ref, bf16[512,320]{1,0:T(8,128)(2,1)S(1)} %get-tuple-element.53.h1_ref, bf16[512,320]{1,0:T(8,128)(2,1)S(1)} %copy-done.14, ...), custom_call_target="tpu_custom_call" | custom-call | flops 1500000000 | bytes 8000000 | tf_op jit(solution)/shard_map/pallas_call | solution.py:348
  133.2 10.2 %all-to-all-done.5 = bf16[16,64,640]{2,1,0:T(8,128)(2,1)S(1)} async-done(((bf16[16,64,640]{2,1,0:T(8,128)(2,1)}), bf16[16,64,640]{2,1,0:T(8,128)(2,1)S(1)}, u32[]{:S(2)}, u32[]{:S(2)}) %all-to-all-start.5) | async-done | bytes 1310752 | tf_op jit(solution)/shard_map/all_to_all | solution.py:565
  143.4 6.6 %collective-permute-start.7 = (bf16[1024,640]{1,0:T(8,128)(2,1)S(1)}, bf16[1024,640]{1,0:T(8,128)(2,1)S(1)}, u32[]{:S(2)}, u32[]{:S(2)}) collective-permute-start(bf16[1024,640]{1,0:T(8,128)(2,1)S(1)} %bitcast.12), channel_id=1, source_target_pairs={{0,16},{16,0},{1,17},{17,1},{2,18},{18,2},{3,19},{19,3},{4,20},{20... | collective-permute-start | bytes 3932168 | tf_op jit(solution)/shard_map/ppermute | solution.py:543
  150.0 2.7 %collective-permute-done.7.other_ref = bf16[1024,640]{1,0:T(8,128)(2,1)S(1)} collective-permute-done((bf16[1024,640]{1,0:T(8,128)(2,1)S(1)}, bf16[1024,640]{1,0:T(8,128)(2,1)S(1)}, u32[]{:S(2)}, u32[]{:S(2)}) %collective-permute-start.7) | collective-permute-done | bytes 1310752 | tf_op jit(solution)/shard_map/ppermute | solution.py:543
  152.7 3.2 %shard_map.101 = (bf16[9,320,320]{2,1,0:T(8,128)(2,1)}, bf16[3,320,320]{2,1,0:T(8,128)(2,1)}) custom-call(bf16[1024,640]{1,0:T(8,128)(2,1)S(1)} %bitcast.13, bf16[1024,640]{1,0:T(8,128)(2,1)S(1)} %collective-permute-done.7.other_ref), custom_call_target="tpu_custom_call" | custom-call | bytes 8000000 | tf_op jit(solution)/shard_map/pallas_call | solution.py:532
  (33 shorter events, 0.1 us)
Async XLA Ops:
  0.6 9.2 %copy-start.17 = (f32[320]{0:T(512)S(1)}, f32[320]{0:T(512)}, u32[]{:S(2)}) copy-start(f32[320]{0:T(512)} %gain_ref.8) | copy-start | bytes 3844
  0.6 9.2 %copy-start.5 = (bf16[1,2,16,32,320]{4,3,2,1,0:T(8,128)(2,1)S(1)}, bf16[1,2,16,32,320]{4,3,2,1,0:T(8,128)(2,1)}, u32[]{:S(2)}) copy-start(bf16[1,2,16,32,320]{4,3,2,1,0:T(8,128)(2,1)} %param.6) | copy-start | bytes 1966084
  2.8 27.2 %collective-permute-start = (bf16[512,320]{1,0:T(8,128)(2,1)}, bf16[512,320]{1,0:T(8,128)(2,1)S(1)}, u32[]{:S(2)}, u32[]{:S(2)}) collective-permute-start(bf16[512,320]{1,0:T(8,128)(2,1)} %bitcast.2), channel_id=1, source_target_pairs={{0,1},{1,2},{2,3},{3,4},{4,5},{5,6},{6,7},{7,8},{8,9},{9,10},{10,1... | collective-permute-start | bytes 983048 | tf_op jit(solution)/shard_map/ppermute | solution.py:537
  8.5 23.8 %collective-permute-start.1 = (bf16[512,320]{1,0:T(8,128)(2,1)}, bf16[512,320]{1,0:T(8,128)(2,1)S(1)}, u32[]{:S(2)}, u32[]{:S(2)}) collective-permute-start(bf16[512,320]{1,0:T(8,128)(2,1)} %bitcast.4), channel_id=1, source_target_pairs={{1,0},{2,1},{3,2},{4,3},{5,4},{6,5},{7,6},{8,7},{9,8},{10,9},{11,1... | collective-permute-start | bytes 983048 | tf_op jit(solution)/shard_map/ppermute | solution.py:538
  9.9 22.5 %copy-start = (bf16[1,2,16,32,320]{4,3,2,1,0:T(8,128)(2,1)S(1)}, bf16[1,2,16,32,320]{4,3,2,1,0:T(8,128)(2,1)}, u32[]{:S(2)}) copy-start(bf16[1,2,16,32,320]{4,3,2,1,0:T(8,128)(2,1)} %param.7) | copy-start | bytes 1966084
  9.9 22.5 %copy-start.7 = (bf16[3,320,320]{2,1,0:T(8,128)(2,1)S(1)}, bf16[3,320,320]{2,1,0:T(8,128)(2,1)}, u32[]{:S(2)}) copy-start(bf16[3,320,320]{2,1,0:T(8,128)(2,1)} %w_ref.3) | copy-start | bytes 1843204
  17.8 14.5 %copy-start.19 = (f32[8,320]{1,0:T(8,128)}, f32[8,320]{1,0:T(8,128)S(1)}, u32[]{:S(2)}) copy-start(f32[8,320]{1,0:T(8,128)S(1)} %get-tuple-element.52.stat_ref) | copy-start | bytes 30724
  17.9 21.1 %all-to-all-start = ((f32[16,2,320]{2,1,0:T(2,128)}), f32[16,2,320]{2,1,0:T(2,128)S(1)}, u32[]{:S(2)}, u32[]{:S(2)}) async-start(f32[16,2,320]{2,1,0:T(2,128)} %get-tuple-element.35), calls=%async_computation | async-start | bytes 98304 | tf_op jit(solution)/shard_map/all_to_all | solution.py:577
  30.0 4.9 %copy-start.9 = (bf16[512,320]{1,0:T(8,128)(2,1)}, bf16[512,320]{1,0:T(8,128)(2,1)S(1)}, u32[]{:S(2)}) copy-start(bf16[512,320]{1,0:T(8,128)(2,1)S(1)} %collective-permute-done.before_ref) | copy-start | bytes 983044
  32.4 2.5 %copy-start.11 = (bf16[512,320]{1,0:T(8,128)(2,1)}, bf16[512,320]{1,0:T(8,128)(2,1)S(1)}, u32[]{:S(2)}) copy-start(bf16[512,320]{1,0:T(8,128)(2,1)S(1)} %collective-permute-done.1.after_ref) | copy-start | bytes 983044
  32.4 9.2 %copy-start.2 = (f32[320]{0:T(512)S(1)}, f32[320]{0:T(512)}, u32[]{:S(2)}) copy-start(f32[320]{0:T(512)} %gain_ref.9) | copy-start | bytes 3844
  39.0 24.2 %collective-permute-start.2 = (bf16[960,1024]{1,0:T(8,128)(2,1)}, bf16[960,1024]{1,0:T(8,128)(2,1)S(1)}, u32[]{:S(2)}, u32[]{:S(2)}) collective-permute-start(bf16[960,1024]{1,0:T(8,128)(2,1)} %get-tuple-element.37.mine_turned_ref), channel_id=1, source_target_pairs={{0,16},{16,0},{1,17},{17,1},{2,18},{18,2},{3,19},{19,3},{4,20},{20... | collective-permute-start | bytes 5898248 | tf_op jit(solution)/shard_map/ppermute | solution.py:543
  41.5 1.1 copy-start.1
  42.7 13.7 %copy-start.10 = (bf16[512,320]{1,0:T(8,128)(2,1)S(1)}, bf16[512,320]{1,0:T(8,128)(2,1)}, u32[]{:S(2)}) copy-start(bf16[512,320]{1,0:T(8,128)(2,1)} %copy-done.9) | copy-start | bytes 983044
  42.7 13.7 %copy-start.12 = (bf16[512,320]{1,0:T(8,128)(2,1)S(1)}, bf16[512,320]{1,0:T(8,128)(2,1)}, u32[]{:S(2)}) copy-start(bf16[512,320]{1,0:T(8,128)(2,1)} %copy-done.11) | copy-start | bytes 983044
  58.2 5.0 %copy-start.4 = (bf16[960,1024]{1,0:T(8,128)(2,1)S(1)}, bf16[960,1024]{1,0:T(8,128)(2,1)}, u32[]{:S(2)}) copy-start(bf16[960,1024]{1,0:T(8,128)(2,1)} %get-tuple-element.37.mine_turned_ref) | copy-start | bytes 5898244
  58.2 5.0 %collective-permute-start.4 = (f32[960,256]{1,0:T(8,128)S(1)}, f32[960,256]{1,0:T(8,128)S(1)}, u32[]{:S(2)}, u32[]{:S(2)}) collective-permute-start(f32[960,256]{1,0:T(8,128)S(1)} %get-tuple-element.48), channel_id=1, source_target_pairs={{0,16},{16,0},{1,17},{17,1},{2,18},{18,2},{3,19},{19,3},{4,20},{20... | collective-permute-start | bytes 2949128 | tf_op jit(solution)/shard_map/ppermute | solution.py:543
  61.0 5.4 %copy-start.15 = (f32[8,320]{1,0:T(8,128)}, f32[8,320]{1,0:T(8,128)S(1)}, u32[]{:S(2)}) copy-start(f32[8,320]{1,0:T(8,128)S(1)} %get-tuple-element.51.total_ref) | copy-start | bytes 30724
  61.0 2.2 %collective-permute-start.3 = (bf16[1024,160]{1,0:T(8,128)(2,1)S(1)}, bf16[1024,160]{1,0:T(8,128)(2,1)S(1)}, u32[]{:S(2)}, u32[]{:S(2)}) collective-permute-start(bf16[1024,160]{1,0:T(8,128)(2,1)S(1)} %get-tuple-element.46), channel_id=1, source_target_pairs={{0,16},{16,0},{1,17},{17,1},{2,18},{18,2},{3,19},{19,3},{4,20},{20... | collective-permute-start | bytes 983048 | tf_op jit(solution)/shard_map/ppermute | solution.py:543
  66.4 8.7 %copy-start.6 = (bf16[1,2,16,32,320]{4,3,2,1,0:T(8,128)(2,1)S(1)}, bf16[1,2,16,32,320]{4,3,2,1,0:T(8,128)(2,1)}, u32[]{:S(2)}) copy-start(bf16[1,2,16,32,320]{4,3,2,1,0:T(8,128)(2,1)} %param.6) | copy-start | bytes 1966084
  66.4 29.7 %all-to-all-start.2 = ((bf16[16,64,640]{2,1,0:T(8,128)(2,1)}), bf16[16,64,640]{2,1,0:T(8,128)(2,1)}, u32[]{:S(2)}, u32[]{:S(2)}) async-start(bf16[16,64,640]{2,1,0:T(8,128)(2,1)} %bitcast.21), calls=%async_computation.2 | async-start | bytes 2621440 | tf_op jit(solution)/shard_map/all_to_all | solution.py:549
  71.3 16.0 %collective-permute-start.5 = (bf16[512,320]{1,0:T(8,128)(2,1)S(1)}, bf16[512,320]{1,0:T(8,128)(2,1)S(1)}, u32[]{:S(2)}, u32[]{:S(2)}) collective-permute-start(bf16[512,320]{1,0:T(8,128)(2,1)S(1)} %get-tuple-element.53.h1_ref), channel_id=1, source_target_pairs={{0,1},{1,2},{2,3},{3,4},{4,5},{5,6},{6,7},{7,8},{8,9},{9,10},{10,1... | collective-permute-start | bytes 983048 | tf_op jit(solution)/shard_map/ppermute | solution.py:537
  73.8 21.6 %collective-permute-start.6 = (bf16[512,320]{1,0:T(8,128)(2,1)S(1)}, bf16[512,320]{1,0:T(8,128)(2,1)S(1)}, u32[]{:S(2)}, u32[]{:S(2)}) collective-permute-start(bf16[512,320]{1,0:T(8,128)(2,1)S(1)} %get-tuple-element.54.h0_ref), channel_id=1, source_target_pairs={{1,0},{2,1},{3,2},{4,3},{5,4},{6,5},{7,6},{8,7},{9,8},{10,9},{11,1... | collective-permute-start | bytes 983048 | tf_op jit(solution)/shard_map/ppermute | solution.py:538
  75.1 1.6 %copy-start.3 = (bf16[3,3,320,320]{3,2,1,0:T(8,128)(2,1)S(1)}, bf16[3,3,320,320]{3,2,1,0:T(8,128)(2,1)}, u32[]{:S(2)}) copy-start(bf16[3,3,320,320]{3,2,1,0:T(8,128)(2,1)} %param.8) | copy-start | bytes 5529604
  76.7 0.7 copy-start.16
  77.4 0.7 copy-start.18
  78.1 0.7 copy-start.20
  95.4 0.7 copy-start.13
  121.4 6.9 %copy-start.8 = (bf16[3,320,320]{2,1,0:T(8,128)(2,1)S(1)}, bf16[3,320,320]{2,1,0:T(8,128)(2,1)}, u32[]{:S(2)}) copy-start(bf16[3,320,320]{2,1,0:T(8,128)(2,1)} %w_ref.3) | copy-start | bytes 1843204
  121.4 22.0 %all-to-all-start.5 = ((bf16[16,64,640]{2,1,0:T(8,128)(2,1)}), bf16[16,64,640]{2,1,0:T(8,128)(2,1)S(1)}, u32[]{:S(2)}, u32[]{:S(2)}) async-start(bf16[16,64,640]{2,1,0:T(8,128)(2,1)} %broadcast_in_dim.5), calls=%async_computation.5 | async-start | bytes 2621440 | tf_op jit(solution)/shard_map/all_to_all | solution.py:565
  128.3 1.0 copy-start.14
  143.4 9.3 %collective-permute-start.7 = (bf16[1024,640]{1,0:T(8,128)(2,1)S(1)}, bf16[1024,640]{1,0:T(8,128)(2,1)S(1)}, u32[]{:S(2)}, u32[]{:S(2)}) collective-permute-start(bf16[1024,640]{1,0:T(8,128)(2,1)S(1)} %bitcast.12), channel_id=1, source_target_pairs={{0,16},{16,0},{1,17},{17,1},{2,18},{18,2},{3,19},{19,3},{4,20},{20... | collective-permute-start | bytes 3932168 | tf_op jit(solution)/shard_map/ppermute | solution.py:543

commit v6 on v5

--- a/solution.py
+++ b/solution.py
@@ -54,6 +54,10 @@
     return pltpu.HBM(dims, kind)
 
 
+def in_hbm(value):
+    return pltpu.with_memory_space_constraint(value, pltpu.HBM)
+
+
 def at(step, size=STEP):
     return pl.ds(pl.multiple_of(step * size, size), size)
 
@@ -84,8 +88,8 @@
 
 
 def forward_body(
-    x_ref, far_w_ref, gain_ref, h0_ref, h1_ref, far_turned_ref, stat_ref, sums_ref,
-    w_ref, wf, x3, y, turned, w_sem, turned_sem,
+    x_ref, far_w_ref, gain_ref, h0_ref, h1_ref, far_turned_ref, far_stat_ref, sums_ref,
+    w_ref, wf, x3, y, turned, stat_ref, w_sem, turned_sem, stat_sem,
 ):
     fetch = pltpu.make_async_copy(far_w_ref, w_ref, w_sem)
     fetch.start()
@@ -104,8 +108,10 @@
         mean = grouped[2 * f : 2 * f + 1]
         var = grouped[2 * f + 1 : 2 * f + 2] - mean * mean
         stats += [mean, lax.rsqrt(var + epsilon)]
-    stat_ref[...] = jnp.concatenate(stats + [jnp.zeros((4, C), F32)])
     gain = gain_ref[...].reshape(1, C)
+    stat_ref[...] = jnp.concatenate([*stats, gain, jnp.zeros((3, C), F32)])
+    sends = [pltpu.make_async_copy(stat_ref, far_stat_ref, stat_sem)]
+    sends[0].start()
     edge = column(C)
 
     def activate(step, mean, scale):
@@ -121,7 +127,6 @@
         ).astype(BF16)
 
     total = (zero, zero)
-    sends = []
     for f in range(2):
         mean, scale = stats[2 * f], stats[2 * f + 1]
 
@@ -198,7 +203,7 @@
             shape((PIX, C), BF16),
             shape((PIX, C), BF16),
             far((3 * C, ROWS), BF16),
-            shape((8, C), F32),
+            far((8, C), F32),
             shape((peers, 2, C), F32),
         ),
         (
@@ -207,14 +212,16 @@
             pltpu.VMEM((ROWS, 3 * C), BF16),
             pltpu.VMEM((2, PIX + 2 * W, 3 * PAD), F32),
             pltpu.VMEM((2, 3 * C, PIX), BF16),
+            pltpu.VMEM((8, C), F32),
             pltpu.SemaphoreType.DMA,
             pltpu.SemaphoreType.DMA((2,)),
+            pltpu.SemaphoreType.DMA,
         ),
         flops=2_500_000_000,
         limit=24,
         ins=[VMEM, FAR, VMEM],
-        outs=(VMEM, VMEM, FAR, VMEM, VMEM),
-    )(x, pltpu.with_memory_space_constraint(weight, pltpu.HBM), gain)
+        outs=(VMEM, VMEM, FAR, FAR, VMEM),
+    )(x, in_hbm(weight), gain)
 
 
 def times_transposed(a, b):
@@ -244,12 +251,18 @@
 
 
 def slope_body(
-    count, sums_ref, h0_ref, h1_ref, grad_ref, cot_ref, gain_ref, part_ref, stat_ref, out_ref
+    count, sums_ref, h0_ref, h1_ref, far_grad_ref, cot_ref, gain_ref,
+    part_ref, stat_ref, out_ref, far_stat_ref, grad_ref, sem, grad_sem,
 ):
+    fetch = pltpu.make_async_copy(far_grad_ref, grad_ref, grad_sem)
+    fetch.start()
     mean, square = clip_stats(sums_ref, count)
     scale = lax.rsqrt(square - mean * mean + epsilon)
-    stat_ref[...] = jnp.concatenate([mean, scale, jnp.zeros((6, C), F32)])
     gain = gain_ref[...].reshape(1, C)
+    stat_ref[...] = jnp.concatenate([mean, scale, gain, jnp.zeros((5, C), F32)])
+    send = pltpu.make_async_copy(stat_ref, far_stat_ref, sem)
+    send.start()
+    fetch.wait()
     zero = jnp.zeros((8, C), F32)
     total = (zero, zero)
     for f, h_ref in enumerate((h0_ref, h1_ref)):
@@ -267,13 +280,17 @@
 
         total = lax.fori_loop(0, PIX // STEP, step_body, total)
     spread(total, out_ref)
+    send.wait()
 
 
 def slopes(sums, h0, h1, grad, cot, gain, count):
     return call(
         functools.partial(slope_body, count),
-        (shape((ROWS, C), F32), shape((8, C), F32), shape(sums.shape, F32)),
-    )(sums, h0, h1, grad, cot, gain)
+        (shape((ROWS, C), F32), shape((8, C), F32), shape(sums.shape, F32), far((8, C), F32)),
+        (pltpu.VMEM((ROWS, C), BF16), pltpu.SemaphoreType.DMA, pltpu.SemaphoreType.DMA),
+        ins=[VMEM] * 3 + [FAR] + [VMEM] * 2,
+        outs=(VMEM, VMEM, VMEM, FAR),
+    )(sums, h0, h1, in_hbm(grad), cot, gain)
 
 
 def mix(h_ref, base, mean, scale, gain):
@@ -282,11 +299,10 @@
 
 
 def mixed_body(
-    h0_ref, h1_ref, before_ref, cot_ref, after_ref, stat_ref, gain_ref, sums_ref,
+    h0_ref, h1_ref, before_ref, cot_ref, after_ref, stat_ref, sums_ref,
     keep_ref, give_ref, turned,
 ):
-    mean, scale = stat_ref[0:1, :], stat_ref[1:2, :]
-    gain = gain_ref[...].reshape(1, C)
+    mean, scale, gain = stat_ref[0:1, :], stat_ref[1:2, :], stat_ref[2:3, :]
     for f, h_ref in enumerate((h0_ref, h1_ref)):
         for step in range(PIX // STEP):
             act = mix(h_ref, step * STEP, mean, scale, gain).astype(BF16)
@@ -306,18 +322,22 @@
         give_ref[k * C : (k + 1) * C, 0:HALF] = jnp.where(core == 0, right, left)
 
 
-def temporal_gradient(h0, h1, before, cot, after, stat, gain, sums):
+def temporal_gradient(h0, h1, before, cot, after, stat, sums):
     return call(
         mixed_body,
         (shape((3 * C, 256), F32), shape((3 * C, 256), F32)),
         (pltpu.VMEM((C, ROWS), BF16),),
         flops=1_500_000_000,
-    )(h0, h1, before, cot, after, stat, gain, sums)
-
-
-def temporal_body(hb_ref, h0_ref, h1_ref, ha_ref, stat_ref, gain_ref, w_ref, out_ref, mx_ref):
-    mean, scale = stat_ref[0:1, :], stat_ref[1:2, :]
-    gain = gain_ref[...].reshape(1, C)
+    )(h0, h1, before, cot, after, stat, sums)
+
+
+def temporal_body(
+    hb_ref, h0_ref, h1_ref, ha_ref, far_stat_ref, w_ref, out_ref, mx_ref, stat_ref, sem
+):
+    fetch = pltpu.make_async_copy(far_stat_ref, stat_ref, sem)
+    fetch.start()
+    fetch.wait()
+    mean, scale, gain = stat_ref[0:1, :], stat_ref[1:2, :], stat_ref[2:3, :]
     place = lax.axis_index(FRAME)
     live = (place > 0, None, None, place < lax.axis_size(FRAME) - 1)
     for n, h_ref in enumerate((hb_ref, h0_ref, h1_ref, ha_ref)):
@@ -344,13 +364,15 @@
         out_ref[f * PIX : (f + 1) * PIX, :] = (h_ref[...].astype(F32) + low).astype(BF16)
 
 
-def temporal(before, h0, h1, after, stat, gain, weight):
+def temporal(before, h0, h1, after, stat, weight):
     return call(
         temporal_body,
         shape((ROWS, C), BF16),
-        (pltpu.VMEM((4 * PIX, C), BF16),),
+        (pltpu.VMEM((4 * PIX, C), BF16), pltpu.VMEM((8, C), F32), pltpu.SemaphoreType.DMA),
         flops=1_500_000_000,
-    )(before, h0, h1, after, stat, gain, weight)
+        ins=[VMEM] * 4 + [FAR, VMEM],
+        outs=VMEM,
+    )(before, h0, h1, after, in_hbm(stat), weight)
 
 
 def whole_grad(part_ref, h_ref, stat_ref, sums, base, f):
@@ -360,10 +382,13 @@
 
 
 def hidden_grad_body(
-    count, sums_ref, stat_ref, part_ref, h0_ref, h1_ref, keep_ref, give_ref, total_ref
+    count, sums_ref, stat_ref, part_ref, h0_ref, h1_ref,
+    keep_ref, give_ref, far_total_ref, total_ref, sem,
 ):
     sums = clip_stats(sums_ref, count)
     total_ref[...] = jnp.concatenate([*sums, jnp.zeros((6, C), F32)])
+    send = pltpu.make_async_copy(total_ref, far_total_ref, sem)
+    send.start()
     core = lax.axis_index("c")
     for f, h_ref in enumerate((h0_ref, h1_ref)):
 
@@ -377,12 +402,16 @@
             return carry
 
         lax.fori_loop(0, PIX // STEP, step_body, 0)
+    send.wait()
 
 
 def hidden_gradient(sums, stat, part, h0, h1, count):
     return call(
         functools.partial(hidden_grad_body, count),
-        (shape((ROWS, HALF), BF16), shape((ROWS, HALF), BF16), shape((8, C), F32)),
+        (shape((ROWS, HALF), BF16), shape((ROWS, HALF), BF16), far((8, C), F32)),
+        (pltpu.VMEM((8, C), F32), pltpu.SemaphoreType.DMA),
+        ins=[VMEM] * 5,
+        outs=(VMEM, VMEM, FAR),
     )(sums, stat, part, h0, h1)
 
 
@@ -437,15 +466,20 @@
 
 
 def input_grad_body(
-    part_ref, h0_ref, h1_ref, clip_ref, total_ref, x_ref, stat_ref, gain_ref, w_ref,
-    out_ref, wb, rows, z, dh, grads, lows,
+    part_ref, h0_ref, h1_ref, far_clip_ref, far_total_ref, x_ref, far_stat_ref, far_w_ref,
+    out_ref, wb, rows, z, dh, grads, lows, clip_ref, total_ref, stat_ref, w_ref, sem,
 ):
+    pairs = (far_clip_ref, clip_ref), (far_total_ref, total_ref), (far_stat_ref, stat_ref)
+    fetches = [
+        pltpu.make_async_copy(one, two, sem.at[n])
+        for n, (one, two) in enumerate((*pairs, (far_w_ref, w_ref)))
+    ]
+    for fetch in fetches:
+        fetch.start()
+    for fetch in fetches[:3]:
+        fetch.wait()
     clip_sums = total_ref[0:1, :], total_ref[1:2, :]
-    for j in range(3):
-        for i in range(3):
-            wb[PAD * j : PAD * j + C, C * i : C * (i + 1)] = w_ref[3 * i + j]
-        wb[PAD * j + C : PAD * (j + 1), :] = jnp.zeros((PAD - C, 3 * C), BF16)
-    gain = gain_ref[...].reshape(1, C)
+    gain = stat_ref[4:5, :]
     edge = column(C)
     half = PIX // STEP
     for f in range(2):
@@ -460,6 +494,12 @@
             return carry
 
         lax.fori_loop(0, half, grad_body, 0)
+        if f == 0:
+            fetches[3].wait()
+            for j in range(3):
+                for i in range(3):
+                    wb[PAD * j : PAD * j + C, C * i : C * (i + 1)] = w_ref[3 * i + j]
+                wb[PAD * j + C : PAD * (j + 1), :] = jnp.zeros((PAD - C, 3 * C), BF16)
         for i, tap in enumerate(row_taps(lows[...])):
             rows[:, i * C : (i + 1) * C] = tap
         z[...] = times_transposed(rows[...], wb[...])
@@ -494,7 +534,7 @@
         lax.fori_loop(0, half, last_body, 0)
 
 
-def input_gradient(part, h0, h1, clip_stat, total, x, stat, gain, weight):
+def input_gradient(part, h0, h1, clip_stat, total, x, stat, weight):
     return call(
         input_grad_body,
         shape((ROWS, C), BF16),
@@ -505,10 +545,17 @@
             pltpu.VMEM((PIX, C), F32),
             pltpu.VMEM((PIX, C), F32),
             pltpu.VMEM((PIX, C), BF16),
+            pltpu.VMEM((8, C), F32),
+            pltpu.VMEM((8, C), F32),
+            pltpu.VMEM((8, C), F32),
+            pltpu.VMEM((9, C, C), BF16),
+            pltpu.SemaphoreType.DMA((4,)),
         ),
         flops=2_500_000_000,
-        limit=16,
-    )(part, h0, h1, clip_stat, total, x, stat, gain, weight)
+        limit=18,
+        ins=[VMEM] * 3 + [FAR] * 2 + [VMEM] + [FAR] * 2,
+        outs=VMEM,
+    )(part, h0, h1, in_hbm(clip_stat), in_hbm(total), x, in_hbm(stat), in_hbm(weight))
 
 
 def unpack_body(mine_ref, other_ref, spatial_ref, temporal_ref):
@@ -549,14 +596,15 @@
     return lax.all_to_all(value, PLANE, 0, 0)
 
 
-def everyone_share(value):
+def everyone_share(value, beside):
     plane, line = lax.axis_size(PLANE), lax.axis_size(LINE)
     width = value.shape[2]
     value = jnp.sum(value.astype(F32), axis=0)
     value = value.reshape(line, 1024 // plane // line, width)
     value = jnp.sum(lax.all_to_all(value, LINE, 0, 0), axis=0).astype(BF16)
+    value, *beside = lax.optimization_barrier((value, *beside))
     value = jnp.broadcast_to(value[None], (line,) + value.shape)
-    return lax.all_to_all(value, LINE, 0, 0).reshape(1024 // plane, width)
+    return beside, lax.all_to_all(value, LINE, 0, 0).reshape(1024 // plane, width)
 
 
 def everyone_gets(value):
@@ -578,10 +626,10 @@
     mixed_grad = mixed_gradient(cot_before, cot, cot_after, temporal_weight)
     sums, mine_turned, mixed_grad = barrier((sums, mine_turned, mixed_grad))
     other_turned = swap_cores(mine_turned)
-    part, clip_stat, sums = slopes(sums, h0, h1, mixed_grad, cot, gain_two, count)
+    part, clip_stat, sums, far_stat = slopes(sums, h0, h1, mixed_grad, cot, gain_two, count)
     sums = lax.all_to_all(sums, FRAME, 0, 0)
     temporal_keep, temporal_give = temporal_gradient(
-        h0, h1, cot_before, cot, cot_after, clip_stat, gain_two, sums
+        h0, h1, cot_before, cot, cot_after, clip_stat, sums
     )
     temporal_got = swap_cores(temporal_give)
     low_keep, low_give, total = hidden_gradient(sums, clip_stat, part, h0, h1, count)
@@ -593,12 +641,12 @@
     shares = everyone_total(packed)
     before, after = neighbours(edge0, edge1)
     input_grad = input_gradient(
-        part, h0, h1, clip_stat, total, x, stat_one, gain_one, spatial_weight
-    )
-    shares, input_grad, before, after = barrier((shares, input_grad, before, after))
-    mine = everyone_share(shares)
+        part, h0, h1, far_stat, total, x, stat_one, spatial_weight
+    )
+    shares, input_grad = barrier((shares, input_grad))
+    (before, after), mine = everyone_share(shares, (before, after))
     mine, before, after = barrier((mine, before, after))
-    output = temporal(before, h0, h1, after, clip_stat, gain_two, temporal_weight)
+    output = temporal(before, h0, h1, after, far_stat, temporal_weight)
     mine, output = barrier((everyone_gets(mine), output))
     other = swap_cores(mine)
     spatial_grad, temporal_grad = unpack(mine, other)

time: 157 us -> 151 us (0.962)
  local copies, waits for them, and re-layouts: 10 us -> 3.43 us
  Pallas kernels: 34.6 us -> 38.4 us
  blocking collectives: 34.4 us -> 31.1 us
  waiting for transfers between devices: 29.4 us -> 31.3 us
  starting transfers between devices: 45 us -> 43.3 us
    all_to_all x1, waiting for transfers between devices: 0.01 us -> 9.83 us  [everyone_total(): return lax.all_to_all(value, PLANE, 0, 0)]
    ppermute x2, waiting for transfers between devices: 10.5 us -> 2.38 us  [neighbours(): after = lax.ppermute(first, FRAME, [(i + 1, i) for i in range(size - 1)])]
    unnamed x42 -> x24, local copies, waits for them, and re-layouts: 6.66 us -> 0.06 us
    all_to_all x1, blocking collectives: 12.9 us -> 9.58 us  [everyone_share(): value = jnp.sum(lax.all_to_all(value, LINE, 0, 0), axis=0).astype(BF16)]
    pallas_call x1, Pallas kernels: 3.88 us -> 5.59 us  [temporal(): call(temporal_body, shape((ROWS, C), BF16), (pltpu.VMEM((4 * PIX, C), BF1...]
  transfers between devices with their start and end apart: 11 -> 11, of which waited for: 6 -> 6; matrix products, arithmetic and copies ran while one was open for 0% -> 1% of each run, Pallas kernels for 18% -> 21%
where the time goes in v6:
time: 151 us; the launch traced here: 150 us
  starting transfers between devices  43.3 us (29%)
  Pallas kernels  38.4 us (25%)
  waiting for transfers between devices  31.3 us (21%)
  blocking collectives  31.1 us (21%)
  local copies, waits for them, and re-layouts  3.43 us (2%)
  other arithmetic  1.52 us (1%)
    all_to_all x1, starting transfers between devices, on_device(): sums = lax.all_to_all(sums, FRAME, 0, 0)  12.1 us
    all_to_all x1, blocking collectives, on_device(): sums = lax.all_to_all(sums, FRAME, 0, 0)  11.9 us
    all_to_all x1, waiting for transfers between devices, everyone_gets(): return lax.all_to_all(value, PLANE, 0, 0).reshape(1024, value.shape[2])  10.4 us
    all_to_all x1, waiting for transfers between devices, everyone_total(): return lax.all_to_all(value, PLANE, 0, 0)  9.83 us
    pallas_call x1, Pallas kernels, input_gradient(): call(input_grad_body, shape((ROWS, C), BF16), (pltpu.VMEM((3 * PAD, 3 * C...  9.74 us
    all_to_all x1, blocking collectives, everyone_share(): value = jnp.sum(lax.all_to_all(value, LINE, 0, 0), axis=0).astype(BF16)  9.58 us
    all_to_all x1, blocking collectives, everyone_share(): lax.all_to_all(value, LINE, 0, 0).reshape(1024 // plane, width)  9.55 us
    ppermute x4, starting transfers between devices, swap_cores(): return lax.ppermute(value, 'c', [(0, 1), (1, 0)])  9.48 us
  transfers between devices with their start and end apart: 11, of which 6 were waited for; matrix products, arithmetic and copies ran while one was open for 1% of the time, Pallas kernels for 21%

profile of v6, /device:TPU:1, one launch (start us, length us, event | category | flops | bytes accessed | tf_op | source)
XLA Modules:
  0.0 149.9 jit_solution(2103250710359997814)
XLA Ops:
  0.6 0.0 copy-start.3
  0.7 2.1 %fusion = (bf16[1,1,16,32,320]{4,3,2,1,0:T(8,128)(2,1)}, bf16[1,1,16,32,320]{4,3,2,1,0:T(8,128)(2,1)}) fusion(bf16[1,2,16,32,320]{4,3,2,1,0:T(8,128)(2,1)} %param.7), kind=kLoop, calls=%fused_computation.1 | loop fusion | bytes 1310720 | tf_op jit(solution)/shard_map/slice | solution.py:623
  2.8 5.7 %collective-permute-start = (bf16[512,320]{1,0:T(8,128)(2,1)}, bf16[512,320]{1,0:T(8,128)(2,1)S(1)}, u32[]{:S(2)}, u32[]{:S(2)}) collective-permute-start(bf16[512,320]{1,0:T(8,128)(2,1)} %bitcast.2), channel_id=1, source_target_pairs={{0,1},{1,2},{2,3},{3,4},{4,5},{5,6},{6,7},{7,8},{8,9},{9,10},{10,1... | collective-permute-start | bytes 983048 | tf_op jit(solution)/shard_map/ppermute | solution.py:584
  8.5 1.3 collective-permute-start.1
  9.9 0.0 copy-start
  9.9 0.0 copy-start.5
  9.9 8.0 %shard_map.93 = (bf16[512,320]{1,0:T(8,128)(2,1)S(1)}, bf16[512,320]{1,0:T(8,128)(2,1)S(1)}, bf16[960,1024]{1,0:T(8,128)(2,1)}, f32[8,320]{1,0:T(8,128)}, f32[16,2,320]{2,1,0:T(2,128)}) custom-call(bf16[1024,320]{1,0:T(8,128)(2,1)S(1)} %bitcast.17, bf16[9,320,320]{2,1,0:T(8,128)(2,1)} %bitcast.22, f32[320]{0:T(512)S(1)} %copy-done.11), custom_call_target="tpu_custom_call" | custom-call | flops 2500000000 | bytes 8000000 | tf_op jit(solution)/shard_map/pallas_call | solution.py:200
  17.8 12.1 %all-to-all-start = ((f32[16,2,320]{2,1,0:T(2,128)}), f32[16,2,320]{2,1,0:T(2,128)S(1)}, u32[]{:S(2)}, u32[]{:S(2)}) async-start(f32[16,2,320]{2,1,0:T(2,128)} %get-tuple-element.37), calls=%async_computation | async-start | bytes 98304 | tf_op jit(solution)/shard_map/all_to_all | solution.py:625
  30.0 0.0 collective-permute-done.before_ref
  30.0 0.0 copy-start.7
  30.0 2.4 %collective-permute-done.1.after_ref = bf16[512,320]{1,0:T(8,128)(2,1)S(1)} collective-permute-done((bf16[512,320]{1,0:T(8,128)(2,1)}, bf16[512,320]{1,0:T(8,128)(2,1)S(1)}, u32[]{:S(2)}, u32[]{:S(2)}) %collective-permute-start.1) | collective-permute-done | bytes 327712 | tf_op jit(solution)/shard_map/ppermute | solution.py:585
  32.4 0.0 copy-done.5
  32.4 2.5 %shard_map.94.far_grad_ref = bf16[1024,320]{1,0:T(8,128)(2,1)} custom-call(bf16[512,320]{1,0:T(8,128)(2,1)S(1)} %collective-permute-done.before_ref, bf16[1024,320]{1,0:T(8,128)(2,1)S(1)} %bitcast.14, bf16[512,320]{1,0:T(8,128)(2,1)S(1)} %collective-permute-done.1.after_ref, bf16[3,320,320]{2,1,0:T(8,128)(2,1)S(1)} %copy-done.5), custom_call_target="tpu_custom_call" | custom-call | flops 1500000000 | bytes 8000000 | tf_op jit(solution)/shard_map/pallas_call | solution.py:248
  34.9 0.0 copy-done.9
  34.9 4.1 %all-to-all-done.sums_ref = f32[16,2,320]{2,1,0:T(2,128)S(1)} async-done(((f32[16,2,320]{2,1,0:T(2,128)}), f32[16,2,320]{2,1,0:T(2,128)S(1)}, u32[]{:S(2)}, u32[]{:S(2)}) %all-to-all-start) | async-done | bytes 40992 | tf_op jit(solution)/shard_map/all_to_all | solution.py:625
  39.0 2.6 %collective-permute-start.2 = (bf16[960,1024]{1,0:T(8,128)(2,1)}, bf16[960,1024]{1,0:T(8,128)(2,1)S(1)}, u32[]{:S(2)}, u32[]{:S(2)}) collective-permute-start(bf16[960,1024]{1,0:T(8,128)(2,1)} %get-tuple-element.39.mine_turned_ref), channel_id=1, source_target_pairs={{0,16},{16,0},{1,17},{17,1},{2,18},{18,2},{3,19},{19,3},{4,20},{20... | collective-permute-start | bytes 5898248 | tf_op jit(solution)/shard_map/ppermute | solution.py:590
  41.5 0.0 copy-done.1
  41.5 2.6 %shard_map.95 = (f32[1024,320]{1,0:T(8,128)S(1)}, f32[8,320]{1,0:T(8,128)S(1)}, f32[16,2,320]{2,1,0:T(2,128)S(1)}, f32[8,320]{1,0:T(8,128)}) custom-call(f32[16,2,320]{2,1,0:T(2,128)S(1)} %all-to-all-done.sums_ref, bf16[512,320]{1,0:T(8,128)(2,1)S(1)} %get-tuple-element.58.h0_ref, bf16[512,320]{1,0:T(8,128)(2,1)S(1)} %get-tuple-element.57.h1_ref, ...), custom_call_target="tpu_custom_call" | custom-call | bytes 8000000 | tf_op jit(solution)/shard_map/pallas_call | solution.py:287
  44.1 11.9 %all_to_all.30.sums_ref = f32[16,2,320]{2,1,0:T(2,128)S(1)} all-to-all(f32[16,2,320]{2,1,0:T(2,128)S(1)} %get-tuple-element.44), channel_id=1, replica_groups=mesh['zl'=2,'x'=4,'c'=2,'y'=4,'zh'=4] {'y','zh'}, dimensions={0} | all-to-all | bytes 81920 | tf_op jit(solution)/shard_map/all_to_all | solution.py:630
  56.1 0.0 copy-done.10
  56.1 1.8 %shard_map.97 = (f32[960,256]{1,0:T(8,128)S(1)}, f32[960,256]{1,0:T(8,128)S(1)}) custom-call(bf16[512,320]{1,0:T(8,128)(2,1)S(1)} %get-tuple-element.58.h0_ref, bf16[512,320]{1,0:T(8,128)(2,1)S(1)} %get-tuple-element.57.h1_ref, bf16[512,320]{1,0:T(8,128)(2,1)S(1)} %copy-done.8, bf16[1024,320]{1,0:T(8,128)(2,1)S(1)} %bitcast.16, ...), custom_call_target="tpu_custom_call" | custom-call | flops 1500000000 | bytes 8000000 | tf_op jit(solution)/shard_map/pallas_call | solution.py:326
  57.9 0.0 copy-start.2
  57.9 0.9 collective-permute-start.4
  58.8 1.9 %shard_map.96 = (bf16[1024,160]{1,0:T(8,128)(2,1)S(1)}, bf16[1024,160]{1,0:T(8,128)(2,1)S(1)}, f32[8,320]{1,0:T(8,128)}) custom-call(f32[16,2,320]{2,1,0:T(2,128)S(1)} %all_to_all.30.sums_ref, f32[8,320]{1,0:T(8,128)S(1)} %get-tuple-element.45.stat_ref, f32[1024,320]{1,0:T(8,128)S(1)} %get-tuple-element.46.part_ref, ...), custom_call_target="tpu_custom_call" | custom-call | bytes 8000000 | tf_op jit(solution)/shard_map/pallas_call | solution.py:409
  60.8 0.3 collective-permute-start.3
  61.0 1.9 %collective-permute-done.3.other_ref = bf16[1024,160]{1,0:T(8,128)(2,1)S(1)} collective-permute-done((bf16[1024,160]{1,0:T(8,128)(2,1)S(1)}, bf16[1024,160]{1,0:T(8,128)(2,1)S(1)}, u32[]{:S(2)}, u32[]{:S(2)}) %collective-permute-start.3) | collective-permute-done | bytes 327712 | tf_op jit(solution)/shard_map/ppermute | solution.py:590
  62.9 0.0 collective-permute-done.4.got_ref
  62.9 0.0 collective-permute-done.2.other_turned_ref
  62.9 0.0 copy-done.2
  62.9 3.2 %shard_map.98 = bf16[1024,640]{1,0:T(8,128)(2,1)} custom-call(bf16[960,1024]{1,0:T(8,128)(2,1)S(1)} %copy-done.2, bf16[960,1024]{1,0:T(8,128)(2,1)S(1)} %collective-permute-done.2.other_turned_ref, bf16[1024,160]{1,0:T(8,128)(2,1)S(1)} %get-tuple-element.47.mine_ref, bf16[1024,160]{1,0:T(8,128)(2,1)S(1)} %collective-permute-done.3.other_ref, ...), custom_call_target="tpu_custom_call" | custom-call | flops 2500000000 | bytes 8000000 | tf_op jit(solution)/shard_map/pallas_call | solution.py:454
  66.1 0.0 copy-start.4
  66.1 4.9 %all-to-all-start.2 = ((bf16[16,64,640]{2,1,0:T(8,128)(2,1)}), bf16[16,64,640]{2,1,0:T(8,128)(2,1)}, u32[]{:S(2)}, u32[]{:S(2)}) async-start(bf16[16,64,640]{2,1,0:T(8,128)(2,1)} %bitcast.19), calls=%async_computation.2 | async-start | bytes 2621440 | tf_op jit(solution)/shard_map/all_to_all | solution.py:596
  71.1 2.4 %collective-permute-start.5 = (bf16[512,320]{1,0:T(8,128)(2,1)S(1)}, bf16[512,320]{1,0:T(8,128)(2,1)S(1)}, u32[]{:S(2)}, u32[]{:S(2)}) collective-permute-start(bf16[512,320]{1,0:T(8,128)(2,1)S(1)} %get-tuple-element.57.h1_ref), channel_id=1, source_target_pairs={{0,1},{1,2},{2,3},{3,4},{4,5},{5,6},{6,7},{7,8},{8,9},{9,10},{10,1... | collective-permute-start | bytes 983048 | tf_op jit(solution)/shard_map/ppermute | solution.py:584
  73.4 1.3 collective-permute-start.6
  74.7 9.7 %shard_map.99 = bf16[1024,320]{1,0:T(8,128)(2,1)} custom-call(f32[1024,320]{1,0:T(8,128)S(1)} %get-tuple-element.46.part_ref, bf16[512,320]{1,0:T(8,128)(2,1)S(1)} %get-tuple-element.58.h0_ref, bf16[512,320]{1,0:T(8,128)(2,1)S(1)} %get-tuple-element.57.h1_ref, f32[8,320]{1,0:T(8,128)} %get-tuple-element.53.far_clip_ref.far_stat_ref, ...), custom_call_target="tpu_custom_call" | custom-call | flops 2500000000 | bytes 8000000 | tf_op jit(solution)/shard_map/pallas_call | solution.py:538
  84.5 9.8 %all-to-all-done.2 = bf16[16,64,640]{2,1,0:T(8,128)(2,1)} async-done(((bf16[16,64,640]{2,1,0:T(8,128)(2,1)}), bf16[16,64,640]{2,1,0:T(8,128)(2,1)}, u32[]{:S(2)}, u32[]{:S(2)}) %all-to-all-start.2) | async-done | bytes 1310752 | tf_op jit(solution)/shard_map/all_to_all | solution.py:596
  94.3 1.5 %convert_reduce_fusion = f32[64,640]{1,0:T(8,128)S(1)} fusion(bf16[16,64,640]{2,1,0:T(8,128)(2,1)} %all-to-all-done.2), kind=kLoop, calls=%fused_computation | loop fusion | flops 1269760 | bytes 1474560 | tf_op jit(solution)/shard_map/reduce_sum | solution.py:602
  95.8 9.6 %all_to_all.31 = f32[8,8,640]{2,1,0:T(8,128)S(1)} all-to-all(f32[8,8,640]{2,1,0:T(8,128)S(1)} %bitcast.20), channel_id=1, replica_groups=mesh['zl'=2,'x'=4,'c'=2,'y'=4,'zh'=4] {'zl','zh'}, dimensions={0} | all-to-all | bytes 327680 | tf_op jit(solution)/shard_map/all_to_all | solution.py:604
  105.4 0.0 collective-permute-done.5.hb_ref
  105.4 0.0 collective-permute-done.6.ha_ref
  105.5 9.6 %all_to_all.32 = bf16[8,8,640]{2,1,0:T(8,128)(2,1)S(1)} all-to-all(bf16[8,8,640]{2,1,0:T(8,128)(2,1)S(1)} %broadcast_in_dim.4), channel_id=1, replica_groups=mesh['zl'=2,'x'=4,'c'=2,'y'=4,'zh'=4] {'zl','zh'}, dimensions={0} | all-to-all | bytes 163840 | tf_op jit(solution)/shard_map/all_to_all | solution.py:607
  115.0 1.2 broadcast_in_dim.5
  116.2 6.1 %all-to-all-start.5 = ((bf16[16,64,640]{2,1,0:T(8,128)(2,1)}), bf16[16,64,640]{2,1,0:T(8,128)(2,1)S(1)}, u32[]{:S(2)}, u32[]{:S(2)}) async-start(bf16[16,64,640]{2,1,0:T(8,128)(2,1)} %broadcast_in_dim.5), calls=%async_computation.5 | async-start | bytes 2621440 | tf_op jit(solution)/shard_map/all_to_all | solution.py:613
  122.3 5.6 %shard_map.100 = bf16[1024,320]{1,0:T(8,128)(2,1)} custom-call(bf16[512,320]{1,0:T(8,128)(2,1)S(1)} %collective-permute-done.5.hb_ref, bf16[512,320]{1,0:T(8,128)(2,1)S(1)} %get-tuple-element.58.h0_ref, bf16[512,320]{1,0:T(8,128)(2,1)S(1)} %get-tuple-element.57.h1_ref, bf16[512,320]{1,0:T(8,128)(2,1)} %collective-permute-done.6.ha_ref, ...), custom_call_target="tpu_custom_call" | custom-call | flops 1500000000 | bytes 8000000 | tf_op jit(solution)/shard_map/pallas_call | solution.py:368
  127.9 10.4 %all-to-all-done.5 = bf16[16,64,640]{2,1,0:T(8,128)(2,1)S(1)} async-done(((bf16[16,64,640]{2,1,0:T(8,128)(2,1)}), bf16[16,64,640]{2,1,0:T(8,128)(2,1)S(1)}, u32[]{:S(2)}, u32[]{:S(2)}) %all-to-all-start.5) | async-done | bytes 1310752 | tf_op jit(solution)/shard_map/all_to_all | solution.py:613
  138.4 5.7 %collective-permute-start.7 = (bf16[1024,640]{1,0:T(8,128)(2,1)S(1)}, bf16[1024,640]{1,0:T(8,128)(2,1)S(1)}, u32[]{:S(2)}, u32[]{:S(2)}) collective-permute-start(bf16[1024,640]{1,0:T(8,128)(2,1)S(1)} %bitcast.12), channel_id=1, source_target_pairs={{0,16},{16,0},{1,17},{17,1},{2,18},{18,2},{3,19},{19,3},{4,20},{20... | collective-permute-start | bytes 3932168 | tf_op jit(solution)/shard_map/ppermute | solution.py:590
  144.1 2.7 %collective-permute-done.7.other_ref = bf16[1024,640]{1,0:T(8,128)(2,1)S(1)} collective-permute-done((bf16[1024,640]{1,0:T(8,128)(2,1)S(1)}, bf16[1024,640]{1,0:T(8,128)(2,1)S(1)}, u32[]{:S(2)}, u32[]{:S(2)}) %collective-permute-start.7) | collective-permute-done | bytes 1310752 | tf_op jit(solution)/shard_map/ppermute | solution.py:590
  146.7 3.2 %shard_map.101 = (bf16[9,320,320]{2,1,0:T(8,128)(2,1)}, bf16[3,320,320]{2,1,0:T(8,128)(2,1)}) custom-call(bf16[1024,640]{1,0:T(8,128)(2,1)S(1)} %bitcast.13, bf16[1024,640]{1,0:T(8,128)(2,1)S(1)} %collective-permute-done.7.other_ref), custom_call_target="tpu_custom_call" | custom-call | bytes 8000000 | tf_op jit(solution)/shard_map/pallas_call | solution.py:579
  (15 shorter events, 0.0 us)
Async XLA Ops:
  0.6 9.2 %copy-start.11 = (f32[320]{0:T(512)S(1)}, f32[320]{0:T(512)}, u32[]{:S(2)}) copy-start(f32[320]{0:T(512)} %gain_ref.2) | copy-start | bytes 3844
  0.6 9.2 %copy-start.3 = (bf16[1,2,16,32,320]{4,3,2,1,0:T(8,128)(2,1)S(1)}, bf16[1,2,16,32,320]{4,3,2,1,0:T(8,128)(2,1)}, u32[]{:S(2)}) copy-start(bf16[1,2,16,32,320]{4,3,2,1,0:T(8,128)(2,1)} %param.6) | copy-start | bytes 1966084
  2.8 27.2 %collective-permute-start = (bf16[512,320]{1,0:T(8,128)(2,1)}, bf16[512,320]{1,0:T(8,128)(2,1)S(1)}, u32[]{:S(2)}, u32[]{:S(2)}) collective-permute-start(bf16[512,320]{1,0:T(8,128)(2,1)} %bitcast.2), channel_id=1, source_target_pairs={{0,1},{1,2},{2,3},{3,4},{4,5},{5,6},{6,7},{7,8},{8,9},{9,10},{10,1... | collective-permute-start | bytes 983048 | tf_op jit(solution)/shard_map/ppermute | solution.py:584
  8.5 23.8 %collective-permute-start.1 = (bf16[512,320]{1,0:T(8,128)(2,1)}, bf16[512,320]{1,0:T(8,128)(2,1)S(1)}, u32[]{:S(2)}, u32[]{:S(2)}) collective-permute-start(bf16[512,320]{1,0:T(8,128)(2,1)} %bitcast.4), channel_id=1, source_target_pairs={{1,0},{2,1},{3,2},{4,3},{5,4},{6,5},{7,6},{8,7},{9,8},{10,9},{11,1... | collective-permute-start | bytes 983048 | tf_op jit(solution)/shard_map/ppermute | solution.py:585
  9.9 22.5 %copy-start = (bf16[1,2,16,32,320]{4,3,2,1,0:T(8,128)(2,1)S(1)}, bf16[1,2,16,32,320]{4,3,2,1,0:T(8,128)(2,1)}, u32[]{:S(2)}) copy-start(bf16[1,2,16,32,320]{4,3,2,1,0:T(8,128)(2,1)} %param.7) | copy-start | bytes 1966084
  9.9 22.5 %copy-start.5 = (bf16[3,320,320]{2,1,0:T(8,128)(2,1)S(1)}, bf16[3,320,320]{2,1,0:T(8,128)(2,1)}, u32[]{:S(2)}) copy-start(bf16[3,320,320]{2,1,0:T(8,128)(2,1)} %w_ref.3) | copy-start | bytes 1843204
  17.8 21.1 %all-to-all-start = ((f32[16,2,320]{2,1,0:T(2,128)}), f32[16,2,320]{2,1,0:T(2,128)S(1)}, u32[]{:S(2)}, u32[]{:S(2)}) async-start(f32[16,2,320]{2,1,0:T(2,128)} %get-tuple-element.37), calls=%async_computation | async-start | bytes 98304 | tf_op jit(solution)/shard_map/all_to_all | solution.py:625
  30.0 4.9 %copy-start.7 = (bf16[512,320]{1,0:T(8,128)(2,1)}, bf16[512,320]{1,0:T(8,128)(2,1)S(1)}, u32[]{:S(2)}) copy-start(bf16[512,320]{1,0:T(8,128)(2,1)S(1)} %collective-permute-done.before_ref) | copy-start | bytes 983044
  32.4 2.5 %copy-start.9 = (bf16[512,320]{1,0:T(8,128)(2,1)}, bf16[512,320]{1,0:T(8,128)(2,1)S(1)}, u32[]{:S(2)}) copy-start(bf16[512,320]{1,0:T(8,128)(2,1)S(1)} %collective-permute-done.1.after_ref) | copy-start | bytes 983044
  32.4 9.2 %copy-start.1 = (f32[320]{0:T(512)S(1)}, f32[320]{0:T(512)}, u32[]{:S(2)}) copy-start(f32[320]{0:T(512)} %gain_ref.3) | copy-start | bytes 3844
  39.0 17.1 %copy-start.8 = (bf16[512,320]{1,0:T(8,128)(2,1)S(1)}, bf16[512,320]{1,0:T(8,128)(2,1)}, u32[]{:S(2)}) copy-start(bf16[512,320]{1,0:T(8,128)(2,1)} %copy-done.7) | copy-start | bytes 983044
  39.0 17.1 %copy-start.10 = (bf16[512,320]{1,0:T(8,128)(2,1)S(1)}, bf16[512,320]{1,0:T(8,128)(2,1)}, u32[]{:S(2)}) copy-start(bf16[512,320]{1,0:T(8,128)(2,1)} %copy-done.9) | copy-start | bytes 983044
  39.0 24.0 %collective-permute-start.2 = (bf16[960,1024]{1,0:T(8,128)(2,1)}, bf16[960,1024]{1,0:T(8,128)(2,1)S(1)}, u32[]{:S(2)}, u32[]{:S(2)}) collective-permute-start(bf16[960,1024]{1,0:T(8,128)(2,1)} %get-tuple-element.39.mine_turned_ref), channel_id=1, source_target_pairs={{0,16},{16,0},{1,17},{17,1},{2,18},{18,2},{3,19},{19,3},{4,20},{20... | collective-permute-start | bytes 5898248 | tf_op jit(solution)/shard_map/ppermute | solution.py:590
  57.9 5.0 %copy-start.2 = (bf16[960,1024]{1,0:T(8,128)(2,1)S(1)}, bf16[960,1024]{1,0:T(8,128)(2,1)}, u32[]{:S(2)}) copy-start(bf16[960,1024]{1,0:T(8,128)(2,1)} %get-tuple-element.39.mine_turned_ref) | copy-start | bytes 5898244
  57.9 5.0 %collective-permute-start.4 = (f32[960,256]{1,0:T(8,128)S(1)}, f32[960,256]{1,0:T(8,128)S(1)}, u32[]{:S(2)}, u32[]{:S(2)}) collective-permute-start(f32[960,256]{1,0:T(8,128)S(1)} %get-tuple-element.50), channel_id=1, source_target_pairs={{0,16},{16,0},{1,17},{17,1},{2,18},{18,2},{3,19},{19,3},{4,20},{20... | collective-permute-start | bytes 2949128 | tf_op jit(solution)/shard_map/ppermute | solution.py:590
  60.8 2.2 %collective-permute-start.3 = (bf16[1024,160]{1,0:T(8,128)(2,1)S(1)}, bf16[1024,160]{1,0:T(8,128)(2,1)S(1)}, u32[]{:S(2)}, u32[]{:S(2)}) collective-permute-start(bf16[1024,160]{1,0:T(8,128)(2,1)S(1)} %get-tuple-element.48), channel_id=1, source_target_pairs={{0,16},{16,0},{1,17},{17,1},{2,18},{18,2},{3,19},{19,3},{4,20},{20... | collective-permute-start | bytes 983048 | tf_op jit(solution)/shard_map/ppermute | solution.py:590
  66.1 8.6 %copy-start.4 = (bf16[1,2,16,32,320]{4,3,2,1,0:T(8,128)(2,1)S(1)}, bf16[1,2,16,32,320]{4,3,2,1,0:T(8,128)(2,1)}, u32[]{:S(2)}) copy-start(bf16[1,2,16,32,320]{4,3,2,1,0:T(8,128)(2,1)} %param.6) | copy-start | bytes 1966084
  66.1 28.2 %all-to-all-start.2 = ((bf16[16,64,640]{2,1,0:T(8,128)(2,1)}), bf16[16,64,640]{2,1,0:T(8,128)(2,1)}, u32[]{:S(2)}, u32[]{:S(2)}) async-start(bf16[16,64,640]{2,1,0:T(8,128)(2,1)} %bitcast.19), calls=%async_computation.2 | async-start | bytes 2621440 | tf_op jit(solution)/shard_map/all_to_all | solution.py:596
  71.1 34.4 %collective-permute-start.5 = (bf16[512,320]{1,0:T(8,128)(2,1)S(1)}, bf16[512,320]{1,0:T(8,128)(2,1)S(1)}, u32[]{:S(2)}, u32[]{:S(2)}) collective-permute-start(bf16[512,320]{1,0:T(8,128)(2,1)S(1)} %get-tuple-element.57.h1_ref), channel_id=1, source_target_pairs={{0,1},{1,2},{2,3},{3,4},{4,5},{5,6},{6,7},{7,8},{8,9},{9,10},{10,1... | collective-permute-start | bytes 983048 | tf_op jit(solution)/shard_map/ppermute | solution.py:584
  73.4 32.0 %collective-permute-start.6 = (bf16[512,320]{1,0:T(8,128)(2,1)S(1)}, bf16[512,320]{1,0:T(8,128)(2,1)}, u32[]{:S(2)}, u32[]{:S(2)}) collective-permute-start(bf16[512,320]{1,0:T(8,128)(2,1)S(1)} %get-tuple-element.58.h0_ref), channel_id=1, source_target_pairs={{1,0},{2,1},{3,2},{4,3},{5,4},{6,5},{7,6},{8,7},{9,8},{10,9},{11,1... | collective-permute-start | bytes 983048 | tf_op jit(solution)/shard_map/ppermute | solution.py:585
  116.2 6.1 %copy-start.6 = (bf16[3,320,320]{2,1,0:T(8,128)(2,1)S(1)}, bf16[3,320,320]{2,1,0:T(8,128)(2,1)}, u32[]{:S(2)}) copy-start(bf16[3,320,320]{2,1,0:T(8,128)(2,1)} %w_ref.3) | copy-start | bytes 1843204
  116.2 22.1 %all-to-all-start.5 = ((bf16[16,64,640]{2,1,0:T(8,128)(2,1)}), bf16[16,64,640]{2,1,0:T(8,128)(2,1)S(1)}, u32[]{:S(2)}, u32[]{:S(2)}) async-start(bf16[16,64,640]{2,1,0:T(8,128)(2,1)} %broadcast_in_dim.5), calls=%async_computation.5 | async-start | bytes 2621440 | tf_op jit(solution)/shard_map/all_to_all | solution.py:613
  138.4 8.4 %collective-permute-start.7 = (bf16[1024,640]{1,0:T(8,128)(2,1)S(1)}, bf16[1024,640]{1,0:T(8,128)(2,1)S(1)}, u32[]{:S(2)}, u32[]{:S(2)}) collective-permute-start(bf16[1024,640]{1,0:T(8,128)(2,1)S(1)} %bitcast.12), channel_id=1, source_target_pairs={{0,16},{16,0},{1,17},{17,1},{2,18},{18,2},{3,19},{19,3},{4,20},{20... | collective-permute-start | bytes 3932168 | tf_op jit(solution)/shard_map/ppermute | solution.py:590

commit v7 on v6

--- a/solution.py
+++ b/solution.py
@@ -134,8 +134,8 @@
             activate(step, mean, scale)
             return carry
 
-        lax.fori_loop(f * half, (f + 1) * half, act_step, 0)
         if f == 0:
+            lax.fori_loop(f * half, (f + 1) * half, act_step, 0)
             fetch.wait()
             for i in range(3):
                 for j in range(3):
@@ -145,6 +145,9 @@
         y[f, W : W + PIX, :] = jnp.dot(
             x3[f * PIX : (f + 1) * PIX, :], wf[...], preferred_element_type=F32
         )
+        if f == 0:
+            for step in range(half, 2 * half):
+                activate(step, stats[2], stats[3])
 
         turn(x3[f * PIX : (f + 1) * PIX, C : 2 * C], turned.at[f])
         send = pltpu.make_async_copy(
@@ -466,9 +469,9 @@
 
 
 def input_grad_body(
-    part_ref, h0_ref, h1_ref, far_clip_ref, far_total_ref, x_ref, far_stat_ref, far_w_ref,
-    out_ref, wb, rows, z, dh, grads, lows, clip_ref, total_ref, stat_ref, w_ref, sem,
+    f, part_ref, h_ref, far_clip_ref, far_total_ref, x_ref, far_stat_ref, far_w_ref, *rest
 ):
+    far_out_ref, wb, rows, z, dh, grads, lows, clip_ref, total_ref, stat_ref, w_ref, sem = rest[f:]
     pairs = (far_clip_ref, clip_ref), (far_total_ref, total_ref), (far_stat_ref, stat_ref)
     fetches = [
         pltpu.make_async_copy(one, two, sem.at[n])
@@ -482,63 +485,64 @@
     gain = stat_ref[4:5, :]
     edge = column(C)
     half = PIX // STEP
-    for f in range(2):
-        mean, scale = stat_ref[2 * f : 2 * f + 1, :], stat_ref[2 * f + 1 : 2 * f + 2, :]
-        h_ref = (h0_ref, h1_ref)[f]
-
-        def grad_body(step, carry, f=f, h_ref=h_ref):
-            base = pl.multiple_of(step * STEP, STEP)
-            grad = whole_grad(part_ref, h_ref, clip_ref, clip_sums, base, f)
-            grads[pl.ds(base, STEP), :] = grad
-            lows[pl.ds(base, STEP), :] = grad.astype(BF16)
-            return carry
-
-        lax.fori_loop(0, half, grad_body, 0)
-        if f == 0:
-            fetches[3].wait()
-            for j in range(3):
-                for i in range(3):
-                    wb[PAD * j : PAD * j + C, C * i : C * (i + 1)] = w_ref[3 * i + j]
-                wb[PAD * j + C : PAD * (j + 1), :] = jnp.zeros((PAD - C, 3 * C), BF16)
-        for i, tap in enumerate(row_taps(lows[...])):
-            rows[:, i * C : (i + 1) * C] = tap
-        z[...] = times_transposed(rows[...], wb[...])
-
-        def step_body(step, carry, f=f, mean=mean, scale=scale):
-            base = pl.multiple_of(step * STEP, STEP)
-            here = pl.ds(base, STEP)
-            right = jnp.where(edge == W - 1, 0.0, pltpu.roll(z[here, 0:C], STEP - 1, 0))
-            left = jnp.where(edge == 0, 0.0, pltpu.roll(z[here, 2 * PAD : 2 * PAD + C], 1, 0))
-            acts_grad = right + z[here, PAD : PAD + C] + left
-            hat = (x_ref[pl.ds(base + f * PIX, STEP), :].astype(F32) - mean) * scale
-            pre = hat * gain
-            s = sigmoid(pre)
-            dhat = acts_grad * (s * (1.0 + pre * (1.0 - s))) * gain
-            dh[here, :] = dhat
-            return carry[0] + fold(dhat), carry[1] + fold(dhat * hat)
-
-        zero = jnp.zeros((8, C), F32)
-        sums = lax.fori_loop(0, half, step_body, (zero, zero))
-        grouped = group_sum(four(*sums)) * (1.0 / (PIX * C // GROUPS))
-        first, second = grouped[0:1], grouped[1:2]
-
-        def last_body(step, carry, f=f, mean=mean, scale=scale, first=first, second=second):
-            base = pl.multiple_of(step * STEP, STEP)
-            there = pl.ds(base + f * PIX, STEP)
-            hat = (x_ref[there, :].astype(F32) - mean) * scale
-            here = pl.ds(base, STEP)
-            value = grads[here, :] + scale * (dh[here, :] - first - hat * second)
-            out_ref[there, :] = value.astype(BF16)
-            return carry
-
-        lax.fori_loop(0, half, last_body, 0)
-
-
-def input_gradient(part, h0, h1, clip_stat, total, x, stat, weight):
-    return call(
-        input_grad_body,
-        shape((ROWS, C), BF16),
-        (
+    mean, scale = stat_ref[2 * f : 2 * f + 1, :], stat_ref[2 * f + 1 : 2 * f + 2, :]
+
+    def grad_body(step, carry):
+        base = pl.multiple_of(step * STEP, STEP)
+        grad = whole_grad(part_ref, h_ref, clip_ref, clip_sums, base, f)
+        grads[pl.ds(base, STEP), :] = grad
+        lows[pl.ds(base, STEP), :] = grad.astype(BF16)
+        return carry
+
+    lax.fori_loop(0, half, grad_body, 0)
+    fetches[3].wait()
+    for j in range(3):
+        for i in range(3):
+            wb[PAD * j : PAD * j + C, C * i : C * (i + 1)] = w_ref[3 * i + j]
+        wb[PAD * j + C : PAD * (j + 1), :] = jnp.zeros((PAD - C, 3 * C), BF16)
+    for i, tap in enumerate(row_taps(lows[...])):
+        rows[:, i * C : (i + 1) * C] = tap
+    z[...] = times_transposed(rows[...], wb[...])
+
+    def step_body(step, carry):
+        base = pl.multiple_of(step * STEP, STEP)
+        here = pl.ds(base, STEP)
+        right = jnp.where(edge == W - 1, 0.0, pltpu.roll(z[here, 0:C], STEP - 1, 0))
+        left = jnp.where(edge == 0, 0.0, pltpu.roll(z[here, 2 * PAD : 2 * PAD + C], 1, 0))
+        acts_grad = right + z[here, PAD : PAD + C] + left
+        hat = (x_ref[pl.ds(base + f * PIX, STEP), :].astype(F32) - mean) * scale
+        pre = hat * gain
+        s = sigmoid(pre)
+        dhat = acts_grad * (s * (1.0 + pre * (1.0 - s))) * gain
+        dh[here, :] = dhat
+        return carry[0] + fold(dhat), carry[1] + fold(dhat * hat)
+
+    zero = jnp.zeros((8, C), F32)
+    sums = lax.fori_loop(0, half, step_body, (zero, zero))
+    grouped = group_sum(four(*sums)) * (1.0 / (PIX * C // GROUPS))
+    first, second = grouped[0:1], grouped[1:2]
+
+    def last_body(step, carry):
+        base = pl.multiple_of(step * STEP, STEP)
+        here = pl.ds(base, STEP)
+        hat = (x_ref[pl.ds(base + f * PIX, STEP), :].astype(F32) - mean) * scale
+        value = grads[here, :] + scale * (dh[here, :] - first - hat * second)
+        lows[here, :] = value.astype(BF16)
+        return carry
+
+    lax.fori_loop(0, half, last_body, 0)
+    send = pltpu.make_async_copy(lows, far_out_ref.at[f * PIX : (f + 1) * PIX, :], sem.at[4])
+    send.start()
+    send.wait()
+
+
+def input_gradient(f, part, h, clip_stat, total, x, stat, weight, *held):
+    return pl.pallas_call(
+        functools.partial(input_grad_body, f),
+        out_shape=far((ROWS, C), BF16),
+        in_specs=[VMEM] * 2 + [FAR] * 2 + [VMEM] + [FAR] * (2 + f),
+        out_specs=FAR,
+        scratch_shapes=[
             pltpu.VMEM((3 * PAD, 3 * C), BF16),
             pltpu.VMEM((PIX, 3 * C), BF16),
             pltpu.VMEM((PIX, 3 * PAD), F32),
@@ -549,34 +553,67 @@
             pltpu.VMEM((8, C), F32),
             pltpu.VMEM((8, C), F32),
             pltpu.VMEM((9, C, C), BF16),
-            pltpu.SemaphoreType.DMA((4,)),
+            pltpu.SemaphoreType.DMA((5,)),
+        ],
+        input_output_aliases={7: 0} if held else {},
+        compiler_params=pltpu.CompilerParams(vmem_limit_bytes=16 * MIB),
+        cost_estimate=pl.CostEstimate(
+            flops=1_500_000_000, transcendentals=0, bytes_accessed=8_000_000
         ),
-        flops=2_500_000_000,
-        limit=18,
-        ins=[VMEM] * 3 + [FAR] * 2 + [VMEM] + [FAR] * 2,
-        outs=VMEM,
-    )(part, h0, h1, in_hbm(clip_stat), in_hbm(total), x, in_hbm(stat), in_hbm(weight))
-
-
-def unpack_body(mine_ref, other_ref, spatial_ref, temporal_ref):
+    )(part, h, in_hbm(clip_stat), in_hbm(total), x, in_hbm(stat), in_hbm(weight), *held)
+
+
+def unpack_body(mine_ref, other_ref, far_spatial_ref, far_temporal_ref, taps, sem):
     core = lax.axis_index("c")
+    sends = []
     for j in range(3):
         here = slice(j * C, (j + 1) * C)
         mine, other = mine_ref[here, :], other_ref[here, :]
         left = jnp.where(core == 0, mine, other)
         right = jnp.where(core == 0, other, mine)
         for i in range(4):
+            n = 3 * i + j
             lanes = slice(i * HALF, (i + 1) * HALF)
-            if i < 3:
-                spatial_ref[3 * i + j, :, 0:HALF] = left[:, lanes]
-                spatial_ref[3 * i + j, :, HALF:C] = right[:, lanes]
-            else:
-                temporal_ref[j, :, 0:HALF] = left[:, lanes]
-                temporal_ref[j, :, HALF:C] = right[:, lanes]
+            taps[n, :, 0:HALF] = left[:, lanes]
+            taps[n, :, HALF:C] = right[:, lanes]
+            target = far_spatial_ref.at[n] if i < 3 else far_temporal_ref.at[j]
+            send = pltpu.make_async_copy(taps.at[n], target, sem.at[n])
+            send.start()
+            sends.append(send)
+    for send in sends:
+        send.wait()
 
 
 def unpack(mine, other):
-    return call(unpack_body, (shape((9, C, C), BF16), shape((3, C, C), BF16)))(mine, other)
+    return call(
+        unpack_body,
+        (far((9, C, C), BF16), far((3, C, C), BF16)),
+        (pltpu.VMEM((12, C, C), BF16), pltpu.SemaphoreType.DMA((12,))),
+        ins=[VMEM] * 2,
+        outs=(FAR, FAR),
+    )(mine, other)
+
+
+def frames_body(value_ref, first_ref, second_ref, sem):
+    copies = [
+        pltpu.make_async_copy(value_ref.at[0:PIX, :], first_ref, sem.at[0]),
+        pltpu.make_async_copy(value_ref.at[PIX:ROWS, :], second_ref, sem.at[1]),
+    ]
+    for copy in copies:
+        copy.start()
+    for copy in copies:
+        copy.wait()
+
+
+def frames(value):
+    return call(
+        frames_body,
+        (far((PIX, C), BF16), far((PIX, C), BF16)),
+        (pltpu.SemaphoreType.DMA((2,)),),
+        limit=1,
+        ins=[FAR],
+        outs=(FAR, FAR),
+    )(in_hbm(value))
 
 
 def neighbours(first, second):
@@ -620,7 +657,7 @@
     cot = cotangent.reshape(ROWS, C)
     spatial_weight = spatial_weight.reshape(9, C, C)
     barrier = lax.optimization_barrier
-    cot_before, cot_after = neighbours(cot[:PIX], cot[PIX:])
+    cot_before, cot_after = neighbours(*frames(cot))
     h0, h1, mine_turned, stat_one, sums = forward(x, spatial_weight, gain_one, size)
     sums = lax.all_to_all(sums, FRAME, 0, 0)
     mixed_grad = mixed_gradient(cot_before, cot, cot_after, temporal_weight)
@@ -640,14 +677,15 @@
     packed, total, edge0, edge1 = barrier((packed, total, h0, h1))
     shares = everyone_total(packed)
     before, after = neighbours(edge0, edge1)
-    input_grad = input_gradient(
-        part, h0, h1, far_stat, total, x, stat_one, spatial_weight
-    )
+    input_grad = input_gradient(0, part, h0, far_stat, total, x, stat_one, spatial_weight)
     shares, input_grad = barrier((shares, input_grad))
     (before, after), mine = everyone_share(shares, (before, after))
-    mine, before, after = barrier((mine, before, after))
+    mine, before, after, input_grad = barrier((mine, before, after, input_grad))
+    input_grad = input_gradient(
+        1, part, h1, far_stat, total, x, stat_one, spatial_weight, input_grad
+    )
     output = temporal(before, h0, h1, after, far_stat, temporal_weight)
-    mine, output = barrier((everyone_gets(mine), output))
+    mine, output, input_grad = barrier((everyone_gets(mine), output, input_grad))
     other = swap_cores(mine)
     spatial_grad, temporal_grad = unpack(mine, other)
     return (

time: 151 us -> 176 us (1.17)
  Pallas kernels: 38.4 us -> 64.5 us
  waiting for transfers between devices: 31.3 us -> 28.3 us
  local copies, waits for them, and re-layouts: 3.43 us -> 5.21 us
    pallas_call x2 -> x4, Pallas kernels: 12.9 us -> 39.3 us  [the longest x1 24.9 us: frames(): call(frames_body, (far((PIX, C), BF16), far((PIX, C), BF16)), (pltpu.Sema...]
    all_to_all x1, waiting for transfers between devices: 10.4 us -> 3.55 us  [everyone_gets(): return lax.all_to_all(value, PLANE, 0, 0).reshape(1024, value.shape[2])]
    unnamed x24 -> x30, local copies, waits for them, and re-layouts: 0.06 us -> 3.99 us
    all_to_all x1, waiting for transfers between devices: 9.83 us -> 13.7 us  [everyone_total(): return lax.all_to_all(value, PLANE, 0, 0)]
    slice x1 -> x0, local copies, waits for them, and re-layouts: 2.15 us -> none  [on_device(): cot_before, cot_after = neighbours(cot[:PIX], cot[PIX:])]
    ppermute x4, starting transfers between devices: 9.48 us -> 7.54 us  [swap_cores(): return lax.ppermute(value, 'c', [(0, 1), (1, 0)])]
  transfers between devices with their start and end apart: 11 -> 11, of which waited for: 6 -> 6; matrix products, arithmetic and copies ran while one was open for 1% -> 1% of each run, Pallas kernels for 21% -> 19%
where the time goes in v7:
time: 176 us; the launch traced here: 175 us
  Pallas kernels  64.5 us (37%)
  starting transfers between devices  43.8 us (25%)
  blocking collectives  31.1 us (18%)
  waiting for transfers between devices  28.3 us (16%)
  local copies, waits for them, and re-layouts  5.21 us (3%)
    pallas_call x1, Pallas kernels, frames(): call(frames_body, (far((PIX, C), BF16), far((PIX, C), BF16)), (pltpu.Sema...  24.9 us
    all_to_all x1, waiting for transfers between devices, everyone_total(): return lax.all_to_all(value, PLANE, 0, 0)  13.7 us
    all_to_all x1, starting transfers between devices, on_device(): sums = lax.all_to_all(sums, FRAME, 0, 0)  12.1 us
    all_to_all x1, blocking collectives, on_device(): sums = lax.all_to_all(sums, FRAME, 0, 0)  11.9 us
    pallas_call x2, Pallas kernels, input_gradient(): pl.pallas_call(functools.partial(input_grad_body, f), out_shape=far((ROWS...  11.8 us
    all_to_all x1, blocking collectives, everyone_share(): value = jnp.sum(lax.all_to_all(value, LINE, 0, 0), axis=0).astype(BF16)  9.57 us
    all_to_all x1, blocking collectives, everyone_share(): lax.all_to_all(value, LINE, 0, 0).reshape(1024 // plane, width)  9.56 us
    ppermute x2, starting transfers between devices, neighbours(): before = lax.ppermute(second, FRAME, [(i, i + 1) for i in range(size - 1)])  8.9 us
  transfers between devices with their start and end apart: 11, of which 6 were waited for; matrix products, arithmetic and copies ran while one was open for 1% of the time, Pallas kernels for 19%

profile of v7, /device:TPU:1, one launch (start us, length us, event | category | flops | bytes accessed | tf_op | source)
XLA Modules:
  0.0 175.4 jit_solution(11912713438287327441)
XLA Ops:
  0.6 24.9 %shard_map.94 = (bf16[512,320]{1,0:T(8,128)(2,1)}, bf16[512,320]{1,0:T(8,128)(2,1)}) custom-call(bf16[1024,320]{1,0:T(8,128)(2,1)} %bitcast.12), custom_call_target="tpu_custom_call" | custom-call | bytes 8000000 | tf_op jit(solution)/shard_map/pallas_call | solution.py:609
  25.6 5.7 %collective-permute-start = (bf16[512,320]{1,0:T(8,128)(2,1)}, bf16[512,320]{1,0:T(8,128)(2,1)S(1)}, u32[]{:S(2)}, u32[]{:S(2)}) collective-permute-start(bf16[512,320]{1,0:T(8,128)(2,1)} %get-tuple-element.43), channel_id=1, source_target_pairs={{0,1},{1,2},{2,3},{3,4},{4,5},{5,6},{6,7},{7,8},{8,9},{9,10},{10,1... | collective-permute-start | bytes 983048 | tf_op jit(solution)/shard_map/ppermute | solution.py:621
  31.3 1.3 collective-permute-start.1
  32.6 0.0 copy-start.3
  32.6 1.1 copy-done.3
  33.8 0.7 copy-done.14
  34.5 7.4 %shard_map.93 = (bf16[512,320]{1,0:T(8,128)(2,1)S(1)}, bf16[512,320]{1,0:T(8,128)(2,1)S(1)}, bf16[960,1024]{1,0:T(8,128)(2,1)}, f32[8,320]{1,0:T(8,128)}, f32[16,2,320]{2,1,0:T(2,128)}) custom-call(bf16[1024,320]{1,0:T(8,128)(2,1)S(1)} %bitcast.16, bf16[9,320,320]{2,1,0:T(8,128)(2,1)} %bitcast.19, f32[320]{0:T(512)S(1)} %copy-done.14), custom_call_target="tpu_custom_call" | custom-call | flops 2500000000 | bytes 8000000 | tf_op jit(solution)/shard_map/pallas_call | solution.py:203
  41.9 0.0 copy-start
  41.9 12.1 %all-to-all-start = ((f32[16,2,320]{2,1,0:T(2,128)}), f32[16,2,320]{2,1,0:T(2,128)S(1)}, u32[]{:S(2)}, u32[]{:S(2)}) async-start(f32[16,2,320]{2,1,0:T(2,128)} %get-tuple-element.41), calls=%async_computation | async-start | bytes 98304 | tf_op jit(solution)/shard_map/all_to_all | solution.py:662
  54.0 0.0 copy-start.6
  54.1 0.0 copy-start.10
  54.1 1.1 collective-permute-done.1.after_ref
  55.2 2.5 %shard_map.95.far_grad_ref = bf16[1024,320]{1,0:T(8,128)(2,1)} custom-call(bf16[512,320]{1,0:T(8,128)(2,1)S(1)} %collective-permute-done.before_ref, bf16[1024,320]{1,0:T(8,128)(2,1)S(1)} %bitcast.13, bf16[512,320]{1,0:T(8,128)(2,1)S(1)} %collective-permute-done.1.after_ref, bf16[3,320,320]{2,1,0:T(8,128)(2,1)S(1)} %copy-done.8), custom_call_target="tpu_custom_call" | custom-call | flops 1500000000 | bytes 8000000 | tf_op jit(solution)/shard_map/pallas_call | solution.py:251
  57.6 5.4 %all-to-all-done.sums_ref = f32[16,2,320]{2,1,0:T(2,128)S(1)} async-done(((f32[16,2,320]{2,1,0:T(2,128)}), f32[16,2,320]{2,1,0:T(2,128)S(1)}, u32[]{:S(2)}, u32[]{:S(2)}) %all-to-all-start) | async-done | bytes 40992 | tf_op jit(solution)/shard_map/all_to_all | solution.py:662
  63.0 2.6 %collective-permute-start.2 = (bf16[960,1024]{1,0:T(8,128)(2,1)}, bf16[960,1024]{1,0:T(8,128)(2,1)S(1)}, u32[]{:S(2)}, u32[]{:S(2)}) collective-permute-start(bf16[960,1024]{1,0:T(8,128)(2,1)} %get-tuple-element.45.mine_turned_ref), channel_id=1, source_target_pairs={{0,16},{16,0},{1,17},{17,1},{2,18},{18,2},{3,19},{19,3},{4,20},{20... | collective-permute-start | bytes 5898248 | tf_op jit(solution)/shard_map/ppermute | solution.py:627
  65.6 2.6 %shard_map.96 = (f32[1024,320]{1,0:T(8,128)S(1)}, f32[8,320]{1,0:T(8,128)S(1)}, f32[16,2,320]{2,1,0:T(2,128)S(1)}, f32[8,320]{1,0:T(8,128)}) custom-call(f32[16,2,320]{2,1,0:T(2,128)S(1)} %all-to-all-done.sums_ref, bf16[512,320]{1,0:T(8,128)(2,1)S(1)} %get-tuple-element.64.h0_ref.h_ref, bf16[512,320]{1,0:T(8,128)(2,1)S(1)} %get-tuple-element.63.h1_ref.h_ref, ...), custom_call_target="tpu_custom_call" | custom-call | bytes 8000000 | tf_op jit(solution)/shard_map/pallas_call | solution.py:290
  68.2 11.9 %all_to_all.30.sums_ref = f32[16,2,320]{2,1,0:T(2,128)S(1)} all-to-all(f32[16,2,320]{2,1,0:T(2,128)S(1)} %get-tuple-element.50), channel_id=1, replica_groups=mesh['zl'=2,'x'=4,'c'=2,'y'=4,'zh'=4] {'y','zh'}, dimensions={0} | all-to-all | bytes 81920 | tf_op jit(solution)/shard_map/all_to_all | solution.py:667
  80.1 1.9 %shard_map.98 = (f32[960,256]{1,0:T(8,128)S(1)}, f32[960,256]{1,0:T(8,128)S(1)}) custom-call(bf16[512,320]{1,0:T(8,128)(2,1)S(1)} %get-tuple-element.64.h0_ref.h_ref, bf16[512,320]{1,0:T(8,128)(2,1)S(1)} %get-tuple-element.63.h1_ref.h_ref, bf16[512,320]{1,0:T(8,128)(2,1)S(1)} %copy-done.11, bf16[1024,320]{1,0:T(8,128)(2,1)S(1)} %bitcast.15, ...), custom_call_target="tpu_custom_call" | custom-call | flops 1500000000 | bytes 8000000 | tf_op jit(solution)/shard_map/pallas_call | solution.py:329
  82.0 0.0 copy-start.7
  82.0 0.9 collective-permute-start.4
  82.9 1.9 %shard_map.97 = (bf16[1024,160]{1,0:T(8,128)(2,1)S(1)}, bf16[1024,160]{1,0:T(8,128)(2,1)S(1)}, f32[8,320]{1,0:T(8,128)}) custom-call(f32[16,2,320]{2,1,0:T(2,128)S(1)} %all_to_all.30.sums_ref, f32[8,320]{1,0:T(8,128)S(1)} %get-tuple-element.51.stat_ref, f32[1024,320]{1,0:T(8,128)S(1)} %get-tuple-element.52.part_ref, ...), custom_call_target="tpu_custom_call" | custom-call | bytes 8000000 | tf_op jit(solution)/shard_map/pallas_call | solution.py:412
  84.8 0.3 collective-permute-start.3
  85.1 1.9 %collective-permute-done.3.other_ref = bf16[1024,160]{1,0:T(8,128)(2,1)S(1)} collective-permute-done((bf16[1024,160]{1,0:T(8,128)(2,1)S(1)}, bf16[1024,160]{1,0:T(8,128)(2,1)S(1)}, u32[]{:S(2)}, u32[]{:S(2)}) %collective-permute-start.3) | collective-permute-done | bytes 327712 | tf_op jit(solution)/shard_map/ppermute | solution.py:627
  87.0 0.0 collective-permute-done.4.got_ref
  87.0 0.0 collective-permute-done.2.other_turned_ref
  87.0 3.2 %shard_map.99 = bf16[1024,640]{1,0:T(8,128)(2,1)} custom-call(bf16[960,1024]{1,0:T(8,128)(2,1)S(1)} %copy-done.7, bf16[960,1024]{1,0:T(8,128)(2,1)S(1)} %collective-permute-done.2.other_turned_ref, bf16[1024,160]{1,0:T(8,128)(2,1)S(1)} %get-tuple-element.53.mine_ref, bf16[1024,160]{1,0:T(8,128)(2,1)S(1)} %collective-permute-done.3.other_ref, ...), custom_call_target="tpu_custom_call" | custom-call | flops 2500000000 | bytes 8000000 | tf_op jit(solution)/shard_map/pallas_call | solution.py:457
  90.2 0.0 copy-start.4
  90.2 4.9 %all-to-all-start.2 = ((bf16[16,64,640]{2,1,0:T(8,128)(2,1)}), bf16[16,64,640]{2,1,0:T(8,128)(2,1)}, u32[]{:S(2)}, u32[]{:S(2)}) async-start(bf16[16,64,640]{2,1,0:T(8,128)(2,1)} %bitcast.23), calls=%async_computation.2 | async-start | bytes 2621440 | tf_op jit(solution)/shard_map/all_to_all | solution.py:633
  95.1 3.2 %collective-permute-start.5 = (bf16[512,320]{1,0:T(8,128)(2,1)S(1)}, bf16[512,320]{1,0:T(8,128)(2,1)}, u32[]{:S(2)}, u32[]{:S(2)}) collective-permute-start(bf16[512,320]{1,0:T(8,128)(2,1)S(1)} %get-tuple-element.63.h1_ref.h_ref), channel_id=1, source_target_pairs={{0,1},{1,2},{2,3},{3,4},{4,5},{5,6},{6,7},{7,8},{8,9},{9,10},{10,1... | collective-permute-start | bytes 983048 | tf_op jit(solution)/shard_map/ppermute | solution.py:621
  98.3 1.3 collective-permute-start.6
  99.6 5.9 %shard_map.100.rest_0_ = bf16[1024,320]{1,0:T(8,128)(2,1)} custom-call(f32[1024,320]{1,0:T(8,128)S(1)} %get-tuple-element.52.part_ref, bf16[512,320]{1,0:T(8,128)(2,1)S(1)} %get-tuple-element.64.h0_ref.h_ref, f32[8,320]{1,0:T(8,128)} %get-tuple-element.59.far_clip_ref.far_stat_ref, f32[8,320]{1,0:T(8,128)} %get-tuple-element.60.far_total_ref, ...), custom_call_target="tpu_custom_call" | custom-call | flops 1500000000 | bytes 8000000 | tf_op jit(solution)/shard_map/pallas_call | solution.py:540
  105.5 13.7 %all-to-all-done.2 = bf16[16,64,640]{2,1,0:T(8,128)(2,1)} async-done(((bf16[16,64,640]{2,1,0:T(8,128)(2,1)}), bf16[16,64,640]{2,1,0:T(8,128)(2,1)}, u32[]{:S(2)}, u32[]{:S(2)}) %all-to-all-start.2) | async-done | bytes 1310752 | tf_op jit(solution)/shard_map/all_to_all | solution.py:633
  119.2 1.5 convert_reduce_fusion
  120.7 9.6 %all_to_all.31 = f32[8,8,640]{2,1,0:T(8,128)S(1)} all-to-all(f32[8,8,640]{2,1,0:T(8,128)S(1)} %bitcast.24), channel_id=1, replica_groups=mesh['zl'=2,'x'=4,'c'=2,'y'=4,'zh'=4] {'zl','zh'}, dimensions={0} | all-to-all | bytes 327680 | tf_op jit(solution)/shard_map/all_to_all | solution.py:641
  130.3 0.0 collective-permute-done.5.hb_ref
  130.3 0.0 collective-permute-done.6.ha_ref
  130.4 9.6 %all_to_all.32 = bf16[8,8,640]{2,1,0:T(8,128)(2,1)S(1)} all-to-all(bf16[8,8,640]{2,1,0:T(8,128)(2,1)S(1)} %broadcast_in_dim.4), channel_id=1, replica_groups=mesh['zl'=2,'x'=4,'c'=2,'y'=4,'zh'=4] {'zl','zh'}, dimensions={0} | all-to-all | bytes 163840 | tf_op jit(solution)/shard_map/all_to_all | solution.py:644
  139.9 1.2 broadcast_in_dim.5
  141.1 7.8 %all-to-all-start.5 = ((bf16[16,64,640]{2,1,0:T(8,128)(2,1)}), bf16[16,64,640]{2,1,0:T(8,128)(2,1)S(1)}, u32[]{:S(2)}, u32[]{:S(2)}) async-start(bf16[16,64,640]{2,1,0:T(8,128)(2,1)} %broadcast_in_dim.5), calls=%async_computation.5 | async-start | bytes 2621440 | tf_op jit(solution)/shard_map/all_to_all | solution.py:650
  148.9 0.0 copy-start.1
  148.9 1.0 copy-done.1
  149.9 1.1 copy-done.5
  151.1 6.0 %shard_map.102 = bf16[1024,320]{1,0:T(8,128)(2,1)} custom-call(f32[1024,320]{1,0:T(8,128)S(1)} %get-tuple-element.52.part_ref, bf16[512,320]{1,0:T(8,128)(2,1)S(1)} %copy-done.1, f32[8,320]{1,0:T(8,128)} %get-tuple-element.59.far_clip_ref.far_stat_ref, f32[8,320]{1,0:T(8,128)} %get-tuple-element.60.far_total_ref, ...), custom_call_target="tpu_custom_call", output_to_operand_aliasing={{}: (7, {})} | custom-call | flops 1500000000 | bytes 8000000 | tf_op jit(solution)/shard_map/pallas_call | solution.py:540
  157.0 5.7 %shard_map.101 = bf16[1024,320]{1,0:T(8,128)(2,1)} custom-call(bf16[512,320]{1,0:T(8,128)(2,1)} %collective-permute-done.5.hb_ref, bf16[512,320]{1,0:T(8,128)(2,1)S(1)} %get-tuple-element.64.h0_ref.h_ref, bf16[512,320]{1,0:T(8,128)(2,1)S(1)} %copy-done.1, bf16[512,320]{1,0:T(8,128)(2,1)} %collective-permute-done.6.ha_ref, ...), custom_call_target="tpu_custom_call" | custom-call | flops 1500000000 | bytes 8000000 | tf_op jit(solution)/shard_map/pallas_call | solution.py:371
  162.7 3.5 %all-to-all-done.5 = bf16[16,64,640]{2,1,0:T(8,128)(2,1)S(1)} async-done(((bf16[16,64,640]{2,1,0:T(8,128)(2,1)}), bf16[16,64,640]{2,1,0:T(8,128)(2,1)S(1)}, u32[]{:S(2)}, u32[]{:S(2)}) %all-to-all-start.5) | async-done | bytes 1310752 | tf_op jit(solution)/shard_map/all_to_all | solution.py:650
  166.3 3.8 %collective-permute-start.7 = (bf16[1024,640]{1,0:T(8,128)(2,1)S(1)}, bf16[1024,640]{1,0:T(8,128)(2,1)S(1)}, u32[]{:S(2)}, u32[]{:S(2)}) collective-permute-start(bf16[1024,640]{1,0:T(8,128)(2,1)S(1)} %bitcast.10), channel_id=1, source_target_pairs={{0,16},{16,0},{1,17},{17,1},{2,18},{18,2},{3,19},{19,3},{4,20},{20... | collective-permute-start | bytes 3932168 | tf_op jit(solution)/shard_map/ppermute | solution.py:627
  170.1 2.7 %collective-permute-done.7.other_ref = bf16[1024,640]{1,0:T(8,128)(2,1)S(1)} collective-permute-done((bf16[1024,640]{1,0:T(8,128)(2,1)S(1)}, bf16[1024,640]{1,0:T(8,128)(2,1)S(1)}, u32[]{:S(2)}, u32[]{:S(2)}) %collective-permute-start.7) | collective-permute-done | bytes 1310752 | tf_op jit(solution)/shard_map/ppermute | solution.py:627
  172.7 2.6 %shard_map.103 = (bf16[9,320,320]{2,1,0:T(8,128)(2,1)}, bf16[3,320,320]{2,1,0:T(8,128)(2,1)}) custom-call(bf16[1024,640]{1,0:T(8,128)(2,1)S(1)} %bitcast.11, bf16[1024,640]{1,0:T(8,128)(2,1)S(1)} %collective-permute-done.7.other_ref), custom_call_target="tpu_custom_call" | custom-call | bytes 8000000 | tf_op jit(solution)/shard_map/pallas_call | solution.py:588
  (22 shorter events, 0.1 us)
Async XLA Ops:
  25.6 28.5 %collective-permute-start = (bf16[512,320]{1,0:T(8,128)(2,1)}, bf16[512,320]{1,0:T(8,128)(2,1)S(1)}, u32[]{:S(2)}, u32[]{:S(2)}) collective-permute-start(bf16[512,320]{1,0:T(8,128)(2,1)} %get-tuple-element.43), channel_id=1, source_target_pairs={{0,1},{1,2},{2,3},{3,4},{4,5},{5,6},{6,7},{7,8},{8,9},{9,10},{10,1... | collective-permute-start | bytes 983048 | tf_op jit(solution)/shard_map/ppermute | solution.py:621
  31.3 23.8 %collective-permute-start.1 = (bf16[512,320]{1,0:T(8,128)(2,1)}, bf16[512,320]{1,0:T(8,128)(2,1)S(1)}, u32[]{:S(2)}, u32[]{:S(2)}) collective-permute-start(bf16[512,320]{1,0:T(8,128)(2,1)} %get-tuple-element.44), channel_id=1, source_target_pairs={{1,0},{2,1},{3,2},{4,3},{5,4},{6,5},{7,6},{8,7},{9,8},{10,9},{11,1... | collective-permute-start | bytes 983048 | tf_op jit(solution)/shard_map/ppermute | solution.py:622
  32.6 1.1 copy-start.3
  33.8 0.7 copy-start.14
  34.5 20.7 %copy-start.2 = (bf16[1,2,16,32,320]{4,3,2,1,0:T(8,128)(2,1)S(1)}, bf16[1,2,16,32,320]{4,3,2,1,0:T(8,128)(2,1)}, u32[]{:S(2)}) copy-start(bf16[1,2,16,32,320]{4,3,2,1,0:T(8,128)(2,1)} %param.7) | copy-start | bytes 1966084
  34.5 20.7 %copy-start.8 = (bf16[3,320,320]{2,1,0:T(8,128)(2,1)S(1)}, bf16[3,320,320]{2,1,0:T(8,128)(2,1)}, u32[]{:S(2)}) copy-start(bf16[3,320,320]{2,1,0:T(8,128)(2,1)} %w_ref.3) | copy-start | bytes 1843204
  41.9 53.2 %copy-start = (bf16[512,320]{1,0:T(8,128)(2,1)}, bf16[512,320]{1,0:T(8,128)(2,1)S(1)}, u32[]{:S(2)}) copy-start(bf16[512,320]{1,0:T(8,128)(2,1)S(1)} %get-tuple-element.63.h1_ref.h_ref) | copy-start | bytes 983044
  41.9 21.1 %all-to-all-start = ((f32[16,2,320]{2,1,0:T(2,128)}), f32[16,2,320]{2,1,0:T(2,128)S(1)}, u32[]{:S(2)}, u32[]{:S(2)}) async-start(f32[16,2,320]{2,1,0:T(2,128)} %get-tuple-element.41), calls=%async_computation | async-start | bytes 98304 | tf_op jit(solution)/shard_map/all_to_all | solution.py:662
  54.0 11.6 %copy-start.6 = (f32[320]{0:T(512)S(1)}, f32[320]{0:T(512)}, u32[]{:S(2)}) copy-start(f32[320]{0:T(512)} %gain_ref.3) | copy-start | bytes 3844
  54.1 3.6 %copy-start.10 = (bf16[512,320]{1,0:T(8,128)(2,1)}, bf16[512,320]{1,0:T(8,128)(2,1)S(1)}, u32[]{:S(2)}) copy-start(bf16[512,320]{1,0:T(8,128)(2,1)S(1)} %collective-permute-done.before_ref) | copy-start | bytes 983044
  55.2 2.5 %copy-start.12 = (bf16[512,320]{1,0:T(8,128)(2,1)}, bf16[512,320]{1,0:T(8,128)(2,1)S(1)}, u32[]{:S(2)}) copy-start(bf16[512,320]{1,0:T(8,128)(2,1)S(1)} %collective-permute-done.1.after_ref) | copy-start | bytes 983044
  63.0 17.1 %copy-start.11 = (bf16[512,320]{1,0:T(8,128)(2,1)S(1)}, bf16[512,320]{1,0:T(8,128)(2,1)}, u32[]{:S(2)}) copy-start(bf16[512,320]{1,0:T(8,128)(2,1)} %copy-done.10) | copy-start | bytes 983044
  63.0 17.1 %copy-start.13 = (bf16[512,320]{1,0:T(8,128)(2,1)S(1)}, bf16[512,320]{1,0:T(8,128)(2,1)}, u32[]{:S(2)}) copy-start(bf16[512,320]{1,0:T(8,128)(2,1)} %copy-done.12) | copy-start | bytes 983044
  63.0 24.0 %collective-permute-start.2 = (bf16[960,1024]{1,0:T(8,128)(2,1)}, bf16[960,1024]{1,0:T(8,128)(2,1)S(1)}, u32[]{:S(2)}, u32[]{:S(2)}) collective-permute-start(bf16[960,1024]{1,0:T(8,128)(2,1)} %get-tuple-element.45.mine_turned_ref), channel_id=1, source_target_pairs={{0,16},{16,0},{1,17},{17,1},{2,18},{18,2},{3,19},{19,3},{4,20},{20... | collective-permute-start | bytes 5898248 | tf_op jit(solution)/shard_map/ppermute | solution.py:627
  82.0 5.0 %copy-start.7 = (bf16[960,1024]{1,0:T(8,128)(2,1)S(1)}, bf16[960,1024]{1,0:T(8,128)(2,1)}, u32[]{:S(2)}) copy-start(bf16[960,1024]{1,0:T(8,128)(2,1)} %get-tuple-element.45.mine_turned_ref) | copy-start | bytes 5898244
  82.0 5.0 %collective-permute-start.4 = (f32[960,256]{1,0:T(8,128)S(1)}, f32[960,256]{1,0:T(8,128)S(1)}, u32[]{:S(2)}, u32[]{:S(2)}) collective-permute-start(f32[960,256]{1,0:T(8,128)S(1)} %get-tuple-element.56), channel_id=1, source_target_pairs={{0,16},{16,0},{1,17},{17,1},{2,18},{18,2},{3,19},{19,3},{4,20},{20... | collective-permute-start | bytes 2949128 | tf_op jit(solution)/shard_map/ppermute | solution.py:627
  84.8 2.2 %collective-permute-start.3 = (bf16[1024,160]{1,0:T(8,128)(2,1)S(1)}, bf16[1024,160]{1,0:T(8,128)(2,1)S(1)}, u32[]{:S(2)}, u32[]{:S(2)}) collective-permute-start(bf16[1024,160]{1,0:T(8,128)(2,1)S(1)} %get-tuple-element.54), channel_id=1, source_target_pairs={{0,16},{16,0},{1,17},{17,1},{2,18},{18,2},{3,19},{19,3},{4,20},{20... | collective-permute-start | bytes 983048 | tf_op jit(solution)/shard_map/ppermute | solution.py:627
  90.2 9.4 %copy-start.4 = (bf16[1,2,16,32,320]{4,3,2,1,0:T(8,128)(2,1)S(1)}, bf16[1,2,16,32,320]{4,3,2,1,0:T(8,128)(2,1)}, u32[]{:S(2)}) copy-start(bf16[1,2,16,32,320]{4,3,2,1,0:T(8,128)(2,1)} %param.6) | copy-start | bytes 1966084
  90.2 29.0 %all-to-all-start.2 = ((bf16[16,64,640]{2,1,0:T(8,128)(2,1)}), bf16[16,64,640]{2,1,0:T(8,128)(2,1)}, u32[]{:S(2)}, u32[]{:S(2)}) async-start(bf16[16,64,640]{2,1,0:T(8,128)(2,1)} %bitcast.23), calls=%async_computation.2 | async-start | bytes 2621440 | tf_op jit(solution)/shard_map/all_to_all | solution.py:633
  95.1 35.2 %collective-permute-start.5 = (bf16[512,320]{1,0:T(8,128)(2,1)S(1)}, bf16[512,320]{1,0:T(8,128)(2,1)}, u32[]{:S(2)}, u32[]{:S(2)}) collective-permute-start(bf16[512,320]{1,0:T(8,128)(2,1)S(1)} %get-tuple-element.63.h1_ref.h_ref), channel_id=1, source_target_pairs={{0,1},{1,2},{2,3},{3,4},{4,5},{5,6},{6,7},{7,8},{8,9},{9,10},{10,1... | collective-permute-start | bytes 983048 | tf_op jit(solution)/shard_map/ppermute | solution.py:621
  98.3 32.0 %collective-permute-start.6 = (bf16[512,320]{1,0:T(8,128)(2,1)S(1)}, bf16[512,320]{1,0:T(8,128)(2,1)}, u32[]{:S(2)}, u32[]{:S(2)}) collective-permute-start(bf16[512,320]{1,0:T(8,128)(2,1)S(1)} %get-tuple-element.64.h0_ref.h_ref), channel_id=1, source_target_pairs={{1,0},{2,1},{3,2},{4,3},{5,4},{6,5},{7,6},{8,7},{9,8},{10,9},{11,1... | collective-permute-start | bytes 983048 | tf_op jit(solution)/shard_map/ppermute | solution.py:622
  141.1 25.2 %all-to-all-start.5 = ((bf16[16,64,640]{2,1,0:T(8,128)(2,1)}), bf16[16,64,640]{2,1,0:T(8,128)(2,1)S(1)}, u32[]{:S(2)}, u32[]{:S(2)}) async-start(bf16[16,64,640]{2,1,0:T(8,128)(2,1)} %broadcast_in_dim.5), calls=%async_computation.5 | async-start | bytes 2621440 | tf_op jit(solution)/shard_map/all_to_all | solution.py:650
  148.9 1.0 copy-start.1
  149.9 1.1 copy-start.5
  151.0 6.0 %copy-start.9 = (bf16[3,320,320]{2,1,0:T(8,128)(2,1)S(1)}, bf16[3,320,320]{2,1,0:T(8,128)(2,1)}, u32[]{:S(2)}) copy-start(bf16[3,320,320]{2,1,0:T(8,128)(2,1)} %w_ref.3) | copy-start | bytes 1843204
  166.3 6.4 %collective-permute-start.7 = (bf16[1024,640]{1,0:T(8,128)(2,1)S(1)}, bf16[1024,640]{1,0:T(8,128)(2,1)S(1)}, u32[]{:S(2)}, u32[]{:S(2)}) collective-permute-start(bf16[1024,640]{1,0:T(8,128)(2,1)S(1)} %bitcast.10), channel_id=1, source_target_pairs={{0,16},{16,0},{1,17},{17,1},{2,18},{18,2},{3,19},{19,3},{4,20},{20... | collective-permute-start | bytes 3932168 | tf_op jit(solution)/shard_map/ppermute | solution.py:627

commit v8 on v6

--- a/solution.py
+++ b/solution.py
@@ -134,8 +134,8 @@
             activate(step, mean, scale)
             return carry
 
-        lax.fori_loop(f * half, (f + 1) * half, act_step, 0)
         if f == 0:
+            lax.fori_loop(f * half, (f + 1) * half, act_step, 0)
             fetch.wait()
             for i in range(3):
                 for j in range(3):
@@ -145,6 +145,9 @@
         y[f, W : W + PIX, :] = jnp.dot(
             x3[f * PIX : (f + 1) * PIX, :], wf[...], preferred_element_type=F32
         )
+        if f == 0:
+            for step in range(half, 2 * half):
+                activate(step, stats[2], stats[3])
 
         turn(x3[f * PIX : (f + 1) * PIX, C : 2 * C], turned.at[f])
         send = pltpu.make_async_copy(
@@ -234,20 +237,32 @@
     return grouped[0:1], grouped[1:2]
 
 
-def mixed_grad_body(before_ref, cot_ref, after_ref, w_ref, out_ref):
+def mixed_grad_body(before_ref, cot_ref, after_ref, w_ref, far_ref, out_ref, sem):
+    sends = []
     for f in range(2):
+        here = slice(f * PIX, (f + 1) * PIX)
         last = cot_ref[0:PIX, :] if f else before_ref[...]
         later = after_ref[...] if f else cot_ref[PIX:ROWS, :]
         total = times_transposed(later, w_ref[0])
-        total = total + times_transposed(cot_ref[f * PIX : (f + 1) * PIX, :], w_ref[1])
+        total = total + times_transposed(cot_ref[here, :], w_ref[1])
         total = total + times_transposed(last, w_ref[2])
-        out_ref[f * PIX : (f + 1) * PIX, :] = total.astype(BF16)
+        out_ref[here, :] = total.astype(BF16)
+        send = pltpu.make_async_copy(out_ref.at[here, :], far_ref.at[here, :], sem.at[f])
+        send.start()
+        sends.append(send)
+    for send in sends:
+        send.wait()
 
 
 def mixed_gradient(before, cot, after, weight):
-    return call(mixed_grad_body, far((ROWS, C), BF16), flops=1_500_000_000)(
-        before, cot, after, weight
-    )
+    return call(
+        mixed_grad_body,
+        far((ROWS, C), BF16),
+        (pltpu.VMEM((ROWS, C), BF16), pltpu.SemaphoreType.DMA((2,))),
+        flops=1_500_000_000,
+        ins=[VMEM] * 4,
+        outs=FAR,
+    )(before, cot, after, weight)
 
 
 def slope_body(
@@ -558,25 +573,57 @@
     )(part, h0, h1, in_hbm(clip_stat), in_hbm(total), x, in_hbm(stat), in_hbm(weight))
 
 
-def unpack_body(mine_ref, other_ref, spatial_ref, temporal_ref):
+def unpack_body(mine_ref, other_ref, far_spatial_ref, far_temporal_ref, taps, sem):
     core = lax.axis_index("c")
+    sends = []
     for j in range(3):
         here = slice(j * C, (j + 1) * C)
         mine, other = mine_ref[here, :], other_ref[here, :]
         left = jnp.where(core == 0, mine, other)
         right = jnp.where(core == 0, other, mine)
         for i in range(4):
+            n = 3 * i + j
             lanes = slice(i * HALF, (i + 1) * HALF)
-            if i < 3:
-                spatial_ref[3 * i + j, :, 0:HALF] = left[:, lanes]
-                spatial_ref[3 * i + j, :, HALF:C] = right[:, lanes]
-            else:
-                temporal_ref[j, :, 0:HALF] = left[:, lanes]
-                temporal_ref[j, :, HALF:C] = right[:, lanes]
+            taps[n, :, 0:HALF] = left[:, lanes]
+            taps[n, :, HALF:C] = right[:, lanes]
+            target = far_spatial_ref.at[n] if i < 3 else far_temporal_ref.at[j]
+            send = pltpu.make_async_copy(taps.at[n], target, sem.at[n])
+            send.start()
+            sends.append(send)
+    for send in sends:
+        send.wait()
 
 
 def unpack(mine, other):
-    return call(unpack_body, (shape((9, C, C), BF16), shape((3, C, C), BF16)))(mine, other)
+    return call(
+        unpack_body,
+        (far((9, C, C), BF16), far((3, C, C), BF16)),
+        (pltpu.VMEM((12, C, C), BF16), pltpu.SemaphoreType.DMA((12,))),
+        ins=[VMEM] * 2,
+        outs=(FAR, FAR),
+    )(mine, other)
+
+
+def frames_body(value_ref, first_ref, second_ref, sem):
+    copies = [
+        pltpu.make_async_copy(value_ref.at[0:PIX, :], first_ref, sem.at[0]),
+        pltpu.make_async_copy(value_ref.at[PIX:ROWS, :], second_ref, sem.at[1]),
+    ]
+    for copy in copies:
+        copy.start()
+    for copy in copies:
+        copy.wait()
+
+
+def frames(value):
+    return call(
+        frames_body,
+        (shape((PIX, C), BF16), shape((PIX, C), BF16)),
+        (pltpu.SemaphoreType.DMA((2,)),),
+        limit=2,
+        ins=[FAR],
+        outs=(VMEM, VMEM),
+    )(in_hbm(value))
 
 
 def neighbours(first, second):
@@ -596,15 +643,9 @@
     return lax.all_to_all(value, PLANE, 0, 0)
 
 
-def everyone_share(value, beside):
-    plane, line = lax.axis_size(PLANE), lax.axis_size(LINE)
-    width = value.shape[2]
+def everyone_share(value):
     value = jnp.sum(value.astype(F32), axis=0)
-    value = value.reshape(line, 1024 // plane // line, width)
-    value = jnp.sum(lax.all_to_all(value, LINE, 0, 0), axis=0).astype(BF16)
-    value, *beside = lax.optimization_barrier((value, *beside))
-    value = jnp.broadcast_to(value[None], (line,) + value.shape)
-    return beside, lax.all_to_all(value, LINE, 0, 0).reshape(1024 // plane, width)
+    return lax.psum(value, LINE).astype(BF16)
 
 
 def everyone_gets(value):
@@ -620,7 +661,7 @@
     cot = cotangent.reshape(ROWS, C)
     spatial_weight = spatial_weight.reshape(9, C, C)
     barrier = lax.optimization_barrier
-    cot_before, cot_after = neighbours(cot[:PIX], cot[PIX:])
+    cot_before, cot_after = neighbours(*frames(cot))
     h0, h1, mine_turned, stat_one, sums = forward(x, spatial_weight, gain_one, size)
     sums = lax.all_to_all(sums, FRAME, 0, 0)
     mixed_grad = mixed_gradient(cot_before, cot, cot_after, temporal_weight)
@@ -644,7 +685,7 @@
         part, h0, h1, far_stat, total, x, stat_one, spatial_weight
     )
     shares, input_grad = barrier((shares, input_grad))
-    (before, after), mine = everyone_share(shares, (before, after))
+    mine = everyone_share(shares)
     mine, before, after = barrier((mine, before, after))
     output = temporal(before, h0, h1, after, far_stat, temporal_weight)
     mine, output = barrier((everyone_gets(mine), output))

time: 151 us -> 162 us (1.073)
  starting transfers between devices: 43.3 us -> 49.2 us
  blocking collectives: 31.1 us -> 36.8 us
  waiting for transfers between devices: 31.3 us -> 29.4 us
    psum x0 -> x1, blocking collectives: none -> 24.9 us  [everyone_share(): return lax.psum(value, LINE).astype(BF16)]
    all_to_all x2 -> x0, blocking collectives: 19.1 us -> none  [the longest x1 9.58 us: everyone_share(): value = jnp.sum(lax.all_to_all(value, LINE, 0, 0), axis=0).astype(BF16)]
    ppermute x4, starting transfers between devices: 9.48 us -> 14 us  [swap_cores(): return lax.ppermute(value, 'c', [(0, 1), (1, 0)])]
    all_to_all x1, waiting for transfers between devices: 10.4 us -> 7.75 us  [everyone_gets(): return lax.all_to_all(value, PLANE, 0, 0).reshape(1024, value.shape[2])]
    slice x1 -> x0, local copies, waits for them, and re-layouts: 2.15 us -> none  [on_device(): cot_before, cot_after = neighbours(cot[:PIX], cot[PIX:])]
    unnamed x24, local copies, waits for them, and re-layouts: 0.06 us -> 1.86 us
    pallas_call x2 -> x3, Pallas kernels: 5.65 us -> 6.93 us  [the longest x1 2.56 us: unpack(): call(unpack_body, (far((9, C, C), BF16), far((3, C, C), BF16)), (pltpu.VM...]
  transfers between devices with their start and end apart: 11 -> 11, of which waited for: 6 -> 6; matrix products, arithmetic and copies ran while one was open for 1% -> 1% of each run, Pallas kernels for 21% -> 20%
where the time goes in v8:
time: 162 us; the launch traced here: 160 us
  starting transfers between devices  49.2 us (30%)
  Pallas kernels  39.1 us (24%)
  blocking collectives  36.8 us (23%)
  waiting for transfers between devices  29.4 us (18%)
  local copies, waits for them, and re-layouts  3.07 us (2%)
    psum x1, blocking collectives, everyone_share(): return lax.psum(value, LINE).astype(BF16)  24.9 us
    ppermute x4, starting transfers between devices, swap_cores(): return lax.ppermute(value, 'c', [(0, 1), (1, 0)])  14 us
    all_to_all x1, starting transfers between devices, on_device(): sums = lax.all_to_all(sums, FRAME, 0, 0)  12.1 us
    all_to_all x1, blocking collectives, on_device(): sums = lax.all_to_all(sums, FRAME, 0, 0)  11.9 us
    all_to_all x1, waiting for transfers between devices, everyone_total(): return lax.all_to_all(value, PLANE, 0, 0)  10.5 us
    pallas_call x1, Pallas kernels, input_gradient(): call(input_grad_body, shape((ROWS, C), BF16), (pltpu.VMEM((3 * PAD, 3 * C...  9.73 us
    ppermute x2, starting transfers between devices, neighbours(): before = lax.ppermute(second, FRAME, [(i, i + 1) for i in range(size - 1)])  8.16 us
    all_to_all x1, waiting for transfers between devices, everyone_gets(): return lax.all_to_all(value, PLANE, 0, 0).reshape(1024, value.shape[2])  7.75 us
  transfers between devices with their start and end apart: 11, of which 6 were waited for; matrix products, arithmetic and copies ran while one was open for 1% of the time, Pallas kernels for 20%

profile of v8, /device:TPU:1, one launch (start us, length us, event | category | flops | bytes accessed | tf_op | source)
XLA Modules:
  0.0 160.2 jit_solution(4231080751762672232)
XLA Ops:
  0.6 2.0 %shard_map.94 = (bf16[512,320]{1,0:T(8,128)(2,1)}, bf16[512,320]{1,0:T(8,128)(2,1)}) custom-call(bf16[1024,320]{1,0:T(8,128)(2,1)} %bitcast.10), custom_call_target="tpu_custom_call" | custom-call | bytes 8000000 | tf_op jit(solution)/shard_map/pallas_call | solution.py:619
  2.6 5.7 %collective-permute-start = (bf16[512,320]{1,0:T(8,128)(2,1)}, bf16[512,320]{1,0:T(8,128)(2,1)S(1)}, u32[]{:S(2)}, u32[]{:S(2)}) collective-permute-start(bf16[512,320]{1,0:T(8,128)(2,1)} %get-tuple-element.38), channel_id=1, source_target_pairs={{0,1},{1,2},{2,3},{3,4},{4,5},{5,6},{6,7},{7,8},{8,9},{9,10},{10,1... | collective-permute-start | bytes 983048 | tf_op jit(solution)/shard_map/ppermute | solution.py:631
  8.4 1.3 collective-permute-start.1
  9.7 0.0 copy-start.3
  9.7 1.1 copy-done.3
  10.8 0.7 copy-done.11
  11.5 7.4 %shard_map.93 = (bf16[512,320]{1,0:T(8,128)(2,1)S(1)}, bf16[512,320]{1,0:T(8,128)(2,1)S(1)}, bf16[960,1024]{1,0:T(8,128)(2,1)}, f32[8,320]{1,0:T(8,128)}, f32[16,2,320]{2,1,0:T(2,128)}) custom-call(bf16[1024,320]{1,0:T(8,128)(2,1)S(1)} %bitcast.14, bf16[9,320,320]{2,1,0:T(8,128)(2,1)} %bitcast.17, f32[320]{0:T(512)S(1)} %copy-done.11), custom_call_target="tpu_custom_call" | custom-call | flops 2500000000 | bytes 8000000 | tf_op jit(solution)/shard_map/pallas_call | solution.py:203
  19.0 12.1 %all-to-all-start = ((f32[16,2,320]{2,1,0:T(2,128)}), f32[16,2,320]{2,1,0:T(2,128)S(1)}, u32[]{:S(2)}, u32[]{:S(2)}) async-start(f32[16,2,320]{2,1,0:T(2,128)} %get-tuple-element.36), calls=%async_computation | async-start | bytes 98304 | tf_op jit(solution)/shard_map/all_to_all | solution.py:666
  31.1 0.0 copy-start.1
  31.1 0.0 collective-permute-done.before_ref
  31.1 0.0 copy-start.7
  31.1 1.1 collective-permute-done.1.after_ref
  32.2 0.0 copy-done
  32.2 0.0 copy-done.5
  32.2 2.4 %shard_map.95.far_grad_ref = bf16[1024,320]{1,0:T(8,128)(2,1)} custom-call(bf16[512,320]{1,0:T(8,128)(2,1)S(1)} %collective-permute-done.before_ref, bf16[1024,320]{1,0:T(8,128)(2,1)S(1)} %bitcast.11, bf16[512,320]{1,0:T(8,128)(2,1)S(1)} %collective-permute-done.1.after_ref, bf16[3,320,320]{2,1,0:T(8,128)(2,1)S(1)} %copy-done.5), custom_call_target="tpu_custom_call" | custom-call | flops 1500000000 | bytes 8000000 | tf_op jit(solution)/shard_map/pallas_call | solution.py:258
  34.6 0.0 copy-done.7
  34.6 5.5 %all-to-all-done.sums_ref = f32[16,2,320]{2,1,0:T(2,128)S(1)} async-done(((f32[16,2,320]{2,1,0:T(2,128)}), f32[16,2,320]{2,1,0:T(2,128)S(1)}, u32[]{:S(2)}, u32[]{:S(2)}) %all-to-all-start) | async-done | bytes 40992 | tf_op jit(solution)/shard_map/all_to_all | solution.py:666
  40.1 2.6 %collective-permute-start.2 = (bf16[960,1024]{1,0:T(8,128)(2,1)}, bf16[960,1024]{1,0:T(8,128)(2,1)S(1)}, u32[]{:S(2)}, u32[]{:S(2)}) collective-permute-start(bf16[960,1024]{1,0:T(8,128)(2,1)} %get-tuple-element.40.mine_turned_ref), channel_id=1, source_target_pairs={{0,16},{16,0},{1,17},{17,1},{2,18},{18,2},{3,19},{19,3},{4,20},{20... | collective-permute-start | bytes 5898248 | tf_op jit(solution)/shard_map/ppermute | solution.py:637
  42.6 0.0 copy-done.1
  42.7 2.6 %shard_map.96 = (f32[1024,320]{1,0:T(8,128)S(1)}, f32[8,320]{1,0:T(8,128)S(1)}, f32[16,2,320]{2,1,0:T(2,128)S(1)}, f32[8,320]{1,0:T(8,128)}) custom-call(f32[16,2,320]{2,1,0:T(2,128)S(1)} %all-to-all-done.sums_ref, bf16[512,320]{1,0:T(8,128)(2,1)S(1)} %get-tuple-element.59.h0_ref, bf16[512,320]{1,0:T(8,128)(2,1)S(1)} %get-tuple-element.58.h1_ref, ...), custom_call_target="tpu_custom_call" | custom-call | bytes 8000000 | tf_op jit(solution)/shard_map/pallas_call | solution.py:302
  45.2 11.9 %all_to_all.20.sums_ref = f32[16,2,320]{2,1,0:T(2,128)S(1)} all-to-all(f32[16,2,320]{2,1,0:T(2,128)S(1)} %get-tuple-element.45), channel_id=1, replica_groups=mesh['zl'=2,'x'=4,'c'=2,'y'=4,'zh'=4] {'y','zh'}, dimensions={0} | all-to-all | bytes 81920 | tf_op jit(solution)/shard_map/all_to_all | solution.py:671
  57.2 1.8 %shard_map.98 = (f32[960,256]{1,0:T(8,128)S(1)}, f32[960,256]{1,0:T(8,128)S(1)}) custom-call(bf16[512,320]{1,0:T(8,128)(2,1)S(1)} %get-tuple-element.59.h0_ref, bf16[512,320]{1,0:T(8,128)(2,1)S(1)} %get-tuple-element.58.h1_ref, bf16[512,320]{1,0:T(8,128)(2,1)S(1)} %copy-done.8, bf16[1024,320]{1,0:T(8,128)(2,1)S(1)} %bitcast.13, ...), custom_call_target="tpu_custom_call" | custom-call | flops 1500000000 | bytes 8000000 | tf_op jit(solution)/shard_map/pallas_call | solution.py:341
  59.0 0.0 copy-start.2
  59.0 0.9 collective-permute-start.4
  60.0 1.9 %shard_map.97 = (bf16[1024,160]{1,0:T(8,128)(2,1)S(1)}, bf16[1024,160]{1,0:T(8,128)(2,1)S(1)}, f32[8,320]{1,0:T(8,128)}) custom-call(f32[16,2,320]{2,1,0:T(2,128)S(1)} %all_to_all.20.sums_ref, f32[8,320]{1,0:T(8,128)S(1)} %get-tuple-element.46.stat_ref, f32[1024,320]{1,0:T(8,128)S(1)} %get-tuple-element.47.part_ref, ...), custom_call_target="tpu_custom_call" | custom-call | bytes 8000000 | tf_op jit(solution)/shard_map/pallas_call | solution.py:424
  61.9 0.3 collective-permute-start.3
  62.1 1.9 %collective-permute-done.3.other_ref = bf16[1024,160]{1,0:T(8,128)(2,1)S(1)} collective-permute-done((bf16[1024,160]{1,0:T(8,128)(2,1)S(1)}, bf16[1024,160]{1,0:T(8,128)(2,1)S(1)}, u32[]{:S(2)}, u32[]{:S(2)}) %collective-permute-start.3) | collective-permute-done | bytes 327712 | tf_op jit(solution)/shard_map/ppermute | solution.py:637
  64.0 0.0 collective-permute-done.4.got_ref
  64.0 0.0 collective-permute-done.2.other_turned_ref
  64.0 3.2 %shard_map.99 = bf16[1024,640]{1,0:T(8,128)(2,1)} custom-call(bf16[960,1024]{1,0:T(8,128)(2,1)S(1)} %copy-done.2, bf16[960,1024]{1,0:T(8,128)(2,1)S(1)} %collective-permute-done.2.other_turned_ref, bf16[1024,160]{1,0:T(8,128)(2,1)S(1)} %get-tuple-element.48.mine_ref, bf16[1024,160]{1,0:T(8,128)(2,1)S(1)} %collective-permute-done.3.other_ref, ...), custom_call_target="tpu_custom_call" | custom-call | flops 2500000000 | bytes 8000000 | tf_op jit(solution)/shard_map/pallas_call | solution.py:469
  67.2 0.0 copy-start.4
  67.2 4.9 %all-to-all-start.2 = ((bf16[16,64,640]{2,1,0:T(8,128)(2,1)}), bf16[16,64,640]{2,1,0:T(8,128)(2,1)}, u32[]{:S(2)}, u32[]{:S(2)}) async-start(bf16[16,64,640]{2,1,0:T(8,128)(2,1)} %bitcast.16), calls=%async_computation.2 | async-start | bytes 2621440 | tf_op jit(solution)/shard_map/all_to_all | solution.py:643
  72.2 2.4 %collective-permute-start.5 = (bf16[512,320]{1,0:T(8,128)(2,1)S(1)}, bf16[512,320]{1,0:T(8,128)(2,1)S(1)}, u32[]{:S(2)}, u32[]{:S(2)}) collective-permute-start(bf16[512,320]{1,0:T(8,128)(2,1)S(1)} %get-tuple-element.58.h1_ref), channel_id=1, source_target_pairs={{0,1},{1,2},{2,3},{3,4},{4,5},{5,6},{6,7},{7,8},{8,9},{9,10},{10,1... | collective-permute-start | bytes 983048 | tf_op jit(solution)/shard_map/ppermute | solution.py:631
  74.6 1.3 collective-permute-start.6
  75.9 0.0 copy-done.4
  75.9 9.7 %shard_map.100 = bf16[1024,320]{1,0:T(8,128)(2,1)} custom-call(f32[1024,320]{1,0:T(8,128)S(1)} %get-tuple-element.47.part_ref, bf16[512,320]{1,0:T(8,128)(2,1)S(1)} %get-tuple-element.59.h0_ref, bf16[512,320]{1,0:T(8,128)(2,1)S(1)} %get-tuple-element.58.h1_ref, f32[8,320]{1,0:T(8,128)} %get-tuple-element.54.far_clip_ref.far_stat_ref, ...), custom_call_target="tpu_custom_call" | custom-call | flops 2500000000 | bytes 8000000 | tf_op jit(solution)/shard_map/pallas_call | solution.py:553
  85.6 10.5 %all-to-all-done.2 = bf16[16,64,640]{2,1,0:T(8,128)(2,1)} async-done(((bf16[16,64,640]{2,1,0:T(8,128)(2,1)}), bf16[16,64,640]{2,1,0:T(8,128)(2,1)}, u32[]{:S(2)}, u32[]{:S(2)}) %all-to-all-start.2) | async-done | bytes 1310752 | tf_op jit(solution)/shard_map/all_to_all | solution.py:643
  96.1 1.5 convert_reduce_fusion
  97.6 24.9 %all-reduce.1 = bf16[64,640]{1,0:T(8,128)(2,1)S(1)} all-reduce(f32[64,640]{1,0:T(8,128)S(1)} %convert_reduce_fusion), channel_id=1, replica_groups=mesh['zl'=2,'x'=4,'c'=2,'y'=4,'zh'=4] {'zl','zh'}, use_global_device_ids=true, to_apply=%region_1.0 | all-reduce | flops 40960 | bytes 245760 | tf_op jit(solution)/shard_map/psum | solution.py:648
  122.5 0.0 collective-permute-done.5.hb_ref
  122.5 0.0 collective-permute-done.6.ha_ref
  122.5 1.2 broadcast_in_dim.2
  123.7 7.5 %all-to-all-start.3 = ((bf16[16,64,640]{2,1,0:T(8,128)(2,1)}), bf16[16,64,640]{2,1,0:T(8,128)(2,1)S(1)}, u32[]{:S(2)}, u32[]{:S(2)}) async-start(bf16[16,64,640]{2,1,0:T(8,128)(2,1)} %broadcast_in_dim.2), calls=%async_computation.3 | async-start | bytes 2621440 | tf_op jit(solution)/shard_map/all_to_all | solution.py:654
  131.2 5.6 %shard_map.101 = bf16[1024,320]{1,0:T(8,128)(2,1)} custom-call(bf16[512,320]{1,0:T(8,128)(2,1)S(1)} %collective-permute-done.5.hb_ref, bf16[512,320]{1,0:T(8,128)(2,1)S(1)} %get-tuple-element.59.h0_ref, bf16[512,320]{1,0:T(8,128)(2,1)S(1)} %get-tuple-element.58.h1_ref, bf16[512,320]{1,0:T(8,128)(2,1)} %collective-permute-done.6.ha_ref, ...), custom_call_target="tpu_custom_call" | custom-call | flops 1500000000 | bytes 8000000 | tf_op jit(solution)/shard_map/pallas_call | solution.py:383
  136.8 7.8 %all-to-all-done.3 = bf16[16,64,640]{2,1,0:T(8,128)(2,1)S(1)} async-done(((bf16[16,64,640]{2,1,0:T(8,128)(2,1)}), bf16[16,64,640]{2,1,0:T(8,128)(2,1)S(1)}, u32[]{:S(2)}, u32[]{:S(2)}) %all-to-all-start.3) | async-done | bytes 1310752 | tf_op jit(solution)/shard_map/all_to_all | solution.py:654
  144.6 10.2 %collective-permute-start.7 = (bf16[1024,640]{1,0:T(8,128)(2,1)S(1)}, bf16[1024,640]{1,0:T(8,128)(2,1)S(1)}, u32[]{:S(2)}, u32[]{:S(2)}) collective-permute-start(bf16[1024,640]{1,0:T(8,128)(2,1)S(1)} %bitcast.8), channel_id=1, source_target_pairs={{0,16},{16,0},{1,17},{17,1},{2,18},{18,2},{3,19},{19,3},{4,20},{20... | collective-permute-start | bytes 3932168 | tf_op jit(solution)/shard_map/ppermute | solution.py:637
  154.8 2.7 %collective-permute-done.7.other_ref = bf16[1024,640]{1,0:T(8,128)(2,1)S(1)} collective-permute-done((bf16[1024,640]{1,0:T(8,128)(2,1)S(1)}, bf16[1024,640]{1,0:T(8,128)(2,1)S(1)}, u32[]{:S(2)}, u32[]{:S(2)}) %collective-permute-start.7) | collective-permute-done | bytes 1310752 | tf_op jit(solution)/shard_map/ppermute | solution.py:637
  157.5 2.6 %shard_map.102 = (bf16[9,320,320]{2,1,0:T(8,128)(2,1)}, bf16[3,320,320]{2,1,0:T(8,128)(2,1)}) custom-call(bf16[1024,640]{1,0:T(8,128)(2,1)S(1)} %bitcast.9, bf16[1024,640]{1,0:T(8,128)(2,1)S(1)} %collective-permute-done.7.other_ref), custom_call_target="tpu_custom_call" | custom-call | bytes 8000000 | tf_op jit(solution)/shard_map/pallas_call | solution.py:598
  (12 shorter events, 0.0 us)
Async XLA Ops:
  2.6 28.4 %collective-permute-start = (bf16[512,320]{1,0:T(8,128)(2,1)}, bf16[512,320]{1,0:T(8,128)(2,1)S(1)}, u32[]{:S(2)}, u32[]{:S(2)}) collective-permute-start(bf16[512,320]{1,0:T(8,128)(2,1)} %get-tuple-element.38), channel_id=1, source_target_pairs={{0,1},{1,2},{2,3},{3,4},{4,5},{5,6},{6,7},{7,8},{8,9},{9,10},{10,1... | collective-permute-start | bytes 983048 | tf_op jit(solution)/shard_map/ppermute | solution.py:631
  8.4 23.8 %collective-permute-start.1 = (bf16[512,320]{1,0:T(8,128)(2,1)}, bf16[512,320]{1,0:T(8,128)(2,1)S(1)}, u32[]{:S(2)}, u32[]{:S(2)}) collective-permute-start(bf16[512,320]{1,0:T(8,128)(2,1)} %get-tuple-element.39), channel_id=1, source_target_pairs={{1,0},{2,1},{3,2},{4,3},{5,4},{6,5},{7,6},{8,7},{9,8},{10,9},{11,1... | collective-permute-start | bytes 983048 | tf_op jit(solution)/shard_map/ppermute | solution.py:632
  9.7 1.1 copy-start.3
  10.8 0.7 copy-start.11
  11.5 20.7 %copy-start = (bf16[1,2,16,32,320]{4,3,2,1,0:T(8,128)(2,1)S(1)}, bf16[1,2,16,32,320]{4,3,2,1,0:T(8,128)(2,1)}, u32[]{:S(2)}) copy-start(bf16[1,2,16,32,320]{4,3,2,1,0:T(8,128)(2,1)} %param.7) | copy-start | bytes 1966084
  11.5 20.7 %copy-start.5 = (bf16[3,320,320]{2,1,0:T(8,128)(2,1)S(1)}, bf16[3,320,320]{2,1,0:T(8,128)(2,1)}, u32[]{:S(2)}) copy-start(bf16[3,320,320]{2,1,0:T(8,128)(2,1)} %w_ref.3) | copy-start | bytes 1843204
  19.0 21.1 %all-to-all-start = ((f32[16,2,320]{2,1,0:T(2,128)}), f32[16,2,320]{2,1,0:T(2,128)S(1)}, u32[]{:S(2)}, u32[]{:S(2)}) async-start(f32[16,2,320]{2,1,0:T(2,128)} %get-tuple-element.36), calls=%async_computation | async-start | bytes 98304 | tf_op jit(solution)/shard_map/all_to_all | solution.py:666
  31.1 11.6 %copy-start.1 = (f32[320]{0:T(512)S(1)}, f32[320]{0:T(512)}, u32[]{:S(2)}) copy-start(f32[320]{0:T(512)} %gain_ref.3) | copy-start | bytes 3844
  31.1 3.5 %copy-start.7 = (bf16[512,320]{1,0:T(8,128)(2,1)}, bf16[512,320]{1,0:T(8,128)(2,1)S(1)}, u32[]{:S(2)}) copy-start(bf16[512,320]{1,0:T(8,128)(2,1)S(1)} %collective-permute-done.before_ref) | copy-start | bytes 983044
  32.2 2.4 %copy-start.9 = (bf16[512,320]{1,0:T(8,128)(2,1)}, bf16[512,320]{1,0:T(8,128)(2,1)S(1)}, u32[]{:S(2)}) copy-start(bf16[512,320]{1,0:T(8,128)(2,1)S(1)} %collective-permute-done.1.after_ref) | copy-start | bytes 983044
  40.1 17.1 %copy-start.8 = (bf16[512,320]{1,0:T(8,128)(2,1)S(1)}, bf16[512,320]{1,0:T(8,128)(2,1)}, u32[]{:S(2)}) copy-start(bf16[512,320]{1,0:T(8,128)(2,1)} %copy-done.7) | copy-start | bytes 983044
  40.1 17.1 %copy-start.10 = (bf16[512,320]{1,0:T(8,128)(2,1)S(1)}, bf16[512,320]{1,0:T(8,128)(2,1)}, u32[]{:S(2)}) copy-start(bf16[512,320]{1,0:T(8,128)(2,1)} %copy-done.9) | copy-start | bytes 983044
  40.1 24.0 %collective-permute-start.2 = (bf16[960,1024]{1,0:T(8,128)(2,1)}, bf16[960,1024]{1,0:T(8,128)(2,1)S(1)}, u32[]{:S(2)}, u32[]{:S(2)}) collective-permute-start(bf16[960,1024]{1,0:T(8,128)(2,1)} %get-tuple-element.40.mine_turned_ref), channel_id=1, source_target_pairs={{0,16},{16,0},{1,17},{17,1},{2,18},{18,2},{3,19},{19,3},{4,20},{20... | collective-permute-start | bytes 5898248 | tf_op jit(solution)/shard_map/ppermute | solution.py:637
  59.0 5.0 %copy-start.2 = (bf16[960,1024]{1,0:T(8,128)(2,1)S(1)}, bf16[960,1024]{1,0:T(8,128)(2,1)}, u32[]{:S(2)}) copy-start(bf16[960,1024]{1,0:T(8,128)(2,1)} %get-tuple-element.40.mine_turned_ref) | copy-start | bytes 5898244
  59.0 5.0 %collective-permute-start.4 = (f32[960,256]{1,0:T(8,128)S(1)}, f32[960,256]{1,0:T(8,128)S(1)}, u32[]{:S(2)}, u32[]{:S(2)}) collective-permute-start(f32[960,256]{1,0:T(8,128)S(1)} %get-tuple-element.51), channel_id=1, source_target_pairs={{0,16},{16,0},{1,17},{17,1},{2,18},{18,2},{3,19},{19,3},{4,20},{20... | collective-permute-start | bytes 2949128 | tf_op jit(solution)/shard_map/ppermute | solution.py:637
  61.9 2.2 %collective-permute-start.3 = (bf16[1024,160]{1,0:T(8,128)(2,1)S(1)}, bf16[1024,160]{1,0:T(8,128)(2,1)S(1)}, u32[]{:S(2)}, u32[]{:S(2)}) collective-permute-start(bf16[1024,160]{1,0:T(8,128)(2,1)S(1)} %get-tuple-element.49), channel_id=1, source_target_pairs={{0,16},{16,0},{1,17},{17,1},{2,18},{18,2},{3,19},{19,3},{4,20},{20... | collective-permute-start | bytes 983048 | tf_op jit(solution)/shard_map/ppermute | solution.py:637
  67.2 8.7 %copy-start.4 = (bf16[1,2,16,32,320]{4,3,2,1,0:T(8,128)(2,1)S(1)}, bf16[1,2,16,32,320]{4,3,2,1,0:T(8,128)(2,1)}, u32[]{:S(2)}) copy-start(bf16[1,2,16,32,320]{4,3,2,1,0:T(8,128)(2,1)} %param.6) | copy-start | bytes 1966084
  67.2 28.9 %all-to-all-start.2 = ((bf16[16,64,640]{2,1,0:T(8,128)(2,1)}), bf16[16,64,640]{2,1,0:T(8,128)(2,1)}, u32[]{:S(2)}, u32[]{:S(2)}) async-start(bf16[16,64,640]{2,1,0:T(8,128)(2,1)} %bitcast.16), calls=%async_computation.2 | async-start | bytes 2621440 | tf_op jit(solution)/shard_map/all_to_all | solution.py:643
  72.2 50.3 %collective-permute-start.5 = (bf16[512,320]{1,0:T(8,128)(2,1)S(1)}, bf16[512,320]{1,0:T(8,128)(2,1)S(1)}, u32[]{:S(2)}, u32[]{:S(2)}) collective-permute-start(bf16[512,320]{1,0:T(8,128)(2,1)S(1)} %get-tuple-element.58.h1_ref), channel_id=1, source_target_pairs={{0,1},{1,2},{2,3},{3,4},{4,5},{5,6},{6,7},{7,8},{8,9},{9,10},{10,1... | collective-permute-start | bytes 983048 | tf_op jit(solution)/shard_map/ppermute | solution.py:631
  74.6 47.9 %collective-permute-start.6 = (bf16[512,320]{1,0:T(8,128)(2,1)S(1)}, bf16[512,320]{1,0:T(8,128)(2,1)}, u32[]{:S(2)}, u32[]{:S(2)}) collective-permute-start(bf16[512,320]{1,0:T(8,128)(2,1)S(1)} %get-tuple-element.59.h0_ref), channel_id=1, source_target_pairs={{1,0},{2,1},{3,2},{4,3},{5,4},{6,5},{7,6},{8,7},{9,8},{10,9},{11,1... | collective-permute-start | bytes 983048 | tf_op jit(solution)/shard_map/ppermute | solution.py:632
  123.7 7.5 %copy-start.6 = (bf16[3,320,320]{2,1,0:T(8,128)(2,1)S(1)}, bf16[3,320,320]{2,1,0:T(8,128)(2,1)}, u32[]{:S(2)}) copy-start(bf16[3,320,320]{2,1,0:T(8,128)(2,1)} %w_ref.3) | copy-start | bytes 1843204
  123.7 20.8 %all-to-all-start.3 = ((bf16[16,64,640]{2,1,0:T(8,128)(2,1)}), bf16[16,64,640]{2,1,0:T(8,128)(2,1)S(1)}, u32[]{:S(2)}, u32[]{:S(2)}) async-start(bf16[16,64,640]{2,1,0:T(8,128)(2,1)} %broadcast_in_dim.2), calls=%async_computation.3 | async-start | bytes 2621440 | tf_op jit(solution)/shard_map/all_to_all | solution.py:654
  144.6 12.9 %collective-permute-start.7 = (bf16[1024,640]{1,0:T(8,128)(2,1)S(1)}, bf16[1024,640]{1,0:T(8,128)(2,1)S(1)}, u32[]{:S(2)}, u32[]{:S(2)}) collective-permute-start(bf16[1024,640]{1,0:T(8,128)(2,1)S(1)} %bitcast.8), channel_id=1, source_target_pairs={{0,16},{16,0},{1,17},{17,1},{2,18},{18,2},{3,19},{19,3},{4,20},{20... | collective-permute-start | bytes 3932168 | tf_op jit(solution)/shard_map/ppermute | solution.py:637

commit v9 on v8

--- a/solution.py
+++ b/solution.py
@@ -126,51 +126,57 @@
             edge == W - 1, 0.0, pltpu.roll(act, STEP - 1, 0)
         ).astype(BF16)
 
-    total = (zero, zero)
-    for f in range(2):
-        mean, scale = stats[2 * f], stats[2 * f + 1]
-
-        def act_step(step, carry, mean=mean, scale=scale):
-            activate(step, mean, scale)
-            return carry
-
-        if f == 0:
-            lax.fori_loop(f * half, (f + 1) * half, act_step, 0)
-            fetch.wait()
-            for i in range(3):
-                for j in range(3):
-                    wf[C * j : C * (j + 1), PAD * i : PAD * i + C] = w_ref[3 * i + j]
+    def act_step(step, carry):
+        activate(step, stats[0], stats[1])
+        return carry
+
+    lax.fori_loop(0, half, act_step, 0)
+    fetch.wait()
+    for i in range(3):
+        for j in range(3):
+            wf[C * j : C * (j + 1), PAD * i : PAD * i + C] = w_ref[3 * i + j]
+
+    def product(f):
         y[f, 0:W, :] = jnp.zeros((W, 3 * PAD), F32)
         y[f, W + PIX : 2 * W + PIX, :] = jnp.zeros((W, 3 * PAD), F32)
         y[f, W : W + PIX, :] = jnp.dot(
             x3[f * PIX : (f + 1) * PIX, :], wf[...], preferred_element_type=F32
         )
-        if f == 0:
-            for step in range(half, 2 * half):
-                activate(step, stats[2], stats[3])
-
+
+    def turn_frame(f):
         turn(x3[f * PIX : (f + 1) * PIX, C : 2 * C], turned.at[f])
         send = pltpu.make_async_copy(
             turned.at[f], far_turned_ref.at[:, f * PIX : (f + 1) * PIX], turned_sem.at[f]
         )
         send.start()
         sends.append(send)
-        h_ref = (h0_ref, h1_ref)[f]
-
-        def finish(step, carry, f=f, h_ref=h_ref):
-            base = pl.multiple_of(step * STEP, STEP)
-            conv = (
-                y[f, pl.ds(base, STEP), 0:C]
-                + y[f, pl.ds(base + W, STEP), PAD : PAD + C]
-                + y[f, pl.ds(base + 2 * W, STEP), 2 * PAD : 2 * PAD + C]
-            )
-            value = x_ref[pl.ds(base + f * PIX, STEP), :].astype(F32)
-            low = (value + conv).astype(BF16)
-            h_ref[pl.ds(base, STEP), :] = low
-            value = low.astype(F32)
-            return carry[0] + fold(value), carry[1] + fold(value * value)
-
-        total = lax.fori_loop(0, half, finish, total)
+
+    def finish(f, h_ref, base, carry):
+        conv = (
+            y[f, pl.ds(base, STEP), 0:C]
+            + y[f, pl.ds(base + W, STEP), PAD : PAD + C]
+            + y[f, pl.ds(base + 2 * W, STEP), 2 * PAD : 2 * PAD + C]
+        )
+        value = x_ref[pl.ds(base + f * PIX, STEP), :].astype(F32)
+        low = (value + conv).astype(BF16)
+        h_ref[pl.ds(base, STEP), :] = low
+        value = low.astype(F32)
+        return carry[0] + fold(value), carry[1] + fold(value * value)
+
+    product(0)
+    for step in range(half, 2 * half):
+        activate(step, stats[2], stats[3])
+    turn_frame(0)
+    product(1)
+    total = (zero, zero)
+    for step in range(half):
+        total = finish(0, h0_ref, step * STEP, total)
+    turn_frame(1)
+
+    def last_step(step, carry):
+        return finish(1, h1_ref, pl.multiple_of(step * STEP, STEP), carry)
+
+    total = lax.fori_loop(0, half, last_step, total)
     spread(total, sums_ref)
     for send in sends:
         send.wait()
@@ -604,28 +610,6 @@
     )(mine, other)
 
 
-def frames_body(value_ref, first_ref, second_ref, sem):
-    copies = [
-        pltpu.make_async_copy(value_ref.at[0:PIX, :], first_ref, sem.at[0]),
-        pltpu.make_async_copy(value_ref.at[PIX:ROWS, :], second_ref, sem.at[1]),
-    ]
-    for copy in copies:
-        copy.start()
-    for copy in copies:
-        copy.wait()
-
-
-def frames(value):
-    return call(
-        frames_body,
-        (shape((PIX, C), BF16), shape((PIX, C), BF16)),
-        (pltpu.SemaphoreType.DMA((2,)),),
-        limit=2,
-        ins=[FAR],
-        outs=(VMEM, VMEM),
-    )(in_hbm(value))
-
-
 def neighbours(first, second):
     size = lax.axis_size(FRAME)
     before = lax.ppermute(second, FRAME, [(i, i + 1) for i in range(size - 1)])
@@ -643,9 +627,15 @@
     return lax.all_to_all(value, PLANE, 0, 0)
 
 
-def everyone_share(value):
+def everyone_share(value, beside):
+    plane, line = lax.axis_size(PLANE), lax.axis_size(LINE)
+    width = value.shape[2]
     value = jnp.sum(value.astype(F32), axis=0)
-    return lax.psum(value, LINE).astype(BF16)
+    value = value.reshape(line, 1024 // plane // line, width)
+    value = jnp.sum(lax.all_to_all(value, LINE, 0, 0), axis=0).astype(BF16)
+    value, *beside = lax.optimization_barrier((value, *beside))
+    value = jnp.broadcast_to(value[None], (line,) + value.shape)
+    return beside, lax.all_to_all(value, LINE, 0, 0).reshape(1024 // plane, width)
 
 
 def everyone_gets(value):
@@ -661,7 +651,7 @@
     cot = cotangent.reshape(ROWS, C)
     spatial_weight = spatial_weight.reshape(9, C, C)
     barrier = lax.optimization_barrier
-    cot_before, cot_after = neighbours(*frames(cot))
+    cot_before, cot_after = neighbours(cot[:PIX], cot[PIX:])
     h0, h1, mine_turned, stat_one, sums = forward(x, spatial_weight, gain_one, size)
     sums = lax.all_to_all(sums, FRAME, 0, 0)
     mixed_grad = mixed_gradient(cot_before, cot, cot_after, temporal_weight)
@@ -685,7 +675,7 @@
         part, h0, h1, far_stat, total, x, stat_one, spatial_weight
     )
     shares, input_grad = barrier((shares, input_grad))
-    mine = everyone_share(shares)
+    (before, after), mine = everyone_share(shares, (before, after))
     mine, before, after = barrier((mine, before, after))
     output = temporal(before, h0, h1, after, far_stat, temporal_weight)
     mine, output = barrier((everyone_gets(mine), output))

time: 162 us -> 151 us (0.932)
  blocking collectives: 36.8 us -> 31 us
  starting transfers between devices: 49.2 us -> 45 us
  Pallas kernels: 39.1 us -> 37 us
    psum x1 -> x0, blocking collectives: 24.9 us -> none  [everyone_share(): return lax.psum(value, LINE).astype(BF16)]
    all_to_all x0 -> x2, blocking collectives: none -> 19.1 us  [the longest x1 9.57 us: everyone_share(): value = jnp.sum(lax.all_to_all(value, LINE, 0, 0), axis=0).astype(BF16)]
    ppermute x4, starting transfers between devices: 14 us -> 10.1 us  [swap_cores(): return lax.ppermute(value, 'c', [(0, 1), (1, 0)])]
    all_to_all x1, waiting for transfers between devices: 7.75 us -> 10.5 us  [everyone_gets(): return lax.all_to_all(value, PLANE, 0, 0).reshape(1024, value.shape[2])]
    slice x0 -> x1, local copies, waits for them, and re-layouts: none -> 2.15 us  [on_device(): cot_before, cot_after = neighbours(cot[:PIX], cot[PIX:])]
    pallas_call x1 -> x0, Pallas kernels: 2.01 us -> none  [frames(): call(frames_body, (shape((PIX, C), BF16), shape((PIX, C), BF16)), (pltpu....]
    all_to_all x1, waiting for transfers between devices: 5.46 us -> 3.49 us  [on_device(): sums = lax.all_to_all(sums, FRAME, 0, 0)]
    ppermute x2, waiting for transfers between devices: 1.12 us -> 3.08 us  [neighbours(): after = lax.ppermute(first, FRAME, [(i + 1, i) for i in range(size - 1)])]
  transfers between devices with their start and end apart: 11 -> 11, of which waited for: 6 -> 6; matrix products, arithmetic and copies ran while one was open for 1% -> 1% of each run, Pallas kernels for 20% -> 21%
where the time goes in v9:
time: 151 us; the launch traced here: 150 us
  starting transfers between devices  45 us (30%)
  Pallas kernels  37 us (25%)
  blocking collectives  31 us (21%)
  waiting for transfers between devices  30.8 us (20%)
  local copies, waits for them, and re-layouts  3.43 us (2%)
  other arithmetic  1.52 us (1%)
    all_to_all x1, starting transfers between devices, on_device(): sums = lax.all_to_all(sums, FRAME, 0, 0)  12.1 us
    all_to_all x1, blocking collectives, on_device(): sums = lax.all_to_all(sums, FRAME, 0, 0)  11.9 us
    all_to_all x1, waiting for transfers between devices, everyone_gets(): return lax.all_to_all(value, PLANE, 0, 0).reshape(1024, value.shape[2])  10.5 us
    ppermute x4, starting transfers between devices, swap_cores(): return lax.ppermute(value, 'c', [(0, 1), (1, 0)])  10.1 us
    pallas_call x1, Pallas kernels, input_gradient(): call(input_grad_body, shape((ROWS, C), BF16), (pltpu.VMEM((3 * PAD, 3 * C...  9.74 us
    all_to_all x1, blocking collectives, everyone_share(): value = jnp.sum(lax.all_to_all(value, LINE, 0, 0), axis=0).astype(BF16)  9.57 us
    all_to_all x1, blocking collectives, everyone_share(): lax.all_to_all(value, LINE, 0, 0).reshape(1024 // plane, width)  9.56 us
    all_to_all x1, waiting for transfers between devices, everyone_total(): return lax.all_to_all(value, PLANE, 0, 0)  9.22 us
  transfers between devices with their start and end apart: 11, of which 6 were waited for; matrix products, arithmetic and copies ran while one was open for 1% of the time, Pallas kernels for 21%

profile of v9, /device:TPU:1, one launch (start us, length us, event | category | flops | bytes accessed | tf_op | source)
XLA Modules:
  0.0 149.8 jit_solution(15914725431504979931)
XLA Ops:
  0.6 0.0 copy-start.11
  0.6 0.0 copy-start.3
  0.7 2.1 %fusion = (bf16[1,1,16,32,320]{4,3,2,1,0:T(8,128)(2,1)}, bf16[1,1,16,32,320]{4,3,2,1,0:T(8,128)(2,1)}) fusion(bf16[1,2,16,32,320]{4,3,2,1,0:T(8,128)(2,1)} %param.7), kind=kLoop, calls=%fused_computation.1 | loop fusion | bytes 1310720 | tf_op jit(solution)/shard_map/slice | solution.py:654
  2.8 5.7 %collective-permute-start = (bf16[512,320]{1,0:T(8,128)(2,1)}, bf16[512,320]{1,0:T(8,128)(2,1)S(1)}, u32[]{:S(2)}, u32[]{:S(2)}) collective-permute-start(bf16[512,320]{1,0:T(8,128)(2,1)} %bitcast.2), channel_id=1, source_target_pairs={{0,1},{1,2},{2,3},{3,4},{4,5},{5,6},{6,7},{7,8},{8,9},{9,10},{10,1... | collective-permute-start | bytes 983048 | tf_op jit(solution)/shard_map/ppermute | solution.py:615
  8.5 1.3 collective-permute-start.1
  9.8 0.0 copy-done.11
  9.9 0.0 copy-done.3
  9.9 0.0 copy-start
  9.9 0.0 copy-start.5
  9.9 7.2 %shard_map.93 = (bf16[512,320]{1,0:T(8,128)(2,1)S(1)}, bf16[512,320]{1,0:T(8,128)(2,1)S(1)}, bf16[960,1024]{1,0:T(8,128)(2,1)}, f32[8,320]{1,0:T(8,128)}, f32[16,2,320]{2,1,0:T(2,128)}) custom-call(bf16[1024,320]{1,0:T(8,128)(2,1)S(1)} %bitcast.17, bf16[9,320,320]{2,1,0:T(8,128)(2,1)} %bitcast.22, f32[320]{0:T(512)S(1)} %copy-done.11), custom_call_target="tpu_custom_call" | custom-call | flops 2500000000 | bytes 8000000 | tf_op jit(solution)/shard_map/pallas_call | solution.py:209
  17.1 12.1 %all-to-all-start = ((f32[16,2,320]{2,1,0:T(2,128)}), f32[16,2,320]{2,1,0:T(2,128)S(1)}, u32[]{:S(2)}, u32[]{:S(2)}) async-start(f32[16,2,320]{2,1,0:T(2,128)} %get-tuple-element.37), calls=%async_computation | async-start | bytes 98304 | tf_op jit(solution)/shard_map/all_to_all | solution.py:656
  29.3 0.0 collective-permute-done.before_ref
  29.3 0.0 copy-start.7
  29.3 3.1 %collective-permute-done.1.after_ref = bf16[512,320]{1,0:T(8,128)(2,1)S(1)} collective-permute-done((bf16[512,320]{1,0:T(8,128)(2,1)}, bf16[512,320]{1,0:T(8,128)(2,1)S(1)}, u32[]{:S(2)}, u32[]{:S(2)}) %collective-permute-start.1) | collective-permute-done | bytes 327712 | tf_op jit(solution)/shard_map/ppermute | solution.py:616
  32.4 0.0 copy-done
  32.4 2.4 %shard_map.94.far_grad_ref = bf16[1024,320]{1,0:T(8,128)(2,1)} custom-call(bf16[512,320]{1,0:T(8,128)(2,1)S(1)} %collective-permute-done.before_ref, bf16[1024,320]{1,0:T(8,128)(2,1)S(1)} %bitcast.14, bf16[512,320]{1,0:T(8,128)(2,1)S(1)} %collective-permute-done.1.after_ref, bf16[3,320,320]{2,1,0:T(8,128)(2,1)S(1)} %copy-done.5), custom_call_target="tpu_custom_call" | custom-call | flops 1500000000 | bytes 8000000 | tf_op jit(solution)/shard_map/pallas_call | solution.py:264
  34.8 3.5 %all-to-all-done.sums_ref = f32[16,2,320]{2,1,0:T(2,128)S(1)} async-done(((f32[16,2,320]{2,1,0:T(2,128)}), f32[16,2,320]{2,1,0:T(2,128)S(1)}, u32[]{:S(2)}, u32[]{:S(2)}) %all-to-all-start) | async-done | bytes 40992 | tf_op jit(solution)/shard_map/all_to_all | solution.py:656
  38.3 2.6 %collective-permute-start.2 = (bf16[960,1024]{1,0:T(8,128)(2,1)}, bf16[960,1024]{1,0:T(8,128)(2,1)S(1)}, u32[]{:S(2)}, u32[]{:S(2)}) collective-permute-start(bf16[960,1024]{1,0:T(8,128)(2,1)} %get-tuple-element.39.mine_turned_ref), channel_id=1, source_target_pairs={{0,16},{16,0},{1,17},{17,1},{2,18},{18,2},{3,19},{19,3},{4,20},{20... | collective-permute-start | bytes 5898248 | tf_op jit(solution)/shard_map/ppermute | solution.py:621
  40.8 2.6 %shard_map.95 = (f32[1024,320]{1,0:T(8,128)S(1)}, f32[8,320]{1,0:T(8,128)S(1)}, f32[16,2,320]{2,1,0:T(2,128)S(1)}, f32[8,320]{1,0:T(8,128)}) custom-call(f32[16,2,320]{2,1,0:T(2,128)S(1)} %all-to-all-done.sums_ref, bf16[512,320]{1,0:T(8,128)(2,1)S(1)} %get-tuple-element.58.h0_ref, bf16[512,320]{1,0:T(8,128)(2,1)S(1)} %get-tuple-element.57.h1_ref, ...), custom_call_target="tpu_custom_call" | custom-call | bytes 8000000 | tf_op jit(solution)/shard_map/pallas_call | solution.py:308
  43.4 11.9 %all_to_all.30.sums_ref = f32[16,2,320]{2,1,0:T(2,128)S(1)} all-to-all(f32[16,2,320]{2,1,0:T(2,128)S(1)} %get-tuple-element.44), channel_id=1, replica_groups=mesh['zl'=2,'x'=4,'c'=2,'y'=4,'zh'=4] {'y','zh'}, dimensions={0} | all-to-all | bytes 81920 | tf_op jit(solution)/shard_map/all_to_all | solution.py:661
  55.3 1.8 %shard_map.97 = (f32[960,256]{1,0:T(8,128)S(1)}, f32[960,256]{1,0:T(8,128)S(1)}) custom-call(bf16[512,320]{1,0:T(8,128)(2,1)S(1)} %get-tuple-element.58.h0_ref, bf16[512,320]{1,0:T(8,128)(2,1)S(1)} %get-tuple-element.57.h1_ref, bf16[512,320]{1,0:T(8,128)(2,1)S(1)} %copy-done.8, bf16[1024,320]{1,0:T(8,128)(2,1)S(1)} %bitcast.16, ...), custom_call_target="tpu_custom_call" | custom-call | flops 1500000000 | bytes 8000000 | tf_op jit(solution)/shard_map/pallas_call | solution.py:347
  57.1 0.0 copy-start.2
  57.2 1.6 %collective-permute-start.4 = (f32[960,256]{1,0:T(8,128)S(1)}, f32[960,256]{1,0:T(8,128)S(1)}, u32[]{:S(2)}, u32[]{:S(2)}) collective-permute-start(f32[960,256]{1,0:T(8,128)S(1)} %get-tuple-element.50), channel_id=1, source_target_pairs={{0,16},{16,0},{1,17},{17,1},{2,18},{18,2},{3,19},{19,3},{4,20},{20... | collective-permute-start | bytes 2949128 | tf_op jit(solution)/shard_map/ppermute | solution.py:621
  58.7 1.9 %shard_map.96 = (bf16[1024,160]{1,0:T(8,128)(2,1)S(1)}, bf16[1024,160]{1,0:T(8,128)(2,1)S(1)}, f32[8,320]{1,0:T(8,128)}) custom-call(f32[16,2,320]{2,1,0:T(2,128)S(1)} %all_to_all.30.sums_ref, f32[8,320]{1,0:T(8,128)S(1)} %get-tuple-element.45.stat_ref, f32[1024,320]{1,0:T(8,128)S(1)} %get-tuple-element.46.part_ref, ...), custom_call_target="tpu_custom_call" | custom-call | bytes 8000000 | tf_op jit(solution)/shard_map/pallas_call | solution.py:430
  60.7 0.3 collective-permute-start.3
  60.9 1.9 %collective-permute-done.3.other_ref = bf16[1024,160]{1,0:T(8,128)(2,1)S(1)} collective-permute-done((bf16[1024,160]{1,0:T(8,128)(2,1)S(1)}, bf16[1024,160]{1,0:T(8,128)(2,1)S(1)}, u32[]{:S(2)}, u32[]{:S(2)}) %collective-permute-start.3) | collective-permute-done | bytes 327712 | tf_op jit(solution)/shard_map/ppermute | solution.py:621
  62.8 0.0 collective-permute-done.4.got_ref
  62.8 0.0 collective-permute-done.2.other_turned_ref
  62.8 0.0 copy-done.2
  62.8 3.2 %shard_map.98 = bf16[1024,640]{1,0:T(8,128)(2,1)} custom-call(bf16[960,1024]{1,0:T(8,128)(2,1)S(1)} %copy-done.2, bf16[960,1024]{1,0:T(8,128)(2,1)S(1)} %collective-permute-done.2.other_turned_ref, bf16[1024,160]{1,0:T(8,128)(2,1)S(1)} %get-tuple-element.47.mine_ref, bf16[1024,160]{1,0:T(8,128)(2,1)S(1)} %collective-permute-done.3.other_ref, ...), custom_call_target="tpu_custom_call" | custom-call | flops 2500000000 | bytes 8000000 | tf_op jit(solution)/shard_map/pallas_call | solution.py:475
  66.0 0.0 copy-start.4
  66.0 4.8 %all-to-all-start.2 = ((bf16[16,64,640]{2,1,0:T(8,128)(2,1)}), bf16[16,64,640]{2,1,0:T(8,128)(2,1)}, u32[]{:S(2)}, u32[]{:S(2)}) async-start(bf16[16,64,640]{2,1,0:T(8,128)(2,1)} %bitcast.19), calls=%async_computation.2 | async-start | bytes 2621440 | tf_op jit(solution)/shard_map/all_to_all | solution.py:627
  70.8 2.3 %collective-permute-start.5 = (bf16[512,320]{1,0:T(8,128)(2,1)S(1)}, bf16[512,320]{1,0:T(8,128)(2,1)S(1)}, u32[]{:S(2)}, u32[]{:S(2)}) collective-permute-start(bf16[512,320]{1,0:T(8,128)(2,1)S(1)} %get-tuple-element.57.h1_ref), channel_id=1, source_target_pairs={{0,1},{1,2},{2,3},{3,4},{4,5},{5,6},{6,7},{7,8},{8,9},{9,10},{10,1... | collective-permute-start | bytes 983048 | tf_op jit(solution)/shard_map/ppermute | solution.py:615
  73.1 1.3 collective-permute-start.6
  74.4 9.7 %shard_map.99 = bf16[1024,320]{1,0:T(8,128)(2,1)} custom-call(f32[1024,320]{1,0:T(8,128)S(1)} %get-tuple-element.46.part_ref, bf16[512,320]{1,0:T(8,128)(2,1)S(1)} %get-tuple-element.58.h0_ref, bf16[512,320]{1,0:T(8,128)(2,1)S(1)} %get-tuple-element.57.h1_ref, f32[8,320]{1,0:T(8,128)} %get-tuple-element.53.far_clip_ref.far_stat_ref, ...), custom_call_target="tpu_custom_call" | custom-call | flops 2500000000 | bytes 8000000 | tf_op jit(solution)/shard_map/pallas_call | solution.py:559
  84.2 9.2 %all-to-all-done.2 = bf16[16,64,640]{2,1,0:T(8,128)(2,1)} async-done(((bf16[16,64,640]{2,1,0:T(8,128)(2,1)}), bf16[16,64,640]{2,1,0:T(8,128)(2,1)}, u32[]{:S(2)}, u32[]{:S(2)}) %all-to-all-start.2) | async-done | bytes 1310752 | tf_op jit(solution)/shard_map/all_to_all | solution.py:627
  93.4 1.5 %convert_reduce_fusion = f32[64,640]{1,0:T(8,128)S(1)} fusion(bf16[16,64,640]{2,1,0:T(8,128)(2,1)} %all-to-all-done.2), kind=kLoop, calls=%fused_computation | loop fusion | flops 1269760 | bytes 1474560 | tf_op jit(solution)/shard_map/reduce_sum | solution.py:633
  94.9 9.6 %all_to_all.31 = f32[8,8,640]{2,1,0:T(8,128)S(1)} all-to-all(f32[8,8,640]{2,1,0:T(8,128)S(1)} %bitcast.20), channel_id=1, replica_groups=mesh['zl'=2,'x'=4,'c'=2,'y'=4,'zh'=4] {'zl','zh'}, dimensions={0} | all-to-all | bytes 327680 | tf_op jit(solution)/shard_map/all_to_all | solution.py:635
  104.5 0.0 collective-permute-done.5.hb_ref
  104.5 0.0 collective-permute-done.6.ha_ref
  104.5 9.6 %all_to_all.32 = bf16[8,8,640]{2,1,0:T(8,128)(2,1)S(1)} all-to-all(bf16[8,8,640]{2,1,0:T(8,128)(2,1)S(1)} %broadcast_in_dim.4), channel_id=1, replica_groups=mesh['zl'=2,'x'=4,'c'=2,'y'=4,'zh'=4] {'zl','zh'}, dimensions={0} | all-to-all | bytes 163840 | tf_op jit(solution)/shard_map/all_to_all | solution.py:638
  114.1 1.2 broadcast_in_dim.5
  115.3 7.4 %all-to-all-start.5 = ((bf16[16,64,640]{2,1,0:T(8,128)(2,1)}), bf16[16,64,640]{2,1,0:T(8,128)(2,1)S(1)}, u32[]{:S(2)}, u32[]{:S(2)}) async-start(bf16[16,64,640]{2,1,0:T(8,128)(2,1)} %broadcast_in_dim.5), calls=%async_computation.5 | async-start | bytes 2621440 | tf_op jit(solution)/shard_map/all_to_all | solution.py:644
  122.7 5.6 %shard_map.100 = bf16[1024,320]{1,0:T(8,128)(2,1)} custom-call(bf16[512,320]{1,0:T(8,128)(2,1)S(1)} %collective-permute-done.5.hb_ref, bf16[512,320]{1,0:T(8,128)(2,1)S(1)} %get-tuple-element.58.h0_ref, bf16[512,320]{1,0:T(8,128)(2,1)S(1)} %get-tuple-element.57.h1_ref, bf16[512,320]{1,0:T(8,128)(2,1)} %collective-permute-done.6.ha_ref, ...), custom_call_target="tpu_custom_call" | custom-call | flops 1500000000 | bytes 8000000 | tf_op jit(solution)/shard_map/pallas_call | solution.py:389
  128.3 10.5 %all-to-all-done.5 = bf16[16,64,640]{2,1,0:T(8,128)(2,1)S(1)} async-done(((bf16[16,64,640]{2,1,0:T(8,128)(2,1)}), bf16[16,64,640]{2,1,0:T(8,128)(2,1)S(1)}, u32[]{:S(2)}, u32[]{:S(2)}) %all-to-all-start.5) | async-done | bytes 1310752 | tf_op jit(solution)/shard_map/all_to_all | solution.py:644
  138.7 5.7 %collective-permute-start.7 = (bf16[1024,640]{1,0:T(8,128)(2,1)S(1)}, bf16[1024,640]{1,0:T(8,128)(2,1)S(1)}, u32[]{:S(2)}, u32[]{:S(2)}) collective-permute-start(bf16[1024,640]{1,0:T(8,128)(2,1)S(1)} %bitcast.12), channel_id=1, source_target_pairs={{0,16},{16,0},{1,17},{17,1},{2,18},{18,2},{3,19},{19,3},{4,20},{20... | collective-permute-start | bytes 3932168 | tf_op jit(solution)/shard_map/ppermute | solution.py:621
  144.4 2.7 %collective-permute-done.7.other_ref = bf16[1024,640]{1,0:T(8,128)(2,1)S(1)} collective-permute-done((bf16[1024,640]{1,0:T(8,128)(2,1)S(1)}, bf16[1024,640]{1,0:T(8,128)(2,1)S(1)}, u32[]{:S(2)}, u32[]{:S(2)}) %collective-permute-start.7) | collective-permute-done | bytes 1310752 | tf_op jit(solution)/shard_map/ppermute | solution.py:621
  147.1 2.6 %shard_map.101 = (bf16[9,320,320]{2,1,0:T(8,128)(2,1)}, bf16[3,320,320]{2,1,0:T(8,128)(2,1)}) custom-call(bf16[1024,640]{1,0:T(8,128)(2,1)S(1)} %bitcast.13, bf16[1024,640]{1,0:T(8,128)(2,1)S(1)} %collective-permute-done.7.other_ref), custom_call_target="tpu_custom_call" | custom-call | bytes 8000000 | tf_op jit(solution)/shard_map/pallas_call | solution.py:604
  (15 shorter events, 0.0 us)
Async XLA Ops:
  0.6 9.2 %copy-start.11 = (f32[320]{0:T(512)S(1)}, f32[320]{0:T(512)}, u32[]{:S(2)}) copy-start(f32[320]{0:T(512)} %gain_ref.2) | copy-start | bytes 3844
  0.6 9.2 %copy-start.3 = (bf16[1,2,16,32,320]{4,3,2,1,0:T(8,128)(2,1)S(1)}, bf16[1,2,16,32,320]{4,3,2,1,0:T(8,128)(2,1)}, u32[]{:S(2)}) copy-start(bf16[1,2,16,32,320]{4,3,2,1,0:T(8,128)(2,1)} %param.6) | copy-start | bytes 1966084
  2.8 26.5 %collective-permute-start = (bf16[512,320]{1,0:T(8,128)(2,1)}, bf16[512,320]{1,0:T(8,128)(2,1)S(1)}, u32[]{:S(2)}, u32[]{:S(2)}) collective-permute-start(bf16[512,320]{1,0:T(8,128)(2,1)} %bitcast.2), channel_id=1, source_target_pairs={{0,1},{1,2},{2,3},{3,4},{4,5},{5,6},{6,7},{7,8},{8,9},{9,10},{10,1... | collective-permute-start | bytes 983048 | tf_op jit(solution)/shard_map/ppermute | solution.py:615
  8.5 23.8 %collective-permute-start.1 = (bf16[512,320]{1,0:T(8,128)(2,1)}, bf16[512,320]{1,0:T(8,128)(2,1)S(1)}, u32[]{:S(2)}, u32[]{:S(2)}) collective-permute-start(bf16[512,320]{1,0:T(8,128)(2,1)} %bitcast.4), channel_id=1, source_target_pairs={{1,0},{2,1},{3,2},{4,3},{5,4},{6,5},{7,6},{8,7},{9,8},{10,9},{11,1... | collective-permute-start | bytes 983048 | tf_op jit(solution)/shard_map/ppermute | solution.py:616
  9.9 22.5 %copy-start = (bf16[1,2,16,32,320]{4,3,2,1,0:T(8,128)(2,1)S(1)}, bf16[1,2,16,32,320]{4,3,2,1,0:T(8,128)(2,1)}, u32[]{:S(2)}) copy-start(bf16[1,2,16,32,320]{4,3,2,1,0:T(8,128)(2,1)} %param.7) | copy-start | bytes 1966084
  9.9 22.5 %copy-start.5 = (bf16[3,320,320]{2,1,0:T(8,128)(2,1)S(1)}, bf16[3,320,320]{2,1,0:T(8,128)(2,1)}, u32[]{:S(2)}) copy-start(bf16[3,320,320]{2,1,0:T(8,128)(2,1)} %w_ref.3) | copy-start | bytes 1843204
  17.1 21.1 %all-to-all-start = ((f32[16,2,320]{2,1,0:T(2,128)}), f32[16,2,320]{2,1,0:T(2,128)S(1)}, u32[]{:S(2)}, u32[]{:S(2)}) async-start(f32[16,2,320]{2,1,0:T(2,128)} %get-tuple-element.37), calls=%async_computation | async-start | bytes 98304 | tf_op jit(solution)/shard_map/all_to_all | solution.py:656
  29.3 5.5 %copy-start.7 = (bf16[512,320]{1,0:T(8,128)(2,1)}, bf16[512,320]{1,0:T(8,128)(2,1)S(1)}, u32[]{:S(2)}) copy-start(bf16[512,320]{1,0:T(8,128)(2,1)S(1)} %collective-permute-done.before_ref) | copy-start | bytes 983044
  32.4 2.4 %copy-start.9 = (bf16[512,320]{1,0:T(8,128)(2,1)}, bf16[512,320]{1,0:T(8,128)(2,1)S(1)}, u32[]{:S(2)}) copy-start(bf16[512,320]{1,0:T(8,128)(2,1)S(1)} %collective-permute-done.1.after_ref) | copy-start | bytes 983044
  32.4 8.5 %copy-start.1 = (f32[320]{0:T(512)S(1)}, f32[320]{0:T(512)}, u32[]{:S(2)}) copy-start(f32[320]{0:T(512)} %gain_ref.3) | copy-start | bytes 3844
  38.3 17.1 %copy-start.8 = (bf16[512,320]{1,0:T(8,128)(2,1)S(1)}, bf16[512,320]{1,0:T(8,128)(2,1)}, u32[]{:S(2)}) copy-start(bf16[512,320]{1,0:T(8,128)(2,1)} %copy-done.7) | copy-start | bytes 983044
  38.3 17.1 %copy-start.10 = (bf16[512,320]{1,0:T(8,128)(2,1)S(1)}, bf16[512,320]{1,0:T(8,128)(2,1)}, u32[]{:S(2)}) copy-start(bf16[512,320]{1,0:T(8,128)(2,1)} %copy-done.9) | copy-start | bytes 983044
  38.3 24.6 %collective-permute-start.2 = (bf16[960,1024]{1,0:T(8,128)(2,1)}, bf16[960,1024]{1,0:T(8,128)(2,1)S(1)}, u32[]{:S(2)}, u32[]{:S(2)}) collective-permute-start(bf16[960,1024]{1,0:T(8,128)(2,1)} %get-tuple-element.39.mine_turned_ref), channel_id=1, source_target_pairs={{0,16},{16,0},{1,17},{17,1},{2,18},{18,2},{3,19},{19,3},{4,20},{20... | collective-permute-start | bytes 5898248 | tf_op jit(solution)/shard_map/ppermute | solution.py:621
  57.1 5.7 %copy-start.2 = (bf16[960,1024]{1,0:T(8,128)(2,1)S(1)}, bf16[960,1024]{1,0:T(8,128)(2,1)}, u32[]{:S(2)}) copy-start(bf16[960,1024]{1,0:T(8,128)(2,1)} %get-tuple-element.39.mine_turned_ref) | copy-start | bytes 5898244
  57.2 5.7 %collective-permute-start.4 = (f32[960,256]{1,0:T(8,128)S(1)}, f32[960,256]{1,0:T(8,128)S(1)}, u32[]{:S(2)}, u32[]{:S(2)}) collective-permute-start(f32[960,256]{1,0:T(8,128)S(1)} %get-tuple-element.50), channel_id=1, source_target_pairs={{0,16},{16,0},{1,17},{17,1},{2,18},{18,2},{3,19},{19,3},{4,20},{20... | collective-permute-start | bytes 2949128 | tf_op jit(solution)/shard_map/ppermute | solution.py:621
  60.7 2.2 %collective-permute-start.3 = (bf16[1024,160]{1,0:T(8,128)(2,1)S(1)}, bf16[1024,160]{1,0:T(8,128)(2,1)S(1)}, u32[]{:S(2)}, u32[]{:S(2)}) collective-permute-start(bf16[1024,160]{1,0:T(8,128)(2,1)S(1)} %get-tuple-element.48), channel_id=1, source_target_pairs={{0,16},{16,0},{1,17},{17,1},{2,18},{18,2},{3,19},{19,3},{4,20},{20... | collective-permute-start | bytes 983048 | tf_op jit(solution)/shard_map/ppermute | solution.py:621
  66.0 8.4 %copy-start.4 = (bf16[1,2,16,32,320]{4,3,2,1,0:T(8,128)(2,1)S(1)}, bf16[1,2,16,32,320]{4,3,2,1,0:T(8,128)(2,1)}, u32[]{:S(2)}) copy-start(bf16[1,2,16,32,320]{4,3,2,1,0:T(8,128)(2,1)} %param.6) | copy-start | bytes 1966084
  66.0 27.4 %all-to-all-start.2 = ((bf16[16,64,640]{2,1,0:T(8,128)(2,1)}), bf16[16,64,640]{2,1,0:T(8,128)(2,1)}, u32[]{:S(2)}, u32[]{:S(2)}) async-start(bf16[16,64,640]{2,1,0:T(8,128)(2,1)} %bitcast.19), calls=%async_computation.2 | async-start | bytes 2621440 | tf_op jit(solution)/shard_map/all_to_all | solution.py:627
  70.8 33.7 %collective-permute-start.5 = (bf16[512,320]{1,0:T(8,128)(2,1)S(1)}, bf16[512,320]{1,0:T(8,128)(2,1)S(1)}, u32[]{:S(2)}, u32[]{:S(2)}) collective-permute-start(bf16[512,320]{1,0:T(8,128)(2,1)S(1)} %get-tuple-element.57.h1_ref), channel_id=1, source_target_pairs={{0,1},{1,2},{2,3},{3,4},{4,5},{5,6},{6,7},{7,8},{8,9},{9,10},{10,1... | collective-permute-start | bytes 983048 | tf_op jit(solution)/shard_map/ppermute | solution.py:615
  73.1 31.4 %collective-permute-start.6 = (bf16[512,320]{1,0:T(8,128)(2,1)S(1)}, bf16[512,320]{1,0:T(8,128)(2,1)}, u32[]{:S(2)}, u32[]{:S(2)}) collective-permute-start(bf16[512,320]{1,0:T(8,128)(2,1)S(1)} %get-tuple-element.58.h0_ref), channel_id=1, source_target_pairs={{1,0},{2,1},{3,2},{4,3},{5,4},{6,5},{7,6},{8,7},{9,8},{10,9},{11,1... | collective-permute-start | bytes 983048 | tf_op jit(solution)/shard_map/ppermute | solution.py:616
  115.3 7.4 %copy-start.6 = (bf16[3,320,320]{2,1,0:T(8,128)(2,1)S(1)}, bf16[3,320,320]{2,1,0:T(8,128)(2,1)}, u32[]{:S(2)}) copy-start(bf16[3,320,320]{2,1,0:T(8,128)(2,1)} %w_ref.3) | copy-start | bytes 1843204
  115.3 23.4 %all-to-all-start.5 = ((bf16[16,64,640]{2,1,0:T(8,128)(2,1)}), bf16[16,64,640]{2,1,0:T(8,128)(2,1)S(1)}, u32[]{:S(2)}, u32[]{:S(2)}) async-start(bf16[16,64,640]{2,1,0:T(8,128)(2,1)} %broadcast_in_dim.5), calls=%async_computation.5 | async-start | bytes 2621440 | tf_op jit(solution)/shard_map/all_to_all | solution.py:644
  138.7 8.3 %collective-permute-start.7 = (bf16[1024,640]{1,0:T(8,128)(2,1)S(1)}, bf16[1024,640]{1,0:T(8,128)(2,1)S(1)}, u32[]{:S(2)}, u32[]{:S(2)}) collective-permute-start(bf16[1024,640]{1,0:T(8,128)(2,1)S(1)} %bitcast.12), channel_id=1, source_target_pairs={{0,16},{16,0},{1,17},{17,1},{2,18},{18,2},{3,19},{19,3},{4,20},{20... | collective-permute-start | bytes 3932168 | tf_op jit(solution)/shard_map/ppermute | solution.py:621

commit v10 on v9

--- a/solution.py
+++ b/solution.py
@@ -320,8 +320,8 @@
 
 
 def mixed_body(
-    h0_ref, h1_ref, before_ref, cot_ref, after_ref, stat_ref, sums_ref,
-    keep_ref, give_ref, turned,
+    h0_ref, h1_ref, before_ref, cot_ref, after_ref, stat_ref,
+    far_keep_ref, far_give_ref, turned, keep_ref, give_ref, sem,
 ):
     mean, scale, gain = stat_ref[0:1, :], stat_ref[1:2, :], stat_ref[2:3, :]
     for f, h_ref in enumerate((h0_ref, h1_ref)):
@@ -330,6 +330,7 @@
             turned[:, f * PIX + step * STEP : f * PIX + (step + 1) * STEP] = act.T
     core = lax.axis_index("c")
     first, second = turned[:, 0:PIX], turned[:, PIX:ROWS]
+    sends = []
     for k in range(3):
         if k == 1:
             part = jnp.dot(turned[...], cot_ref[...], preferred_element_type=F32)
@@ -341,15 +342,31 @@
         left, right = part[:, 0:HALF], part[:, HALF:C]
         keep_ref[k * C : (k + 1) * C, 0:HALF] = jnp.where(core == 0, left, right)
         give_ref[k * C : (k + 1) * C, 0:HALF] = jnp.where(core == 0, right, left)
-
-
-def temporal_gradient(h0, h1, before, cot, after, stat, sums):
+        here = slice(k * C, (k + 1) * C)
+        sends += [
+            pltpu.make_async_copy(give_ref.at[here, :], far_give_ref.at[here, :], sem.at[2 * k]),
+            pltpu.make_async_copy(keep_ref.at[here, :], far_keep_ref.at[here, :], sem.at[2 * k + 1]),
+        ]
+        for send in sends[-2:]:
+            send.start()
+    for send in sends:
+        send.wait()
+
+
+def temporal_gradient(h0, h1, before, cot, after, stat):
     return call(
         mixed_body,
-        (shape((3 * C, 256), F32), shape((3 * C, 256), F32)),
-        (pltpu.VMEM((C, ROWS), BF16),),
+        (far((3 * C, 256), F32), far((3 * C, 256), F32)),
+        (
+            pltpu.VMEM((C, ROWS), BF16),
+            pltpu.VMEM((3 * C, 256), F32),
+            pltpu.VMEM((3 * C, 256), F32),
+            pltpu.SemaphoreType.DMA((6,)),
+        ),
         flops=1_500_000_000,
-    )(h0, h1, before, cot, after, stat, sums)
+        ins=[VMEM] * 6,
+        outs=(FAR, FAR),
+    )(h0, h1, before, cot, after, stat)
 
 
 def temporal_body(
@@ -660,8 +677,9 @@
     part, clip_stat, sums, far_stat = slopes(sums, h0, h1, mixed_grad, cot, gain_two, count)
     sums = lax.all_to_all(sums, FRAME, 0, 0)
     temporal_keep, temporal_give = temporal_gradient(
-        h0, h1, cot_before, cot, cot_after, clip_stat, sums
+        h0, h1, cot_before, cot, cot_after, clip_stat
     )
+    sums, temporal_give = barrier((sums, temporal_give))
     temporal_got = swap_cores(temporal_give)
     low_keep, low_give, total = hidden_gradient(sums, clip_stat, part, h0, h1, count)
     low_got = swap_cores(low_give)

time: 151 us -> 152 us (level)
  blocking collectives: 31 us -> 19.1 us
  waiting for transfers between devices: 30.8 us -> 34.7 us
  starting transfers between devices: 45 us -> 48.2 us
  local copies, waits for them, and re-layouts: 3.43 us -> 6.6 us
  Pallas kernels: 37 us -> 40.1 us
    all_to_all x1 -> x0, blocking collectives: 11.9 us -> none  [on_device(): sums = lax.all_to_all(sums, FRAME, 0, 0)]
    all_to_all x1 -> x2, waiting for transfers between devices: 3.49 us -> 7.94 us  [on_device(): sums = lax.all_to_all(sums, FRAME, 0, 0)]
    all_to_all x1 -> x2, starting transfers between devices: 12.1 us -> 15.6 us  [on_device(): sums = lax.all_to_all(sums, FRAME, 0, 0)]
    unnamed x24 -> x26, local copies, waits for them, and re-layouts: 0.06 us -> 3.23 us
    pallas_call x1, Pallas kernels: 3.17 us -> 4.71 us  [weight_gradients(): call(weight_grad_body, far((1024, 4 * HALF), BF16), (pltpu.VMEM((2, ROWS,...]
  transfers between devices with their start and end apart: 11 -> 12, of which waited for: 6 -> 7; matrix products, arithmetic and copies ran while one was open for 1% -> 1% of each run, Pallas kernels for 21% -> 22%
where the time goes in v10:
time: 152 us; the launch traced here: 151 us
  starting transfers between devices  48.2 us (32%)
  Pallas kernels  40.1 us (26%)
  waiting for transfers between devices  34.7 us (23%)
  blocking collectives  19.1 us (13%)
  local copies, waits for them, and re-layouts  6.6 us (4%)
  other arithmetic  1.52 us (1%)
    all_to_all x2, starting transfers between devices, on_device(): sums = lax.all_to_all(sums, FRAME, 0, 0)  15.6 us
    ppermute x4, starting transfers between devices, swap_cores(): return lax.ppermute(value, 'c', [(0, 1), (1, 0)])  10.1 us
    all_to_all x1, waiting for transfers between devices, everyone_gets(): return lax.all_to_all(value, PLANE, 0, 0).reshape(1024, value.shape[2])  9.85 us
    pallas_call x1, Pallas kernels, input_gradient(): call(input_grad_body, shape((ROWS, C), BF16), (pltpu.VMEM((3 * PAD, 3 * C...  9.74 us
    all_to_all x1, blocking collectives, everyone_share(): value = jnp.sum(lax.all_to_all(value, LINE, 0, 0), axis=0).astype(BF16)  9.58 us
    all_to_all x1, blocking collectives, everyone_share(): lax.all_to_all(value, LINE, 0, 0).reshape(1024 // plane, width)  9.56 us
    all_to_all x1, waiting for transfers between devices, everyone_total(): return lax.all_to_all(value, PLANE, 0, 0)  9.21 us
    ppermute x2, starting transfers between devices, neighbours(): before = lax.ppermute(second, FRAME, [(i, i + 1) for i in range(size - 1)])  8.02 us
  transfers between devices with their start and end apart: 12, of which 7 were waited for; matrix products, arithmetic and copies ran while one was open for 1% of the time, Pallas kernels for 22%

profile of v10, /device:TPU:1, one launch (start us, length us, event | category | flops | bytes accessed | tf_op | source)
XLA Modules:
  0.0 151.3 jit_solution(4325556269146907248)
XLA Ops:
  0.6 0.0 copy-start.11
  0.6 0.0 copy-start.3
  0.7 2.1 %fusion = (bf16[1,1,16,32,320]{4,3,2,1,0:T(8,128)(2,1)}, bf16[1,1,16,32,320]{4,3,2,1,0:T(8,128)(2,1)}) fusion(bf16[1,2,16,32,320]{4,3,2,1,0:T(8,128)(2,1)} %param.7), kind=kLoop, calls=%fused_computation.1 | loop fusion | bytes 1310720 | tf_op jit(solution)/shard_map/slice | solution.py:671
  2.8 5.7 %collective-permute-start = (bf16[512,320]{1,0:T(8,128)(2,1)}, bf16[512,320]{1,0:T(8,128)(2,1)S(1)}, u32[]{:S(2)}, u32[]{:S(2)}) collective-permute-start(bf16[512,320]{1,0:T(8,128)(2,1)} %bitcast.2), channel_id=1, source_target_pairs={{0,1},{1,2},{2,3},{3,4},{4,5},{5,6},{6,7},{7,8},{8,9},{9,10},{10,1... | collective-permute-start | bytes 983048 | tf_op jit(solution)/shard_map/ppermute | solution.py:632
  8.5 1.3 collective-permute-start.1
  9.9 0.0 copy-start
  9.9 0.0 copy-start.5
  9.9 7.2 %shard_map.93 = (bf16[512,320]{1,0:T(8,128)(2,1)S(1)}, bf16[512,320]{1,0:T(8,128)(2,1)S(1)}, bf16[960,1024]{1,0:T(8,128)(2,1)}, f32[8,320]{1,0:T(8,128)}, f32[16,2,320]{2,1,0:T(2,128)}) custom-call(bf16[1024,320]{1,0:T(8,128)(2,1)S(1)} %bitcast.17, bf16[9,320,320]{2,1,0:T(8,128)(2,1)} %bitcast.22, f32[320]{0:T(512)S(1)} %copy-done.11), custom_call_target="tpu_custom_call" | custom-call | flops 2500000000 | bytes 8000000 | tf_op jit(solution)/shard_map/pallas_call | solution.py:209
  17.1 12.1 %all-to-all-start = ((f32[16,2,320]{2,1,0:T(2,128)}), f32[16,2,320]{2,1,0:T(2,128)S(1)}, u32[]{:S(2)}, u32[]{:S(2)}) async-start(f32[16,2,320]{2,1,0:T(2,128)} %get-tuple-element.39), calls=%async_computation | async-start | bytes 98304 | tf_op jit(solution)/shard_map/all_to_all | solution.py:673
  29.3 0.0 collective-permute-done.before_ref
  29.3 0.0 copy-start.7
  29.3 3.1 %collective-permute-done.1.after_ref = bf16[512,320]{1,0:T(8,128)(2,1)S(1)} collective-permute-done((bf16[512,320]{1,0:T(8,128)(2,1)}, bf16[512,320]{1,0:T(8,128)(2,1)S(1)}, u32[]{:S(2)}, u32[]{:S(2)}) %collective-permute-start.1) | collective-permute-done | bytes 327712 | tf_op jit(solution)/shard_map/ppermute | solution.py:633
  32.4 2.4 %shard_map.94.far_grad_ref = bf16[1024,320]{1,0:T(8,128)(2,1)} custom-call(bf16[512,320]{1,0:T(8,128)(2,1)S(1)} %collective-permute-done.before_ref, bf16[1024,320]{1,0:T(8,128)(2,1)S(1)} %bitcast.14, bf16[512,320]{1,0:T(8,128)(2,1)S(1)} %collective-permute-done.1.after_ref, bf16[3,320,320]{2,1,0:T(8,128)(2,1)S(1)} %copy-done.5), custom_call_target="tpu_custom_call" | custom-call | flops 1500000000 | bytes 8000000 | tf_op jit(solution)/shard_map/pallas_call | solution.py:264
  34.8 3.5 %all-to-all-done.sums_ref = f32[16,2,320]{2,1,0:T(2,128)S(1)} async-done(((f32[16,2,320]{2,1,0:T(2,128)}), f32[16,2,320]{2,1,0:T(2,128)S(1)}, u32[]{:S(2)}, u32[]{:S(2)}) %all-to-all-start) | async-done | bytes 40992 | tf_op jit(solution)/shard_map/all_to_all | solution.py:673
  38.3 2.6 %collective-permute-start.2 = (bf16[960,1024]{1,0:T(8,128)(2,1)}, bf16[960,1024]{1,0:T(8,128)(2,1)}, u32[]{:S(2)}, u32[]{:S(2)}) collective-permute-start(bf16[960,1024]{1,0:T(8,128)(2,1)} %get-tuple-element.41.mine_turned_ref), channel_id=1, source_target_pairs={{0,16},{16,0},{1,17},{17,1},{2,18},{18,2},{3,19},{19,3},{4,20},{20... | collective-permute-start | bytes 5898248 | tf_op jit(solution)/shard_map/ppermute | solution.py:638
  40.8 3.2 %shard_map.95 = (f32[1024,320]{1,0:T(8,128)S(1)}, f32[8,320]{1,0:T(8,128)S(1)}, f32[16,2,320]{2,1,0:T(2,128)}, f32[8,320]{1,0:T(8,128)}) custom-call(f32[16,2,320]{2,1,0:T(2,128)S(1)} %all-to-all-done.sums_ref, bf16[512,320]{1,0:T(8,128)(2,1)S(1)} %get-tuple-element.62.h0_ref, bf16[512,320]{1,0:T(8,128)(2,1)S(1)} %get-tuple-element.61.h1_ref, ...), custom_call_target="tpu_custom_call" | custom-call | bytes 8000000 | tf_op jit(solution)/shard_map/pallas_call | solution.py:308
  44.0 3.5 %all-to-all-start.1 = ((f32[16,2,320]{2,1,0:T(2,128)}), f32[16,2,320]{2,1,0:T(2,128)S(1)}, u32[]{:S(2)}, u32[]{:S(2)}) async-start(f32[16,2,320]{2,1,0:T(2,128)} %get-tuple-element.46), calls=%async_computation.1 | async-start | bytes 98304 | tf_op jit(solution)/shard_map/all_to_all | solution.py:678
  47.6 0.0 copy-start.8
  47.6 1.0 copy-done.8
  48.6 1.0 copy-done.10
  49.6 2.7 %shard_map.96 = (f32[960,256]{1,0:T(8,128)}, f32[960,256]{1,0:T(8,128)}) custom-call(bf16[512,320]{1,0:T(8,128)(2,1)S(1)} %get-tuple-element.62.h0_ref, bf16[512,320]{1,0:T(8,128)(2,1)S(1)} %get-tuple-element.61.h1_ref, bf16[512,320]{1,0:T(8,128)(2,1)S(1)} %copy-done.8, bf16[1024,320]{1,0:T(8,128)(2,1)S(1)} %bitcast.16, bf16[512,320]{1,0:T(8,128)(2,1)S(1)} %copy-done.10, ...), custom_call_target="tpu_custom_call" | custom-call | flops 1500000000 | bytes 8000000 | tf_op jit(solution)/shard_map/pallas_call | solution.py:357
  52.3 4.5 %all-to-all-done.1.sums_ref = f32[16,2,320]{2,1,0:T(2,128)S(1)} async-done(((f32[16,2,320]{2,1,0:T(2,128)}), f32[16,2,320]{2,1,0:T(2,128)S(1)}, u32[]{:S(2)}, u32[]{:S(2)}) %all-to-all-start.1) | async-done | bytes 40992 | tf_op jit(solution)/shard_map/all_to_all | solution.py:678
  56.8 1.0 collective-permute-start.4
  57.7 1.9 %shard_map.97 = (bf16[1024,160]{1,0:T(8,128)(2,1)S(1)}, bf16[1024,160]{1,0:T(8,128)(2,1)S(1)}, f32[8,320]{1,0:T(8,128)}) custom-call(f32[16,2,320]{2,1,0:T(2,128)S(1)} %all-to-all-done.1.sums_ref, f32[8,320]{1,0:T(8,128)S(1)} %get-tuple-element.47.stat_ref, f32[1024,320]{1,0:T(8,128)S(1)} %get-tuple-element.50.part_ref, ...), custom_call_target="tpu_custom_call" | custom-call | bytes 8000000 | tf_op jit(solution)/shard_map/pallas_call | solution.py:447
  59.6 0.3 collective-permute-start.3
  59.9 1.9 %collective-permute-done.3.other_ref = bf16[1024,160]{1,0:T(8,128)(2,1)S(1)} collective-permute-done((bf16[1024,160]{1,0:T(8,128)(2,1)S(1)}, bf16[1024,160]{1,0:T(8,128)(2,1)S(1)}, u32[]{:S(2)}, u32[]{:S(2)}) %collective-permute-start.3) | collective-permute-done | bytes 327712 | tf_op jit(solution)/shard_map/ppermute | solution.py:638
  61.8 0.0 collective-permute-done.4.got_ref
  61.8 0.0 collective-permute-done.2.other_turned_ref
  61.8 1.2 copy-done.12
  63.0 4.7 %shard_map.98 = bf16[1024,640]{1,0:T(8,128)(2,1)} custom-call(bf16[960,1024]{1,0:T(8,128)(2,1)S(1)} %copy-done.2, bf16[960,1024]{1,0:T(8,128)(2,1)} %collective-permute-done.2.other_turned_ref, bf16[1024,160]{1,0:T(8,128)(2,1)S(1)} %get-tuple-element.51.mine_ref, bf16[1024,160]{1,0:T(8,128)(2,1)S(1)} %collective-permute-done.3.other_ref, ...), custom_call_target="tpu_custom_call" | custom-call | flops 2500000000 | bytes 8000000 | tf_op jit(solution)/shard_map/pallas_call | solution.py:492
  67.8 0.0 copy-start.4
  67.8 4.8 %all-to-all-start.2 = ((bf16[16,64,640]{2,1,0:T(8,128)(2,1)}), bf16[16,64,640]{2,1,0:T(8,128)(2,1)}, u32[]{:S(2)}, u32[]{:S(2)}) async-start(bf16[16,64,640]{2,1,0:T(8,128)(2,1)} %bitcast.19), calls=%async_computation.2 | async-start | bytes 2621440 | tf_op jit(solution)/shard_map/all_to_all | solution.py:644
  72.5 2.3 %collective-permute-start.5 = (bf16[512,320]{1,0:T(8,128)(2,1)S(1)}, bf16[512,320]{1,0:T(8,128)(2,1)S(1)}, u32[]{:S(2)}, u32[]{:S(2)}) collective-permute-start(bf16[512,320]{1,0:T(8,128)(2,1)S(1)} %get-tuple-element.61.h1_ref), channel_id=1, source_target_pairs={{0,1},{1,2},{2,3},{3,4},{4,5},{5,6},{6,7},{7,8},{8,9},{9,10},{10,1... | collective-permute-start | bytes 983048 | tf_op jit(solution)/shard_map/ppermute | solution.py:632
  74.8 1.3 collective-permute-start.6
  76.1 9.7 %shard_map.99 = bf16[1024,320]{1,0:T(8,128)(2,1)} custom-call(f32[1024,320]{1,0:T(8,128)S(1)} %get-tuple-element.50.part_ref, bf16[512,320]{1,0:T(8,128)(2,1)S(1)} %get-tuple-element.62.h0_ref, bf16[512,320]{1,0:T(8,128)(2,1)S(1)} %get-tuple-element.61.h1_ref, f32[8,320]{1,0:T(8,128)} %get-tuple-element.57.far_clip_ref.far_stat_ref, ...), custom_call_target="tpu_custom_call" | custom-call | flops 2500000000 | bytes 8000000 | tf_op jit(solution)/shard_map/pallas_call | solution.py:576
  85.9 9.2 %all-to-all-done.2 = bf16[16,64,640]{2,1,0:T(8,128)(2,1)} async-done(((bf16[16,64,640]{2,1,0:T(8,128)(2,1)}), bf16[16,64,640]{2,1,0:T(8,128)(2,1)}, u32[]{:S(2)}, u32[]{:S(2)}) %all-to-all-start.2) | async-done | bytes 1310752 | tf_op jit(solution)/shard_map/all_to_all | solution.py:644
  95.1 1.5 convert_reduce_fusion
  96.6 9.6 %all_to_all.30 = f32[8,8,640]{2,1,0:T(8,128)S(1)} all-to-all(f32[8,8,640]{2,1,0:T(8,128)S(1)} %bitcast.20), channel_id=1, replica_groups=mesh['zl'=2,'x'=4,'c'=2,'y'=4,'zh'=4] {'zl','zh'}, dimensions={0} | all-to-all | bytes 327680 | tf_op jit(solution)/shard_map/all_to_all | solution.py:652
  106.2 0.0 collective-permute-done.5.hb_ref
  106.2 0.0 collective-permute-done.6.ha_ref
  106.2 9.6 %all_to_all.31 = bf16[8,8,640]{2,1,0:T(8,128)(2,1)S(1)} all-to-all(bf16[8,8,640]{2,1,0:T(8,128)(2,1)S(1)} %broadcast_in_dim.4), channel_id=1, replica_groups=mesh['zl'=2,'x'=4,'c'=2,'y'=4,'zh'=4] {'zl','zh'}, dimensions={0} | all-to-all | bytes 163840 | tf_op jit(solution)/shard_map/all_to_all | solution.py:655
  115.8 1.2 broadcast_in_dim.5
  117.0 7.1 %all-to-all-start.5 = ((bf16[16,64,640]{2,1,0:T(8,128)(2,1)}), bf16[16,64,640]{2,1,0:T(8,128)(2,1)S(1)}, u32[]{:S(2)}, u32[]{:S(2)}) async-start(bf16[16,64,640]{2,1,0:T(8,128)(2,1)} %broadcast_in_dim.5), calls=%async_computation.5 | async-start | bytes 2621440 | tf_op jit(solution)/shard_map/all_to_all | solution.py:661
  124.1 5.6 %shard_map.100 = bf16[1024,320]{1,0:T(8,128)(2,1)} custom-call(bf16[512,320]{1,0:T(8,128)(2,1)S(1)} %collective-permute-done.5.hb_ref, bf16[512,320]{1,0:T(8,128)(2,1)S(1)} %get-tuple-element.62.h0_ref, bf16[512,320]{1,0:T(8,128)(2,1)S(1)} %get-tuple-element.61.h1_ref, bf16[512,320]{1,0:T(8,128)(2,1)} %collective-permute-done.6.ha_ref, ...), custom_call_target="tpu_custom_call" | custom-call | flops 1500000000 | bytes 8000000 | tf_op jit(solution)/shard_map/pallas_call | solution.py:406
  129.7 9.8 %all-to-all-done.5 = bf16[16,64,640]{2,1,0:T(8,128)(2,1)S(1)} async-done(((bf16[16,64,640]{2,1,0:T(8,128)(2,1)}), bf16[16,64,640]{2,1,0:T(8,128)(2,1)S(1)}, u32[]{:S(2)}, u32[]{:S(2)}) %all-to-all-start.5) | async-done | bytes 1310752 | tf_op jit(solution)/shard_map/all_to_all | solution.py:661
  139.6 6.3 %collective-permute-start.7 = (bf16[1024,640]{1,0:T(8,128)(2,1)S(1)}, bf16[1024,640]{1,0:T(8,128)(2,1)S(1)}, u32[]{:S(2)}, u32[]{:S(2)}) collective-permute-start(bf16[1024,640]{1,0:T(8,128)(2,1)S(1)} %bitcast.12), channel_id=1, source_target_pairs={{0,16},{16,0},{1,17},{17,1},{2,18},{18,2},{3,19},{19,3},{4,20},{20... | collective-permute-start | bytes 3932168 | tf_op jit(solution)/shard_map/ppermute | solution.py:638
  145.9 2.7 %collective-permute-done.7.other_ref = bf16[1024,640]{1,0:T(8,128)(2,1)S(1)} collective-permute-done((bf16[1024,640]{1,0:T(8,128)(2,1)S(1)}, bf16[1024,640]{1,0:T(8,128)(2,1)S(1)}, u32[]{:S(2)}, u32[]{:S(2)}) %collective-permute-start.7) | collective-permute-done | bytes 1310752 | tf_op jit(solution)/shard_map/ppermute | solution.py:638
  148.5 2.6 %shard_map.101 = (bf16[9,320,320]{2,1,0:T(8,128)(2,1)}, bf16[3,320,320]{2,1,0:T(8,128)(2,1)}) custom-call(bf16[1024,640]{1,0:T(8,128)(2,1)S(1)} %bitcast.13, bf16[1024,640]{1,0:T(8,128)(2,1)S(1)} %collective-permute-done.7.other_ref), custom_call_target="tpu_custom_call" | custom-call | bytes 8000000 | tf_op jit(solution)/shard_map/pallas_call | solution.py:621
  (18 shorter events, 0.1 us)
Async XLA Ops:
  0.6 9.2 %copy-start.11 = (f32[320]{0:T(512)S(1)}, f32[320]{0:T(512)}, u32[]{:S(2)}) copy-start(f32[320]{0:T(512)} %gain_ref.2) | copy-start | bytes 3844
  0.6 9.2 %copy-start.3 = (bf16[1,2,16,32,320]{4,3,2,1,0:T(8,128)(2,1)S(1)}, bf16[1,2,16,32,320]{4,3,2,1,0:T(8,128)(2,1)}, u32[]{:S(2)}) copy-start(bf16[1,2,16,32,320]{4,3,2,1,0:T(8,128)(2,1)} %param.6) | copy-start | bytes 1966084
  2.8 26.5 %collective-permute-start = (bf16[512,320]{1,0:T(8,128)(2,1)}, bf16[512,320]{1,0:T(8,128)(2,1)S(1)}, u32[]{:S(2)}, u32[]{:S(2)}) collective-permute-start(bf16[512,320]{1,0:T(8,128)(2,1)} %bitcast.2), channel_id=1, source_target_pairs={{0,1},{1,2},{2,3},{3,4},{4,5},{5,6},{6,7},{7,8},{8,9},{9,10},{10,1... | collective-permute-start | bytes 983048 | tf_op jit(solution)/shard_map/ppermute | solution.py:632
  8.5 23.8 %collective-permute-start.1 = (bf16[512,320]{1,0:T(8,128)(2,1)}, bf16[512,320]{1,0:T(8,128)(2,1)S(1)}, u32[]{:S(2)}, u32[]{:S(2)}) collective-permute-start(bf16[512,320]{1,0:T(8,128)(2,1)} %bitcast.4), channel_id=1, source_target_pairs={{1,0},{2,1},{3,2},{4,3},{5,4},{6,5},{7,6},{8,7},{9,8},{10,9},{11,1... | collective-permute-start | bytes 983048 | tf_op jit(solution)/shard_map/ppermute | solution.py:633
  9.9 22.5 %copy-start = (bf16[1,2,16,32,320]{4,3,2,1,0:T(8,128)(2,1)S(1)}, bf16[1,2,16,32,320]{4,3,2,1,0:T(8,128)(2,1)}, u32[]{:S(2)}) copy-start(bf16[1,2,16,32,320]{4,3,2,1,0:T(8,128)(2,1)} %param.7) | copy-start | bytes 1966084
  9.9 22.5 %copy-start.5 = (bf16[3,320,320]{2,1,0:T(8,128)(2,1)S(1)}, bf16[3,320,320]{2,1,0:T(8,128)(2,1)}, u32[]{:S(2)}) copy-start(bf16[3,320,320]{2,1,0:T(8,128)(2,1)} %w_ref.3) | copy-start | bytes 1843204
  17.1 21.1 %all-to-all-start = ((f32[16,2,320]{2,1,0:T(2,128)}), f32[16,2,320]{2,1,0:T(2,128)S(1)}, u32[]{:S(2)}, u32[]{:S(2)}) async-start(f32[16,2,320]{2,1,0:T(2,128)} %get-tuple-element.39), calls=%async_computation | async-start | bytes 98304 | tf_op jit(solution)/shard_map/all_to_all | solution.py:673
  29.3 5.5 %copy-start.7 = (bf16[512,320]{1,0:T(8,128)(2,1)}, bf16[512,320]{1,0:T(8,128)(2,1)S(1)}, u32[]{:S(2)}) copy-start(bf16[512,320]{1,0:T(8,128)(2,1)S(1)} %collective-permute-done.before_ref) | copy-start | bytes 983044
  32.4 2.4 %copy-start.9 = (bf16[512,320]{1,0:T(8,128)(2,1)}, bf16[512,320]{1,0:T(8,128)(2,1)S(1)}, u32[]{:S(2)}) copy-start(bf16[512,320]{1,0:T(8,128)(2,1)S(1)} %collective-permute-done.1.after_ref) | copy-start | bytes 983044
  32.4 8.5 %copy-start.1 = (f32[320]{0:T(512)S(1)}, f32[320]{0:T(512)}, u32[]{:S(2)}) copy-start(f32[320]{0:T(512)} %gain_ref.3) | copy-start | bytes 3844
  38.3 23.6 %collective-permute-start.2 = (bf16[960,1024]{1,0:T(8,128)(2,1)}, bf16[960,1024]{1,0:T(8,128)(2,1)}, u32[]{:S(2)}, u32[]{:S(2)}) collective-permute-start(bf16[960,1024]{1,0:T(8,128)(2,1)} %get-tuple-element.41.mine_turned_ref), channel_id=1, source_target_pairs={{0,16},{16,0},{1,17},{17,1},{2,18},{18,2},{3,19},{19,3},{4,20},{20... | collective-permute-start | bytes 5898248 | tf_op jit(solution)/shard_map/ppermute | solution.py:638
  44.0 12.7 %all-to-all-start.1 = ((f32[16,2,320]{2,1,0:T(2,128)}), f32[16,2,320]{2,1,0:T(2,128)S(1)}, u32[]{:S(2)}, u32[]{:S(2)}) async-start(f32[16,2,320]{2,1,0:T(2,128)} %get-tuple-element.46), calls=%async_computation.1 | async-start | bytes 98304 | tf_op jit(solution)/shard_map/all_to_all | solution.py:678
  47.6 1.0 copy-start.8
  48.6 1.0 copy-start.10
  56.7 5.1 %copy-start.2 = (bf16[960,1024]{1,0:T(8,128)(2,1)S(1)}, bf16[960,1024]{1,0:T(8,128)(2,1)}, u32[]{:S(2)}) copy-start(bf16[960,1024]{1,0:T(8,128)(2,1)} %get-tuple-element.41.mine_turned_ref) | copy-start | bytes 5898244
  56.8 5.1 %collective-permute-start.4 = (f32[960,256]{1,0:T(8,128)}, f32[960,256]{1,0:T(8,128)S(1)}, u32[]{:S(2)}, u32[]{:S(2)}) collective-permute-start(f32[960,256]{1,0:T(8,128)} %get-tuple-element.54), channel_id=1, source_target_pairs={{0,16},{16,0},{1,17},{17,1},{2,18},{18,2},{3,19},{19,3},{4,20},{20... | collective-permute-start | bytes 2949128 | tf_op jit(solution)/shard_map/ppermute | solution.py:638
  59.6 2.2 %collective-permute-start.3 = (bf16[1024,160]{1,0:T(8,128)(2,1)S(1)}, bf16[1024,160]{1,0:T(8,128)(2,1)S(1)}, u32[]{:S(2)}, u32[]{:S(2)}) collective-permute-start(bf16[1024,160]{1,0:T(8,128)(2,1)S(1)} %get-tuple-element.52), channel_id=1, source_target_pairs={{0,16},{16,0},{1,17},{17,1},{2,18},{18,2},{3,19},{19,3},{4,20},{20... | collective-permute-start | bytes 983048 | tf_op jit(solution)/shard_map/ppermute | solution.py:638
  61.8 1.2 copy-start.12
  67.8 8.4 %copy-start.4 = (bf16[1,2,16,32,320]{4,3,2,1,0:T(8,128)(2,1)S(1)}, bf16[1,2,16,32,320]{4,3,2,1,0:T(8,128)(2,1)}, u32[]{:S(2)}) copy-start(bf16[1,2,16,32,320]{4,3,2,1,0:T(8,128)(2,1)} %param.6) | copy-start | bytes 1966084
  67.8 27.3 %all-to-all-start.2 = ((bf16[16,64,640]{2,1,0:T(8,128)(2,1)}), bf16[16,64,640]{2,1,0:T(8,128)(2,1)}, u32[]{:S(2)}, u32[]{:S(2)}) async-start(bf16[16,64,640]{2,1,0:T(8,128)(2,1)} %bitcast.19), calls=%async_computation.2 | async-start | bytes 2621440 | tf_op jit(solution)/shard_map/all_to_all | solution.py:644
  72.5 33.7 %collective-permute-start.5 = (bf16[512,320]{1,0:T(8,128)(2,1)S(1)}, bf16[512,320]{1,0:T(8,128)(2,1)S(1)}, u32[]{:S(2)}, u32[]{:S(2)}) collective-permute-start(bf16[512,320]{1,0:T(8,128)(2,1)S(1)} %get-tuple-element.61.h1_ref), channel_id=1, source_target_pairs={{0,1},{1,2},{2,3},{3,4},{4,5},{5,6},{6,7},{7,8},{8,9},{9,10},{10,1... | collective-permute-start | bytes 983048 | tf_op jit(solution)/shard_map/ppermute | solution.py:632
  74.8 31.4 %collective-permute-start.6 = (bf16[512,320]{1,0:T(8,128)(2,1)S(1)}, bf16[512,320]{1,0:T(8,128)(2,1)}, u32[]{:S(2)}, u32[]{:S(2)}) collective-permute-start(bf16[512,320]{1,0:T(8,128)(2,1)S(1)} %get-tuple-element.62.h0_ref), channel_id=1, source_target_pairs={{1,0},{2,1},{3,2},{4,3},{5,4},{6,5},{7,6},{8,7},{9,8},{10,9},{11,1... | collective-permute-start | bytes 983048 | tf_op jit(solution)/shard_map/ppermute | solution.py:633
  117.0 7.1 %copy-start.6 = (bf16[3,320,320]{2,1,0:T(8,128)(2,1)S(1)}, bf16[3,320,320]{2,1,0:T(8,128)(2,1)}, u32[]{:S(2)}) copy-start(bf16[3,320,320]{2,1,0:T(8,128)(2,1)} %w_ref.3) | copy-start | bytes 1843204
  117.0 22.6 %all-to-all-start.5 = ((bf16[16,64,640]{2,1,0:T(8,128)(2,1)}), bf16[16,64,640]{2,1,0:T(8,128)(2,1)S(1)}, u32[]{:S(2)}, u32[]{:S(2)}) async-start(bf16[16,64,640]{2,1,0:T(8,128)(2,1)} %broadcast_in_dim.5), calls=%async_computation.5 | async-start | bytes 2621440 | tf_op jit(solution)/shard_map/all_to_all | solution.py:661
  139.6 9.0 %collective-permute-start.7 = (bf16[1024,640]{1,0:T(8,128)(2,1)S(1)}, bf16[1024,640]{1,0:T(8,128)(2,1)S(1)}, u32[]{:S(2)}, u32[]{:S(2)}) collective-permute-start(bf16[1024,640]{1,0:T(8,128)(2,1)S(1)} %bitcast.12), channel_id=1, source_target_pairs={{0,16},{16,0},{1,17},{17,1},{2,18},{18,2},{3,19},{19,3},{4,20},{20... | collective-permute-start | bytes 3932168 | tf_op jit(solution)/shard_map/ppermute | solution.py:638

commit v11 on v10

--- a/solution.py
+++ b/solution.py
@@ -463,18 +463,33 @@
 
 
 def weight_grad_body(
-    mine_turned_ref, other_turned_ref, mine_ref, other_ref, keep_ref, got_ref, far_ref, rhs, out, sem
+    far_mine_ref, far_other_ref, mine_ref, other_ref, far_keep_ref, got_ref, far_ref,
+    rhs, out, turned, keep_ref, sem, fetch_sem, keep_sem,
 ):
+    fetches = []
+    for j in range(3):
+        here = slice(j * C, (j + 1) * C)
+        for n, ref in enumerate((far_mine_ref, far_other_ref)):
+            fetch = pltpu.make_async_copy(
+                ref.at[here, :], turned.at[n, here, :], fetch_sem.at[2 * j + n]
+            )
+            fetch.start()
+            fetches.append(fetch)
+    keep_fetch = pltpu.make_async_copy(far_keep_ref, keep_ref, keep_sem)
+    keep_fetch.start()
     for n, ref in enumerate((mine_ref, other_ref)):
         for f in range(2):
             where = slice(f * PIX, (f + 1) * PIX)
             for i, tap in enumerate(row_taps(ref[where, :])):
                 rhs[n, where, i * HALF : (i + 1) * HALF] = tap
+    keep_fetch.wait()
     sends = []
     for j in range(3):
         here = slice(j * C, (j + 1) * C)
-        total = jnp.dot(mine_turned_ref[here, :], rhs[0], preferred_element_type=F32)
-        total = total + jnp.dot(other_turned_ref[here, :], rhs[1], preferred_element_type=F32)
+        for fetch in fetches[2 * j : 2 * j + 2]:
+            fetch.wait()
+        total = jnp.dot(turned[0, here, :], rhs[0], preferred_element_type=F32)
+        total = total + jnp.dot(turned[1, here, :], rhs[1], preferred_element_type=F32)
         out[here, 0 : 3 * HALF] = total.astype(BF16)
         kept = keep_ref[here, 0:HALF] + got_ref[here, 0:HALF]
         out[here, 3 * HALF : 4 * HALF] = kept.astype(BF16)
@@ -495,12 +510,17 @@
         (
             pltpu.VMEM((2, ROWS, 3 * HALF), BF16),
             pltpu.VMEM((1024, 4 * HALF), BF16),
+            pltpu.VMEM((2, 3 * C, ROWS), BF16),
+            pltpu.VMEM((3 * C, 256), F32),
             pltpu.SemaphoreType.DMA((3,)),
+            pltpu.SemaphoreType.DMA((6,)),
+            pltpu.SemaphoreType.DMA,
         ),
         flops=2_500_000_000,
-        ins=[VMEM] * 6,
+        limit=16,
+        ins=[FAR] * 2 + [VMEM] * 2 + [FAR, VMEM],
         outs=FAR,
-    )(mine_turned, other_turned, mine, other, keep, got)
+    )(in_hbm(mine_turned), in_hbm(other_turned), mine, other, in_hbm(keep), got)
 
 
 def input_grad_body(

time: 152 us -> 152 us (level)
    unnamed x26 -> x22, local copies, waits for them, and re-layouts: 3.23 us -> 2.03 us
where the time goes in v11:
time: 152 us; the launch traced here: 151 us
  starting transfers between devices  48.2 us (32%)
  Pallas kernels  41 us (27%)
  waiting for transfers between devices  34.6 us (23%)
  blocking collectives  19.1 us (13%)
  local copies, waits for them, and re-layouts  5.4 us (4%)
  other arithmetic  1.52 us (1%)
    all_to_all x2, starting transfers between devices, on_device(): sums = lax.all_to_all(sums, FRAME, 0, 0)  15.6 us
    ppermute x4, starting transfers between devices, swap_cores(): return lax.ppermute(value, 'c', [(0, 1), (1, 0)])  10.1 us
    all_to_all x1, waiting for transfers between devices, everyone_gets(): return lax.all_to_all(value, PLANE, 0, 0).reshape(1024, value.shape[2])  9.85 us
    pallas_call x1, Pallas kernels, input_gradient(): call(input_grad_body, shape((ROWS, C), BF16), (pltpu.VMEM((3 * PAD, 3 * C...  9.74 us
    all_to_all x1, blocking collectives, everyone_share(): value = jnp.sum(lax.all_to_all(value, LINE, 0, 0), axis=0).astype(BF16)  9.58 us
    all_to_all x1, blocking collectives, everyone_share(): lax.all_to_all(value, LINE, 0, 0).reshape(1024 // plane, width)  9.56 us
    all_to_all x1, waiting for transfers between devices, everyone_total(): return lax.all_to_all(value, PLANE, 0, 0)  9.21 us
    ppermute x2, starting transfers between devices, neighbours(): before = lax.ppermute(second, FRAME, [(i, i + 1) for i in range(size - 1)])  8.02 us
  transfers between devices with their start and end apart: 12, of which 7 were waited for; matrix products, arithmetic and copies ran while one was open for 1% of the time, Pallas kernels for 22%

profile of v11, /device:TPU:1, one launch (start us, length us, event | category | flops | bytes accessed | tf_op | source)
XLA Modules:
  0.0 151.0 jit_solution(1368698883011412532)
XLA Ops:
  0.6 0.0 copy-start.10
  0.6 0.0 copy-start.2
  0.7 2.1 %fusion = (bf16[1,1,16,32,320]{4,3,2,1,0:T(8,128)(2,1)}, bf16[1,1,16,32,320]{4,3,2,1,0:T(8,128)(2,1)}) fusion(bf16[1,2,16,32,320]{4,3,2,1,0:T(8,128)(2,1)} %param.7), kind=kLoop, calls=%fused_computation.1 | loop fusion | bytes 1310720 | tf_op jit(solution)/shard_map/slice | solution.py:691
  2.8 5.7 %collective-permute-start = (bf16[512,320]{1,0:T(8,128)(2,1)}, bf16[512,320]{1,0:T(8,128)(2,1)S(1)}, u32[]{:S(2)}, u32[]{:S(2)}) collective-permute-start(bf16[512,320]{1,0:T(8,128)(2,1)} %bitcast.2), channel_id=1, source_target_pairs={{0,1},{1,2},{2,3},{3,4},{4,5},{5,6},{6,7},{7,8},{8,9},{9,10},{10,1... | collective-permute-start | bytes 983048 | tf_op jit(solution)/shard_map/ppermute | solution.py:652
  8.5 1.3 collective-permute-start.1
  9.9 0.0 copy-start
  9.9 0.0 copy-start.4
  9.9 7.2 %shard_map.93 = (bf16[512,320]{1,0:T(8,128)(2,1)S(1)}, bf16[512,320]{1,0:T(8,128)(2,1)S(1)}, bf16[960,1024]{1,0:T(8,128)(2,1)}, f32[8,320]{1,0:T(8,128)}, f32[16,2,320]{2,1,0:T(2,128)}) custom-call(bf16[1024,320]{1,0:T(8,128)(2,1)S(1)} %bitcast.17, bf16[9,320,320]{2,1,0:T(8,128)(2,1)} %bitcast.22, f32[320]{0:T(512)S(1)} %copy-done.10), custom_call_target="tpu_custom_call" | custom-call | flops 2500000000 | bytes 8000000 | tf_op jit(solution)/shard_map/pallas_call | solution.py:209
  17.1 12.1 %all-to-all-start = ((f32[16,2,320]{2,1,0:T(2,128)}), f32[16,2,320]{2,1,0:T(2,128)S(1)}, u32[]{:S(2)}, u32[]{:S(2)}) async-start(f32[16,2,320]{2,1,0:T(2,128)} %get-tuple-element.39), calls=%async_computation | async-start | bytes 98304 | tf_op jit(solution)/shard_map/all_to_all | solution.py:693
  29.3 0.0 collective-permute-done.before_ref
  29.3 0.0 copy-start.6
  29.3 3.1 %collective-permute-done.1.after_ref = bf16[512,320]{1,0:T(8,128)(2,1)S(1)} collective-permute-done((bf16[512,320]{1,0:T(8,128)(2,1)}, bf16[512,320]{1,0:T(8,128)(2,1)S(1)}, u32[]{:S(2)}, u32[]{:S(2)}) %collective-permute-start.1) | collective-permute-done | bytes 327712 | tf_op jit(solution)/shard_map/ppermute | solution.py:653
  32.4 0.0 copy-done.4
  32.4 2.4 %shard_map.94.far_grad_ref = bf16[1024,320]{1,0:T(8,128)(2,1)} custom-call(bf16[512,320]{1,0:T(8,128)(2,1)S(1)} %collective-permute-done.before_ref, bf16[1024,320]{1,0:T(8,128)(2,1)S(1)} %bitcast.14, bf16[512,320]{1,0:T(8,128)(2,1)S(1)} %collective-permute-done.1.after_ref, bf16[3,320,320]{2,1,0:T(8,128)(2,1)S(1)} %copy-done.4), custom_call_target="tpu_custom_call" | custom-call | flops 1500000000 | bytes 8000000 | tf_op jit(solution)/shard_map/pallas_call | solution.py:264
  34.8 3.5 %all-to-all-done.sums_ref = f32[16,2,320]{2,1,0:T(2,128)S(1)} async-done(((f32[16,2,320]{2,1,0:T(2,128)}), f32[16,2,320]{2,1,0:T(2,128)S(1)}, u32[]{:S(2)}, u32[]{:S(2)}) %all-to-all-start) | async-done | bytes 40992 | tf_op jit(solution)/shard_map/all_to_all | solution.py:693
  38.3 2.6 %collective-permute-start.2 = (bf16[960,1024]{1,0:T(8,128)(2,1)}, bf16[960,1024]{1,0:T(8,128)(2,1)}, u32[]{:S(2)}, u32[]{:S(2)}) collective-permute-start(bf16[960,1024]{1,0:T(8,128)(2,1)} %get-tuple-element.41.far_mine_ref), channel_id=1, source_target_pairs={{0,16},{16,0},{1,17},{17,1},{2,18},{18,2},{3,19},{19,3},{4,20},{20... | collective-permute-start | bytes 5898248 | tf_op jit(solution)/shard_map/ppermute | solution.py:658
  40.8 3.2 %shard_map.95 = (f32[1024,320]{1,0:T(8,128)S(1)}, f32[8,320]{1,0:T(8,128)S(1)}, f32[16,2,320]{2,1,0:T(2,128)}, f32[8,320]{1,0:T(8,128)}) custom-call(f32[16,2,320]{2,1,0:T(2,128)S(1)} %all-to-all-done.sums_ref, bf16[512,320]{1,0:T(8,128)(2,1)S(1)} %get-tuple-element.62.h0_ref, bf16[512,320]{1,0:T(8,128)(2,1)S(1)} %get-tuple-element.61.h1_ref, ...), custom_call_target="tpu_custom_call" | custom-call | bytes 8000000 | tf_op jit(solution)/shard_map/pallas_call | solution.py:308
  44.0 3.5 %all-to-all-start.1 = ((f32[16,2,320]{2,1,0:T(2,128)}), f32[16,2,320]{2,1,0:T(2,128)S(1)}, u32[]{:S(2)}, u32[]{:S(2)}) async-start(f32[16,2,320]{2,1,0:T(2,128)} %get-tuple-element.46), calls=%async_computation.1 | async-start | bytes 98304 | tf_op jit(solution)/shard_map/all_to_all | solution.py:698
  47.6 0.0 copy-start.7
  47.6 1.0 copy-done.7
  48.6 1.0 copy-done.9
  49.5 2.8 %shard_map.96 = (f32[960,256]{1,0:T(8,128)}, f32[960,256]{1,0:T(8,128)}) custom-call(bf16[512,320]{1,0:T(8,128)(2,1)S(1)} %get-tuple-element.62.h0_ref, bf16[512,320]{1,0:T(8,128)(2,1)S(1)} %get-tuple-element.61.h1_ref, bf16[512,320]{1,0:T(8,128)(2,1)S(1)} %copy-done.7, bf16[1024,320]{1,0:T(8,128)(2,1)S(1)} %bitcast.16, bf16[512,320]{1,0:T(8,128)(2,1)S(1)} %copy-done.9, ...), custom_call_target="tpu_custom_call" | custom-call | flops 1500000000 | bytes 8000000 | tf_op jit(solution)/shard_map/pallas_call | solution.py:357
  52.3 4.4 %all-to-all-done.1.sums_ref = f32[16,2,320]{2,1,0:T(2,128)S(1)} async-done(((f32[16,2,320]{2,1,0:T(2,128)}), f32[16,2,320]{2,1,0:T(2,128)S(1)}, u32[]{:S(2)}, u32[]{:S(2)}) %all-to-all-start.1) | async-done | bytes 40992 | tf_op jit(solution)/shard_map/all_to_all | solution.py:698
  56.7 1.0 collective-permute-start.4
  57.7 1.9 %shard_map.97 = (bf16[1024,160]{1,0:T(8,128)(2,1)S(1)}, bf16[1024,160]{1,0:T(8,128)(2,1)S(1)}, f32[8,320]{1,0:T(8,128)}) custom-call(f32[16,2,320]{2,1,0:T(2,128)S(1)} %all-to-all-done.1.sums_ref, f32[8,320]{1,0:T(8,128)S(1)} %get-tuple-element.47.stat_ref, f32[1024,320]{1,0:T(8,128)S(1)} %get-tuple-element.50.part_ref, ...), custom_call_target="tpu_custom_call" | custom-call | bytes 8000000 | tf_op jit(solution)/shard_map/pallas_call | solution.py:447
  59.6 0.3 collective-permute-start.3
  59.9 1.9 %collective-permute-done.3.other_ref = bf16[1024,160]{1,0:T(8,128)(2,1)S(1)} collective-permute-done((bf16[1024,160]{1,0:T(8,128)(2,1)S(1)}, bf16[1024,160]{1,0:T(8,128)(2,1)S(1)}, u32[]{:S(2)}, u32[]{:S(2)}) %collective-permute-start.3) | collective-permute-done | bytes 327712 | tf_op jit(solution)/shard_map/ppermute | solution.py:658
  61.8 0.0 collective-permute-done.4.got_ref
  61.8 0.0 collective-permute-done.2.far_other_ref
  61.8 5.7 %shard_map.98 = bf16[1024,640]{1,0:T(8,128)(2,1)} custom-call(bf16[960,1024]{1,0:T(8,128)(2,1)} %get-tuple-element.41.far_mine_ref, bf16[960,1024]{1,0:T(8,128)(2,1)} %collective-permute-done.2.far_other_ref, bf16[1024,160]{1,0:T(8,128)(2,1)S(1)} %get-tuple-element.51.mine_ref, bf16[1024,160]{1,0:T(8,128)(2,1)S(1)} %collective-permute-done.3.other_ref, ...), custom_call_target="tpu_custom_call" | custom-call | flops 2500000000 | bytes 8000000 | tf_op jit(solution)/shard_map/pallas_call | solution.py:507
  67.5 0.0 copy-start.3
  67.5 4.8 %all-to-all-start.2 = ((bf16[16,64,640]{2,1,0:T(8,128)(2,1)}), bf16[16,64,640]{2,1,0:T(8,128)(2,1)}, u32[]{:S(2)}, u32[]{:S(2)}) async-start(bf16[16,64,640]{2,1,0:T(8,128)(2,1)} %bitcast.19), calls=%async_computation.2 | async-start | bytes 2621440 | tf_op jit(solution)/shard_map/all_to_all | solution.py:664
  72.3 2.3 %collective-permute-start.5 = (bf16[512,320]{1,0:T(8,128)(2,1)S(1)}, bf16[512,320]{1,0:T(8,128)(2,1)S(1)}, u32[]{:S(2)}, u32[]{:S(2)}) collective-permute-start(bf16[512,320]{1,0:T(8,128)(2,1)S(1)} %get-tuple-element.61.h1_ref), channel_id=1, source_target_pairs={{0,1},{1,2},{2,3},{3,4},{4,5},{5,6},{6,7},{7,8},{8,9},{9,10},{10,1... | collective-permute-start | bytes 983048 | tf_op jit(solution)/shard_map/ppermute | solution.py:652
  74.6 1.3 collective-permute-start.6
  75.9 9.7 %shard_map.99 = bf16[1024,320]{1,0:T(8,128)(2,1)} custom-call(f32[1024,320]{1,0:T(8,128)S(1)} %get-tuple-element.50.part_ref, bf16[512,320]{1,0:T(8,128)(2,1)S(1)} %get-tuple-element.62.h0_ref, bf16[512,320]{1,0:T(8,128)(2,1)S(1)} %get-tuple-element.61.h1_ref, f32[8,320]{1,0:T(8,128)} %get-tuple-element.57.far_clip_ref.far_stat_ref, ...), custom_call_target="tpu_custom_call" | custom-call | flops 2500000000 | bytes 8000000 | tf_op jit(solution)/shard_map/pallas_call | solution.py:596
  85.6 9.2 %all-to-all-done.2 = bf16[16,64,640]{2,1,0:T(8,128)(2,1)} async-done(((bf16[16,64,640]{2,1,0:T(8,128)(2,1)}), bf16[16,64,640]{2,1,0:T(8,128)(2,1)}, u32[]{:S(2)}, u32[]{:S(2)}) %all-to-all-start.2) | async-done | bytes 1310752 | tf_op jit(solution)/shard_map/all_to_all | solution.py:664
  94.8 1.5 convert_reduce_fusion
  96.3 9.6 %all_to_all.30 = f32[8,8,640]{2,1,0:T(8,128)S(1)} all-to-all(f32[8,8,640]{2,1,0:T(8,128)S(1)} %bitcast.20), channel_id=1, replica_groups=mesh['zl'=2,'x'=4,'c'=2,'y'=4,'zh'=4] {'zl','zh'}, dimensions={0} | all-to-all | bytes 327680 | tf_op jit(solution)/shard_map/all_to_all | solution.py:672
  105.9 0.0 collective-permute-done.5.hb_ref
  105.9 0.0 collective-permute-done.6.ha_ref
  106.0 9.6 %all_to_all.31 = bf16[8,8,640]{2,1,0:T(8,128)(2,1)S(1)} all-to-all(bf16[8,8,640]{2,1,0:T(8,128)(2,1)S(1)} %broadcast_in_dim.4), channel_id=1, replica_groups=mesh['zl'=2,'x'=4,'c'=2,'y'=4,'zh'=4] {'zl','zh'}, dimensions={0} | all-to-all | bytes 163840 | tf_op jit(solution)/shard_map/all_to_all | solution.py:675
  115.5 1.2 broadcast_in_dim.5
  116.7 7.1 %all-to-all-start.5 = ((bf16[16,64,640]{2,1,0:T(8,128)(2,1)}), bf16[16,64,640]{2,1,0:T(8,128)(2,1)S(1)}, u32[]{:S(2)}, u32[]{:S(2)}) async-start(bf16[16,64,640]{2,1,0:T(8,128)(2,1)} %broadcast_in_dim.5), calls=%async_computation.5 | async-start | bytes 2621440 | tf_op jit(solution)/shard_map/all_to_all | solution.py:681
  123.9 5.6 %shard_map.100 = bf16[1024,320]{1,0:T(8,128)(2,1)} custom-call(bf16[512,320]{1,0:T(8,128)(2,1)S(1)} %collective-permute-done.5.hb_ref, bf16[512,320]{1,0:T(8,128)(2,1)S(1)} %get-tuple-element.62.h0_ref, bf16[512,320]{1,0:T(8,128)(2,1)S(1)} %get-tuple-element.61.h1_ref, bf16[512,320]{1,0:T(8,128)(2,1)} %collective-permute-done.6.ha_ref, ...), custom_call_target="tpu_custom_call" | custom-call | flops 1500000000 | bytes 8000000 | tf_op jit(solution)/shard_map/pallas_call | solution.py:406
  129.5 9.8 %all-to-all-done.5 = bf16[16,64,640]{2,1,0:T(8,128)(2,1)S(1)} async-done(((bf16[16,64,640]{2,1,0:T(8,128)(2,1)}), bf16[16,64,640]{2,1,0:T(8,128)(2,1)S(1)}, u32[]{:S(2)}, u32[]{:S(2)}) %all-to-all-start.5) | async-done | bytes 1310752 | tf_op jit(solution)/shard_map/all_to_all | solution.py:681
  139.3 6.3 %collective-permute-start.7 = (bf16[1024,640]{1,0:T(8,128)(2,1)S(1)}, bf16[1024,640]{1,0:T(8,128)(2,1)S(1)}, u32[]{:S(2)}, u32[]{:S(2)}) collective-permute-start(bf16[1024,640]{1,0:T(8,128)(2,1)S(1)} %bitcast.12), channel_id=1, source_target_pairs={{0,16},{16,0},{1,17},{17,1},{2,18},{18,2},{3,19},{19,3},{4,20},{20... | collective-permute-start | bytes 3932168 | tf_op jit(solution)/shard_map/ppermute | solution.py:658
  145.6 2.7 %collective-permute-done.7.other_ref = bf16[1024,640]{1,0:T(8,128)(2,1)S(1)} collective-permute-done((bf16[1024,640]{1,0:T(8,128)(2,1)S(1)}, bf16[1024,640]{1,0:T(8,128)(2,1)S(1)}, u32[]{:S(2)}, u32[]{:S(2)}) %collective-permute-start.7) | collective-permute-done | bytes 1310752 | tf_op jit(solution)/shard_map/ppermute | solution.py:658
  148.3 2.6 %shard_map.101 = (bf16[9,320,320]{2,1,0:T(8,128)(2,1)}, bf16[3,320,320]{2,1,0:T(8,128)(2,1)}) custom-call(bf16[1024,640]{1,0:T(8,128)(2,1)S(1)} %bitcast.13, bf16[1024,640]{1,0:T(8,128)(2,1)S(1)} %collective-permute-done.7.other_ref), custom_call_target="tpu_custom_call" | custom-call | bytes 8000000 | tf_op jit(solution)/shard_map/pallas_call | solution.py:641
  (14 shorter events, 0.0 us)
Async XLA Ops:
  0.6 9.2 %copy-start.10 = (f32[320]{0:T(512)S(1)}, f32[320]{0:T(512)}, u32[]{:S(2)}) copy-start(f32[320]{0:T(512)} %gain_ref.2) | copy-start | bytes 3844
  0.6 9.2 %copy-start.2 = (bf16[1,2,16,32,320]{4,3,2,1,0:T(8,128)(2,1)S(1)}, bf16[1,2,16,32,320]{4,3,2,1,0:T(8,128)(2,1)}, u32[]{:S(2)}) copy-start(bf16[1,2,16,32,320]{4,3,2,1,0:T(8,128)(2,1)} %param.6) | copy-start | bytes 1966084
  2.8 26.5 %collective-permute-start = (bf16[512,320]{1,0:T(8,128)(2,1)}, bf16[512,320]{1,0:T(8,128)(2,1)S(1)}, u32[]{:S(2)}, u32[]{:S(2)}) collective-permute-start(bf16[512,320]{1,0:T(8,128)(2,1)} %bitcast.2), channel_id=1, source_target_pairs={{0,1},{1,2},{2,3},{3,4},{4,5},{5,6},{6,7},{7,8},{8,9},{9,10},{10,1... | collective-permute-start | bytes 983048 | tf_op jit(solution)/shard_map/ppermute | solution.py:652
  8.5 23.8 %collective-permute-start.1 = (bf16[512,320]{1,0:T(8,128)(2,1)}, bf16[512,320]{1,0:T(8,128)(2,1)S(1)}, u32[]{:S(2)}, u32[]{:S(2)}) collective-permute-start(bf16[512,320]{1,0:T(8,128)(2,1)} %bitcast.4), channel_id=1, source_target_pairs={{1,0},{2,1},{3,2},{4,3},{5,4},{6,5},{7,6},{8,7},{9,8},{10,9},{11,1... | collective-permute-start | bytes 983048 | tf_op jit(solution)/shard_map/ppermute | solution.py:653
  9.9 22.5 %copy-start = (bf16[1,2,16,32,320]{4,3,2,1,0:T(8,128)(2,1)S(1)}, bf16[1,2,16,32,320]{4,3,2,1,0:T(8,128)(2,1)}, u32[]{:S(2)}) copy-start(bf16[1,2,16,32,320]{4,3,2,1,0:T(8,128)(2,1)} %param.7) | copy-start | bytes 1966084
  9.9 22.5 %copy-start.4 = (bf16[3,320,320]{2,1,0:T(8,128)(2,1)S(1)}, bf16[3,320,320]{2,1,0:T(8,128)(2,1)}, u32[]{:S(2)}) copy-start(bf16[3,320,320]{2,1,0:T(8,128)(2,1)} %w_ref.3) | copy-start | bytes 1843204
  17.1 21.1 %all-to-all-start = ((f32[16,2,320]{2,1,0:T(2,128)}), f32[16,2,320]{2,1,0:T(2,128)S(1)}, u32[]{:S(2)}, u32[]{:S(2)}) async-start(f32[16,2,320]{2,1,0:T(2,128)} %get-tuple-element.39), calls=%async_computation | async-start | bytes 98304 | tf_op jit(solution)/shard_map/all_to_all | solution.py:693
  29.3 5.5 %copy-start.6 = (bf16[512,320]{1,0:T(8,128)(2,1)}, bf16[512,320]{1,0:T(8,128)(2,1)S(1)}, u32[]{:S(2)}) copy-start(bf16[512,320]{1,0:T(8,128)(2,1)S(1)} %collective-permute-done.before_ref) | copy-start | bytes 983044
  32.4 2.4 %copy-start.8 = (bf16[512,320]{1,0:T(8,128)(2,1)}, bf16[512,320]{1,0:T(8,128)(2,1)S(1)}, u32[]{:S(2)}) copy-start(bf16[512,320]{1,0:T(8,128)(2,1)S(1)} %collective-permute-done.1.after_ref) | copy-start | bytes 983044
  32.4 8.5 %copy-start.1 = (f32[320]{0:T(512)S(1)}, f32[320]{0:T(512)}, u32[]{:S(2)}) copy-start(f32[320]{0:T(512)} %gain_ref.3) | copy-start | bytes 3844
  38.3 23.6 %collective-permute-start.2 = (bf16[960,1024]{1,0:T(8,128)(2,1)}, bf16[960,1024]{1,0:T(8,128)(2,1)}, u32[]{:S(2)}, u32[]{:S(2)}) collective-permute-start(bf16[960,1024]{1,0:T(8,128)(2,1)} %get-tuple-element.41.far_mine_ref), channel_id=1, source_target_pairs={{0,16},{16,0},{1,17},{17,1},{2,18},{18,2},{3,19},{19,3},{4,20},{20... | collective-permute-start | bytes 5898248 | tf_op jit(solution)/shard_map/ppermute | solution.py:658
  44.0 12.7 %all-to-all-start.1 = ((f32[16,2,320]{2,1,0:T(2,128)}), f32[16,2,320]{2,1,0:T(2,128)S(1)}, u32[]{:S(2)}, u32[]{:S(2)}) async-start(f32[16,2,320]{2,1,0:T(2,128)} %get-tuple-element.46), calls=%async_computation.1 | async-start | bytes 98304 | tf_op jit(solution)/shard_map/all_to_all | solution.py:698
  47.6 1.0 copy-start.7
  48.6 1.0 copy-start.9
  56.7 5.1 %collective-permute-start.4 = (f32[960,256]{1,0:T(8,128)}, f32[960,256]{1,0:T(8,128)S(1)}, u32[]{:S(2)}, u32[]{:S(2)}) collective-permute-start(f32[960,256]{1,0:T(8,128)} %get-tuple-element.54), channel_id=1, source_target_pairs={{0,16},{16,0},{1,17},{17,1},{2,18},{18,2},{3,19},{19,3},{4,20},{20... | collective-permute-start | bytes 2949128 | tf_op jit(solution)/shard_map/ppermute | solution.py:658
  59.6 2.2 %collective-permute-start.3 = (bf16[1024,160]{1,0:T(8,128)(2,1)S(1)}, bf16[1024,160]{1,0:T(8,128)(2,1)S(1)}, u32[]{:S(2)}, u32[]{:S(2)}) collective-permute-start(bf16[1024,160]{1,0:T(8,128)(2,1)S(1)} %get-tuple-element.52), channel_id=1, source_target_pairs={{0,16},{16,0},{1,17},{17,1},{2,18},{18,2},{3,19},{19,3},{4,20},{20... | collective-permute-start | bytes 983048 | tf_op jit(solution)/shard_map/ppermute | solution.py:658
  67.5 8.4 %copy-start.3 = (bf16[1,2,16,32,320]{4,3,2,1,0:T(8,128)(2,1)S(1)}, bf16[1,2,16,32,320]{4,3,2,1,0:T(8,128)(2,1)}, u32[]{:S(2)}) copy-start(bf16[1,2,16,32,320]{4,3,2,1,0:T(8,128)(2,1)} %param.6) | copy-start | bytes 1966084
  67.5 27.3 %all-to-all-start.2 = ((bf16[16,64,640]{2,1,0:T(8,128)(2,1)}), bf16[16,64,640]{2,1,0:T(8,128)(2,1)}, u32[]{:S(2)}, u32[]{:S(2)}) async-start(bf16[16,64,640]{2,1,0:T(8,128)(2,1)} %bitcast.19), calls=%async_computation.2 | async-start | bytes 2621440 | tf_op jit(solution)/shard_map/all_to_all | solution.py:664
  72.3 33.7 %collective-permute-start.5 = (bf16[512,320]{1,0:T(8,128)(2,1)S(1)}, bf16[512,320]{1,0:T(8,128)(2,1)S(1)}, u32[]{:S(2)}, u32[]{:S(2)}) collective-permute-start(bf16[512,320]{1,0:T(8,128)(2,1)S(1)} %get-tuple-element.61.h1_ref), channel_id=1, source_target_pairs={{0,1},{1,2},{2,3},{3,4},{4,5},{5,6},{6,7},{7,8},{8,9},{9,10},{10,1... | collective-permute-start | bytes 983048 | tf_op jit(solution)/shard_map/ppermute | solution.py:652
  74.6 31.4 %collective-permute-start.6 = (bf16[512,320]{1,0:T(8,128)(2,1)S(1)}, bf16[512,320]{1,0:T(8,128)(2,1)}, u32[]{:S(2)}, u32[]{:S(2)}) collective-permute-start(bf16[512,320]{1,0:T(8,128)(2,1)S(1)} %get-tuple-element.62.h0_ref), channel_id=1, source_target_pairs={{1,0},{2,1},{3,2},{4,3},{5,4},{6,5},{7,6},{8,7},{9,8},{10,9},{11,1... | collective-permute-start | bytes 983048 | tf_op jit(solution)/shard_map/ppermute | solution.py:653
  116.7 7.1 %copy-start.5 = (bf16[3,320,320]{2,1,0:T(8,128)(2,1)S(1)}, bf16[3,320,320]{2,1,0:T(8,128)(2,1)}, u32[]{:S(2)}) copy-start(bf16[3,320,320]{2,1,0:T(8,128)(2,1)} %w_ref.3) | copy-start | bytes 1843204
  116.7 22.6 %all-to-all-start.5 = ((bf16[16,64,640]{2,1,0:T(8,128)(2,1)}), bf16[16,64,640]{2,1,0:T(8,128)(2,1)S(1)}, u32[]{:S(2)}, u32[]{:S(2)}) async-start(bf16[16,64,640]{2,1,0:T(8,128)(2,1)} %broadcast_in_dim.5), calls=%async_computation.5 | async-start | bytes 2621440 | tf_op jit(solution)/shard_map/all_to_all | solution.py:681
  139.3 9.0 %collective-permute-start.7 = (bf16[1024,640]{1,0:T(8,128)(2,1)S(1)}, bf16[1024,640]{1,0:T(8,128)(2,1)S(1)}, u32[]{:S(2)}, u32[]{:S(2)}) collective-permute-start(bf16[1024,640]{1,0:T(8,128)(2,1)S(1)} %bitcast.12), channel_id=1, source_target_pairs={{0,16},{16,0},{1,17},{17,1},{2,18},{18,2},{3,19},{19,3},{4,20},{20... | collective-permute-start | bytes 3932168 | tf_op jit(solution)/shard_map/ppermute | solution.py:658

commit v12 on v9

--- a/solution.py
+++ b/solution.py
@@ -243,7 +243,17 @@
     return grouped[0:1], grouped[1:2]
 
 
-def mixed_grad_body(before_ref, cot_ref, after_ref, w_ref, far_ref, out_ref, sem):
+def mixed_grad_body(
+    far_before_ref, cot_ref, far_after_ref, w_ref, far_ref, out_ref, sem, before_ref, after_ref, halo_sem
+):
+    fetches = [
+        pltpu.make_async_copy(far_before_ref, before_ref, halo_sem.at[0]),
+        pltpu.make_async_copy(far_after_ref, after_ref, halo_sem.at[1]),
+    ]
+    for fetch in fetches:
+        fetch.start()
+    for fetch in fetches:
+        fetch.wait()
     sends = []
     for f in range(2):
         here = slice(f * PIX, (f + 1) * PIX)
@@ -264,11 +274,11 @@
     return call(
         mixed_grad_body,
         far((ROWS, C), BF16),
-        (pltpu.VMEM((ROWS, C), BF16), pltpu.SemaphoreType.DMA((2,))),
+        (pltpu.VMEM((ROWS, C), BF16), pltpu.SemaphoreType.DMA((2,)), pltpu.VMEM((PIX, C), BF16), pltpu.VMEM((PIX, C), BF16), pltpu.SemaphoreType.DMA((2,))),
         flops=1_500_000_000,
-        ins=[VMEM] * 4,
+        ins=[FAR, VMEM, FAR, VMEM],
         outs=FAR,
-    )(before, cot, after, weight)
+    )(in_hbm(before), cot, in_hbm(after), weight)
 
 
 def slope_body(
@@ -320,15 +330,23 @@
 
 
 def mixed_body(
-    h0_ref, h1_ref, before_ref, cot_ref, after_ref, stat_ref, sums_ref,
-    keep_ref, give_ref, turned,
+    h0_ref, h1_ref, far_before_ref, cot_ref, far_after_ref, stat_ref, sums_ref,
+    keep_ref, give_ref, turned, before_ref, after_ref, halo_sem,
 ):
+    fetches = [
+        pltpu.make_async_copy(far_before_ref, before_ref, halo_sem.at[0]),
+        pltpu.make_async_copy(far_after_ref, after_ref, halo_sem.at[1]),
+    ]
+    for fetch in fetches:
+        fetch.start()
     mean, scale, gain = stat_ref[0:1, :], stat_ref[1:2, :], stat_ref[2:3, :]
     for f, h_ref in enumerate((h0_ref, h1_ref)):
         for step in range(PIX // STEP):
             act = mix(h_ref, step * STEP, mean, scale, gain).astype(BF16)
             turned[:, f * PIX + step * STEP : f * PIX + (step + 1) * STEP] = act.T
     core = lax.axis_index("c")
+    for fetch in fetches:
+        fetch.wait()
     first, second = turned[:, 0:PIX], turned[:, PIX:ROWS]
     for k in range(3):
         if k == 1:
@@ -347,9 +365,11 @@
     return call(
         mixed_body,
         (shape((3 * C, 256), F32), shape((3 * C, 256), F32)),
-        (pltpu.VMEM((C, ROWS), BF16),),
+        (pltpu.VMEM((C, ROWS), BF16), pltpu.VMEM((PIX, C), BF16), pltpu.VMEM((PIX, C), BF16), pltpu.SemaphoreType.DMA((2,))),
         flops=1_500_000_000,
-    )(h0, h1, before, cot, after, stat, sums)
+        ins=[VMEM] * 2 + [FAR, VMEM, FAR] + [VMEM] * 2,
+        outs=(VMEM, VMEM),
+    )(h0, h1, in_hbm(before), cot, in_hbm(after), stat, sums)
 
 
 def temporal_body(

time: 151 us -> 153 us (1.013)
  Pallas kernels: 37 us -> 39.4 us
  waiting for transfers between devices: 30.8 us -> 32.6 us
    ppermute x4, starting transfers between devices: 10.1 us -> 8.02 us  [swap_cores(): return lax.ppermute(value, 'c', [(0, 1), (1, 0)])]
    all_to_all x1, waiting for transfers between devices: 9.22 us -> 10.8 us  [everyone_total(): return lax.all_to_all(value, PLANE, 0, 0)]
  transfers between devices with their start and end apart: 11 -> 11, of which waited for: 6 -> 6; matrix products, arithmetic and copies ran while one was open for 1% -> 1% of each run, Pallas kernels for 21% -> 22%
where the time goes in v12:
time: 153 us; the launch traced here: 152 us
  starting transfers between devices  43.6 us (28%)
  Pallas kernels  39.4 us (26%)
  waiting for transfers between devices  32.6 us (21%)
  blocking collectives  31.6 us (21%)
  local copies, waits for them, and re-layouts  2.53 us (2%)
    all_to_all x1, blocking collectives, on_device(): sums = lax.all_to_all(sums, FRAME, 0, 0)  12.4 us
    all_to_all x1, waiting for transfers between devices, everyone_gets(): return lax.all_to_all(value, PLANE, 0, 0).reshape(1024, value.shape[2])  11.8 us
    all_to_all x1, starting transfers between devices, on_device(): sums = lax.all_to_all(sums, FRAME, 0, 0)  11.4 us
    all_to_all x1, waiting for transfers between devices, everyone_total(): return lax.all_to_all(value, PLANE, 0, 0)  10.8 us
    pallas_call x1, Pallas kernels, input_gradient(): call(input_grad_body, shape((ROWS, C), BF16), (pltpu.VMEM((3 * PAD, 3 * C...  9.74 us
    all_to_all x1, blocking collectives, everyone_share(): value = jnp.sum(lax.all_to_all(value, LINE, 0, 0), axis=0).astype(BF16)  9.57 us
    all_to_all x1, blocking collectives, everyone_share(): lax.all_to_all(value, LINE, 0, 0).reshape(1024 // plane, width)  9.56 us
    ppermute x2, starting transfers between devices, neighbours(): before = lax.ppermute(second, FRAME, [(i, i + 1) for i in range(size - 1)])  8.77 us
  transfers between devices with their start and end apart: 11, of which 6 were waited for; matrix products, arithmetic and copies ran while one was open for 1% of the time, Pallas kernels for 22%

profile of v12, /device:TPU:1, one launch (start us, length us, event | category | flops | bytes accessed | tf_op | source)
XLA Modules:
  0.0 152.2 jit_solution(14445166580497958802)
XLA Ops:
  0.6 0.0 copy-start.7
  0.6 0.0 copy-start.3
  0.7 1.3 fusion
  1.9 6.5 %collective-permute-start = (bf16[512,320]{1,0:T(8,128)(2,1)S(1)}, bf16[512,320]{1,0:T(8,128)(2,1)}, u32[]{:S(2)}, u32[]{:S(2)}) collective-permute-start(bf16[512,320]{1,0:T(8,128)(2,1)S(1)} %bitcast.22), channel_id=1, source_target_pairs={{0,1},{1,2},{2,3},{3,4},{4,5},{5,6},{6,7},{7,8},{8,9},{9,10},{10,1... | collective-permute-start | bytes 983048 | tf_op jit(solution)/shard_map/ppermute | solution.py:635
  8.4 1.3 collective-permute-start.1
  9.7 0.0 copy-done.7
  9.7 0.0 copy-done.3
  9.7 0.0 copy-start
  9.7 0.0 copy-start.5
  9.7 7.3 %shard_map.93 = (bf16[512,320]{1,0:T(8,128)(2,1)S(1)}, bf16[512,320]{1,0:T(8,128)(2,1)S(1)}, bf16[960,1024]{1,0:T(8,128)(2,1)}, f32[8,320]{1,0:T(8,128)}, f32[16,2,320]{2,1,0:T(2,128)}) custom-call(bf16[1024,320]{1,0:T(8,128)(2,1)S(1)} %bitcast.17, bf16[9,320,320]{2,1,0:T(8,128)(2,1)} %bitcast.24, f32[320]{0:T(512)S(1)} %copy-done.7), custom_call_target="tpu_custom_call" | custom-call | flops 2500000000 | bytes 8000000 | tf_op jit(solution)/shard_map/pallas_call | solution.py:209
  17.0 11.4 %all-to-all-start = ((f32[16,2,320]{2,1,0:T(2,128)}), f32[16,2,320]{2,1,0:T(2,128)S(1)}, u32[]{:S(2)}, u32[]{:S(2)}) async-start(f32[16,2,320]{2,1,0:T(2,128)} %get-tuple-element.37), calls=%async_computation | async-start | bytes 98304 | tf_op jit(solution)/shard_map/all_to_all | solution.py:676
  28.4 0.0 collective-permute-done.far_before_ref
  28.5 3.0 %collective-permute-done.1.far_after_ref = bf16[512,320]{1,0:T(8,128)(2,1)} collective-permute-done((bf16[512,320]{1,0:T(8,128)(2,1)S(1)}, bf16[512,320]{1,0:T(8,128)(2,1)}, u32[]{:S(2)}, u32[]{:S(2)}) %collective-permute-start.1) | collective-permute-done | bytes 327712 | tf_op jit(solution)/shard_map/ppermute | solution.py:636
  31.4 0.0 copy-done
  31.4 0.0 copy-done.5
  31.4 3.5 %shard_map.94.far_grad_ref = bf16[1024,320]{1,0:T(8,128)(2,1)} custom-call(bf16[512,320]{1,0:T(8,128)(2,1)} %collective-permute-done.far_before_ref, bf16[1024,320]{1,0:T(8,128)(2,1)S(1)} %bitcast.14, bf16[512,320]{1,0:T(8,128)(2,1)} %collective-permute-done.1.far_after_ref, bf16[3,320,320]{2,1,0:T(8,128)(2,1)S(1)} %copy-done.5), custom_call_target="tpu_custom_call" | custom-call | flops 1500000000 | bytes 8000000 | tf_op jit(solution)/shard_map/pallas_call | solution.py:274
  34.9 2.5 %all-to-all-done.sums_ref = f32[16,2,320]{2,1,0:T(2,128)S(1)} async-done(((f32[16,2,320]{2,1,0:T(2,128)}), f32[16,2,320]{2,1,0:T(2,128)S(1)}, u32[]{:S(2)}, u32[]{:S(2)}) %all-to-all-start) | async-done | bytes 40992 | tf_op jit(solution)/shard_map/all_to_all | solution.py:676
  37.4 2.6 %collective-permute-start.2 = (bf16[960,1024]{1,0:T(8,128)(2,1)}, bf16[960,1024]{1,0:T(8,128)(2,1)S(1)}, u32[]{:S(2)}, u32[]{:S(2)}) collective-permute-start(bf16[960,1024]{1,0:T(8,128)(2,1)} %get-tuple-element.39.mine_turned_ref), channel_id=1, source_target_pairs={{0,16},{16,0},{1,17},{17,1},{2,18},{18,2},{3,19},{19,3},{4,20},{20... | collective-permute-start | bytes 5898248 | tf_op jit(solution)/shard_map/ppermute | solution.py:641
  40.0 0.0 copy-done.1
  40.0 2.6 %shard_map.95 = (f32[1024,320]{1,0:T(8,128)S(1)}, f32[8,320]{1,0:T(8,128)S(1)}, f32[16,2,320]{2,1,0:T(2,128)S(1)}, f32[8,320]{1,0:T(8,128)}) custom-call(f32[16,2,320]{2,1,0:T(2,128)S(1)} %all-to-all-done.sums_ref, bf16[512,320]{1,0:T(8,128)(2,1)S(1)} %get-tuple-element.58.h0_ref, bf16[512,320]{1,0:T(8,128)(2,1)S(1)} %get-tuple-element.57.h1_ref, ...), custom_call_target="tpu_custom_call" | custom-call | bytes 8000000 | tf_op jit(solution)/shard_map/pallas_call | solution.py:318
  42.6 12.4 %all_to_all.30.sums_ref = f32[16,2,320]{2,1,0:T(2,128)S(1)} all-to-all(f32[16,2,320]{2,1,0:T(2,128)S(1)} %get-tuple-element.44), channel_id=1, replica_groups=mesh['zl'=2,'x'=4,'c'=2,'y'=4,'zh'=4] {'y','zh'}, dimensions={0} | all-to-all | bytes 81920 | tf_op jit(solution)/shard_map/all_to_all | solution.py:681
  55.0 3.1 %shard_map.97 = (f32[960,256]{1,0:T(8,128)S(1)}, f32[960,256]{1,0:T(8,128)S(1)}) custom-call(bf16[512,320]{1,0:T(8,128)(2,1)S(1)} %get-tuple-element.58.h0_ref, bf16[512,320]{1,0:T(8,128)(2,1)S(1)} %get-tuple-element.57.h1_ref, bf16[512,320]{1,0:T(8,128)(2,1)} %collective-permute-done.far_before_ref, bf16[1024,320]{1,0:T(8,128)(2,1)S(1)} %bitcast.16, ...), custom_call_target="tpu_custom_call" | custom-call | flops 1500000000 | bytes 8000000 | tf_op jit(solution)/shard_map/pallas_call | solution.py:365
  58.2 0.0 copy-start.2
  58.2 1.4 collective-permute-start.4
  59.6 1.9 %shard_map.96 = (bf16[1024,160]{1,0:T(8,128)(2,1)S(1)}, bf16[1024,160]{1,0:T(8,128)(2,1)S(1)}, f32[8,320]{1,0:T(8,128)}) custom-call(f32[16,2,320]{2,1,0:T(2,128)S(1)} %all_to_all.30.sums_ref, f32[8,320]{1,0:T(8,128)S(1)} %get-tuple-element.45.stat_ref, f32[1024,320]{1,0:T(8,128)S(1)} %get-tuple-element.46.part_ref, ...), custom_call_target="tpu_custom_call" | custom-call | bytes 8000000 | tf_op jit(solution)/shard_map/pallas_call | solution.py:450
  61.5 0.3 collective-permute-start.3
  61.8 1.9 %collective-permute-done.3.other_ref = bf16[1024,160]{1,0:T(8,128)(2,1)S(1)} collective-permute-done((bf16[1024,160]{1,0:T(8,128)(2,1)S(1)}, bf16[1024,160]{1,0:T(8,128)(2,1)S(1)}, u32[]{:S(2)}, u32[]{:S(2)}) %collective-permute-start.3) | collective-permute-done | bytes 327712 | tf_op jit(solution)/shard_map/ppermute | solution.py:641
  63.7 0.0 collective-permute-done.4.got_ref
  63.7 0.0 collective-permute-done.2.other_turned_ref
  63.7 3.2 %shard_map.98 = bf16[1024,640]{1,0:T(8,128)(2,1)} custom-call(bf16[960,1024]{1,0:T(8,128)(2,1)S(1)} %copy-done.2, bf16[960,1024]{1,0:T(8,128)(2,1)S(1)} %collective-permute-done.2.other_turned_ref, bf16[1024,160]{1,0:T(8,128)(2,1)S(1)} %get-tuple-element.47.mine_ref, bf16[1024,160]{1,0:T(8,128)(2,1)S(1)} %collective-permute-done.3.other_ref, ...), custom_call_target="tpu_custom_call" | custom-call | flops 2500000000 | bytes 8000000 | tf_op jit(solution)/shard_map/pallas_call | solution.py:495
  66.8 0.0 copy-start.4
  66.9 4.9 %all-to-all-start.2 = ((bf16[16,64,640]{2,1,0:T(8,128)(2,1)}), bf16[16,64,640]{2,1,0:T(8,128)(2,1)}, u32[]{:S(2)}, u32[]{:S(2)}) async-start(bf16[16,64,640]{2,1,0:T(8,128)(2,1)} %bitcast.19), calls=%async_computation.2 | async-start | bytes 2621440 | tf_op jit(solution)/shard_map/all_to_all | solution.py:647
  71.8 2.3 %collective-permute-start.5 = (bf16[512,320]{1,0:T(8,128)(2,1)S(1)}, bf16[512,320]{1,0:T(8,128)(2,1)S(1)}, u32[]{:S(2)}, u32[]{:S(2)}) collective-permute-start(bf16[512,320]{1,0:T(8,128)(2,1)S(1)} %get-tuple-element.57.h1_ref), channel_id=1, source_target_pairs={{0,1},{1,2},{2,3},{3,4},{4,5},{5,6},{6,7},{7,8},{8,9},{9,10},{10,1... | collective-permute-start | bytes 983048 | tf_op jit(solution)/shard_map/ppermute | solution.py:635
  74.1 1.3 collective-permute-start.6
  75.4 9.7 %shard_map.99 = bf16[1024,320]{1,0:T(8,128)(2,1)} custom-call(f32[1024,320]{1,0:T(8,128)S(1)} %get-tuple-element.46.part_ref, bf16[512,320]{1,0:T(8,128)(2,1)S(1)} %get-tuple-element.58.h0_ref, bf16[512,320]{1,0:T(8,128)(2,1)S(1)} %get-tuple-element.57.h1_ref, f32[8,320]{1,0:T(8,128)} %get-tuple-element.53.far_clip_ref.far_stat_ref, ...), custom_call_target="tpu_custom_call" | custom-call | flops 2500000000 | bytes 8000000 | tf_op jit(solution)/shard_map/pallas_call | solution.py:579
  85.1 10.8 %all-to-all-done.2 = bf16[16,64,640]{2,1,0:T(8,128)(2,1)} async-done(((bf16[16,64,640]{2,1,0:T(8,128)(2,1)}), bf16[16,64,640]{2,1,0:T(8,128)(2,1)}, u32[]{:S(2)}, u32[]{:S(2)}) %all-to-all-start.2) | async-done | bytes 1310752 | tf_op jit(solution)/shard_map/all_to_all | solution.py:647
  95.9 1.5 convert_reduce_fusion
  97.4 9.6 %all_to_all.31 = f32[8,8,640]{2,1,0:T(8,128)S(1)} all-to-all(f32[8,8,640]{2,1,0:T(8,128)S(1)} %bitcast.20), channel_id=1, replica_groups=mesh['zl'=2,'x'=4,'c'=2,'y'=4,'zh'=4] {'zl','zh'}, dimensions={0} | all-to-all | bytes 327680 | tf_op jit(solution)/shard_map/all_to_all | solution.py:655
  107.0 0.0 collective-permute-done.5.hb_ref
  107.0 0.0 collective-permute-done.6.ha_ref
  107.0 9.6 %all_to_all.32 = bf16[8,8,640]{2,1,0:T(8,128)(2,1)S(1)} all-to-all(bf16[8,8,640]{2,1,0:T(8,128)(2,1)S(1)} %broadcast_in_dim.4), channel_id=1, replica_groups=mesh['zl'=2,'x'=4,'c'=2,'y'=4,'zh'=4] {'zl','zh'}, dimensions={0} | all-to-all | bytes 163840 | tf_op jit(solution)/shard_map/all_to_all | solution.py:658
  116.6 1.2 broadcast_in_dim.5
  117.8 7.9 %all-to-all-start.5 = ((bf16[16,64,640]{2,1,0:T(8,128)(2,1)}), bf16[16,64,640]{2,1,0:T(8,128)(2,1)S(1)}, u32[]{:S(2)}, u32[]{:S(2)}) async-start(bf16[16,64,640]{2,1,0:T(8,128)(2,1)} %broadcast_in_dim.5), calls=%async_computation.5 | async-start | bytes 2621440 | tf_op jit(solution)/shard_map/all_to_all | solution.py:664
  125.7 5.6 %shard_map.100 = bf16[1024,320]{1,0:T(8,128)(2,1)} custom-call(bf16[512,320]{1,0:T(8,128)(2,1)S(1)} %collective-permute-done.5.hb_ref, bf16[512,320]{1,0:T(8,128)(2,1)S(1)} %get-tuple-element.58.h0_ref, bf16[512,320]{1,0:T(8,128)(2,1)S(1)} %get-tuple-element.57.h1_ref, bf16[512,320]{1,0:T(8,128)(2,1)} %collective-permute-done.6.ha_ref, ...), custom_call_target="tpu_custom_call" | custom-call | flops 1500000000 | bytes 8000000 | tf_op jit(solution)/shard_map/pallas_call | solution.py:409
  131.3 11.8 %all-to-all-done.5 = bf16[16,64,640]{2,1,0:T(8,128)(2,1)S(1)} async-done(((bf16[16,64,640]{2,1,0:T(8,128)(2,1)}), bf16[16,64,640]{2,1,0:T(8,128)(2,1)S(1)}, u32[]{:S(2)}, u32[]{:S(2)}) %all-to-all-start.5) | async-done | bytes 1310752 | tf_op jit(solution)/shard_map/all_to_all | solution.py:664
  143.1 3.8 %collective-permute-start.7 = (bf16[1024,640]{1,0:T(8,128)(2,1)S(1)}, bf16[1024,640]{1,0:T(8,128)(2,1)S(1)}, u32[]{:S(2)}, u32[]{:S(2)}) collective-permute-start(bf16[1024,640]{1,0:T(8,128)(2,1)S(1)} %bitcast.12), channel_id=1, source_target_pairs={{0,16},{16,0},{1,17},{17,1},{2,18},{18,2},{3,19},{19,3},{4,20},{20... | collective-permute-start | bytes 3932168 | tf_op jit(solution)/shard_map/ppermute | solution.py:641
  146.8 2.7 %collective-permute-done.7.other_ref = bf16[1024,640]{1,0:T(8,128)(2,1)S(1)} collective-permute-done((bf16[1024,640]{1,0:T(8,128)(2,1)S(1)}, bf16[1024,640]{1,0:T(8,128)(2,1)S(1)}, u32[]{:S(2)}, u32[]{:S(2)}) %collective-permute-start.7) | collective-permute-done | bytes 1310752 | tf_op jit(solution)/shard_map/ppermute | solution.py:641
  149.5 2.6 %shard_map.101 = (bf16[9,320,320]{2,1,0:T(8,128)(2,1)}, bf16[3,320,320]{2,1,0:T(8,128)(2,1)}) custom-call(bf16[1024,640]{1,0:T(8,128)(2,1)S(1)} %bitcast.13, bf16[1024,640]{1,0:T(8,128)(2,1)S(1)} %collective-permute-done.7.other_ref), custom_call_target="tpu_custom_call" | custom-call | bytes 8000000 | tf_op jit(solution)/shard_map/pallas_call | solution.py:624
  (7 shorter events, 0.0 us)
Async XLA Ops:
  0.6 9.1 %copy-start.7 = (f32[320]{0:T(512)S(1)}, f32[320]{0:T(512)}, u32[]{:S(2)}) copy-start(f32[320]{0:T(512)} %gain_ref.2) | copy-start | bytes 3844
  0.6 9.1 %copy-start.3 = (bf16[1,2,16,32,320]{4,3,2,1,0:T(8,128)(2,1)S(1)}, bf16[1,2,16,32,320]{4,3,2,1,0:T(8,128)(2,1)}, u32[]{:S(2)}) copy-start(bf16[1,2,16,32,320]{4,3,2,1,0:T(8,128)(2,1)} %param.6) | copy-start | bytes 1966084
  1.9 26.5 %collective-permute-start = (bf16[512,320]{1,0:T(8,128)(2,1)S(1)}, bf16[512,320]{1,0:T(8,128)(2,1)}, u32[]{:S(2)}, u32[]{:S(2)}) collective-permute-start(bf16[512,320]{1,0:T(8,128)(2,1)S(1)} %bitcast.22), channel_id=1, source_target_pairs={{0,1},{1,2},{2,3},{3,4},{4,5},{5,6},{6,7},{7,8},{8,9},{9,10},{10,1... | collective-permute-start | bytes 983048 | tf_op jit(solution)/shard_map/ppermute | solution.py:635
  8.4 23.0 %collective-permute-start.1 = (bf16[512,320]{1,0:T(8,128)(2,1)S(1)}, bf16[512,320]{1,0:T(8,128)(2,1)}, u32[]{:S(2)}, u32[]{:S(2)}) collective-permute-start(bf16[512,320]{1,0:T(8,128)(2,1)S(1)} %bitcast.21), channel_id=1, source_target_pairs={{1,0},{2,1},{3,2},{4,3},{5,4},{6,5},{7,6},{8,7},{9,8},{10,9},{11,1... | collective-permute-start | bytes 983048 | tf_op jit(solution)/shard_map/ppermute | solution.py:636
  9.7 21.7 %copy-start = (bf16[1,2,16,32,320]{4,3,2,1,0:T(8,128)(2,1)S(1)}, bf16[1,2,16,32,320]{4,3,2,1,0:T(8,128)(2,1)}, u32[]{:S(2)}) copy-start(bf16[1,2,16,32,320]{4,3,2,1,0:T(8,128)(2,1)} %param.7) | copy-start | bytes 1966084
  9.7 21.7 %copy-start.5 = (bf16[3,320,320]{2,1,0:T(8,128)(2,1)S(1)}, bf16[3,320,320]{2,1,0:T(8,128)(2,1)}, u32[]{:S(2)}) copy-start(bf16[3,320,320]{2,1,0:T(8,128)(2,1)} %w_ref.3) | copy-start | bytes 1843204
  17.0 20.4 %all-to-all-start = ((f32[16,2,320]{2,1,0:T(2,128)}), f32[16,2,320]{2,1,0:T(2,128)S(1)}, u32[]{:S(2)}, u32[]{:S(2)}) async-start(f32[16,2,320]{2,1,0:T(2,128)} %get-tuple-element.37), calls=%async_computation | async-start | bytes 98304 | tf_op jit(solution)/shard_map/all_to_all | solution.py:676
  31.4 8.6 %copy-start.1 = (f32[320]{0:T(512)S(1)}, f32[320]{0:T(512)}, u32[]{:S(2)}) copy-start(f32[320]{0:T(512)} %gain_ref.3) | copy-start | bytes 3844
  37.4 26.2 %collective-permute-start.2 = (bf16[960,1024]{1,0:T(8,128)(2,1)}, bf16[960,1024]{1,0:T(8,128)(2,1)S(1)}, u32[]{:S(2)}, u32[]{:S(2)}) collective-permute-start(bf16[960,1024]{1,0:T(8,128)(2,1)} %get-tuple-element.39.mine_turned_ref), channel_id=1, source_target_pairs={{0,16},{16,0},{1,17},{17,1},{2,18},{18,2},{3,19},{19,3},{4,20},{20... | collective-permute-start | bytes 5898248 | tf_op jit(solution)/shard_map/ppermute | solution.py:641
  58.2 5.5 %copy-start.2 = (bf16[960,1024]{1,0:T(8,128)(2,1)S(1)}, bf16[960,1024]{1,0:T(8,128)(2,1)}, u32[]{:S(2)}) copy-start(bf16[960,1024]{1,0:T(8,128)(2,1)} %get-tuple-element.39.mine_turned_ref) | copy-start | bytes 5898244
  58.2 5.5 %collective-permute-start.4 = (f32[960,256]{1,0:T(8,128)S(1)}, f32[960,256]{1,0:T(8,128)S(1)}, u32[]{:S(2)}, u32[]{:S(2)}) collective-permute-start(f32[960,256]{1,0:T(8,128)S(1)} %get-tuple-element.50), channel_id=1, source_target_pairs={{0,16},{16,0},{1,17},{17,1},{2,18},{18,2},{3,19},{19,3},{4,20},{20... | collective-permute-start | bytes 2949128 | tf_op jit(solution)/shard_map/ppermute | solution.py:641
  61.5 2.2 %collective-permute-start.3 = (bf16[1024,160]{1,0:T(8,128)(2,1)S(1)}, bf16[1024,160]{1,0:T(8,128)(2,1)S(1)}, u32[]{:S(2)}, u32[]{:S(2)}) collective-permute-start(bf16[1024,160]{1,0:T(8,128)(2,1)S(1)} %get-tuple-element.48), channel_id=1, source_target_pairs={{0,16},{16,0},{1,17},{17,1},{2,18},{18,2},{3,19},{19,3},{4,20},{20... | collective-permute-start | bytes 983048 | tf_op jit(solution)/shard_map/ppermute | solution.py:641
  66.8 8.5 %copy-start.4 = (bf16[1,2,16,32,320]{4,3,2,1,0:T(8,128)(2,1)S(1)}, bf16[1,2,16,32,320]{4,3,2,1,0:T(8,128)(2,1)}, u32[]{:S(2)}) copy-start(bf16[1,2,16,32,320]{4,3,2,1,0:T(8,128)(2,1)} %param.6) | copy-start | bytes 1966084
  66.9 29.0 %all-to-all-start.2 = ((bf16[16,64,640]{2,1,0:T(8,128)(2,1)}), bf16[16,64,640]{2,1,0:T(8,128)(2,1)}, u32[]{:S(2)}, u32[]{:S(2)}) async-start(bf16[16,64,640]{2,1,0:T(8,128)(2,1)} %bitcast.19), calls=%async_computation.2 | async-start | bytes 2621440 | tf_op jit(solution)/shard_map/all_to_all | solution.py:647
  71.8 35.2 %collective-permute-start.5 = (bf16[512,320]{1,0:T(8,128)(2,1)S(1)}, bf16[512,320]{1,0:T(8,128)(2,1)S(1)}, u32[]{:S(2)}, u32[]{:S(2)}) collective-permute-start(bf16[512,320]{1,0:T(8,128)(2,1)S(1)} %get-tuple-element.57.h1_ref), channel_id=1, source_target_pairs={{0,1},{1,2},{2,3},{3,4},{4,5},{5,6},{6,7},{7,8},{8,9},{9,10},{10,1... | collective-permute-start | bytes 983048 | tf_op jit(solution)/shard_map/ppermute | solution.py:635
  74.1 32.9 %collective-permute-start.6 = (bf16[512,320]{1,0:T(8,128)(2,1)S(1)}, bf16[512,320]{1,0:T(8,128)(2,1)}, u32[]{:S(2)}, u32[]{:S(2)}) collective-permute-start(bf16[512,320]{1,0:T(8,128)(2,1)S(1)} %get-tuple-element.58.h0_ref), channel_id=1, source_target_pairs={{1,0},{2,1},{3,2},{4,3},{5,4},{6,5},{7,6},{8,7},{9,8},{10,9},{11,1... | collective-permute-start | bytes 983048 | tf_op jit(solution)/shard_map/ppermute | solution.py:636
  117.8 7.9 %copy-start.6 = (bf16[3,320,320]{2,1,0:T(8,128)(2,1)S(1)}, bf16[3,320,320]{2,1,0:T(8,128)(2,1)}, u32[]{:S(2)}) copy-start(bf16[3,320,320]{2,1,0:T(8,128)(2,1)} %w_ref.3) | copy-start | bytes 1843204
  117.8 25.3 %all-to-all-start.5 = ((bf16[16,64,640]{2,1,0:T(8,128)(2,1)}), bf16[16,64,640]{2,1,0:T(8,128)(2,1)S(1)}, u32[]{:S(2)}, u32[]{:S(2)}) async-start(bf16[16,64,640]{2,1,0:T(8,128)(2,1)} %broadcast_in_dim.5), calls=%async_computation.5 | async-start | bytes 2621440 | tf_op jit(solution)/shard_map/all_to_all | solution.py:664
  143.1 6.4 %collective-permute-start.7 = (bf16[1024,640]{1,0:T(8,128)(2,1)S(1)}, bf16[1024,640]{1,0:T(8,128)(2,1)S(1)}, u32[]{:S(2)}, u32[]{:S(2)}) collective-permute-start(bf16[1024,640]{1,0:T(8,128)(2,1)S(1)} %bitcast.12), channel_id=1, source_target_pairs={{0,16},{16,0},{1,17},{17,1},{2,18},{18,2},{3,19},{19,3},{4,20},{20... | collective-permute-start | bytes 3932168 | tf_op jit(solution)/shard_map/ppermute | solution.py:641
